TPU v7x, 32 devices: a whole 2x2x4 slice. The times are simulated.
32 devices in a mesh: runs: 2 (over y), shot: 4 (over x, core), slab: 4 (over z).
Axes of the slice: x: 2, y: 2, z: 4, core: 2. Of those that a mesh axis runs over, the one named last changes fastest.
Arguments:
- source_now: float32 [16, 64, 16, 256], P(('runs', 'shot'), 'slab'), parts along dimension 0, may hold values from -4 to 4
- source_prev: float32 [16, 64, 16, 256], P(('runs', 'shot'), 'slab'), parts along dimension 0, may hold values from -4 to 4
- receiver_now: float32 [16, 64, 16, 256], P(('runs', 'shot'), 'slab'), parts along dimension 0, may hold values from -4 to 4
- receiver_prev: float32 [16, 64, 16, 256], P(('runs', 'shot'), 'slab'), parts along dimension 0, may hold values from -4 to 4
- courant_sq: float32 [128, 16, 256], P(('runs', 'slab')), parts along dimension 0, may hold values from 0.26 to 0.52
- source_cell: int32 [16], P(('runs', 'shot')), parts along dimension 0, may hold values from 0 to 1023
- wavelet: float32 [8, 16], P(None, ('runs', 'shot')), parts along dimension 1, may hold values from -12 to 12
- receiver_cell: int32 [16, 256], P(('runs', 'shot')), parts along dimension 0, may hold values from 0 to 1023
- traces: float32 [8, 16, 256], P(None, ('runs', 'shot')), parts along dimension 1, may hold values from -10 to 10
- offset_perm: int32 [16], P('runs'), parts along dimension 0, may hold values from 0 to 7, each once
Outputs:
- offset_image: float32 [16, 64, 16, 256], P(('runs', 'shot'), 'slab'), parts along dimension 0
- source_final: float32 [16, 64, 16, 256], P(('runs', 'shot'), 'slab'), parts along dimension 0
- receiver_final: float32 [16, 64, 16, 256], P(('runs', 'shot'), 'slab'), parts along dimension 0
There are 2 independent parts, one for each index of `runs`. A program takes and returns all parts, laid end to end along the dimension named above; each array names one. Nothing has to cross between parts.
Inputs may be any that keep to these rules, and one draw needn't show every extreme that they name: `source_cell`: a surface cell index. `receiver_cell`: surface cell indices; two receivers may share a cell. `offset_perm`: every offset index appears once.
All inputs are finite; a program needn't handle non-finite values.
Results may differ from a plain program's by a relative error of at most 0.0003.
Values sent between devices are 32-bit elements; how exact they have to be, the bound alone decides.
No kernel may reach another device: no remote copies, remote signals or barrier semaphores. Data moves between devices by JAX's collectives and lax.ppermute only.
A program may use at most 64 MiB of HBM per device.

v0:
```python
import jax
import jax.numpy as jnp
from jax import lax
from jax.sharding import PartitionSpec as P

OFF_DEV = 2
STEPS = 8
INJECT_Z = 4


stencil_weights = (-205.0 / 72.0, 8.0 / 5.0, -1.0 / 5.0, 8.0 / 315.0, -1.0 / 560.0)
side_weight = 1.0 / 16.0


def extended_2(cells, sides, width):
    for axis, dim in sides:
        count = lax.axis_size(axis)
        ends = count - 1
        head = lax.slice_in_dim(cells, 0, width, axis=dim)
        tail = lax.slice_in_dim(cells, cells.shape[dim] - width, cells.shape[dim], axis=dim)
        cells = jnp.concatenate(
            [
                lax.ppermute(tail, axis, [(i, (i + 1) % count) for i in range(ends)]),
                cells,
                lax.ppermute(head, axis, [((i + 1) % count, i) for i in range(ends)]),
            ],
            axis=dim,
        )
    return cells


def laplace_rows(extended):
    row_count = extended.shape[2] - 8
    centre = extended[:, :, 4 : 4 + row_count]
    size_y = centre.shape[3]
    size_z = centre.shape[4]
    padded = jnp.pad(centre, ((0, 0), (0, 0), (0, 0), (4, 4), (4, 4)))
    summed = (1.0 + 2.0 * side_weight) * stencil_weights[0] * centre
    for distance in range(1, 5):
        weight = stencil_weights[distance]
        summed = summed + weight * (
            extended[:, :, 4 + distance : 4 + distance + row_count]
            + extended[:, :, 4 - distance : 4 - distance + row_count]
        )
        summed = summed + side_weight * weight * (
            padded[:, :, :, 4 + distance : 4 + distance + size_y, 4 : 4 + size_z]
            + padded[:, :, :, 4 - distance : 4 - distance + size_y, 4 : 4 + size_z]
        )
        summed = summed + side_weight * weight * (
            padded[:, :, :, 4 : 4 + size_y, 4 + distance : 4 + distance + size_z]
            + padded[:, :, :, 4 : 4 + size_y, 4 - distance : 4 - distance + size_z]
        )
    return summed


def hot_tables(source_cell, receiver_cell, first_row, row_count, cells_y):
    positions = lax.broadcasted_iota(jnp.int32, (1, row_count * cells_y), 1) + first_row * cells_y
    source_hot = (source_cell[:, None] == positions).astype(jnp.float32)
    receiver_hot = (receiver_cell[:, :, None] == positions[None]).astype(jnp.float32)
    return (source_hot, receiver_hot)


def correlate(source_pad, receiver_pad, shift_by, half_span, extent):
    shifted_source = lax.dynamic_slice_in_dim(source_pad, half_span - shift_by, extent, axis=2)
    shifted_receiver = lax.dynamic_slice_in_dim(receiver_pad, half_span + shift_by, extent, axis=2)
    return jnp.sum(shifted_source * shifted_receiver, axis=0)


def body(
    source_now,
    source_prev,
    receiver_now,
    receiver_prev,
    courant_sq,
    source_cell,
    wavelet,
    receiver_cell,
    traces,
    offset_perm,
):
    shots_here, rows_here, cells_y, cells_z = source_now.shape
    slab_start = lax.axis_index("slab") * rows_here
    grid_rows = rows_here * lax.axis_size("slab")
    fields = jnp.stack([source_now, receiver_now])
    before = jnp.stack([source_prev, receiver_prev])
    local_tables = hot_tables(source_cell, receiver_cell, slab_start, rows_here, cells_y)
    for moment in range(STEPS):
        extended = extended_2(fields, (("slab", 2),), 4)
        row_count = extended.shape[2] - 8
        centre = extended[:, :, 4 : 4 + row_count]
        updated = 2.0 * centre - before + courant_sq * laplace_rows(extended)
        source_hot, receiver_hot = local_tables
        source_plane = source_hot * wavelet[moment][:, None]
        receiver_plane = jnp.einsum(
            "sr,src->sc", traces[moment], receiver_hot, precision=lax.Precision.HIGHEST
        )
        planes = jnp.stack([source_plane, receiver_plane]).reshape(
            2, shots_here, row_count, cells_y
        )
        updated = updated.at[:, :, :, :, INJECT_Z].add(planes)
        global_rows = slab_start + lax.broadcasted_iota(jnp.int32, (row_count,), 0)
        inside = (global_rows >= 0) & (global_rows < grid_rows)
        updated = jnp.where(inside[None, None, :, None, None], updated, 0.0)
        before, fields = (fields, updated)
    half_span = offset_perm.shape[0] // 2
    pad_widths = ((0, 0), (0, 0), (half_span, half_span), (0, 0))
    own_lags = lax.dynamic_slice_in_dim(offset_perm, lax.axis_index("shot") * OFF_DEV, OFF_DEV)
    shard_piece = lax.all_gather(fields, "shot", axis=1, tiled=True)
    source_pad = jnp.pad(shard_piece[0], pad_widths)
    receiver_pad = jnp.pad(shard_piece[1], pad_widths)
    products = [
        correlate(source_pad, receiver_pad, own_lags[slot_index] - half_span, half_span, cells_y)
        for slot_index in range(OFF_DEV)
    ]
    offset_image = jnp.stack(products)
    return (offset_image, fields[0], fields[1])


def solution(mesh):
    in_specs = (
        P(("runs", "shot"), "slab", None, None),
        P(("runs", "shot"), "slab", None, None),
        P(("runs", "shot"), "slab", None, None),
        P(("runs", "shot"), "slab", None, None),
        P(("runs", "slab"), None, None),
        P(("runs", "shot")),
        P(None, ("runs", "shot")),
        P(("runs", "shot"), None),
        P(None, ("runs", "shot"), None),
        P("runs"),
    )
    out_specs = (
        P(("runs", "shot"), "slab", None, None),
        P(("runs", "shot"), "slab", None, None),
        P(("runs", "shot"), "slab", None, None),
    )
    return jax.shard_map(body, mesh=mesh, in_specs=in_specs, out_specs=out_specs, check_vma=False)
```

profile of v0, /device:TPU:0, one launch (start us, length us, event | category | flops | bytes accessed | tf_op | source)
XLA Modules:
  0.0 271.8 jit_solution(146948616227826346)
XLA Ops:
  7.2 1.2 fusion.362
  8.5 1.4 collective-permute-start
  9.9 5.6 %collective-permute-start.1 = (f32[2,2,4,16,256]{4,3,2,1,0:T(8,128)S(1)}, f32[2,2,4,16,256]{4,3,2,1,0:T(8,128)S(1)}, u32[]{:S(2)}, u32[]{:S(2)}) collective-permute-start(f32[2,2,4,16,256]{4,3,2,1,0:T(8,128)S(1)} %get-tuple-element.139), channel_id=1, source_target_pairs={{0,1},{1,2},{2,3},{4,5},{5,6},{6,7},{8,9},{9,10},{10,11},{12,13},{... | collective-permute-start | bytes 786440 | tf_op jit(solution)/shard_map/ppermute | solution.py:23
  17.8 2.1 collective-permute-done
  21.5 2.5 fusion.216
  25.1 5.3 %scatter-add.26 = f32[2,2,16,16,256]{4,3,2,1,0:T(8,128)S(1)} dynamic-update-slice(f32[2,2,16,16,256]{4,3,2,1,0:T(8,128)S(1)} %fusion.216, f32[2,2,16,16,1]{4,3,2,1,0:T(8,128)S(1)} %copy.241, s32[]{:T(128)} %constant.214.clone.1, s32[]{:T(128)} %constant.214.clone.1, s32[]{:T(128)} %constant.214.clone.1, s32[]{:T(128)} %constant.214.clone.1, s32[]{:T(128)} %constant.228.clone.1) | dynamic-update-slice | bytes 8196 | tf_op jit(solution)/shard_map/scatter-add | solution.py:100
  31.7 1.3 collective-permute-start.2
  33.0 5.7 %collective-permute-start.3 = (f32[2,2,4,16,256]{4,3,2,1,0:T(8,128)S(1)}, f32[2,2,4,16,256]{4,3,2,1,0:T(8,128)}, u32[]{:S(2)}, u32[]{:S(2)}) collective-permute-start(f32[2,2,4,16,256]{4,3,2,1,0:T(8,128)S(1)} %get-tuple-element.135), channel_id=1, source_target_pairs={{0,1},{1,2},{2,3},{4,5},{5,6},{6,7},{8,9},{9,10},{10,11},{12,13},{... | collective-permute-start | bytes 786440 | tf_op jit(solution)/shard_map/ppermute | solution.py:23
  39.1 2.4 collective-permute-done.2
  42.7 14.2 %fusion.186 = f32[2,2,16,16,256]{4,3,2,1,0:T(8,128)S(1)} fusion(f32[2,2,16,16,256]{4,3,2,1,0:T(8,128)} %copy-done.10, f32[2,2,4,16,256]{4,3,2,1,0:T(8,128)} %collective-permute-done.3, f32[2,2,4,16,256]{4,3,2,1,0:T(8,128)} %copy-done.13, f32[16,16,256]{2,1,0:T(8,128)S(1)} %copy-done, f32[1,2,16,16,256]{4,3,2,1,0:T(8,128)S(1)} %bitcast.77, ...), kind=kLoop, calls=%fused_computation.411 | loop fusion | flops 13107200 | bytes 3932160 | tf_op jit(solution)/shard_map/add | solution.py:91
  58.0 6.7 %scatter-add.29 = f32[2,2,16,16,256]{4,3,2,1,0:T(8,128)} dynamic-update-slice(f32[2,2,16,16,256]{4,3,2,1,0:T(8,128)} %copy-done.5, f32[2,2,16,16,1]{4,3,2,1,0:T(8,128)S(1)} %copy.244, s32[]{:T(128)} %constant.214.clone.1, s32[]{:T(128)} %constant.214.clone.1, s32[]{:T(128)} %constant.214.clone.1, s32[]{:T(128)} %constant.214.clone.1, s32[]{:T(128)} %constant.228.clone.1) | dynamic-update-slice | bytes 8196 | tf_op jit(solution)/shard_map/scatter-add | solution.py:100
  64.8 1.4 broadcast_select_fusion.6
  66.2 1.3 collective-permute-start.4
  67.5 5.1 %collective-permute-start.5 = (f32[2,2,4,16,256]{4,3,2,1,0:T(8,128)S(1)}, f32[2,2,4,16,256]{4,3,2,1,0:T(8,128)S(1)}, u32[]{:S(2)}, u32[]{:S(2)}) collective-permute-start(f32[2,2,4,16,256]{4,3,2,1,0:T(8,128)S(1)} %get-tuple-element.133), channel_id=1, source_target_pairs={{0,1},{1,2},{2,3},{4,5},{5,6},{6,7},{8,9},{9,10},{10,11},{12,13},{... | collective-permute-start | bytes 786440 | tf_op jit(solution)/shard_map/ppermute | solution.py:23
  73.1 2.2 collective-permute-done.4
  76.5 4.5 %fusion.160 = f32[2,2,16,16,256]{4,3,2,1,0:T(8,128)} fusion(f32[2,2,16,16,256]{4,3,2,1,0:T(8,128)S(1)} %broadcast_select_fusion.6, f32[2,2,4,16,256]{4,3,2,1,0:T(8,128)S(1)} %collective-permute-done.5, f32[2,2,4,16,256]{4,3,2,1,0:T(8,128)S(1)} %collective-permute-done.4, f32[16,16,256]{2,1,0:T(8,128)S(1)} %copy-done, ...), kind=kLoop, calls=%fused_computation.385 | loop fusion | flops 13107200 | bytes 3932176 | tf_op jit(solution)/shard_map/add | solution.py:91
  81.0 1.2 slice.1314
  83.1 6.7 %scatter-add.30 = f32[2,2,16,16,256]{4,3,2,1,0:T(8,128)} dynamic-update-slice(f32[2,2,16,16,256]{4,3,2,1,0:T(8,128)} %fusion.160, f32[2,2,16,16,1]{4,3,2,1,0:T(8,128)S(1)} %copy.247, s32[]{:T(128)} %constant.214.clone.1, s32[]{:T(128)} %constant.214.clone.1, s32[]{:T(128)} %constant.214.clone.1, s32[]{:T(128)} %constant.214.clone.1, s32[]{:T(128)} %constant.228.clone.1) | dynamic-update-slice | bytes 8196 | tf_op jit(solution)/shard_map/scatter-add | solution.py:100
  89.9 1.4 broadcast_select_fusion.5
  91.4 1.3 collective-permute-start.6
  92.7 5.2 %collective-permute-start.7 = (f32[2,2,4,16,256]{4,3,2,1,0:T(8,128)S(1)}, f32[2,2,4,16,256]{4,3,2,1,0:T(8,128)S(1)}, u32[]{:S(2)}, u32[]{:S(2)}) collective-permute-start(f32[2,2,4,16,256]{4,3,2,1,0:T(8,128)S(1)} %get-tuple-element.131), channel_id=1, source_target_pairs={{0,1},{1,2},{2,3},{4,5},{5,6},{6,7},{8,9},{9,10},{10,11},{12,13},{... | collective-permute-start | bytes 786440 | tf_op jit(solution)/shard_map/ppermute | solution.py:23
  98.3 1.8 collective-permute-done.6
  100.1 1.5 collective-permute-done.7
  101.5 4.5 %fusion.134 = f32[2,2,16,16,256]{4,3,2,1,0:T(8,128)} fusion(f32[2,2,16,16,256]{4,3,2,1,0:T(8,128)S(1)} %broadcast_select_fusion.5, f32[2,2,4,16,256]{4,3,2,1,0:T(8,128)S(1)} %collective-permute-done.7, f32[2,2,4,16,256]{4,3,2,1,0:T(8,128)S(1)} %collective-permute-done.6, f32[16,16,256]{2,1,0:T(8,128)S(1)} %copy-done, ...), kind=kLoop, calls=%fused_computation.359 | loop fusion | flops 13107200 | bytes 3932176 | tf_op jit(solution)/shard_map/add | solution.py:91
  106.0 1.2 slice.1329
  108.2 6.7 %scatter-add.31 = f32[2,2,16,16,256]{4,3,2,1,0:T(8,128)} dynamic-update-slice(f32[2,2,16,16,256]{4,3,2,1,0:T(8,128)} %fusion.134, f32[2,2,16,16,1]{4,3,2,1,0:T(8,128)S(1)} %copy.250, s32[]{:T(128)} %constant.214.clone.1, s32[]{:T(128)} %constant.214.clone.1, s32[]{:T(128)} %constant.214.clone.1, s32[]{:T(128)} %constant.214.clone.1, s32[]{:T(128)} %constant.228.clone.1) | dynamic-update-slice | bytes 8196 | tf_op jit(solution)/shard_map/scatter-add | solution.py:100
  114.9 1.4 broadcast_select_fusion.4
  116.4 1.3 collective-permute-start.8
  117.7 5.0 %collective-permute-start.9 = (f32[2,2,4,16,256]{4,3,2,1,0:T(8,128)S(1)}, f32[2,2,4,16,256]{4,3,2,1,0:T(8,128)S(1)}, u32[]{:S(2)}, u32[]{:S(2)}) collective-permute-start(f32[2,2,4,16,256]{4,3,2,1,0:T(8,128)S(1)} %get-tuple-element.129), channel_id=1, source_target_pairs={{0,1},{1,2},{2,3},{4,5},{5,6},{6,7},{8,9},{9,10},{10,11},{12,13},{... | collective-permute-start | bytes 786440 | tf_op jit(solution)/shard_map/ppermute | solution.py:23
  123.2 2.0 collective-permute-done.8
  125.1 1.5 collective-permute-done.9
  126.6 4.5 %fusion.108 = f32[2,2,16,16,256]{4,3,2,1,0:T(8,128)} fusion(f32[2,2,16,16,256]{4,3,2,1,0:T(8,128)S(1)} %broadcast_select_fusion.4, f32[2,2,4,16,256]{4,3,2,1,0:T(8,128)S(1)} %collective-permute-done.9, f32[2,2,4,16,256]{4,3,2,1,0:T(8,128)S(1)} %collective-permute-done.8, f32[16,16,256]{2,1,0:T(8,128)S(1)} %copy-done, ...), kind=kLoop, calls=%fused_computation.333 | loop fusion | flops 13107200 | bytes 3932176 | tf_op jit(solution)/shard_map/add | solution.py:91
  131.1 1.2 slice.1344
  133.2 6.7 %scatter-add.34 = f32[2,2,16,16,256]{4,3,2,1,0:T(8,128)} dynamic-update-slice(f32[2,2,16,16,256]{4,3,2,1,0:T(8,128)} %fusion.108, f32[2,2,16,16,1]{4,3,2,1,0:T(8,128)S(1)} %copy.253, s32[]{:T(128)} %constant.214.clone.1, s32[]{:T(128)} %constant.214.clone.1, s32[]{:T(128)} %constant.214.clone.1, s32[]{:T(128)} %constant.214.clone.1, s32[]{:T(128)} %constant.228.clone.1) | dynamic-update-slice | bytes 8196 | tf_op jit(solution)/shard_map/scatter-add | solution.py:100
  140.0 1.4 broadcast_select_fusion.3
  141.4 1.3 collective-permute-start.10
  142.7 5.0 %collective-permute-start.11 = (f32[2,2,4,16,256]{4,3,2,1,0:T(8,128)S(1)}, f32[2,2,4,16,256]{4,3,2,1,0:T(8,128)S(1)}, u32[]{:S(2)}, u32[]{:S(2)}) collective-permute-start(f32[2,2,4,16,256]{4,3,2,1,0:T(8,128)S(1)} %get-tuple-element.127), channel_id=1, source_target_pairs={{0,1},{1,2},{2,3},{4,5},{5,6},{6,7},{8,9},{9,10},{10,11},{12,13},{... | collective-permute-start | bytes 786440 | tf_op jit(solution)/shard_map/ppermute | solution.py:23
  148.2 2.0 collective-permute-done.10
  150.2 1.5 collective-permute-done.11
  151.6 4.5 %fusion.82 = f32[2,2,16,16,256]{4,3,2,1,0:T(8,128)} fusion(f32[2,2,16,16,256]{4,3,2,1,0:T(8,128)S(1)} %broadcast_select_fusion.3, f32[2,2,4,16,256]{4,3,2,1,0:T(8,128)S(1)} %collective-permute-done.11, f32[2,2,4,16,256]{4,3,2,1,0:T(8,128)S(1)} %collective-permute-done.10, f32[16,16,256]{2,1,0:T(8,128)S(1)} %copy-done, ...), kind=kLoop, calls=%fused_computation.307 | loop fusion | flops 13107200 | bytes 3932176 | tf_op jit(solution)/shard_map/add | solution.py:91
  156.1 1.2 slice.1359
  158.3 6.7 %scatter-add.35 = f32[2,2,16,16,256]{4,3,2,1,0:T(8,128)} dynamic-update-slice(f32[2,2,16,16,256]{4,3,2,1,0:T(8,128)} %fusion.82, f32[2,2,16,16,1]{4,3,2,1,0:T(8,128)S(1)} %copy.256, s32[]{:T(128)} %constant.214.clone.1, s32[]{:T(128)} %constant.214.clone.1, s32[]{:T(128)} %constant.214.clone.1, s32[]{:T(128)} %constant.214.clone.1, s32[]{:T(128)} %constant.228.clone.1) | dynamic-update-slice | bytes 8196 | tf_op jit(solution)/shard_map/scatter-add | solution.py:100
  165.0 1.4 broadcast_select_fusion.2
  166.5 1.3 collective-permute-start.12
  167.8 5.3 %collective-permute-start.13 = (f32[2,2,4,16,256]{4,3,2,1,0:T(8,128)S(1)}, f32[2,2,4,16,256]{4,3,2,1,0:T(8,128)S(1)}, u32[]{:S(2)}, u32[]{:S(2)}) collective-permute-start(f32[2,2,4,16,256]{4,3,2,1,0:T(8,128)S(1)} %get-tuple-element.125), channel_id=1, source_target_pairs={{0,1},{1,2},{2,3},{4,5},{5,6},{6,7},{8,9},{9,10},{10,11},{12,13},{... | collective-permute-start | bytes 786440 | tf_op jit(solution)/shard_map/ppermute | solution.py:23
  173.5 1.8 collective-permute-done.12
  175.2 1.5 collective-permute-done.13
  176.7 4.5 %fusion.56 = f32[2,2,16,16,256]{4,3,2,1,0:T(8,128)} fusion(f32[2,2,16,16,256]{4,3,2,1,0:T(8,128)S(1)} %broadcast_select_fusion.2, f32[2,2,4,16,256]{4,3,2,1,0:T(8,128)S(1)} %collective-permute-done.13, f32[2,2,4,16,256]{4,3,2,1,0:T(8,128)S(1)} %collective-permute-done.12, f32[16,16,256]{2,1,0:T(8,128)S(1)} %copy-done, ...), kind=kLoop, calls=%fused_computation.281 | loop fusion | flops 13107200 | bytes 3932176 | tf_op jit(solution)/shard_map/add | solution.py:91
  181.2 1.2 slice.1374
  183.3 6.7 %scatter-add.36 = f32[2,2,16,16,256]{4,3,2,1,0:T(8,128)} dynamic-update-slice(f32[2,2,16,16,256]{4,3,2,1,0:T(8,128)} %fusion.56, f32[2,2,16,16,1]{4,3,2,1,0:T(8,128)S(1)} %copy.259, s32[]{:T(128)} %constant.214.clone.1, s32[]{:T(128)} %constant.214.clone.1, s32[]{:T(128)} %constant.214.clone.1, s32[]{:T(128)} %constant.214.clone.1, s32[]{:T(128)} %constant.228.clone.1) | dynamic-update-slice | bytes 8196 | tf_op jit(solution)/shard_map/scatter-add | solution.py:100
  190.0 1.4 broadcast_select_fusion.1
  191.5 1.3 collective-permute-start.14
  192.8 5.0 %collective-permute-start.15 = (f32[2,2,4,16,256]{4,3,2,1,0:T(8,128)S(1)}, f32[2,2,4,16,256]{4,3,2,1,0:T(8,128)S(1)}, u32[]{:S(2)}, u32[]{:S(2)}) collective-permute-start(f32[2,2,4,16,256]{4,3,2,1,0:T(8,128)S(1)} %get-tuple-element.123), channel_id=1, source_target_pairs={{0,1},{1,2},{2,3},{4,5},{5,6},{6,7},{8,9},{9,10},{10,11},{12,13},{... | collective-permute-start | bytes 786440 | tf_op jit(solution)/shard_map/ppermute | solution.py:23
  198.3 2.0 collective-permute-done.14
  200.3 1.5 collective-permute-done.15
  201.7 4.5 %fusion.30 = f32[2,2,16,16,256]{4,3,2,1,0:T(8,128)} fusion(f32[2,2,16,16,256]{4,3,2,1,0:T(8,128)S(1)} %broadcast_select_fusion.1, f32[2,2,4,16,256]{4,3,2,1,0:T(8,128)S(1)} %collective-permute-done.15, f32[2,2,4,16,256]{4,3,2,1,0:T(8,128)S(1)} %collective-permute-done.14, f32[16,16,256]{2,1,0:T(8,128)S(1)} %copy-done, ...), kind=kLoop, calls=%fused_computation.255 | loop fusion | flops 13107200 | bytes 3932176 | tf_op jit(solution)/shard_map/add | solution.py:91
  206.2 1.2 slice.1389
  208.4 6.7 %scatter-add.39 = f32[2,2,16,16,256]{4,3,2,1,0:T(8,128)} dynamic-update-slice(f32[2,2,16,16,256]{4,3,2,1,0:T(8,128)} %fusion.30, f32[2,2,16,16,1]{4,3,2,1,0:T(8,128)S(1)} %copy.262, s32[]{:T(128)} %constant.214.clone.1, s32[]{:T(128)} %constant.214.clone.1, s32[]{:T(128)} %constant.214.clone.1, s32[]{:T(128)} %constant.214.clone.1, s32[]{:T(128)} %constant.228.clone.1) | dynamic-update-slice | bytes 8196 | tf_op jit(solution)/shard_map/scatter-add | solution.py:100
  215.1 2.4 broadcast_select_fusion
  224.5 30.6 %all-gather.2.cloned.1.call-done = f32[2,8,16,16,256]{4,3,2,1,0:T(8,128)} async-done(((f32[2,2,16,16,256]{4,3,2,1,0:T(8,128)}), f32[2,8,16,16,256]{4,3,2,1,0:T(8,128)}) %all-gather.2.cloned.1.call-update) | async-done | bytes 4194320 | tf_op jit(solution)/shard_map/all_gather | solution.py:108
  255.1 2.7 slice_bitcast_fusion
  257.7 1.8 fusion.1
  259.5 1.3 copy.283
  261.8 1.3 copy.284
  (135 shorter events, 22.7 us)
Async XLA Ops:
  7.2 8.4 %copy-start.9 = (f32[2,16,16,256]{3,2,1,0:T(8,128)S(1)}, f32[2,16,16,256]{3,2,1,0:T(8,128)}, u32[]{:S(2)}) copy-start(f32[2,16,16,256]{3,2,1,0:T(8,128)} %param.26) | copy-start | bytes 1572868
  7.2 8.4 %copy-start.8 = (f32[2,16,16,256]{3,2,1,0:T(8,128)S(1)}, f32[2,16,16,256]{3,2,1,0:T(8,128)}, u32[]{:S(2)}) copy-start(f32[2,16,16,256]{3,2,1,0:T(8,128)} %param.28) | copy-start | bytes 1572868
  7.2 247.9 %all-gather.2.cloned.1.call-start = ((), (), s32[]{:S(2)}) async-start(), calls=%async_computation | async-start | bytes 5242880 | tf_op jit(solution)/shard_map/all_gather | solution.py:108
  8.5 7.2 %copy-start.14 = (f32[8,2]{0,1:T(2,128)S(1)}, f32[8,2]{0,1:T(2,128)}, u32[]{:S(2)}) copy-start(f32[8,2]{0,1:T(2,128)} %param.32) | copy-start | bytes 196
  8.5 7.5 %copy-start.16 = (f32[8,2,256]{2,1,0:T(2,128)S(1)}, f32[8,2,256]{2,1,0:T(2,128)}, u32[]{:S(2)}) copy-start(f32[8,2,256]{2,1,0:T(2,128)} %param.34) | copy-start | bytes 49156
  8.5 8.1 %copy-start.22 = (s32[2,256]{1,0:T(2,128)S(1)}, s32[2,256]{1,0:T(2,128)}, u32[]{:S(2)}) copy-start(s32[2,256]{1,0:T(2,128)} %param.33) | copy-start | bytes 6148
  8.5 9.2 %copy-start.21 = (s32[2]{0:T(128)S(1)}, s32[2]{0:T(128)}, u32[]{:S(2)}) copy-start(s32[2]{0:T(128)} %param.31) | copy-start | bytes 28
  8.5 11.4 %collective-permute-start = (f32[2,2,4,16,256]{4,3,2,1,0:T(8,128)S(1)}, f32[2,2,4,16,256]{4,3,2,1,0:T(8,128)S(1)}, u32[]{:S(2)}, u32[]{:S(2)}) collective-permute-start(f32[2,2,4,16,256]{4,3,2,1,0:T(8,128)S(1)} %get-tuple-element.138), channel_id=1, source_target_pairs={{1,0},{2,1},{3,2},{5,4},{6,5},{7,6},{9,8},{10,9},{11,10},{13,12},{... | collective-permute-start | bytes 786440 | tf_op jit(solution)/shard_map/ppermute | solution.py:25
  9.9 11.1 %collective-permute-start.1 = (f32[2,2,4,16,256]{4,3,2,1,0:T(8,128)S(1)}, f32[2,2,4,16,256]{4,3,2,1,0:T(8,128)S(1)}, u32[]{:S(2)}, u32[]{:S(2)}) collective-permute-start(f32[2,2,4,16,256]{4,3,2,1,0:T(8,128)S(1)} %get-tuple-element.139), channel_id=1, source_target_pairs={{0,1},{1,2},{2,3},{4,5},{5,6},{6,7},{8,9},{9,10},{10,11},{12,13},{... | collective-permute-start | bytes 786440 | tf_op jit(solution)/shard_map/ppermute | solution.py:23
  15.7 2.0 copy-start.26
  17.7 3.7 %copy-start = (f32[16,16,256]{2,1,0:T(8,128)S(1)}, f32[16,16,256]{2,1,0:T(8,128)}, u32[]{:S(2)}) copy-start(f32[16,16,256]{2,1,0:T(8,128)} %param.30) | copy-start | bytes 786436
  17.8 3.7 %copy-start.11 = (f32[2,16,16,256]{3,2,1,0:T(8,128)S(1)}, f32[2,16,16,256]{3,2,1,0:T(8,128)}, u32[]{:S(2)}) copy-start(f32[2,16,16,256]{3,2,1,0:T(8,128)} %param.29) | copy-start | bytes 1572868
  17.8 3.7 %copy-start.12 = (f32[2,16,16,256]{3,2,1,0:T(8,128)S(1)}, f32[2,16,16,256]{3,2,1,0:T(8,128)}, u32[]{:S(2)}) copy-start(f32[2,16,16,256]{3,2,1,0:T(8,128)} %param.27) | copy-start | bytes 1572868
  23.9 0.7 copy-start.15
  30.5 8.2 %copy-start.20 = (f32[2,256,1]{1,0,2:T(2,128)S(1)}, f32[2,256,1]{1,0,2:T(2,128)}, u32[]{:S(2)}) copy-start(f32[2,256,1]{1,0,2:T(2,128)} %get-tuple-element.145) | copy-start | bytes 6148
  30.5 8.2 %copy-start.23 = (s32[2,256]{1,0:T(2,128)S(1)}, s32[2,256]{1,0:T(2,128)}, u32[]{:S(2)}) copy-start(s32[2,256]{1,0:T(2,128)} %param.33) | copy-start | bytes 6148
  30.5 8.2 %copy-start.27 = (s32[256]{0:T(256)S(1)}, s32[256]{0:T(256)}, u32[]{:S(2)}) copy-start(s32[256]{0:T(256)} %copy-done.26) | copy-start | bytes 3076
  30.6 1.0 copy-start.10
  31.7 9.8 %collective-permute-start.2 = (f32[2,2,4,16,256]{4,3,2,1,0:T(8,128)S(1)}, f32[2,2,4,16,256]{4,3,2,1,0:T(8,128)S(1)}, u32[]{:S(2)}, u32[]{:S(2)}) collective-permute-start(f32[2,2,4,16,256]{4,3,2,1,0:T(8,128)S(1)} %get-tuple-element.134), channel_id=1, source_target_pairs={{1,0},{2,1},{3,2},{5,4},{6,5},{7,6},{9,8},{10,9},{11,10},{13,12},{... | collective-permute-start | bytes 786440 | tf_op jit(solution)/shard_map/ppermute | solution.py:25
  33.0 9.7 %collective-permute-start.3 = (f32[2,2,4,16,256]{4,3,2,1,0:T(8,128)S(1)}, f32[2,2,4,16,256]{4,3,2,1,0:T(8,128)}, u32[]{:S(2)}, u32[]{:S(2)}) collective-permute-start(f32[2,2,4,16,256]{4,3,2,1,0:T(8,128)S(1)} %get-tuple-element.135), channel_id=1, source_target_pairs={{0,1},{1,2},{2,3},{4,5},{5,6},{6,7},{8,9},{9,10},{10,11},{12,13},{... | collective-permute-start | bytes 786440 | tf_op jit(solution)/shard_map/ppermute | solution.py:23
  41.5 0.7 copy-start.13
  56.9 1.1 copy-start.5
  64.8 7.9 %copy-start.19 = (f32[2,256,1]{1,0,2:T(2,128)S(1)}, f32[2,256,1]{1,0,2:T(2,128)}, u32[]{:S(2)}) copy-start(f32[2,256,1]{1,0,2:T(2,128)} %get-tuple-element.144) | copy-start | bytes 6148
  64.8 7.9 %copy-start.24 = (s32[2,256]{1,0:T(2,128)S(1)}, s32[2,256]{1,0:T(2,128)}, u32[]{:S(2)}) copy-start(s32[2,256]{1,0:T(2,128)} %param.33) | copy-start | bytes 6148
  64.8 7.9 %copy-start.28 = (s32[256]{0:T(256)S(1)}, s32[256]{0:T(256)}, u32[]{:S(2)}) copy-start(s32[256]{0:T(256)} %copy-done.26) | copy-start | bytes 3076
  66.2 9.1 %collective-permute-start.4 = (f32[2,2,4,16,256]{4,3,2,1,0:T(8,128)S(1)}, f32[2,2,4,16,256]{4,3,2,1,0:T(8,128)S(1)}, u32[]{:S(2)}, u32[]{:S(2)}) collective-permute-start(f32[2,2,4,16,256]{4,3,2,1,0:T(8,128)S(1)} %get-tuple-element.132), channel_id=1, source_target_pairs={{1,0},{2,1},{3,2},{5,4},{6,5},{7,6},{9,8},{10,9},{11,10},{13,12},{... | collective-permute-start | bytes 786440 | tf_op jit(solution)/shard_map/ppermute | solution.py:25
  67.5 9.0 %collective-permute-start.5 = (f32[2,2,4,16,256]{4,3,2,1,0:T(8,128)S(1)}, f32[2,2,4,16,256]{4,3,2,1,0:T(8,128)S(1)}, u32[]{:S(2)}, u32[]{:S(2)}) collective-permute-start(f32[2,2,4,16,256]{4,3,2,1,0:T(8,128)S(1)} %get-tuple-element.133), channel_id=1, source_target_pairs={{0,1},{1,2},{2,3},{4,5},{5,6},{6,7},{8,9},{9,10},{10,11},{12,13},{... | collective-permute-start | bytes 786440 | tf_op jit(solution)/shard_map/ppermute | solution.py:23
  89.8 8.0 %copy-start.18 = (f32[2,256,1]{1,0,2:T(2,128)S(1)}, f32[2,256,1]{1,0,2:T(2,128)}, u32[]{:S(2)}) copy-start(f32[2,256,1]{1,0,2:T(2,128)} %get-tuple-element.143) | copy-start | bytes 6148
  89.9 11.7 %copy-start.6 = (f32[2,2,16,16,256]{4,3,2,1,0:T(8,128)S(1)}, f32[2,2,16,16,256]{4,3,2,1,0:T(8,128)}, u32[]{:S(2)}) copy-start(f32[2,2,16,16,256]{4,3,2,1,0:T(8,128)} %scatter-add.29) | copy-start | bytes 3145732
  91.4 8.7 %collective-permute-start.6 = (f32[2,2,4,16,256]{4,3,2,1,0:T(8,128)S(1)}, f32[2,2,4,16,256]{4,3,2,1,0:T(8,128)S(1)}, u32[]{:S(2)}, u32[]{:S(2)}) collective-permute-start(f32[2,2,4,16,256]{4,3,2,1,0:T(8,128)S(1)} %get-tuple-element.130), channel_id=1, source_target_pairs={{1,0},{2,1},{3,2},{5,4},{6,5},{7,6},{9,8},{10,9},{11,10},{13,12},{... | collective-permute-start | bytes 786440 | tf_op jit(solution)/shard_map/ppermute | solution.py:25
  92.7 8.9 %collective-permute-start.7 = (f32[2,2,4,16,256]{4,3,2,1,0:T(8,128)S(1)}, f32[2,2,4,16,256]{4,3,2,1,0:T(8,128)S(1)}, u32[]{:S(2)}, u32[]{:S(2)}) collective-permute-start(f32[2,2,4,16,256]{4,3,2,1,0:T(8,128)S(1)} %get-tuple-element.131), channel_id=1, source_target_pairs={{0,1},{1,2},{2,3},{4,5},{5,6},{6,7},{8,9},{9,10},{10,11},{12,13},{... | collective-permute-start | bytes 786440 | tf_op jit(solution)/shard_map/ppermute | solution.py:23
  114.9 7.8 %copy-start.17 = (f32[2,256,1]{1,0,2:T(2,128)S(1)}, f32[2,256,1]{1,0,2:T(2,128)}, u32[]{:S(2)}) copy-start(f32[2,256,1]{1,0,2:T(2,128)} %get-tuple-element.142) | copy-start | bytes 6148
  114.9 11.7 %copy-start.1 = (f32[2,2,16,16,256]{4,3,2,1,0:T(8,128)S(1)}, f32[2,2,16,16,256]{4,3,2,1,0:T(8,128)}, u32[]{:S(2)}) copy-start(f32[2,2,16,16,256]{4,3,2,1,0:T(8,128)} %scatter-add.30) | copy-start | bytes 3145732
  116.4 8.7 %collective-permute-start.8 = (f32[2,2,4,16,256]{4,3,2,1,0:T(8,128)S(1)}, f32[2,2,4,16,256]{4,3,2,1,0:T(8,128)S(1)}, u32[]{:S(2)}, u32[]{:S(2)}) collective-permute-start(f32[2,2,4,16,256]{4,3,2,1,0:T(8,128)S(1)} %get-tuple-element.128), channel_id=1, source_target_pairs={{1,0},{2,1},{3,2},{5,4},{6,5},{7,6},{9,8},{10,9},{11,10},{13,12},{... | collective-permute-start | bytes 786440 | tf_op jit(solution)/shard_map/ppermute | solution.py:25
  117.7 8.9 %collective-permute-start.9 = (f32[2,2,4,16,256]{4,3,2,1,0:T(8,128)S(1)}, f32[2,2,4,16,256]{4,3,2,1,0:T(8,128)S(1)}, u32[]{:S(2)}, u32[]{:S(2)}) collective-permute-start(f32[2,2,4,16,256]{4,3,2,1,0:T(8,128)S(1)} %get-tuple-element.129), channel_id=1, source_target_pairs={{0,1},{1,2},{2,3},{4,5},{5,6},{6,7},{8,9},{9,10},{10,11},{12,13},{... | collective-permute-start | bytes 786440 | tf_op jit(solution)/shard_map/ppermute | solution.py:23
  139.9 11.7 %copy-start.2 = (f32[2,2,16,16,256]{4,3,2,1,0:T(8,128)S(1)}, f32[2,2,16,16,256]{4,3,2,1,0:T(8,128)}, u32[]{:S(2)}) copy-start(f32[2,2,16,16,256]{4,3,2,1,0:T(8,128)} %scatter-add.31) | copy-start | bytes 3145732
  141.4 8.7 %collective-permute-start.10 = (f32[2,2,4,16,256]{4,3,2,1,0:T(8,128)S(1)}, f32[2,2,4,16,256]{4,3,2,1,0:T(8,128)S(1)}, u32[]{:S(2)}, u32[]{:S(2)}) collective-permute-start(f32[2,2,4,16,256]{4,3,2,1,0:T(8,128)S(1)} %get-tuple-element.126), channel_id=1, source_target_pairs={{1,0},{2,1},{3,2},{5,4},{6,5},{7,6},{9,8},{10,9},{11,10},{13,12},{... | collective-permute-start | bytes 786440 | tf_op jit(solution)/shard_map/ppermute | solution.py:25
  142.7 8.9 %collective-permute-start.11 = (f32[2,2,4,16,256]{4,3,2,1,0:T(8,128)S(1)}, f32[2,2,4,16,256]{4,3,2,1,0:T(8,128)S(1)}, u32[]{:S(2)}, u32[]{:S(2)}) collective-permute-start(f32[2,2,4,16,256]{4,3,2,1,0:T(8,128)S(1)} %get-tuple-element.127), channel_id=1, source_target_pairs={{0,1},{1,2},{2,3},{4,5},{5,6},{6,7},{8,9},{9,10},{10,11},{12,13},{... | collective-permute-start | bytes 786440 | tf_op jit(solution)/shard_map/ppermute | solution.py:23
  165.0 11.7 %copy-start.3 = (f32[2,2,16,16,256]{4,3,2,1,0:T(8,128)S(1)}, f32[2,2,16,16,256]{4,3,2,1,0:T(8,128)}, u32[]{:S(2)}) copy-start(f32[2,2,16,16,256]{4,3,2,1,0:T(8,128)} %scatter-add.34) | copy-start | bytes 3145732
  166.5 8.7 %collective-permute-start.12 = (f32[2,2,4,16,256]{4,3,2,1,0:T(8,128)S(1)}, f32[2,2,4,16,256]{4,3,2,1,0:T(8,128)S(1)}, u32[]{:S(2)}, u32[]{:S(2)}) collective-permute-start(f32[2,2,4,16,256]{4,3,2,1,0:T(8,128)S(1)} %get-tuple-element.124), channel_id=1, source_target_pairs={{1,0},{2,1},{3,2},{5,4},{6,5},{7,6},{9,8},{10,9},{11,10},{13,12},{... | collective-permute-start | bytes 786440 | tf_op jit(solution)/shard_map/ppermute | solution.py:25
  167.8 8.9 %collective-permute-start.13 = (f32[2,2,4,16,256]{4,3,2,1,0:T(8,128)S(1)}, f32[2,2,4,16,256]{4,3,2,1,0:T(8,128)S(1)}, u32[]{:S(2)}, u32[]{:S(2)}) collective-permute-start(f32[2,2,4,16,256]{4,3,2,1,0:T(8,128)S(1)} %get-tuple-element.125), channel_id=1, source_target_pairs={{0,1},{1,2},{2,3},{4,5},{5,6},{6,7},{8,9},{9,10},{10,11},{12,13},{... | collective-permute-start | bytes 786440 | tf_op jit(solution)/shard_map/ppermute | solution.py:23
  190.0 11.7 %copy-start.4 = (f32[2,2,16,16,256]{4,3,2,1,0:T(8,128)S(1)}, f32[2,2,16,16,256]{4,3,2,1,0:T(8,128)}, u32[]{:S(2)}) copy-start(f32[2,2,16,16,256]{4,3,2,1,0:T(8,128)} %scatter-add.35) | copy-start | bytes 3145732
  191.5 8.7 %collective-permute-start.14 = (f32[2,2,4,16,256]{4,3,2,1,0:T(8,128)S(1)}, f32[2,2,4,16,256]{4,3,2,1,0:T(8,128)S(1)}, u32[]{:S(2)}, u32[]{:S(2)}) collective-permute-start(f32[2,2,4,16,256]{4,3,2,1,0:T(8,128)S(1)} %get-tuple-element.122), channel_id=1, source_target_pairs={{1,0},{2,1},{3,2},{5,4},{6,5},{7,6},{9,8},{10,9},{11,10},{13,12},{... | collective-permute-start | bytes 786440 | tf_op jit(solution)/shard_map/ppermute | solution.py:25
  192.8 8.9 %collective-permute-start.15 = (f32[2,2,4,16,256]{4,3,2,1,0:T(8,128)S(1)}, f32[2,2,4,16,256]{4,3,2,1,0:T(8,128)S(1)}, u32[]{:S(2)}, u32[]{:S(2)}) collective-permute-start(f32[2,2,4,16,256]{4,3,2,1,0:T(8,128)S(1)} %get-tuple-element.123), channel_id=1, source_target_pairs={{0,1},{1,2},{2,3},{4,5},{5,6},{6,7},{8,9},{9,10},{10,11},{12,13},{... | collective-permute-start | bytes 786440 | tf_op jit(solution)/shard_map/ppermute | solution.py:23
  215.1 2.4 copy-start.25
  217.5 5.9 %copy-start.7 = (f32[2,2,16,16,256]{4,3,2,1,0:T(8,128)S(1)}, f32[2,2,16,16,256]{4,3,2,1,0:T(8,128)}, u32[]{:S(2)}) copy-start(f32[2,2,16,16,256]{4,3,2,1,0:T(8,128)} %broadcast_select_fusion) | copy-start | bytes 3145732
Sparse Core Ops, SparseCore 0:
  217.7 37.3 all-gather.1
where the time goes:
time: 273 us; the launch traced here: 272 us
  local copies, waits for them, and re-layouts  80.7 us (30%)
  other arithmetic  59.1 us (22%)
  waiting for transfers between devices  57 us (21%)
  starting transfers between devices  52.5 us (19%)
  between operations  19.9 us (7%)
    scatter-add x8, local copies, waits for them, and re-layouts, body(): updated = updated.at[:, :, :, :, INJECT_Z].add(planes)  52.5 us
    add x8, other arithmetic, body(): updated = 2.0 * centre - before + courant_sq * laplace_rows(extended)  43.4 us
    ppermute x8, starting transfers between devices, extended_2(): lax.ppermute(tail, axis, [(i, (i + 1) % count) for i in range(ends)])  42 us
    all_gather x1, waiting for transfers between devices, body(): shard_piece = lax.all_gather(fields, 'shot', axis=1, tiled=True)  30.6 us
    ppermute x8, waiting for transfers between devices, extended_2(): lax.ppermute(head, axis, [((i + 1) % count, i) for i in range(ends)])  16.2 us
    another operation x16, local copies, waits for them, and re-layouts  11.3 us
    select_n x8, other arithmetic, body(): updated = jnp.where(inside[None, None, :, None, None], updated, 0.0)  11.2 us
    ppermute x8, starting transfers between devices, extended_2(): lax.ppermute(head, axis, [((i + 1) % count, i) for i in range(ends)])  10.5 us
  transfers between devices with their start and end apart: 17, of which 17 were waited for; matrix products, arithmetic and copies ran while one was open for 2% of the time, Pallas kernels for 0%

commit v1 on v0

v1 whole, which is shorter than its diff:
```python
import functools

import jax
import jax.numpy as jnp
from jax import lax
from jax.experimental import pallas as pl
from jax.experimental.pallas import tpu as pltpu
from jax.sharding import PartitionSpec as P

REACH = 4
INJECT_Z = 4
LANES = 128
CHUNK = 8

SCALE = 8.0 / 5.0
SIDE = 1.0 / 16.0
OWN = (1.0 + 2.0 * SIDE) * (-205.0 / 72.0) / SCALE
TAPS = (1.0, -1.0 / 8.0, 1.0 / 63.0, -1.0 / 896.0)

VMEM_LIMIT = 24 * 1024 * 1024


def vmem():
    return pl.BlockSpec(memory_space=pltpu.VMEM)


def smem():
    return pl.BlockSpec(memory_space=pltpu.SMEM)


def hbm():
    return pl.BlockSpec(memory_space=pl.ANY)


def params():
    return pltpu.CompilerParams(vmem_limit_bytes=VMEM_LIMIT)


def struct(shape, dtype=jnp.float32):
    return jax.ShapeDtypeStruct(shape, dtype)


def even_pairs(count):
    pairs = []
    for i in range(0, count - 1, 2):
        pairs += [(i, i + 1), (i + 1, i)]
    return pairs


def odd_pairs(count):
    pairs = []
    for i in range(1, count - 1, 2):
        pairs += [(i, i + 1), (i + 1, i)]
    return pairs


def trade(even_edge, odd_edge):
    count = lax.axis_size("slab")
    return (
        lax.ppermute(even_edge, "slab", even_pairs(count)),
        lax.ppermute(odd_edge, "slab", odd_pairs(count)),
    )


def parity():
    return lax.rem(lax.axis_index("slab"), 2)


def edge_starts(rows, width):
    odd = parity()
    return (1 - odd) * (rows - width), odd * (rows - width)


def halo_starts(rows, width):
    odd = parity()
    return (1 - odd) * (rows + width), odd * (rows + width)


def pack_kernel(groups, rows, *refs):
    source, receiver, courant = refs[:3]
    outs = refs[3 : 3 + 2 * groups]
    sem = refs[-1]
    copies = []
    for side, start in enumerate(edge_starts(rows, REACH)):
        planes = pl.ds(start, REACH)
        for group in range(groups):
            out = outs[2 * group + side]
            pieces = [source.at[group, planes], receiver.at[group, planes]]
            if group == 0:
                pieces.append(courant.at[planes])
            for index, piece in enumerate(pieces):
                copies.append(pltpu.make_async_copy(piece, out.at[index], sem.at[len(copies)]))
    for copy in copies:
        copy.start()
    for copy in copies:
        copy.wait()


def pack(source_now, receiver_now, courant_sq):
    groups, rows, size_y, size_z = source_now.shape
    shapes = []
    for group in range(groups):
        shapes += [struct((3 if group == 0 else 2, REACH, size_y, size_z))] * 2
    return pl.pallas_call(
        functools.partial(pack_kernel, groups, rows),
        out_shape=shapes,
        in_specs=[hbm()] * 3,
        out_specs=[vmem()] * len(shapes),
        scratch_shapes=[pltpu.SemaphoreType.DMA((2 * (2 * groups + 1),))],
        compiler_params=params(),
        name="pack",
    )(source_now, receiver_now, courant_sq)


def band(distance):
    value = jnp.zeros(distance.shape, jnp.float32)
    for step, tap in enumerate(TAPS):
        value = jnp.where(distance == step + 1, SIDE * tap, value)
    return value


def prepare_kernel(rows, source_cell, wavelet, receiver_cell, traces, along_z, along_y, *planes):
    groups = len(planes)
    _, plane_count, size_y, _ = planes[0].shape
    steps = traces.shape[0]
    size_z = along_z.shape[0]
    block = along_y.shape[0]
    row = lax.broadcasted_iota(jnp.int32, (size_z, size_z), 0)
    col = lax.broadcasted_iota(jnp.int32, (size_z, size_z), 1)
    along_z[...] = band(jnp.abs(row - col)).astype(jnp.bfloat16)
    row = lax.broadcasted_iota(jnp.int32, (block, block), 0)
    col = lax.broadcasted_iota(jnp.int32, (block, block), 1)
    same = lax.div(row, size_y) == lax.div(col, size_y)
    half = jnp.where(same, band(jnp.abs(row - col)), 0.0).astype(jnp.bfloat16)
    along_y[:, :block] = half
    along_y[:, block:] = half
    first = (lax.axis_index("slab") * rows - REACH) * size_y
    cells = plane_count * size_y
    lane = lax.broadcasted_iota(jnp.int32, (1, LANES), 1)
    for group in range(groups):
        ids = first + lax.broadcasted_iota(jnp.int32, (cells, 1), 0)
        amplitude = jnp.zeros((1, LANES), jnp.float32)
        for step in range(steps):
            amplitude = jnp.where(lane == step, wavelet[step, group], amplitude)
        hit = jnp.broadcast_to(ids, (cells, LANES)) == source_cell[group]
        spread = jnp.where(hit, jnp.broadcast_to(amplitude, (cells, LANES)), 0.0)
        planes[group][0] = spread.reshape(plane_count, size_y, LANES)
        count = receiver_cell.shape[1]
        wide = first + lax.broadcasted_iota(jnp.int32, (cells, count), 0)
        here = jnp.broadcast_to(receiver_cell[group : group + 1, :], (cells, count))
        hot = (wide == here).astype(jnp.float32)
        data = traces[:, group, :]
        data = jnp.concatenate([data, jnp.zeros((LANES - steps, count), jnp.float32)], axis=0)
        summed = lax.dot_general(
            hot,
            data,
            (((1,), (1,)), ((), ())),
            precision=lax.Precision.HIGHEST,
            preferred_element_type=jnp.float32,
        )
        planes[group][1] = summed.reshape(plane_count, size_y, LANES)


def prepare(source_cell, wavelet, receiver_cell, traces, rows, size_y, size_z):
    groups = source_cell.shape[0]
    block = CHUNK * size_y
    return pl.pallas_call(
        functools.partial(prepare_kernel, rows),
        out_shape=[
            struct((size_z, size_z), jnp.bfloat16),
            struct((block, 2 * block), jnp.bfloat16),
        ]
        + [struct((2, rows + 2 * REACH, size_y, LANES))] * groups,
        in_specs=[smem(), smem(), vmem(), vmem()],
        out_specs=[vmem()] * (2 + groups),
        compiler_params=params(),
        name="prepare",
    )(source_cell, wavelet, receiver_cell, traces)


def advance(now, first, before, before_first, courant, courant_first, inject, inject_first, step, along_z, along_y, write):
    size_y, size_z = now.shape[-2:]
    value = now[first : first + CHUNK].reshape(CHUNK * size_y, size_z)
    high = value.astype(jnp.bfloat16)
    low = (value - high.astype(jnp.float32)).astype(jnp.bfloat16)
    dot = functools.partial(jnp.dot, preferred_element_type=jnp.float32)
    sides = dot(high, along_z) + dot(low, along_z)
    sides = sides + dot(along_y, jnp.concatenate([high, low], axis=0))
    lane = lax.broadcasted_iota(jnp.int32, (size_y, LANES), 1)
    for i in range(CHUNK):
        at = first + i
        own = now[at]
        total = sides[i * size_y : (i + 1) * size_y] + OWN * own
        for distance, tap in enumerate(TAPS, 1):
            pair = now[at + distance] + now[at - distance]
            total = total + (pair if tap == 1.0 else tap * pair)
        new = (own + own) - before[before_first + i] + courant[courant_first + i] * total
        spot = pltpu.roll(inject[inject_first + i], (INJECT_Z - step) % LANES, 1)
        near = new[:, :LANES] + jnp.where(lane == INJECT_Z, spot, 0.0)
        write(i, jnp.concatenate([near, new[:, LANES:]], axis=1))


def first_kernel(group, rows, has_courant, width, source, receiver, source_before, receiver_before, courant, even, odd, inject, along_z, along_y, *refs):
    fresh, held, even_edge, odd_edge = refs[:4]
    before, sem = refs[-2:]
    copies = []
    for kind, (own, past) in enumerate(((source, source_before), (receiver, receiver_before))):
        copies.append(pltpu.make_async_copy(own.at[group], held.at[kind, pl.ds(REACH, rows)], sem.at[2 * kind]))
        copies.append(pltpu.make_async_copy(past.at[group], before.at[kind], sem.at[2 * kind + 1]))
    for copy in copies:
        copy.start()
    even_at, odd_at = halo_starts(rows, REACH)
    if has_courant:
        scaled = refs[4]
        scaled[REACH : REACH + rows] = SCALE * courant[...]
        scaled[pl.ds(even_at, REACH)] = SCALE * even[2]
        scaled[pl.ds(odd_at, REACH)] = SCALE * odd[2]
    else:
        scaled = courant
    z_band, y_band = along_z[...], along_y[...]
    for kind in range(2):
        field = held.at[kind]
        field[pl.ds(even_at, REACH)] = even[kind]
        field[pl.ds(odd_at, REACH)] = odd[kind]
        copies[2 * kind].wait()
        copies[2 * kind + 1].wait()
        for at in range(0, rows, CHUNK):

            def write(i, new, kind=kind, at=at):
                fresh[kind, at + i] = new

            advance(field, REACH + at, before.at[kind], at, scaled, REACH + at, inject.at[kind], REACH + at, 0, z_band, y_band, write)
    send(rows, width, fresh, even_edge, odd_edge)


def send(rows, width, fresh, even_edge, odd_edge):
    even_from, odd_from = edge_starts(rows, width)
    even_edge[...] = fresh[:, pl.ds(even_from, width)]
    odd_edge[...] = fresh[:, pl.ds(odd_from, width)]


def first_round(group, width, fields, courant, halos, inject, along_z, along_y):
    rows, size_y, size_z = fields[0].shape[1:]
    has_courant = group == 0
    edge = struct((2, width, size_y, size_z))
    shapes = [struct((2, rows, size_y, size_z)), struct((2, rows + 2 * REACH, size_y, size_z)), edge, edge]
    if has_courant:
        shapes.append(struct((rows + 2 * REACH, size_y, size_z)))
    return pl.pallas_call(
        functools.partial(first_kernel, group, rows, has_courant, width),
        out_shape=shapes,
        in_specs=[hbm()] * 4 + [vmem()] * 6,
        out_specs=[vmem()] * len(shapes),
        scratch_shapes=[pltpu.VMEM((2, rows, size_y, size_z), jnp.float32), pltpu.SemaphoreType.DMA((4,))],
        compiler_params=params(),
        name=f"first_{group}",
    )(*fields, courant, *halos, inject, along_z, along_y)


def pair_kernel(rows, step, width, now, before, even, odd, courant, inject, along_z, along_y, fresh, held, even_edge, odd_edge, wide):
    reach = 2 * REACH
    even_at, odd_at = halo_starts(rows, reach)
    z_band, y_band = along_z[...], along_y[...]
    for kind in range(2):
        field = wide.at[kind]
        field[reach : reach + rows] = now[kind]
        field[pl.ds(even_at, reach)] = even[kind]
        field[pl.ds(odd_at, reach)] = odd[kind]
        middle = held.at[kind]
        for at in range(0, rows + 2 * REACH, CHUNK):

            def write_middle(i, new, kind=kind, at=at):
                held[kind, at + i] = new

            advance(field, REACH + at, before.at[kind], at, courant, at, inject.at[kind], at, step, z_band, y_band, write_middle)
        for at in range(0, rows, CHUNK):

            def write(i, new, kind=kind, at=at):
                fresh[kind, at + i] = new

            advance(middle, REACH + at, field, reach + at, courant, REACH + at, inject.at[kind], REACH + at, step + 1, z_band, y_band, write)
    send(rows, width, fresh, even_edge, odd_edge)


def pair_round(group, step, width, now, before, halos, courant, inject, along_z, along_y):
    rows, size_y, size_z = now.shape[1:]
    edge = struct((2, width, size_y, size_z))
    shapes = [struct(now.shape), struct((2, rows + 2 * REACH, size_y, size_z)), edge, edge]
    return pl.pallas_call(
        functools.partial(pair_kernel, rows, step, width),
        out_shape=shapes,
        in_specs=[vmem()] * 8,
        out_specs=[vmem()] * 4,
        scratch_shapes=[pltpu.VMEM((2, rows + 4 * REACH, size_y, size_z), jnp.float32)],
        compiler_params=params(),
        name=f"pair_{group}_{step}",
    )(now, before, *halos, courant, inject, along_z, along_y)


def last_kernel(group, rows, step, now, before, even, odd, courant, inject, along_z, along_y, *refs):
    final, source_out, receiver_out, wide, sem = refs[-5:]
    even_at, odd_at = halo_starts(rows, REACH)
    z_band, y_band = along_z[...], along_y[...]
    copies = []
    for kind, out in enumerate((source_out, receiver_out)):
        field = wide.at[kind]
        field[REACH : REACH + rows] = now[kind]
        field[pl.ds(even_at, REACH)] = even[kind]
        field[pl.ds(odd_at, REACH)] = odd[kind]
        for at in range(0, rows, CHUNK):

            def write(i, new, kind=kind, at=at):
                final[kind, at + i] = new

            advance(field, REACH + at, before.at[kind], REACH + at, courant, REACH + at, inject.at[kind], REACH + at, step, z_band, y_band, write)
        copies.append(pltpu.make_async_copy(final.at[kind], out.at[group], sem.at[kind]))
        copies[kind].start()
    for copy in copies:
        copy.wait()


def last_round(group, groups, step, now, before, halos, courant, inject, along_z, along_y, outs):
    rows, size_y, size_z = now.shape[1:]
    whole = struct((groups, rows, size_y, size_z))
    return pl.pallas_call(
        functools.partial(last_kernel, group, rows, step),
        out_shape=[struct(now.shape), whole, whole],
        in_specs=[vmem()] * 8 + [hbm()] * len(outs),
        out_specs=[vmem(), hbm(), hbm()],
        scratch_shapes=[pltpu.VMEM((2, rows + 2 * REACH, size_y, size_z), jnp.float32), pltpu.SemaphoreType.DMA((2,))],
        input_output_aliases={8: 1, 9: 2} if outs else {},
        compiler_params=params(),
        name=f"last_{group}",
    )(now, before, *halos, courant, inject, along_z, along_y, *outs)


def shifted(plane, amount):
    size_y = plane.shape[0]
    if amount == 0:
        return plane
    if abs(amount) >= size_y:
        return jnp.zeros_like(plane)
    row = lax.broadcasted_iota(jnp.int32, plane.shape, 0)
    inside = (row >= amount) if amount > 0 else (row < size_y + amount)
    return jnp.where(inside, pltpu.roll(plane, amount % size_y, 0), 0.0)


def image_kernel(ahead, slots, offset_perm, *refs):
    fields, image = refs[:-1], refs[-1]
    count = offset_perm.shape[0]
    half_span = count // 2
    rows = image.shape[1]
    here = lax.axis_index("shot")
    pairs = lax.axis_size("shot") // 2
    owner = 2 * lax.rem(lax.div(here, 2) + ahead, pairs) + lax.rem(here, 2)

    def one_slot(slot, carry):
        index = offset_perm[owner * slots + slot]
        for lag_index in range(count):
            lag = lag_index - half_span

            @pl.when(index == lag_index)
            def _(lag=lag):
                def one_plane(x, carry):
                    total = None
                    for field in fields:
                        term = field[1, x] * shifted(field[0, x], 2 * lag)
                        total = term if total is None else total + term
                    image[slot, x] = shifted(total, -lag)
                    return carry

                lax.fori_loop(0, rows, one_plane, 0, unroll=2)

        return carry

    lax.fori_loop(0, slots, one_slot, 0)


def image_part(ahead, slots, offset_perm, fields):
    _, rows, size_y, size_z = fields[0].shape
    return pl.pallas_call(
        functools.partial(image_kernel, ahead, slots),
        out_shape=struct((slots, rows, size_y, size_z)),
        in_specs=[smem()] + [vmem()] * len(fields),
        out_specs=vmem(),
        compiler_params=params(),
        name=f"image_{ahead}",
    )(offset_perm, *fields)


def body(source_now, source_prev, receiver_now, receiver_prev, courant_sq, source_cell, wavelet, receiver_cell, traces, offset_perm):
    groups, rows, size_y, size_z = source_now.shape
    steps = wavelet.shape[0]
    shot_devices = lax.axis_size("shot")
    slots = offset_perm.shape[0] // shot_devices
    everyone = range(groups)

    edges = pack(source_now, receiver_now, courant_sq)
    halos = [trade(edges[2 * g], edges[2 * g + 1]) for g in everyone]
    along_z, along_y, *inject = prepare(source_cell, wavelet, receiver_cell, traces, rows, size_y, size_z)

    fields = (source_now, receiver_now, source_prev, receiver_prev)
    now, before = [None] * groups, [None] * groups
    courant = courant_sq
    for g in everyone:
        result = first_round(g, 2 * REACH, fields, courant, halos[g], inject[g], along_z, along_y)
        now[g], before[g] = result[:2]
        if g == 0:
            courant = result[4]
        halos[g] = trade(*result[2:4])
    for step in range(1, steps - 1, 2):
        width = 2 * REACH if step + 2 < steps - 1 else REACH
        for g in everyone:
            now[g], before[g], even, odd = pair_round(g, step, width, now[g], before[g], halos[g], courant, inject[g], along_z, along_y)
            halos[g] = trade(even, odd)
    outs = ()
    final, other = [None] * groups, [None] * groups
    swap = [(i, i ^ 1) for i in range(shot_devices)]
    for g in everyone:
        final[g], *outs = last_round(g, groups, steps - 1, now[g], before[g], halos[g], courant, inject[g], along_z, along_y, outs)
        other[g] = lax.ppermute(final[g], "shot", swap)

    pairs = shot_devices // 2
    arrived = []
    for ahead in range(1, pairs):
        part = image_part(ahead, slots, offset_perm, final + other)
        route = [(2 * p + c, 2 * ((p + ahead) % pairs) + c) for p in range(pairs) for c in range(2)]
        arrived.append(lax.ppermute(part, "shot", route))
    image = image_part(0, slots, offset_perm, final + other)
    for part in arrived:
        image = image + part
    return (image, *outs)


def solution(mesh):
    shots = ("runs", "shot")
    in_specs = (
        P(shots, "slab", None, None),
        P(shots, "slab", None, None),
        P(shots, "slab", None, None),
        P(shots, "slab", None, None),
        P(("runs", "slab"), None, None),
        P(shots),
        P(None, shots),
        P(shots, None),
        P(None, shots, None),
        P("runs"),
    )
    out_specs = (P(shots, "slab", None, None),) * 3
    return jax.shard_map(body, mesh=mesh, in_specs=in_specs, out_specs=out_specs, check_vma=False)
```

time: 273 us -> 87 us (0.32)
  local copies, waits for them, and re-layouts: 80.7 us -> 5.93 us
  other arithmetic: 59.1 us -> 0.87 us
  waiting for transfers between devices: 57 us -> 14.8 us
  between operations: 19.9 us -> 1 us
  Pallas kernels: 0 us -> 18.1 us
  starting transfers between devices: 52.5 us -> 44.8 us
    scatter-add x8 -> x0, local copies, waits for them, and re-layouts: 52.5 us -> none  [body(): updated = updated.at[:, :, :, :, INJECT_Z].add(planes)]
    add x18 -> x1, other arithmetic: 43.6 us -> 0.87 us  [body(): image = image + part]
    all_gather x1 -> x0, waiting for transfers between devices: 30.6 us -> none  [body(): shard_piece = lax.all_gather(fields, 'shot', axis=1, tiled=True)]
    pallas_call x0 -> x14, Pallas kernels: none -> 18.1 us  [the longest x6 8.85 us: pair_round(): pl.pallas_call(functools.partial(pair_kernel, rows, step, width), out_sha...]
    another operation x26 -> x0, local copies, waits for them, and re-layouts: 14.6 us -> none
    ppermute x16 -> x23, waiting for transfers between devices: 26.4 us -> 14.8 us  [the longest x1 11.3 us: body(): arrived.append(lax.ppermute(part, 'shot', route))]
    select_n x8 -> x0, other arithmetic: 11.2 us -> none  [body(): updated = jnp.where(inside[None, None, :, None, None], updated, 0.0)]
    ppermute x16 -> x23, starting transfers between devices: 52.5 us -> 44.8 us  [the longest x10 36 us: trade(): lax.ppermute(even_edge, 'slab', even_pairs(count))]
  transfers between devices with their start and end apart: 17 -> 23, of which waited for: 17 -> 5; matrix products, arithmetic and copies ran while one was open for 2% -> 0% of each run, Pallas kernels for 0% -> 19%
where the time goes in v1:
time: 87 us; the launch traced here: 85.5 us
  starting transfers between devices  44.8 us (51%)
  Pallas kernels  18.1 us (21%)
  waiting for transfers between devices  14.8 us (17%)
  local copies, waits for them, and re-layouts  5.93 us (7%)
  between operations  1 us (1%)
  other arithmetic  0.87 us (1%)
    ppermute x10, starting transfers between devices, trade(): lax.ppermute(even_edge, 'slab', even_pairs(count))  36 us
    ppermute x1, waiting for transfers between devices, body(): arrived.append(lax.ppermute(part, 'shot', route))  11.3 us
    pallas_call x6, Pallas kernels, pair_round(): pl.pallas_call(functools.partial(pair_kernel, rows, step, width), out_sha...  8.85 us
    ppermute x10, starting transfers between devices, trade(): lax.ppermute(odd_edge, 'slab', odd_pairs(count))  6.94 us
    unnamed x27, local copies, waits for them, and re-layouts  5.93 us
    pallas_call x2, Pallas kernels, last_round(): pl.pallas_call(functools.partial(last_kernel, group, rows, step), out_sha...  2.75 us
    pallas_call x2, Pallas kernels, image_part(): pl.pallas_call(functools.partial(image_kernel, ahead, slots), out_shape=s...  2.08 us
    pallas_call x2, Pallas kernels, first_round(): pl.pallas_call(functools.partial(first_kernel, group, rows, has_courant,...  1.97 us
  transfers between devices with their start and end apart: 23, of which 5 were waited for; matrix products, arithmetic and copies ran while one was open for 0% of the time, Pallas kernels for 19%

profile of v1, /device:TPU:0, one launch (start us, length us, event | category | flops | bytes accessed | tf_op | source)
XLA Modules:
  0.0 85.5 jit_solution(4969444721419586216)
XLA Ops:
  0.6 1.0 %copy-done = f32[2,16,16,256]{3,2,1,0:T(8,128)S(1)} copy-done((f32[2,16,16,256]{3,2,1,0:T(8,128)S(1)}, f32[2,16,16,256]{3,2,1,0:T(8,128)}, u32[]{:S(2)}) %copy-start) | copy-done | bytes 524312
  1.7 1.0 %copy-done.2 = f32[2,16,16,256]{3,2,1,0:T(8,128)S(1)} copy-done((f32[2,16,16,256]{3,2,1,0:T(8,128)S(1)}, f32[2,16,16,256]{3,2,1,0:T(8,128)}, u32[]{:S(2)}) %copy-start.2) | copy-done | bytes 524312
  2.7 0.9 %copy-done.6 = f32[16,16,256]{2,1,0:T(8,128)S(1)} copy-done((f32[16,16,256]{2,1,0:T(8,128)S(1)}, f32[16,16,256]{2,1,0:T(8,128)}, u32[]{:S(2)}) %copy-start.6) | copy-done | bytes 262168
  3.7 0.9 %pack.1 = (f32[3,4,16,256]{3,2,1,0:T(8,128)S(1)}, f32[3,4,16,256]{3,2,1,0:T(8,128)S(1)}, f32[2,4,16,256]{3,2,1,0:T(8,128)S(1)}, f32[2,4,16,256]{3,2,1,0:T(8,128)S(1)}) custom-call(f32[2,16,16,256]{3,2,1,0:T(8,128)S(1)} %copy-done, f32[2,16,16,256]{3,2,1,0:T(8,128)S(1)} %copy-done.2, f32[16,16,256]{2,1,0:T(8,128)S(1)} %copy-done.6), custom_call_target="tpu_custom_call" | custom-call | tf_op jit(solution)/shard_map/pack/pallas_call | solution.py:104
  4.6 3.1 %collective-permute-start = (f32[3,4,16,256]{3,2,1,0:T(8,128)S(1)}, f32[3,4,16,256]{3,2,1,0:T(8,128)S(1)}, u32[]{:S(2)}, u32[]{:S(2)}) collective-permute-start(f32[3,4,16,256]{3,2,1,0:T(8,128)S(1)} %get-tuple-element.50), channel_id=1, source_target_pairs={{0,1},{1,0},{2,3},{3,2},{4,5},{5,4},{6,7},{7,6},{8,9},{9,8},{10,11... | collective-permute-start | bytes 589832 | tf_op jit(solution)/shard_map/ppermute | solution.py:60
  7.7 0.7 collective-permute-start.1
  8.4 0.0 copy-start.12
  8.4 4.5 %collective-permute-start.10 = (f32[2,4,16,256]{3,2,1,0:T(8,128)S(1)}, f32[2,4,16,256]{3,2,1,0:T(8,128)S(1)}, u32[]{:S(2)}, u32[]{:S(2)}) collective-permute-start(f32[2,4,16,256]{3,2,1,0:T(8,128)S(1)} %get-tuple-element.73), channel_id=1, source_target_pairs={{0,1},{1,0},{2,3},{3,2},{4,5},{5,4},{6,7},{7,6},{8,9},{9,8},{10,11... | collective-permute-start | bytes 393224 | tf_op jit(solution)/shard_map/ppermute | solution.py:60
  12.9 0.8 collective-permute-start.11
  13.7 0.1 copy.15.wavelet
  13.8 0.7 copy-done.8
  14.5 1.5 %prepare.1 = (bf16[256,256]{1,0:T(8,128)(2,1)S(1)}, bf16[128,256]{1,0:T(8,128)(2,1)S(1)}, f32[2,24,16,128]{3,2,1,0:T(8,128)S(1)}, f32[2,24,16,128]{3,2,1,0:T(8,128)S(1)}) custom-call(s32[2]{0:T(128)S(1)} %copy-done.11, f32[8,2]{1,0:T(8,128)S(1)} %copy.15.wavelet, s32[2,256]{1,0:T(2,128)S(1)} %copy-done.9, f32[8,2,256]{2,1,0:T(2,128)S(1)} %copy-done.8), custom_call_target="tpu_custom_call" | custom-call | tf_op jit(solution)/shard_map/prepare/pallas_call | solution.py:167
  16.0 0.0 collective-permute-done.even
  16.0 0.0 collective-permute-done.1.odd
  16.0 0.0 copy-start.4
  16.1 1.0 %copy-done.4 = f32[2,16,16,256]{3,2,1,0:T(8,128)S(1)} copy-done((f32[2,16,16,256]{3,2,1,0:T(8,128)S(1)}, f32[2,16,16,256]{3,2,1,0:T(8,128)}, u32[]{:S(2)}) %copy-start.4) | copy-done | bytes 524312
  17.1 1.0 %copy-done.5 = f32[2,16,16,256]{3,2,1,0:T(8,128)S(1)} copy-done((f32[2,16,16,256]{3,2,1,0:T(8,128)S(1)}, f32[2,16,16,256]{3,2,1,0:T(8,128)}, u32[]{:S(2)}) %copy-start.5) | copy-done | bytes 524312
  18.1 1.0 %first_0.1 = (f32[2,16,16,256]{3,2,1,0:T(8,128)S(1)}, f32[2,24,16,256]{3,2,1,0:T(8,128)S(1)}, f32[2,8,16,256]{3,2,1,0:T(8,128)S(1)}, f32[2,8,16,256]{3,2,1,0:T(8,128)S(1)}, f32[24,16,256]{2,1,0:T(8,128)S(1)}) custom-call(f32[2,16,16,256]{3,2,1,0:T(8,128)S(1)} %copy-done.1, f32[2,16,16,256]{3,2,1,0:T(8,128)S(1)} %copy-done.3, ...), custom_call_target="tpu_custom_call" | custom-call | tf_op jit(solution)/shard_map/first_0/pallas_call | solution.py:249
  19.1 2.2 %collective-permute-start.2 = (f32[2,8,16,256]{3,2,1,0:T(8,128)S(1)}, f32[2,8,16,256]{3,2,1,0:T(8,128)S(1)}, u32[]{:S(2)}, u32[]{:S(2)}) collective-permute-start(f32[2,8,16,256]{3,2,1,0:T(8,128)S(1)} %get-tuple-element.57), channel_id=1, source_target_pairs={{0,1},{1,0},{2,3},{3,2},{4,5},{5,4},{6,7},{7,6},{8,9},{9,8},{10,11... | collective-permute-start | bytes 786440 | tf_op jit(solution)/shard_map/ppermute | solution.py:60
  21.3 0.7 collective-permute-start.3
  22.0 0.0 collective-permute-done.10.even
  22.0 0.0 collective-permute-done.11.odd
  22.0 1.0 %first_1.1 = (f32[2,16,16,256]{3,2,1,0:T(8,128)S(1)}, f32[2,24,16,256]{3,2,1,0:T(8,128)S(1)}, f32[2,8,16,256]{3,2,1,0:T(8,128)S(1)}, f32[2,8,16,256]{3,2,1,0:T(8,128)S(1)}) custom-call(f32[2,16,16,256]{3,2,1,0:T(8,128)S(1)} %copy-done.1, f32[2,16,16,256]{3,2,1,0:T(8,128)S(1)} %copy-done.3, f32[2,16,16,256]{3,2,1,0:T(8,128)S(1)} %copy-done.4, ...), custom_call_target="tpu_custom_call" | custom-call | tf_op jit(solution)/shard_map/first_1/pallas_call | solution.py:249
  23.0 3.7 %collective-permute-start.12 = (f32[2,8,16,256]{3,2,1,0:T(8,128)S(1)}, f32[2,8,16,256]{3,2,1,0:T(8,128)S(1)}, u32[]{:S(2)}, u32[]{:S(2)}) collective-permute-start(f32[2,8,16,256]{3,2,1,0:T(8,128)S(1)} %get-tuple-element.78), channel_id=1, source_target_pairs={{0,1},{1,0},{2,3},{3,2},{4,5},{5,4},{6,7},{7,6},{8,9},{9,8},{10,11... | collective-permute-start | bytes 786440 | tf_op jit(solution)/shard_map/ppermute | solution.py:60
  26.7 0.7 collective-permute-start.13
  27.4 0.5 collective-permute-done.2.even
  27.9 0.0 collective-permute-done.3.odd
  27.9 1.5 %pair_0_1.1 = (f32[2,16,16,256]{3,2,1,0:T(8,128)S(1)}, f32[2,24,16,256]{3,2,1,0:T(8,128)S(1)}, f32[2,8,16,256]{3,2,1,0:T(8,128)S(1)}, f32[2,8,16,256]{3,2,1,0:T(8,128)S(1)}) custom-call(f32[2,16,16,256]{3,2,1,0:T(8,128)S(1)} %get-tuple-element.55.now, f32[2,24,16,256]{3,2,1,0:T(8,128)S(1)} %get-tuple-element.56.before, ...), custom_call_target="tpu_custom_call" | custom-call | tf_op jit(solution)/shard_map/pair_0_1/pallas_call | solution.py:289
  29.4 4.5 %collective-permute-start.4 = (f32[2,8,16,256]{3,2,1,0:T(8,128)S(1)}, f32[2,8,16,256]{3,2,1,0:T(8,128)S(1)}, u32[]{:S(2)}, u32[]{:S(2)}) collective-permute-start(f32[2,8,16,256]{3,2,1,0:T(8,128)S(1)} %get-tuple-element.62), channel_id=1, source_target_pairs={{0,1},{1,0},{2,3},{3,2},{4,5},{5,4},{6,7},{7,6},{8,9},{9,8},{10,11... | collective-permute-start | bytes 786440 | tf_op jit(solution)/shard_map/ppermute | solution.py:60
  33.9 0.7 collective-permute-start.5
  34.6 0.0 collective-permute-done.13.odd
  34.6 1.5 %pair_1_1.1 = (f32[2,16,16,256]{3,2,1,0:T(8,128)S(1)}, f32[2,24,16,256]{3,2,1,0:T(8,128)S(1)}, f32[2,8,16,256]{3,2,1,0:T(8,128)S(1)}, f32[2,8,16,256]{3,2,1,0:T(8,128)S(1)}) custom-call(f32[2,16,16,256]{3,2,1,0:T(8,128)S(1)} %get-tuple-element.76.now, f32[2,24,16,256]{3,2,1,0:T(8,128)S(1)} %get-tuple-element.77.before, ...), custom_call_target="tpu_custom_call" | custom-call | tf_op jit(solution)/shard_map/pair_1_1/pallas_call | solution.py:289
  36.1 3.8 %collective-permute-start.14 = (f32[2,8,16,256]{3,2,1,0:T(8,128)S(1)}, f32[2,8,16,256]{3,2,1,0:T(8,128)S(1)}, u32[]{:S(2)}, u32[]{:S(2)}) collective-permute-start(f32[2,8,16,256]{3,2,1,0:T(8,128)S(1)} %get-tuple-element.82), channel_id=1, source_target_pairs={{0,1},{1,0},{2,3},{3,2},{4,5},{5,4},{6,7},{7,6},{8,9},{9,8},{10,11... | collective-permute-start | bytes 786440 | tf_op jit(solution)/shard_map/ppermute | solution.py:60
  39.9 0.7 collective-permute-start.15
  40.5 0.0 collective-permute-done.5.odd
  40.6 1.5 %pair_0_3.1 = (f32[2,16,16,256]{3,2,1,0:T(8,128)S(1)}, f32[2,24,16,256]{3,2,1,0:T(8,128)S(1)}, f32[2,8,16,256]{3,2,1,0:T(8,128)S(1)}, f32[2,8,16,256]{3,2,1,0:T(8,128)S(1)}) custom-call(f32[2,16,16,256]{3,2,1,0:T(8,128)S(1)} %get-tuple-element.60.now, f32[2,24,16,256]{3,2,1,0:T(8,128)S(1)} %get-tuple-element.61.before, ...), custom_call_target="tpu_custom_call" | custom-call | tf_op jit(solution)/shard_map/pair_0_3/pallas_call | solution.py:289
  42.0 4.9 %collective-permute-start.6 = (f32[2,8,16,256]{3,2,1,0:T(8,128)S(1)}, f32[2,8,16,256]{3,2,1,0:T(8,128)S(1)}, u32[]{:S(2)}, u32[]{:S(2)}) collective-permute-start(f32[2,8,16,256]{3,2,1,0:T(8,128)S(1)} %get-tuple-element.66), channel_id=1, source_target_pairs={{0,1},{1,0},{2,3},{3,2},{4,5},{5,4},{6,7},{7,6},{8,9},{9,8},{10,11... | collective-permute-start | bytes 786440 | tf_op jit(solution)/shard_map/ppermute | solution.py:60
  47.0 0.7 collective-permute-start.7
  47.6 0.0 collective-permute-done.14.even
  47.7 1.5 %pair_1_3.1 = (f32[2,16,16,256]{3,2,1,0:T(8,128)S(1)}, f32[2,24,16,256]{3,2,1,0:T(8,128)S(1)}, f32[2,8,16,256]{3,2,1,0:T(8,128)S(1)}, f32[2,8,16,256]{3,2,1,0:T(8,128)S(1)}) custom-call(f32[2,16,16,256]{3,2,1,0:T(8,128)S(1)} %get-tuple-element.80.now, f32[2,24,16,256]{3,2,1,0:T(8,128)S(1)} %get-tuple-element.81.before, ...), custom_call_target="tpu_custom_call" | custom-call | tf_op jit(solution)/shard_map/pair_1_3/pallas_call | solution.py:289
  49.1 3.3 %collective-permute-start.16 = (f32[2,8,16,256]{3,2,1,0:T(8,128)S(1)}, f32[2,8,16,256]{3,2,1,0:T(8,128)S(1)}, u32[]{:S(2)}, u32[]{:S(2)}) collective-permute-start(f32[2,8,16,256]{3,2,1,0:T(8,128)S(1)} %get-tuple-element.86), channel_id=1, source_target_pairs={{0,1},{1,0},{2,3},{3,2},{4,5},{5,4},{6,7},{7,6},{8,9},{9,8},{10,11... | collective-permute-start | bytes 786440 | tf_op jit(solution)/shard_map/ppermute | solution.py:60
  52.5 0.7 collective-permute-start.17
  53.2 0.2 collective-permute-done.6.even
  53.4 0.0 collective-permute-done.7.odd
  53.4 1.4 %pair_0_5.1 = (f32[2,16,16,256]{3,2,1,0:T(8,128)S(1)}, f32[2,24,16,256]{3,2,1,0:T(8,128)S(1)}, f32[2,4,16,256]{3,2,1,0:T(8,128)S(1)}, f32[2,4,16,256]{3,2,1,0:T(8,128)S(1)}) custom-call(f32[2,16,16,256]{3,2,1,0:T(8,128)S(1)} %get-tuple-element.64.now, f32[2,24,16,256]{3,2,1,0:T(8,128)S(1)} %get-tuple-element.65.before, ...), custom_call_target="tpu_custom_call" | custom-call | tf_op jit(solution)/shard_map/pair_0_5/pallas_call | solution.py:289
  54.9 3.7 %collective-permute-start.8 = (f32[2,4,16,256]{3,2,1,0:T(8,128)S(1)}, f32[2,4,16,256]{3,2,1,0:T(8,128)S(1)}, u32[]{:S(2)}, u32[]{:S(2)}) collective-permute-start(f32[2,4,16,256]{3,2,1,0:T(8,128)S(1)} %get-tuple-element.70), channel_id=1, source_target_pairs={{0,1},{1,0},{2,3},{3,2},{4,5},{5,4},{6,7},{7,6},{8,9},{9,8},{10,11... | collective-permute-start | bytes 393224 | tf_op jit(solution)/shard_map/ppermute | solution.py:60
  58.6 0.8 collective-permute-start.9
  59.4 0.0 collective-permute-done.16.even
  59.4 1.4 %pair_1_5.1 = (f32[2,16,16,256]{3,2,1,0:T(8,128)S(1)}, f32[2,24,16,256]{3,2,1,0:T(8,128)S(1)}, f32[2,4,16,256]{3,2,1,0:T(8,128)S(1)}, f32[2,4,16,256]{3,2,1,0:T(8,128)S(1)}) custom-call(f32[2,16,16,256]{3,2,1,0:T(8,128)S(1)} %get-tuple-element.84.now, f32[2,24,16,256]{3,2,1,0:T(8,128)S(1)} %get-tuple-element.85.before, ...), custom_call_target="tpu_custom_call" | custom-call | tf_op jit(solution)/shard_map/pair_1_5/pallas_call | solution.py:289
  60.9 2.3 %collective-permute-start.18 = (f32[2,4,16,256]{3,2,1,0:T(8,128)S(1)}, f32[2,4,16,256]{3,2,1,0:T(8,128)S(1)}, u32[]{:S(2)}, u32[]{:S(2)}) collective-permute-start(f32[2,4,16,256]{3,2,1,0:T(8,128)S(1)} %get-tuple-element.90), channel_id=1, source_target_pairs={{0,1},{1,0},{2,3},{3,2},{4,5},{5,4},{6,7},{7,6},{8,9},{9,8},{10,11... | collective-permute-start | bytes 393224 | tf_op jit(solution)/shard_map/ppermute | solution.py:60
  63.2 0.7 collective-permute-start.19
  63.9 0.0 collective-permute-done.9.odd
  63.9 1.4 %last_0.1 = (f32[2,16,16,256]{3,2,1,0:T(8,128)S(1)}, f32[2,16,16,256]{3,2,1,0:T(8,128)}, f32[2,16,16,256]{3,2,1,0:T(8,128)}) custom-call(f32[2,16,16,256]{3,2,1,0:T(8,128)S(1)} %get-tuple-element.68.now, f32[2,24,16,256]{3,2,1,0:T(8,128)S(1)} %get-tuple-element.69.before, f32[2,4,16,256]{3,2,1,0:T(8,128)S(1)} %collective-permute-done.8.even, ...), custom_call_target="tpu_custom_call" | custom-call | tf_op jit(solution)/shard_map/last_0/pallas_call | solution.py:325
  65.3 0.1 collective-permute-start.20
  65.3 0.8 collective-permute-done.18.even
  66.2 1.4 %last_1.1 = (f32[2,16,16,256]{3,2,1,0:T(8,128)S(1)}, f32[2,16,16,256]{3,2,1,0:T(8,128)}, f32[2,16,16,256]{3,2,1,0:T(8,128)}) custom-call(f32[2,16,16,256]{3,2,1,0:T(8,128)S(1)} %get-tuple-element.88.now, f32[2,24,16,256]{3,2,1,0:T(8,128)S(1)} %get-tuple-element.89.before, ...), custom_call_target="tpu_custom_call", output_to_operand_aliasing={{1}: (8, {}), {2}: (9, {})} | custom-call | tf_op jit(solution)/shard_map/last_1/pallas_call | solution.py:325
  67.5 0.0 copy-start.10
  67.5 0.1 collective-permute-start.21
  67.6 1.9 %collective-permute-done.21.refs_3_ = f32[2,16,16,256]{3,2,1,0:T(8,128)S(1)} collective-permute-done((f32[2,16,16,256]{3,2,1,0:T(8,128)S(1)}, f32[2,16,16,256]{3,2,1,0:T(8,128)S(1)}, u32[]{:S(2)}, u32[]{:S(2)}) %collective-permute-start.21) | collective-permute-done | bytes 524320 | tf_op jit(solution)/shard_map/ppermute | solution.py:421
  69.5 1.0 %image_1.1 = f32[2,16,16,256]{3,2,1,0:T(8,128)S(1)} custom-call(s32[8]{0:T(128)S(1)} %copy-done.10, f32[2,16,16,256]{3,2,1,0:T(8,128)S(1)} %get-tuple-element.72.refs_0_, f32[2,16,16,256]{3,2,1,0:T(8,128)S(1)} %get-tuple-element.94.refs_1_, f32[2,16,16,256]{3,2,1,0:T(8,128)S(1)} %collective-permute-done.20.refs_2_, ...), custom_call_target="tpu_custom_call" | custom-call | tf_op jit(solution)/shard_map/image_1/pallas_call | solution.py:381
  70.5 1.7 %collective-permute-start.22 = (f32[2,16,16,256]{3,2,1,0:T(8,128)S(1)}, f32[2,16,16,256]{3,2,1,0:T(8,128)S(1)}, u32[]{:S(2)}, u32[]{:S(2)}) collective-permute-start(f32[2,16,16,256]{3,2,1,0:T(8,128)S(1)} %image_1.1), channel_id=1, source_target_pairs={{0,8},{4,12},{8,0},{12,4},{1,9},{5,13},{9,1},{13,5},{2,10},{6,14},... | collective-permute-start | bytes 1572872 | tf_op jit(solution)/shard_map/ppermute | solution.py:428
  72.2 1.1 %image_0.1 = f32[2,16,16,256]{3,2,1,0:T(8,128)S(1)} custom-call(s32[8]{0:T(128)S(1)} %copy-done.10, f32[2,16,16,256]{3,2,1,0:T(8,128)S(1)} %get-tuple-element.72.refs_0_, f32[2,16,16,256]{3,2,1,0:T(8,128)S(1)} %get-tuple-element.94.refs_1_, f32[2,16,16,256]{3,2,1,0:T(8,128)S(1)} %collective-permute-done.20.refs_2_, ...), custom_call_target="tpu_custom_call" | custom-call | tf_op jit(solution)/shard_map/image_0/pallas_call | solution.py:381
  73.3 11.3 %collective-permute-done.22 = f32[2,16,16,256]{3,2,1,0:T(8,128)S(1)} collective-permute-done((f32[2,16,16,256]{3,2,1,0:T(8,128)S(1)}, f32[2,16,16,256]{3,2,1,0:T(8,128)S(1)}, u32[]{:S(2)}, u32[]{:S(2)}) %collective-permute-start.22) | collective-permute-done | bytes 524320 | tf_op jit(solution)/shard_map/ppermute | solution.py:428
  84.6 0.9 %add.3 = f32[2,16,16,256]{3,2,1,0:T(8,128)} add(f32[2,16,16,256]{3,2,1,0:T(8,128)S(1)} %image_0.1, f32[2,16,16,256]{3,2,1,0:T(8,128)S(1)} %collective-permute-done.22) | non-fusion elementwise | flops 131072 | bytes 1572864 | tf_op jit(solution)/shard_map/add | solution.py:431
  (24 shorter events, 0.0 us)
Async XLA Ops:
  0.6 1.0 %copy-start = (f32[2,16,16,256]{3,2,1,0:T(8,128)S(1)}, f32[2,16,16,256]{3,2,1,0:T(8,128)}, u32[]{:S(2)}) copy-start(f32[2,16,16,256]{3,2,1,0:T(8,128)} %source.3) | copy-start | bytes 1572868
  1.7 1.0 %copy-start.2 = (f32[2,16,16,256]{3,2,1,0:T(8,128)S(1)}, f32[2,16,16,256]{3,2,1,0:T(8,128)}, u32[]{:S(2)}) copy-start(f32[2,16,16,256]{3,2,1,0:T(8,128)} %receiver.3) | copy-start | bytes 1572868
  2.7 0.9 %copy-start.6 = (f32[16,16,256]{2,1,0:T(8,128)S(1)}, f32[16,16,256]{2,1,0:T(8,128)}, u32[]{:S(2)}) copy-start(f32[16,16,256]{2,1,0:T(8,128)} %courant.1) | copy-start | bytes 786436
  3.7 12.4 %copy-start.1 = (f32[2,16,16,256]{3,2,1,0:T(8,128)S(1)}, f32[2,16,16,256]{3,2,1,0:T(8,128)}, u32[]{:S(2)}) copy-start(f32[2,16,16,256]{3,2,1,0:T(8,128)} %source.3) | copy-start | bytes 1572868
  3.7 12.4 %copy-start.3 = (f32[2,16,16,256]{3,2,1,0:T(8,128)S(1)}, f32[2,16,16,256]{3,2,1,0:T(8,128)}, u32[]{:S(2)}) copy-start(f32[2,16,16,256]{3,2,1,0:T(8,128)} %receiver.3) | copy-start | bytes 1572868
  3.7 12.4 %copy-start.7 = (f32[16,16,256]{2,1,0:T(8,128)S(1)}, f32[16,16,256]{2,1,0:T(8,128)}, u32[]{:S(2)}) copy-start(f32[16,16,256]{2,1,0:T(8,128)} %courant.1) | copy-start | bytes 786436
  4.6 11.4 %collective-permute-start = (f32[3,4,16,256]{3,2,1,0:T(8,128)S(1)}, f32[3,4,16,256]{3,2,1,0:T(8,128)S(1)}, u32[]{:S(2)}, u32[]{:S(2)}) collective-permute-start(f32[3,4,16,256]{3,2,1,0:T(8,128)S(1)} %get-tuple-element.50), channel_id=1, source_target_pairs={{0,1},{1,0},{2,3},{3,2},{4,5},{5,4},{6,7},{7,6},{8,9},{9,8},{10,11... | collective-permute-start | bytes 589832 | tf_op jit(solution)/shard_map/ppermute | solution.py:60
  7.7 8.3 %collective-permute-start.1 = (f32[3,4,16,256]{3,2,1,0:T(8,128)S(1)}, f32[3,4,16,256]{3,2,1,0:T(8,128)S(1)}, u32[]{:S(2)}, u32[]{:S(2)}) collective-permute-start(f32[3,4,16,256]{3,2,1,0:T(8,128)S(1)} %get-tuple-element.51), channel_id=1, source_target_pairs={{1,2},{2,1},{5,6},{6,5},{9,10},{10,9},{13,14},{14,13},{17,18},{18,... | collective-permute-start | bytes 589832 | tf_op jit(solution)/shard_map/ppermute | solution.py:61
  8.4 5.3 %copy-start.12 = (f32[8,2]{0,1:T(2,128)S(1)}, f32[8,2]{0,1:T(2,128)}, u32[]{:S(2)}) copy-start(f32[8,2]{0,1:T(2,128)} %param.16) | copy-start | bytes 196
  8.4 13.6 %collective-permute-start.10 = (f32[2,4,16,256]{3,2,1,0:T(8,128)S(1)}, f32[2,4,16,256]{3,2,1,0:T(8,128)S(1)}, u32[]{:S(2)}, u32[]{:S(2)}) collective-permute-start(f32[2,4,16,256]{3,2,1,0:T(8,128)S(1)} %get-tuple-element.73), channel_id=1, source_target_pairs={{0,1},{1,0},{2,3},{3,2},{4,5},{5,4},{6,7},{7,6},{8,9},{9,8},{10,11... | collective-permute-start | bytes 393224 | tf_op jit(solution)/shard_map/ppermute | solution.py:60
  12.9 0.9 %copy-start.9 = (s32[2,256]{1,0:T(2,128)S(1)}, s32[2,256]{1,0:T(2,128)}, u32[]{:S(2)}) copy-start(s32[2,256]{1,0:T(2,128)} %receiver_cell.1) | copy-start | bytes 6148
  12.9 0.9 %copy-start.11 = (s32[2]{0:T(128)S(1)}, s32[2]{0:T(128)}, u32[]{:S(2)}) copy-start(s32[2]{0:T(128)} %source_cell.1) | copy-start | bytes 28
  12.9 9.1 %collective-permute-start.11 = (f32[2,4,16,256]{3,2,1,0:T(8,128)S(1)}, f32[2,4,16,256]{3,2,1,0:T(8,128)S(1)}, u32[]{:S(2)}, u32[]{:S(2)}) collective-permute-start(f32[2,4,16,256]{3,2,1,0:T(8,128)S(1)} %get-tuple-element.74), channel_id=1, source_target_pairs={{1,2},{2,1},{5,6},{6,5},{9,10},{10,9},{13,14},{14,13},{17,18},{18,... | collective-permute-start | bytes 393224 | tf_op jit(solution)/shard_map/ppermute | solution.py:61
  13.8 0.7 copy-start.8
  16.0 1.0 %copy-start.4 = (f32[2,16,16,256]{3,2,1,0:T(8,128)S(1)}, f32[2,16,16,256]{3,2,1,0:T(8,128)}, u32[]{:S(2)}) copy-start(f32[2,16,16,256]{3,2,1,0:T(8,128)} %source_before.3) | copy-start | bytes 1572868
  17.1 1.0 %copy-start.5 = (f32[2,16,16,256]{3,2,1,0:T(8,128)S(1)}, f32[2,16,16,256]{3,2,1,0:T(8,128)}, u32[]{:S(2)}) copy-start(f32[2,16,16,256]{3,2,1,0:T(8,128)} %receiver_before.3) | copy-start | bytes 1572868
  19.1 8.7 %collective-permute-start.2 = (f32[2,8,16,256]{3,2,1,0:T(8,128)S(1)}, f32[2,8,16,256]{3,2,1,0:T(8,128)S(1)}, u32[]{:S(2)}, u32[]{:S(2)}) collective-permute-start(f32[2,8,16,256]{3,2,1,0:T(8,128)S(1)} %get-tuple-element.57), channel_id=1, source_target_pairs={{0,1},{1,0},{2,3},{3,2},{4,5},{5,4},{6,7},{7,6},{8,9},{9,8},{10,11... | collective-permute-start | bytes 786440 | tf_op jit(solution)/shard_map/ppermute | solution.py:60
  21.3 6.6 %collective-permute-start.3 = (f32[2,8,16,256]{3,2,1,0:T(8,128)S(1)}, f32[2,8,16,256]{3,2,1,0:T(8,128)S(1)}, u32[]{:S(2)}, u32[]{:S(2)}) collective-permute-start(f32[2,8,16,256]{3,2,1,0:T(8,128)S(1)} %get-tuple-element.58), channel_id=1, source_target_pairs={{1,2},{2,1},{5,6},{6,5},{9,10},{10,9},{13,14},{14,13},{17,18},{18,... | collective-permute-start | bytes 786440 | tf_op jit(solution)/shard_map/ppermute | solution.py:61
  23.0 11.6 %collective-permute-start.12 = (f32[2,8,16,256]{3,2,1,0:T(8,128)S(1)}, f32[2,8,16,256]{3,2,1,0:T(8,128)S(1)}, u32[]{:S(2)}, u32[]{:S(2)}) collective-permute-start(f32[2,8,16,256]{3,2,1,0:T(8,128)S(1)} %get-tuple-element.78), channel_id=1, source_target_pairs={{0,1},{1,0},{2,3},{3,2},{4,5},{5,4},{6,7},{7,6},{8,9},{9,8},{10,11... | collective-permute-start | bytes 786440 | tf_op jit(solution)/shard_map/ppermute | solution.py:60
  26.7 7.9 %collective-permute-start.13 = (f32[2,8,16,256]{3,2,1,0:T(8,128)S(1)}, f32[2,8,16,256]{3,2,1,0:T(8,128)S(1)}, u32[]{:S(2)}, u32[]{:S(2)}) collective-permute-start(f32[2,8,16,256]{3,2,1,0:T(8,128)S(1)} %get-tuple-element.79), channel_id=1, source_target_pairs={{1,2},{2,1},{5,6},{6,5},{9,10},{10,9},{13,14},{14,13},{17,18},{18,... | collective-permute-start | bytes 786440 | tf_op jit(solution)/shard_map/ppermute | solution.py:61
  29.4 11.2 %collective-permute-start.4 = (f32[2,8,16,256]{3,2,1,0:T(8,128)S(1)}, f32[2,8,16,256]{3,2,1,0:T(8,128)S(1)}, u32[]{:S(2)}, u32[]{:S(2)}) collective-permute-start(f32[2,8,16,256]{3,2,1,0:T(8,128)S(1)} %get-tuple-element.62), channel_id=1, source_target_pairs={{0,1},{1,0},{2,3},{3,2},{4,5},{5,4},{6,7},{7,6},{8,9},{9,8},{10,11... | collective-permute-start | bytes 786440 | tf_op jit(solution)/shard_map/ppermute | solution.py:60
  33.9 6.7 %collective-permute-start.5 = (f32[2,8,16,256]{3,2,1,0:T(8,128)S(1)}, f32[2,8,16,256]{3,2,1,0:T(8,128)S(1)}, u32[]{:S(2)}, u32[]{:S(2)}) collective-permute-start(f32[2,8,16,256]{3,2,1,0:T(8,128)S(1)} %get-tuple-element.63), channel_id=1, source_target_pairs={{1,2},{2,1},{5,6},{6,5},{9,10},{10,9},{13,14},{14,13},{17,18},{18,... | collective-permute-start | bytes 786440 | tf_op jit(solution)/shard_map/ppermute | solution.py:61
  36.1 11.6 %collective-permute-start.14 = (f32[2,8,16,256]{3,2,1,0:T(8,128)S(1)}, f32[2,8,16,256]{3,2,1,0:T(8,128)S(1)}, u32[]{:S(2)}, u32[]{:S(2)}) collective-permute-start(f32[2,8,16,256]{3,2,1,0:T(8,128)S(1)} %get-tuple-element.82), channel_id=1, source_target_pairs={{0,1},{1,0},{2,3},{3,2},{4,5},{5,4},{6,7},{7,6},{8,9},{9,8},{10,11... | collective-permute-start | bytes 786440 | tf_op jit(solution)/shard_map/ppermute | solution.py:60
  39.9 7.8 %collective-permute-start.15 = (f32[2,8,16,256]{3,2,1,0:T(8,128)S(1)}, f32[2,8,16,256]{3,2,1,0:T(8,128)S(1)}, u32[]{:S(2)}, u32[]{:S(2)}) collective-permute-start(f32[2,8,16,256]{3,2,1,0:T(8,128)S(1)} %get-tuple-element.83), channel_id=1, source_target_pairs={{1,2},{2,1},{5,6},{6,5},{9,10},{10,9},{13,14},{14,13},{17,18},{18,... | collective-permute-start | bytes 786440 | tf_op jit(solution)/shard_map/ppermute | solution.py:61
  42.0 11.4 %collective-permute-start.6 = (f32[2,8,16,256]{3,2,1,0:T(8,128)S(1)}, f32[2,8,16,256]{3,2,1,0:T(8,128)S(1)}, u32[]{:S(2)}, u32[]{:S(2)}) collective-permute-start(f32[2,8,16,256]{3,2,1,0:T(8,128)S(1)} %get-tuple-element.66), channel_id=1, source_target_pairs={{0,1},{1,0},{2,3},{3,2},{4,5},{5,4},{6,7},{7,6},{8,9},{9,8},{10,11... | collective-permute-start | bytes 786440 | tf_op jit(solution)/shard_map/ppermute | solution.py:60
  47.0 6.4 %collective-permute-start.7 = (f32[2,8,16,256]{3,2,1,0:T(8,128)S(1)}, f32[2,8,16,256]{3,2,1,0:T(8,128)S(1)}, u32[]{:S(2)}, u32[]{:S(2)}) collective-permute-start(f32[2,8,16,256]{3,2,1,0:T(8,128)S(1)} %get-tuple-element.67), channel_id=1, source_target_pairs={{1,2},{2,1},{5,6},{6,5},{9,10},{10,9},{13,14},{14,13},{17,18},{18,... | collective-permute-start | bytes 786440 | tf_op jit(solution)/shard_map/ppermute | solution.py:61
  49.1 10.3 %collective-permute-start.16 = (f32[2,8,16,256]{3,2,1,0:T(8,128)S(1)}, f32[2,8,16,256]{3,2,1,0:T(8,128)S(1)}, u32[]{:S(2)}, u32[]{:S(2)}) collective-permute-start(f32[2,8,16,256]{3,2,1,0:T(8,128)S(1)} %get-tuple-element.86), channel_id=1, source_target_pairs={{0,1},{1,0},{2,3},{3,2},{4,5},{5,4},{6,7},{7,6},{8,9},{9,8},{10,11... | collective-permute-start | bytes 786440 | tf_op jit(solution)/shard_map/ppermute | solution.py:60
  52.5 6.9 %collective-permute-start.17 = (f32[2,8,16,256]{3,2,1,0:T(8,128)S(1)}, f32[2,8,16,256]{3,2,1,0:T(8,128)S(1)}, u32[]{:S(2)}, u32[]{:S(2)}) collective-permute-start(f32[2,8,16,256]{3,2,1,0:T(8,128)S(1)} %get-tuple-element.87), channel_id=1, source_target_pairs={{1,2},{2,1},{5,6},{6,5},{9,10},{10,9},{13,14},{14,13},{17,18},{18,... | collective-permute-start | bytes 786440 | tf_op jit(solution)/shard_map/ppermute | solution.py:61
  54.9 9.0 %collective-permute-start.8 = (f32[2,4,16,256]{3,2,1,0:T(8,128)S(1)}, f32[2,4,16,256]{3,2,1,0:T(8,128)S(1)}, u32[]{:S(2)}, u32[]{:S(2)}) collective-permute-start(f32[2,4,16,256]{3,2,1,0:T(8,128)S(1)} %get-tuple-element.70), channel_id=1, source_target_pairs={{0,1},{1,0},{2,3},{3,2},{4,5},{5,4},{6,7},{7,6},{8,9},{9,8},{10,11... | collective-permute-start | bytes 393224 | tf_op jit(solution)/shard_map/ppermute | solution.py:60
  58.6 5.3 %collective-permute-start.9 = (f32[2,4,16,256]{3,2,1,0:T(8,128)S(1)}, f32[2,4,16,256]{3,2,1,0:T(8,128)S(1)}, u32[]{:S(2)}, u32[]{:S(2)}) collective-permute-start(f32[2,4,16,256]{3,2,1,0:T(8,128)S(1)} %get-tuple-element.71), channel_id=1, source_target_pairs={{1,2},{2,1},{5,6},{6,5},{9,10},{10,9},{13,14},{14,13},{17,18},{18,... | collective-permute-start | bytes 393224 | tf_op jit(solution)/shard_map/ppermute | solution.py:61
  60.9 5.3 %collective-permute-start.18 = (f32[2,4,16,256]{3,2,1,0:T(8,128)S(1)}, f32[2,4,16,256]{3,2,1,0:T(8,128)S(1)}, u32[]{:S(2)}, u32[]{:S(2)}) collective-permute-start(f32[2,4,16,256]{3,2,1,0:T(8,128)S(1)} %get-tuple-element.90), channel_id=1, source_target_pairs={{0,1},{1,0},{2,3},{3,2},{4,5},{5,4},{6,7},{7,6},{8,9},{9,8},{10,11... | collective-permute-start | bytes 393224 | tf_op jit(solution)/shard_map/ppermute | solution.py:60
  63.2 3.0 %collective-permute-start.19 = (f32[2,4,16,256]{3,2,1,0:T(8,128)S(1)}, f32[2,4,16,256]{3,2,1,0:T(8,128)S(1)}, u32[]{:S(2)}, u32[]{:S(2)}) collective-permute-start(f32[2,4,16,256]{3,2,1,0:T(8,128)S(1)} %get-tuple-element.91), channel_id=1, source_target_pairs={{1,2},{2,1},{5,6},{6,5},{9,10},{10,9},{13,14},{14,13},{17,18},{18,... | collective-permute-start | bytes 393224 | tf_op jit(solution)/shard_map/ppermute | solution.py:61
  65.3 2.4 %collective-permute-start.20 = (f32[2,16,16,256]{3,2,1,0:T(8,128)S(1)}, f32[2,16,16,256]{3,2,1,0:T(8,128)S(1)}, u32[]{:S(2)}, u32[]{:S(2)}) collective-permute-start(f32[2,16,16,256]{3,2,1,0:T(8,128)S(1)} %get-tuple-element.72.refs_0_), channel_id=1, source_target_pairs={{0,4},{4,0},{8,12},{12,8},{1,5},{5,1},{9,13},{13,9},{2,6},{6,2},{1... | collective-permute-start | bytes 1572872 | tf_op jit(solution)/shard_map/ppermute | solution.py:421
  67.5 2.0 %copy-start.10 = (s32[8]{0:T(128)S(1)}, s32[8]{0:T(128)}, u32[]{:S(2)}) copy-start(s32[8]{0:T(128)} %offset_perm.3) | copy-start | bytes 100
  67.5 2.0 %collective-permute-start.21 = (f32[2,16,16,256]{3,2,1,0:T(8,128)S(1)}, f32[2,16,16,256]{3,2,1,0:T(8,128)S(1)}, u32[]{:S(2)}, u32[]{:S(2)}) collective-permute-start(f32[2,16,16,256]{3,2,1,0:T(8,128)S(1)} %get-tuple-element.94.refs_1_), channel_id=1, source_target_pairs={{0,4},{4,0},{8,12},{12,8},{1,5},{5,1},{9,13},{13,9},{2,6},{6,2},{1... | collective-permute-start | bytes 1572872 | tf_op jit(solution)/shard_map/ppermute | solution.py:421
  70.5 14.1 %collective-permute-start.22 = (f32[2,16,16,256]{3,2,1,0:T(8,128)S(1)}, f32[2,16,16,256]{3,2,1,0:T(8,128)S(1)}, u32[]{:S(2)}, u32[]{:S(2)}) collective-permute-start(f32[2,16,16,256]{3,2,1,0:T(8,128)S(1)} %image_1.1), channel_id=1, source_target_pairs={{0,8},{4,12},{8,0},{12,4},{1,9},{5,13},{9,1},{13,5},{2,10},{6,14},... | collective-permute-start | bytes 1572872 | tf_op jit(solution)/shard_map/ppermute | solution.py:428

commit v2 on v1

v2 whole, which is shorter than its diff:
```python
import functools

import jax
import jax.numpy as jnp
from jax import lax
from jax.experimental import pallas as pl
from jax.experimental.pallas import tpu as pltpu
from jax.sharding import PartitionSpec as P


REACH = 4
INJECT_Z = 4
LANES = 128
CHUNK = 8

SCALE = 8.0 / 5.0
SIDE = 1.0 / 16.0
OWN = (1.0 + 2.0 * SIDE) * (-205.0 / 72.0) / SCALE
TAPS = (1.0, -1.0 / 8.0, 1.0 / 63.0, -1.0 / 896.0)

VMEM_LIMIT = 24 * 1024 * 1024


def vmem():
    return pl.BlockSpec(memory_space=pltpu.VMEM)


def smem():
    return pl.BlockSpec(memory_space=pltpu.SMEM)


def hbm():
    return pl.BlockSpec(memory_space=pltpu.HBM)


def params():
    return pltpu.CompilerParams(vmem_limit_bytes=VMEM_LIMIT)


def struct(shape, dtype=jnp.float32):
    return jax.ShapeDtypeStruct(shape, dtype)


def even_pairs(count):
    pairs = []
    for i in range(0, count - 1, 2):
        pairs += [(i, i + 1), (i + 1, i)]
    return pairs


def odd_pairs(count):
    pairs = []
    for i in range(1, count - 1, 2):
        pairs += [(i, i + 1), (i + 1, i)]
    return pairs


def trade(even_edge, odd_edge):
    count = lax.axis_size("slab")
    even = lax.ppermute(even_edge, "slab", even_pairs(count))
    odd = lax.ppermute(odd_edge, "slab", odd_pairs(count))
    return even, odd


def parity():
    return lax.rem(lax.axis_index("slab"), 2)


def edge_starts(rows, width):
    odd = parity()
    return (1 - odd) * (rows - width), odd * (rows - width)


def halo_starts(rows, width):
    odd = parity()
    return (1 - odd) * (rows + width), odd * (rows + width)


def pack_kernel(groups, rows, *refs):
    source, receiver, courant = refs[:3]
    outs = refs[3 : 3 + 2 * groups]
    sem = refs[-1]
    copies = []
    for side, start in enumerate(edge_starts(rows, REACH)):
        planes = pl.ds(start, REACH)
        for group in range(groups):
            out = outs[2 * group + side]
            pieces = [source.at[group, planes], receiver.at[group, planes]]
            if group == 0:
                pieces.append(courant.at[planes])
            for index, piece in enumerate(pieces):
                copies.append(pltpu.make_async_copy(piece, out.at[index], sem.at[len(copies)]))
    for copy in copies:
        copy.start()
    for copy in copies:
        copy.wait()


def stay(*arrays):
    return [pltpu.with_memory_space_constraint(array, pltpu.HBM) for array in arrays]


def pack(source_now, receiver_now, courant_sq):
    groups, rows, size_y, size_z = source_now.shape
    shapes = []
    for group in range(groups):
        shapes += [struct((3 if group == 0 else 2, REACH, size_y, size_z))] * 2
    return pl.pallas_call(
        functools.partial(pack_kernel, groups, rows),
        out_shape=shapes,
        in_specs=[hbm()] * 3,
        out_specs=[vmem()] * len(shapes),
        scratch_shapes=[pltpu.SemaphoreType.DMA((2 * (2 * groups + 1),))],
        compiler_params=params(),
        name="pack",
    )(*stay(source_now, receiver_now, courant_sq))


def band(distance):
    value = jnp.zeros(distance.shape, jnp.float32)
    for step, tap in enumerate(TAPS):
        value = jnp.where(distance == step + 1, SIDE * tap, value)
    return value


def prepare_kernel(groups, rows, source_cell, wavelet, receiver_cell, traces, source, receiver, source_before, receiver_before, along_z, along_y, *refs):
    planes, now, before, sem = refs[:groups], refs[groups : 2 * groups], refs[2 * groups : 3 * groups], refs[-1]
    copies = []
    for group in range(groups):
        pieces = ((source, now, 0), (receiver, now, 1), (source_before, before, 0), (receiver_before, before, 1))
        for array, place, kind in pieces:
            copies.append(pltpu.make_async_copy(array.at[group], place[group].at[kind], sem.at[len(copies)]))
    for copy in copies:
        copy.start()
    _, plane_count, size_y, _ = planes[0].shape
    steps = traces.shape[0]
    size_z = along_z.shape[0]
    block = along_y.shape[0]
    row = lax.broadcasted_iota(jnp.int32, (size_z, size_z), 0)
    col = lax.broadcasted_iota(jnp.int32, (size_z, size_z), 1)
    along_z[...] = band(jnp.abs(row - col)).astype(jnp.bfloat16)
    row = lax.broadcasted_iota(jnp.int32, (block, block), 0)
    col = lax.broadcasted_iota(jnp.int32, (block, block), 1)
    same = lax.div(row, size_y) == lax.div(col, size_y)
    half = jnp.where(same, band(jnp.abs(row - col)), 0.0).astype(jnp.bfloat16)
    along_y[:, :block] = half
    along_y[:, block:] = half
    first = (lax.axis_index("slab") * rows - REACH) * size_y
    cells = plane_count * size_y
    lane = lax.broadcasted_iota(jnp.int32, (1, LANES), 1)
    for group in range(groups):
        ids = first + lax.broadcasted_iota(jnp.int32, (cells, 1), 0)
        amplitude = jnp.zeros((1, LANES), jnp.float32)
        for step in range(steps):
            amplitude = jnp.where(lane == step, wavelet[step, group], amplitude)
        hit = jnp.broadcast_to(ids, (cells, LANES)) == source_cell[group]
        spread = jnp.where(hit, jnp.broadcast_to(amplitude, (cells, LANES)), 0.0)
        planes[group][0] = spread.reshape(plane_count, size_y, LANES)
        count = receiver_cell.shape[1]
        wide = first + lax.broadcasted_iota(jnp.int32, (cells, count), 0)
        here = jnp.broadcast_to(receiver_cell[group : group + 1, :], (cells, count))
        hot = (wide == here).astype(jnp.float32)
        data = traces[:, group, :]
        data = jnp.concatenate([data, jnp.zeros((LANES - steps, count), jnp.float32)], axis=0)
        summed = lax.dot_general(
            hot,
            data,
            (((1,), (1,)), ((), ())),
            precision=lax.Precision.HIGHEST,
            preferred_element_type=jnp.float32,
        )
        planes[group][1] = summed.reshape(plane_count, size_y, LANES)
    for copy in copies:
        copy.wait()


def prepare(source_cell, wavelet, receiver_cell, traces, fields):
    groups, rows, size_y, size_z = fields[0].shape
    block = CHUNK * size_y
    return pl.pallas_call(
        functools.partial(prepare_kernel, groups, rows),
        out_shape=[
            struct((size_z, size_z), jnp.bfloat16),
            struct((block, 2 * block), jnp.bfloat16),
        ]
        + [struct((2, rows + 2 * REACH, size_y, LANES))] * groups
        + [struct((2, rows, size_y, size_z))] * (2 * groups),
        in_specs=[smem(), smem(), vmem(), vmem()] + [hbm()] * 4,
        out_specs=[vmem()] * (2 + 3 * groups),
        scratch_shapes=[pltpu.SemaphoreType.DMA((4 * groups,))],
        compiler_params=params(),
        name="prepare",
    )(source_cell, wavelet, receiver_cell, traces, *stay(*fields))


def advance(now, at, before, before_at, courant, courant_at, inject, inject_at, runs, step, along_z, along_y, write):
    size_y, size_z = now.shape[-2:]
    pieces = [now[at + first : at + first + count].reshape(count * size_y, size_z) for first, count in runs]
    value = pieces[0] if len(pieces) == 1 else jnp.concatenate(pieces, axis=0)
    high = value.astype(jnp.bfloat16)
    low = (value - high.astype(jnp.float32)).astype(jnp.bfloat16)
    dot = functools.partial(jnp.dot, preferred_element_type=jnp.float32)
    sides = dot(high, along_z) + dot(low, along_z)
    sides = sides + dot(along_y, jnp.concatenate([high, low], axis=0))
    lane = lax.broadcasted_iota(jnp.int32, (size_y, LANES), 1)
    for i, plane in enumerate(first + j for first, count in runs for j in range(count)):
        here = at + plane
        own = now[here]
        total = sides[i * size_y : (i + 1) * size_y] + OWN * own
        for distance, tap in enumerate(TAPS, 1):
            pair = now[here + distance] + now[here - distance]
            total = total + (pair if tap == 1.0 else tap * pair)
        new = (own + own) - before[before_at + plane] + courant[courant_at + plane] * total
        spot = pltpu.roll(inject[inject_at + plane], (INJECT_Z - step) % LANES, 1)
        near = new[:, :LANES] + jnp.where(lane == INJECT_Z, spot, 0.0)
        write(i, plane, jnp.concatenate([near, new[:, LANES:]], axis=1))


def chunks(start, stop):
    return [[(at, CHUNK)] for at in range(start, stop, CHUNK)]


def first_kernel(rows, has_courant, width, now, before, courant, even, odd, inject, along_z, along_y, fresh, held, even_edge, odd_edge, *scaled):
    even_at, odd_at = halo_starts(rows, REACH)
    if has_courant:
        (courant_out,) = scaled
        courant_out[REACH : REACH + rows] = SCALE * courant[...]
        courant_out[pl.ds(even_at, REACH)] = SCALE * even[2]
        courant_out[pl.ds(odd_at, REACH)] = SCALE * odd[2]
        courant = courant_out
    z_band, y_band = along_z[...], along_y[...]
    for kind in range(2):
        field = held.at[kind]
        field[REACH : REACH + rows] = now[kind]
        field[pl.ds(even_at, REACH)] = even[kind]
        field[pl.ds(odd_at, REACH)] = odd[kind]

        def write(i, plane, new, kind=kind):
            fresh[kind, plane] = new

        for runs in chunks(0, rows):
            advance(field, REACH, before.at[kind], 0, courant, REACH, inject.at[kind], REACH, runs, 0, z_band, y_band, write)
    send(rows, width, fresh, even_edge, odd_edge)


def send(rows, width, fresh, even_edge, odd_edge):
    even_from, odd_from = edge_starts(rows, width)
    even_edge[...] = fresh[:, pl.ds(even_from, width)]
    odd_edge[...] = fresh[:, pl.ds(odd_from, width)]


def first_round(group, width, now, before, courant, halos, inject, along_z, along_y):
    rows, size_y, size_z = now.shape[1:]
    has_courant = group == 0
    edge = struct((2, width, size_y, size_z))
    shapes = [struct(now.shape), struct((2, rows + 2 * REACH, size_y, size_z)), edge, edge]
    if has_courant:
        shapes.append(struct((rows + 2 * REACH, size_y, size_z)))
    return pl.pallas_call(
        functools.partial(first_kernel, rows, has_courant, width),
        out_shape=shapes,
        in_specs=[vmem()] * 8,
        out_specs=[vmem()] * len(shapes),
        compiler_params=params(),
    )(now, before, courant, *halos, inject, along_z, along_y)


def pair_kernel(rows, step, width, now, before, even, odd, courant, inject, along_z, along_y, fresh, held, even_edge, odd_edge, wide):
    reach = 2 * REACH
    even_at, odd_at = halo_starts(rows, reach)
    z_band, y_band = along_z[...], along_y[...]
    for kind in range(2):
        field = wide.at[kind]
        field[reach : reach + rows] = now[kind]
        field[pl.ds(even_at, reach)] = even[kind]
        field[pl.ds(odd_at, reach)] = odd[kind]
        middle = held.at[kind]

        def write_middle(i, plane, new, kind=kind):
            held[kind, REACH + plane] = new

        def write(i, plane, new, kind=kind):
            fresh[kind, plane] = new

        for runs in chunks(-REACH, rows + REACH):
            advance(field, reach, before.at[kind], REACH, courant, REACH, inject.at[kind], REACH, runs, step, z_band, y_band, write_middle)
        for runs in chunks(0, rows):
            advance(middle, REACH, field, reach, courant, REACH, inject.at[kind], REACH, runs, step + 1, z_band, y_band, write)
    send(rows, width, fresh, even_edge, odd_edge)


def pair_round(step, width, now, before, halos, courant, inject, along_z, along_y):
    rows, size_y, size_z = now.shape[1:]
    edge = struct((2, width, size_y, size_z))
    shapes = [struct(now.shape), struct((2, rows + 2 * REACH, size_y, size_z)), edge, edge]
    return pl.pallas_call(
        functools.partial(pair_kernel, rows, step, width),
        out_shape=shapes,
        in_specs=[vmem()] * 8,
        out_specs=[vmem()] * 4,
        scratch_shapes=[pltpu.VMEM((2, rows + 4 * REACH, size_y, size_z), jnp.float32)],
        compiler_params=params(),
    )(now, before, *halos, courant, inject, along_z, along_y)


def inner_kernel(group, rows, step, now, before, courant, inject, along_z, along_y, *refs):
    final, source_out, receiver_out, sem = refs[-4:]
    count = rows - 2 * REACH
    z_band, y_band = along_z[...], along_y[...]
    copies = []
    for kind, out in enumerate((source_out, receiver_out)):

        def write(i, plane, new, kind=kind):
            final[kind, plane - REACH] = new

        for runs in chunks(REACH, rows - REACH):
            advance(now.at[kind], 0, before.at[kind], REACH, courant, REACH, inject.at[kind], REACH, runs, step, z_band, y_band, write)
        copies.append(pltpu.make_async_copy(final.at[kind], out.at[group, pl.ds(REACH, count)], sem.at[kind]))
        copies[kind].start()
    for copy in copies:
        copy.wait()


def inner_round(group, groups, step, now, before, courant, inject, along_z, along_y, outs):
    rows, size_y, size_z = now.shape[1:]
    whole = struct((groups, rows, size_y, size_z))
    return pl.pallas_call(
        functools.partial(inner_kernel, group, rows, step),
        out_shape=[struct((2, rows - 2 * REACH, size_y, size_z)), whole, whole],
        in_specs=[vmem()] * 6 + [hbm()] * len(outs),
        out_specs=[vmem(), hbm(), hbm()],
        scratch_shapes=[pltpu.SemaphoreType.DMA((2,))],
        input_output_aliases={6: 1, 7: 2} if outs else {},
        compiler_params=params(),
    )(now, before, courant, inject, along_z, along_y, *outs)


def outer_kernel(group, rows, step, now, before, even, odd, courant, inject, along_z, along_y, *refs):
    final, source_out, receiver_out, wide, sem = refs[-5:]
    even_at, odd_at = halo_starts(rows, REACH)
    z_band, y_band = along_z[...], along_y[...]
    copies = []
    for kind, out in enumerate((source_out, receiver_out)):
        field = wide.at[kind]
        field[REACH : REACH + rows] = now[kind]
        field[pl.ds(even_at, REACH)] = even[kind]
        field[pl.ds(odd_at, REACH)] = odd[kind]

        def write(i, plane, new, kind=kind):
            final[kind, i] = new

        runs = [(0, REACH), (rows - REACH, REACH)]
        advance(field, REACH, before.at[kind], REACH, courant, REACH, inject.at[kind], REACH, runs, step, z_band, y_band, write)
        for side, (first, count) in enumerate(runs):
            piece = final.at[kind, pl.ds(side * REACH, REACH)]
            copies.append(pltpu.make_async_copy(piece, out.at[group, pl.ds(first, count)], sem.at[2 * kind + side]))
            copies[-1].start()
    for copy in copies:
        copy.wait()


def outer_round(group, step, now, before, halos, courant, inject, along_z, along_y, outs):
    rows, size_y, size_z = now.shape[1:]
    return pl.pallas_call(
        functools.partial(outer_kernel, group, rows, step),
        out_shape=[struct((2, 2 * REACH, size_y, size_z))] + [struct(out.shape) for out in outs],
        in_specs=[vmem()] * 8 + [hbm()] * len(outs),
        out_specs=[vmem(), hbm(), hbm()],
        scratch_shapes=[pltpu.VMEM((2, rows + 2 * REACH, size_y, size_z), jnp.float32), pltpu.SemaphoreType.DMA((4,))],
        input_output_aliases={8: 1, 9: 2},
        compiler_params=params(),
    )(now, before, *halos, courant, inject, along_z, along_y, *outs)


def shifted(plane, amount):
    size_y = plane.shape[0]
    if amount == 0:
        return plane
    if abs(amount) >= size_y:
        return jnp.zeros_like(plane)
    row = lax.broadcasted_iota(jnp.int32, plane.shape, 0)
    inside = (row >= amount) if amount > 0 else (row < size_y + amount)
    return jnp.where(inside, pltpu.roll(plane, amount % size_y, 0), 0.0)


def partial_image(ahead, offset_perm, fields, image, others=()):
    count = offset_perm.shape[0]
    half_span = count // 2
    slots, rows = image.shape[:2]
    here = lax.axis_index("shot")
    pairs = lax.axis_size("shot") // 2
    owner = 2 * lax.rem(lax.div(here, 2) + ahead, pairs) + lax.rem(here, 2)

    def one_slot(slot, carry):
        index = offset_perm[owner * slots + slot]
        for lag_index in range(count):
            lag = lag_index - half_span

            @pl.when(index == lag_index)
            def _(lag=lag):
                def one_plane(x, carry):
                    total = None
                    for field in fields:
                        term = field[1, x] * shifted(field[0, x], 2 * lag)
                        total = term if total is None else total + term
                    total = shifted(total, -lag)
                    for other in others:
                        total = total + other[slot, x]
                    image[slot, x] = total
                    return carry

                lax.fori_loop(0, rows, one_plane, 0, unroll=2)

        return carry

    lax.fori_loop(0, slots, one_slot, 0)


def image_kernel(ahead, offset_perm, *refs):
    partial_image(ahead, offset_perm, refs[:-1], refs[-1])


def image_part(ahead, slots, offset_perm, fields):
    _, rows, size_y, size_z = fields[0].shape
    return pl.pallas_call(
        functools.partial(image_kernel, ahead),
        out_shape=struct((slots, rows, size_y, size_z)),
        in_specs=[smem()] + [vmem()] * len(fields),
        out_specs=vmem(),
        compiler_params=params(),
    )(offset_perm, *fields)


def inner_image_kernel(shots, offset_perm, *refs):
    inner_fields, outer_fields = refs[:shots], refs[shots : 2 * shots]
    others = refs[2 * shots : -4]
    image, outer, inner, sem = refs[-4:]
    partial_image(0, offset_perm, inner_fields, inner, others)
    copy = pltpu.make_async_copy(inner, image.at[:, pl.ds(REACH, inner.shape[1])], sem)
    copy.start()
    partial_image(0, offset_perm, outer_fields, outer)
    copy.wait()


def inner_image(slots, rows, offset_perm, inner_fields, outer_fields, others):
    _, inner_rows, size_y, size_z = inner_fields[0].shape
    shots = len(inner_fields)
    return pl.pallas_call(
        functools.partial(inner_image_kernel, shots),
        out_shape=[struct((slots, rows, size_y, size_z)), struct((slots, 2 * REACH, size_y, size_z))],
        in_specs=[smem()] + [vmem()] * (2 * shots + len(others)),
        out_specs=[hbm(), vmem()],
        scratch_shapes=[pltpu.VMEM((slots, inner_rows, size_y, size_z), jnp.float32), pltpu.SemaphoreType.DMA(())],
        compiler_params=params(),
        name="image_inner",
    )(offset_perm, *inner_fields, *outer_fields, *others)


def outer_image_kernel(rows, *refs):
    own, others = refs[0], refs[1:-4]
    image, outer, sem = refs[-3:]
    copies = []
    for side, first in enumerate((0, rows - REACH)):
        planes = pl.ds(side * REACH, REACH)
        total = own[:, planes]
        for other in others:
            total = total + other[:, planes]
        outer[:, planes] = total
        copies.append(pltpu.make_async_copy(outer.at[:, planes], image.at[:, pl.ds(first, REACH)], sem.at[side]))
        copies[side].start()
    for copy in copies:
        copy.wait()


def outer_image(image, own, others):
    return pl.pallas_call(
        functools.partial(outer_image_kernel, image.shape[1]),
        out_shape=struct(image.shape),
        in_specs=[vmem()] * (1 + len(others)) + [hbm()],
        out_specs=hbm(),
        scratch_shapes=[pltpu.VMEM(own.shape, jnp.float32), pltpu.SemaphoreType.DMA((2,))],
        input_output_aliases={1 + len(others): 0},
        compiler_params=params(),
        name="image_outer",
    )(own, *others, image)


def program(source_now, source_prev, receiver_now, receiver_prev, courant_sq, source_cell, wavelet, receiver_cell, traces, offset_perm):
    groups, rows, _, _ = source_now.shape
    steps = wavelet.shape[0]
    shot_devices = lax.axis_size("shot")
    slots = offset_perm.shape[0] // shot_devices
    everyone = range(groups)

    edges = pack(source_now, receiver_now, courant_sq)
    halos = [trade(edges[2 * g], edges[2 * g + 1]) for g in everyone]
    fields = (source_now, receiver_now, source_prev, receiver_prev)
    along_z, along_y, *rest = prepare(source_cell, wavelet, receiver_cell, traces, fields)
    inject, now, before = rest[:groups], rest[groups : 2 * groups], rest[2 * groups :]

    courant = courant_sq
    for g in everyone:
        result = first_round(g, 2 * REACH, now[g], before[g], courant, halos[g], inject[g], along_z, along_y)
        now[g], before[g] = result[:2]
        if g == 0:
            courant = result[4]
        halos[g] = trade(*result[2:4])
    outs = ()
    inner, outer = [None] * groups, [None] * groups
    for step in range(1, steps - 1, 2):
        width = 2 * REACH if step + 2 < steps - 1 else REACH
        for g in everyone:
            now[g], before[g], even, odd = pair_round(step, width, now[g], before[g], halos[g], courant, inject[g], along_z, along_y)
            halos[g] = trade(even, odd)
            if width == REACH:
                inner[g], *outs = inner_round(g, groups, steps - 1, now[g], before[g], courant, inject[g], along_z, along_y, outs)

    swap = [(i, i ^ 1) for i in range(shot_devices)]
    pairs = shot_devices // 2

    def travel(parts):
        sums = []
        for ahead, part in enumerate(parts, 1):
            route = [(2 * p + c, 2 * ((p + ahead) % pairs) + c) for p in range(pairs) for c in range(2)]
            sums.append(lax.ppermute(part, "shot", route))
        return sums

    def traded(fields):
        others = []
        for g in everyone:
            others.append(lax.ppermute(fields[g], "shot", swap))
        return fields + others

    inner = traded(inner)
    parts = [image_part(ahead, slots, offset_perm, inner) for ahead in range(1, pairs)]
    inner_sums = travel(parts)
    for g in everyone:
        outer[g], *outs = outer_round(g, steps - 1, now[g], before[g], halos[g], courant, inject[g], along_z, along_y, outs)
    outer = traded(outer)
    outer_sums = travel([image_part(ahead, slots, offset_perm, outer) for ahead in range(1, pairs)])
    image, own = inner_image(slots, rows, offset_perm, inner, outer, inner_sums)
    image = outer_image(image, own, outer_sums)
    return (image, *outs)


def solution(mesh):
    shots = ("runs", "shot")
    in_specs = (
        P(shots, "slab", None, None),
        P(shots, "slab", None, None),
        P(shots, "slab", None, None),
        P(shots, "slab", None, None),
        P(("runs", "slab"), None, None),
        P(shots),
        P(None, shots),
        P(shots, None),
        P(None, shots, None),
        P("runs"),
    )
    out_specs = (P(shots, "slab", None, None),) * 3
    return jax.shard_map(program, mesh=mesh, in_specs=in_specs, out_specs=out_specs, check_vma=False)
```

time: 87 us -> 80.4 us (0.924); the launches traced: 85.5 us -> 79.9 us
  local copies, waits for them, and re-layouts: 5.93 us -> 0.17 us
  Pallas kernels: 18.1 us -> 22.7 us
  waiting for transfers between devices: 14.8 us -> 10.6 us
  other arithmetic: 0.87 us -> 0 us
    unnamed x27 -> x13, local copies, waits for them, and re-layouts: 5.93 us -> 0.17 us
    ppermute x23 -> x26, waiting for transfers between devices: 14.8 us -> 10.6 us  [the longest x2 9.2 us: travel(): sums.append(lax.ppermute(part, 'shot', route))]
    pallas_call x7 -> x11, Pallas kernels: 8.29 us -> 12.4 us  [the longest x2 2.33 us: outer_round(): pl.pallas_call(functools.partial(outer_kernel, group, rows, step), out_sh...]
    add x1 -> x0, other arithmetic: 0.87 us -> none  [body(): image = image + part]
    ppermute x23 -> x26, starting transfers between devices: 44.8 us -> 45.4 us  [the longest x10 35.1 us: trade(): even = lax.ppermute(even_edge, 'slab', even_pairs(count))]
  transfers between devices with their start and end apart: 23 -> 26, of which waited for: 5 -> 4; matrix products, arithmetic and copies ran while one was open for 0% -> 0% of each run, Pallas kernels for 19% -> 26%
where the time goes in v2:
time: 80.4 us; the launch traced here: 79.9 us
  starting transfers between devices  45.4 us (56%)
  Pallas kernels  22.7 us (28%)
  waiting for transfers between devices  10.6 us (13%)
  between operations  1.15 us (1%)
    ppermute x10, starting transfers between devices, trade(): even = lax.ppermute(even_edge, 'slab', even_pairs(count))  35.1 us
    ppermute x2, waiting for transfers between devices, travel(): sums.append(lax.ppermute(part, 'shot', route))  9.2 us
    pallas_call x6, Pallas kernels, pair_round(): pl.pallas_call(functools.partial(pair_kernel, rows, step, width), out_sha...  9.04 us
    ppermute x10, starting transfers between devices, trade(): odd = lax.ppermute(odd_edge, 'slab', odd_pairs(count))  6.94 us
    pallas_call x2, Pallas kernels, outer_round(): pl.pallas_call(functools.partial(outer_kernel, group, rows, step), out_sh...  2.33 us
    pallas_call x2, Pallas kernels, inner_round(): pl.pallas_call(functools.partial(inner_kernel, group, rows, step), out_sh...  2.23 us
    pallas_call x1, Pallas kernels, prepare(): pl.pallas_call(functools.partial(prepare_kernel, groups, rows), out_shape...  2.19 us
    ppermute x2, starting transfers between devices, travel(): sums.append(lax.ppermute(part, 'shot', route))  2.16 us
  transfers between devices with their start and end apart: 26, of which 4 were waited for; matrix products, arithmetic and copies ran while one was open for 0% of the time, Pallas kernels for 26%

profile of v2, /device:TPU:0, one launch (start us, length us, event | category | flops | bytes accessed | tf_op | source)
XLA Modules:
  0.0 79.9 jit_solution(13686934079005045006)
XLA Ops:
  0.6 1.2 %pack.1 = (f32[3,4,16,256]{3,2,1,0:T(8,128)S(1)}, f32[3,4,16,256]{3,2,1,0:T(8,128)S(1)}, f32[2,4,16,256]{3,2,1,0:T(8,128)S(1)}, f32[2,4,16,256]{3,2,1,0:T(8,128)S(1)}) custom-call(f32[2,16,16,256]{3,2,1,0:T(8,128)} %refs_0_.1, f32[2,16,16,256]{3,2,1,0:T(8,128)} %refs_1_.1, f32[16,16,256]{2,1,0:T(8,128)} %courant.1), custom_call_target="tpu_custom_call" | custom-call | tf_op jit(solution)/shard_map/pack/pallas_call | solution.py:108
  1.9 3.1 %collective-permute-start = (f32[3,4,16,256]{3,2,1,0:T(8,128)S(1)}, f32[3,4,16,256]{3,2,1,0:T(8,128)S(1)}, u32[]{:S(2)}, u32[]{:S(2)}) collective-permute-start(f32[3,4,16,256]{3,2,1,0:T(8,128)S(1)} %get-tuple-element.64), channel_id=1, source_target_pairs={{0,1},{1,0},{2,3},{3,2},{4,5},{5,4},{6,7},{7,6},{8,9},{9,8},{10,11... | collective-permute-start | bytes 589832 | tf_op jit(solution)/shard_map/ppermute | solution.py:60
  5.0 0.7 collective-permute-start.1
  5.6 0.0 copy-start.5
  5.7 4.5 %collective-permute-start.8 = (f32[2,4,16,256]{3,2,1,0:T(8,128)S(1)}, f32[2,4,16,256]{3,2,1,0:T(8,128)S(1)}, u32[]{:S(2)}, u32[]{:S(2)}) collective-permute-start(f32[2,4,16,256]{3,2,1,0:T(8,128)S(1)} %get-tuple-element.87), channel_id=1, source_target_pairs={{0,1},{1,0},{2,3},{3,2},{4,5},{5,4},{6,7},{7,6},{8,9},{9,8},{10,11... | collective-permute-start | bytes 393224 | tf_op jit(solution)/shard_map/ppermute | solution.py:60
  10.1 0.8 collective-permute-start.9
  10.9 0.1 copy.20.wavelet
  11.0 2.2 %prepare.1 = (bf16[256,256]{1,0:T(8,128)(2,1)S(1)}, bf16[128,256]{1,0:T(8,128)(2,1)S(1)}, f32[2,24,16,128]{3,2,1,0:T(8,128)S(1)}, f32[2,24,16,128]{3,2,1,0:T(8,1...) custom-call(s32[2]{0:T(128)S(1)} %copy-done.4, ...), custom_call_target="tpu_custom_call" | custom-call | tf_op jit(solution)/shard_map/prepare/pallas_call | solution.py:180
  13.2 0.0 collective-permute-done.even
  13.2 0.0 collective-permute-done.1.odd
  13.3 0.8 shard_map.121
  14.0 2.2 %collective-permute-start.2 = (f32[2,8,16,256]{3,2,1,0:T(8,128)S(1)}, f32[2,8,16,256]{3,2,1,0:T(8,128)S(1)}, u32[]{:S(2)}, u32[]{:S(2)}) collective-permute-start(f32[2,8,16,256]{3,2,1,0:T(8,128)S(1)} %get-tuple-element.71), channel_id=1, source_target_pairs={{0,1},{1,0},{2,3},{3,2},{4,5},{5,4},{6,7},{7,6},{8,9},{9,8},{10,11... | collective-permute-start | bytes 786440 | tf_op jit(solution)/shard_map/ppermute | solution.py:60
  16.2 0.7 collective-permute-start.3
  16.9 0.0 collective-permute-done.8.even
  16.9 0.0 collective-permute-done.9.odd
  16.9 0.8 shard_map.126
  17.7 3.7 %collective-permute-start.10 = (f32[2,8,16,256]{3,2,1,0:T(8,128)S(1)}, f32[2,8,16,256]{3,2,1,0:T(8,128)S(1)}, u32[]{:S(2)}, u32[]{:S(2)}) collective-permute-start(f32[2,8,16,256]{3,2,1,0:T(8,128)S(1)} %get-tuple-element.92), channel_id=1, source_target_pairs={{0,1},{1,0},{2,3},{3,2},{4,5},{5,4},{6,7},{7,6},{8,9},{9,8},{10,11... | collective-permute-start | bytes 786440 | tf_op jit(solution)/shard_map/ppermute | solution.py:60
  21.4 0.7 collective-permute-start.11
  22.1 0.9 %collective-permute-done.2.even = f32[2,8,16,256]{3,2,1,0:T(8,128)S(1)} collective-permute-done((f32[2,8,16,256]{3,2,1,0:T(8,128)S(1)}, f32[2,8,16,256]{3,2,1,0:T(8,128)S(1)}, u32[]{:S(2)}, u32[]{:S(2)}) %collective-permute-start.2) | collective-permute-done | bytes 262176 | tf_op jit(solution)/shard_map/ppermute | solution.py:60
  23.0 0.0 collective-permute-done.3.odd
  23.0 1.5 %shard_map.122 = (f32[2,16,16,256]{3,2,1,0:T(8,128)S(1)}, f32[2,24,16,256]{3,2,1,0:T(8,128)S(1)}, f32[2,8,16,256]{3,2,1,0:T(8,128)S(1)}, f32[2,8,16,256]{3,2,1,0:T(8,128)S(1)}) custom-call(f32[2,16,16,256]{3,2,1,0:T(8,128)S(1)} %get-tuple-element.69.now, f32[2,24,16,256]{3,2,1,0:T(8,128)S(1)} %get-tuple-element.70.before, ...), custom_call_target="tpu_custom_call" | custom-call | tf_op jit(solution)/shard_map/pallas_call | solution.py:296
  24.5 4.1 %collective-permute-start.4 = (f32[2,8,16,256]{3,2,1,0:T(8,128)S(1)}, f32[2,8,16,256]{3,2,1,0:T(8,128)S(1)}, u32[]{:S(2)}, u32[]{:S(2)}) collective-permute-start(f32[2,8,16,256]{3,2,1,0:T(8,128)S(1)} %get-tuple-element.76), channel_id=1, source_target_pairs={{0,1},{1,0},{2,3},{3,2},{4,5},{5,4},{6,7},{7,6},{8,9},{9,8},{10,11... | collective-permute-start | bytes 786440 | tf_op jit(solution)/shard_map/ppermute | solution.py:60
  28.6 0.7 collective-permute-start.5
  29.3 0.0 collective-permute-done.11.odd
  29.3 1.5 %shard_map.127 = (f32[2,16,16,256]{3,2,1,0:T(8,128)S(1)}, f32[2,24,16,256]{3,2,1,0:T(8,128)S(1)}, f32[2,8,16,256]{3,2,1,0:T(8,128)S(1)}, f32[2,8,16,256]{3,2,1,0:T(8,128)S(1)}) custom-call(f32[2,16,16,256]{3,2,1,0:T(8,128)S(1)} %get-tuple-element.90.now, f32[2,24,16,256]{3,2,1,0:T(8,128)S(1)} %get-tuple-element.91.before, ...), custom_call_target="tpu_custom_call" | custom-call | tf_op jit(solution)/shard_map/pallas_call | solution.py:296
  30.8 3.8 %collective-permute-start.12 = (f32[2,8,16,256]{3,2,1,0:T(8,128)S(1)}, f32[2,8,16,256]{3,2,1,0:T(8,128)S(1)}, u32[]{:S(2)}, u32[]{:S(2)}) collective-permute-start(f32[2,8,16,256]{3,2,1,0:T(8,128)S(1)} %get-tuple-element.96), channel_id=1, source_target_pairs={{0,1},{1,0},{2,3},{3,2},{4,5},{5,4},{6,7},{7,6},{8,9},{9,8},{10,11... | collective-permute-start | bytes 786440 | tf_op jit(solution)/shard_map/ppermute | solution.py:60
  34.6 0.7 collective-permute-start.13
  35.3 0.0 collective-permute-done.5.odd
  35.3 1.5 %shard_map.123 = (f32[2,16,16,256]{3,2,1,0:T(8,128)S(1)}, f32[2,24,16,256]{3,2,1,0:T(8,128)S(1)}, f32[2,8,16,256]{3,2,1,0:T(8,128)S(1)}, f32[2,8,16,256]{3,2,1,0:T(8,128)S(1)}) custom-call(f32[2,16,16,256]{3,2,1,0:T(8,128)S(1)} %get-tuple-element.74.now, f32[2,24,16,256]{3,2,1,0:T(8,128)S(1)} %get-tuple-element.75.before, ...), custom_call_target="tpu_custom_call" | custom-call | tf_op jit(solution)/shard_map/pallas_call | solution.py:296
  36.8 4.6 %collective-permute-start.6 = (f32[2,8,16,256]{3,2,1,0:T(8,128)S(1)}, f32[2,8,16,256]{3,2,1,0:T(8,128)S(1)}, u32[]{:S(2)}, u32[]{:S(2)}) collective-permute-start(f32[2,8,16,256]{3,2,1,0:T(8,128)S(1)} %get-tuple-element.80), channel_id=1, source_target_pairs={{0,1},{1,0},{2,3},{3,2},{4,5},{5,4},{6,7},{7,6},{8,9},{9,8},{10,11... | collective-permute-start | bytes 786440 | tf_op jit(solution)/shard_map/ppermute | solution.py:60
  41.4 0.7 collective-permute-start.7
  42.1 1.5 %shard_map.128 = (f32[2,16,16,256]{3,2,1,0:T(8,128)S(1)}, f32[2,24,16,256]{3,2,1,0:T(8,128)S(1)}, f32[2,8,16,256]{3,2,1,0:T(8,128)S(1)}, f32[2,8,16,256]{3,2,1,0:T(8,128)S(1)}) custom-call(f32[2,16,16,256]{3,2,1,0:T(8,128)S(1)} %get-tuple-element.94.now, f32[2,24,16,256]{3,2,1,0:T(8,128)S(1)} %get-tuple-element.95.before, ...), custom_call_target="tpu_custom_call" | custom-call | tf_op jit(solution)/shard_map/pallas_call | solution.py:296
  43.6 3.6 %collective-permute-start.14 = (f32[2,8,16,256]{3,2,1,0:T(8,128)S(1)}, f32[2,8,16,256]{3,2,1,0:T(8,128)S(1)}, u32[]{:S(2)}, u32[]{:S(2)}) collective-permute-start(f32[2,8,16,256]{3,2,1,0:T(8,128)S(1)} %get-tuple-element.100), channel_id=1, source_target_pairs={{0,1},{1,0},{2,3},{3,2},{4,5},{5,4},{6,7},{7,6},{8,9},{9,8},{10,11... | collective-permute-start | bytes 786440 | tf_op jit(solution)/shard_map/ppermute | solution.py:60
  47.3 0.7 collective-permute-start.15
  47.9 0.4 collective-permute-done.6.even
  48.4 0.0 collective-permute-done.7.odd
  48.4 1.5 %shard_map.124 = (f32[2,16,16,256]{3,2,1,0:T(8,128)S(1)}, f32[2,24,16,256]{3,2,1,0:T(8,128)S(1)}, f32[2,4,16,256]{3,2,1,0:T(8,128)S(1)}, f32[2,4,16,256]{3,2,1,0:T(8,128)S(1)}) custom-call(f32[2,16,16,256]{3,2,1,0:T(8,128)S(1)} %get-tuple-element.78.now, f32[2,24,16,256]{3,2,1,0:T(8,128)S(1)} %get-tuple-element.79.before, ...), custom_call_target="tpu_custom_call" | custom-call | tf_op jit(solution)/shard_map/pallas_call | solution.py:296
  49.9 3.7 %collective-permute-start.18 = (f32[2,4,16,256]{3,2,1,0:T(8,128)S(1)}, f32[2,4,16,256]{3,2,1,0:T(8,128)S(1)}, u32[]{:S(2)}, u32[]{:S(2)}) collective-permute-start(f32[2,4,16,256]{3,2,1,0:T(8,128)S(1)} %get-tuple-element.107), channel_id=1, source_target_pairs={{0,1},{1,0},{2,3},{3,2},{4,5},{5,4},{6,7},{7,6},{8,9},{9,8},{10,11... | collective-permute-start | bytes 393224 | tf_op jit(solution)/shard_map/ppermute | solution.py:60
  53.6 0.8 %collective-permute-start.19 = (f32[2,4,16,256]{3,2,1,0:T(8,128)S(1)}, f32[2,4,16,256]{3,2,1,0:T(8,128)S(1)}, u32[]{:S(2)}, u32[]{:S(2)}) collective-permute-start(f32[2,4,16,256]{3,2,1,0:T(8,128)S(1)} %get-tuple-element.108), channel_id=1, source_target_pairs={{1,2},{2,1},{5,6},{6,5},{9,10},{10,9},{13,14},{14,13},{17,18},{18,... | collective-permute-start | bytes 393224 | tf_op jit(solution)/shard_map/ppermute | solution.py:61
  54.5 0.0 collective-permute-done.14.even
  54.5 1.5 %shard_map.129 = (f32[2,16,16,256]{3,2,1,0:T(8,128)S(1)}, f32[2,24,16,256]{3,2,1,0:T(8,128)S(1)}, f32[2,4,16,256]{3,2,1,0:T(8,128)S(1)}, f32[2,4,16,256]{3,2,1,0:T(8,128)S(1)}) custom-call(f32[2,16,16,256]{3,2,1,0:T(8,128)S(1)} %get-tuple-element.98.now, f32[2,24,16,256]{3,2,1,0:T(8,128)S(1)} %get-tuple-element.99.before, ...), custom_call_target="tpu_custom_call" | custom-call | tf_op jit(solution)/shard_map/pallas_call | solution.py:296
  55.9 1.8 %collective-permute-start.20 = (f32[2,4,16,256]{3,2,1,0:T(8,128)S(1)}, f32[2,4,16,256]{3,2,1,0:T(8,128)S(1)}, u32[]{:S(2)}, u32[]{:S(2)}) collective-permute-start(f32[2,4,16,256]{3,2,1,0:T(8,128)S(1)} %get-tuple-element.112), channel_id=1, source_target_pairs={{0,1},{1,0},{2,3},{3,2},{4,5},{5,4},{6,7},{7,6},{8,9},{9,8},{10,11... | collective-permute-start | bytes 393224 | tf_op jit(solution)/shard_map/ppermute | solution.py:60
  57.8 0.7 collective-permute-start.21
  58.4 1.1 %shard_map.125 = (f32[2,8,16,256]{3,2,1,0:T(8,128)S(1)}, f32[2,16,16,256]{3,2,1,0:T(8,128)}, f32[2,16,16,256]{3,2,1,0:T(8,128)}) custom-call(f32[2,16,16,256]{3,2,1,0:T(8,128)S(1)} %get-tuple-element.82.now, f32[2,24,16,256]{3,2,1,0:T(8,128)S(1)} %get-tuple-element.83.before, f32[24,16,256]{2,1,0:T(8,128)S(1)} %get-tuple-element.73.courant, ...), custom_call_target="tpu_custom_call" | custom-call | tf_op jit(solution)/shard_map/pallas_call | solution.py:327
  59.5 1.1 %shard_map.130 = (f32[2,8,16,256]{3,2,1,0:T(8,128)S(1)}, f32[2,16,16,256]{3,2,1,0:T(8,128)}, f32[2,16,16,256]{3,2,1,0:T(8,128)}) custom-call(f32[2,16,16,256]{3,2,1,0:T(8,128)S(1)} %get-tuple-element.102.now, f32[2,24,16,256]{3,2,1,0:T(8,128)S(1)} %get-tuple-element.103.before, ...), custom_call_target="tpu_custom_call", output_to_operand_aliasing={{1}: (6, {}), {2}: (7, {})} | custom-call | tf_op jit(solution)/shard_map/pallas_call | solution.py:327
  60.7 0.1 collective-permute-start.17
  60.7 0.0 collective-permute-done.18.even
  60.8 0.5 collective-permute-start.16
  61.2 1.2 %shard_map.131 = (f32[2,8,16,256]{3,2,1,0:T(8,128)S(1)}, f32[2,16,16,256]{3,2,1,0:T(8,128)}, f32[2,16,16,256]{3,2,1,0:T(8,128)}) custom-call(f32[2,16,16,256]{3,2,1,0:T(8,128)S(1)} %get-tuple-element.82.now, f32[2,24,16,256]{3,2,1,0:T(8,128)S(1)} %get-tuple-element.83.before, ...), custom_call_target="tpu_custom_call", output_to_operand_aliasing={{1}: (8, {}), {2}: (9, {})} | custom-call | tf_op jit(solution)/shard_map/pallas_call | solution.py:364
  62.4 0.0 collective-permute-done.20.even
  62.4 1.2 %shard_map.132 = (f32[2,8,16,256]{3,2,1,0:T(8,128)S(1)}, f32[2,16,16,256]{3,2,1,0:T(8,128)}, f32[2,16,16,256]{3,2,1,0:T(8,128)}) custom-call(f32[2,16,16,256]{3,2,1,0:T(8,128)S(1)} %get-tuple-element.102.now, f32[2,24,16,256]{3,2,1,0:T(8,128)S(1)} %get-tuple-element.103.before, ...), custom_call_target="tpu_custom_call", output_to_operand_aliasing={{1}: (8, {}), {2}: (9, {})} | custom-call | tf_op jit(solution)/shard_map/pallas_call | solution.py:364
  63.6 0.0 copy-start.2
  63.6 0.1 collective-permute-start.23
  63.8 0.4 collective-permute-start.22
  64.2 0.0 collective-permute-done.17.refs_3_
  64.2 0.1 copy-done.2
  64.3 0.9 %shard_map.133 = f32[2,8,16,256]{3,2,1,0:T(8,128)S(1)} custom-call(s32[8]{0:T(128)S(1)} %copy-done.2, f32[2,8,16,256]{3,2,1,0:T(8,128)S(1)} %get-tuple-element.84.refs_0_, f32[2,8,16,256]{3,2,1,0:T(8,128)S(1)} %get-tuple-element.106.refs_1_, f32[2,8,16,256]{3,2,1,0:T(8,128)S(1)} %collective-permute-done.16.refs_2_, ...), custom_call_target="tpu_custom_call" | custom-call | tf_op jit(solution)/shard_map/pallas_call | solution.py:425
  65.2 1.6 %collective-permute-start.24 = (f32[2,8,16,256]{3,2,1,0:T(8,128)S(1)}, f32[2,8,16,256]{3,2,1,0:T(8,128)S(1)}, u32[]{:S(2)}, u32[]{:S(2)}) collective-permute-start(f32[2,8,16,256]{3,2,1,0:T(8,128)S(1)} %shard_map.133), channel_id=1, source_target_pairs={{0,8},{4,12},{8,0},{12,4},{1,9},{5,13},{9,1},{13,5},{2,10},{6,14},... | collective-permute-start | bytes 786440 | tf_op jit(solution)/shard_map/ppermute | solution.py:525
  66.7 0.9 %shard_map.134 = f32[2,8,16,256]{3,2,1,0:T(8,128)S(1)} custom-call(s32[8]{0:T(128)S(1)} %copy-done.2, f32[2,8,16,256]{3,2,1,0:T(8,128)S(1)} %get-tuple-element.111.refs_4_.refs_0_, f32[2,8,16,256]{3,2,1,0:T(8,128)S(1)} %get-tuple-element.116.refs_5_.refs_1_, f32[2,8,16,256]{3,2,1,0:T(8,128)S(1)} %collective-permute-done.22.refs_6_.refs_2_, ...), custom_call_target="tpu_custom_call" | custom-call | tf_op jit(solution)/shard_map/pallas_call | solution.py:425
  67.6 0.6 collective-permute-start.25
  68.2 6.2 %collective-permute-done.24.refs_8_ = f32[2,8,16,256]{3,2,1,0:T(8,128)S(1)} collective-permute-done((f32[2,8,16,256]{3,2,1,0:T(8,128)S(1)}, f32[2,8,16,256]{3,2,1,0:T(8,128)S(1)}, u32[]{:S(2)}, u32[]{:S(2)}) %collective-permute-start.24) | collective-permute-done | bytes 262176 | tf_op jit(solution)/shard_map/ppermute | solution.py:525
  74.4 1.6 %image_inner.1 = (f32[2,16,16,256]{3,2,1,0:T(8,128)}, f32[2,8,16,256]{3,2,1,0:T(8,128)S(1)}) custom-call(s32[8]{0:T(128)S(1)} %copy-done.2, f32[2,8,16,256]{3,2,1,0:T(8,128)S(1)} %get-tuple-element.84.refs_0_, f32[2,8,16,256]{3,2,1,0:T(8,128)S(1)} %get-tuple-element.106.refs_1_, f32[2,8,16,256]{3,2,1,0:T(8,128)S(1)} %collective-permute-done.16.refs_2_, ...), custom_call_target="tpu_custom_call" | custom-call | tf_op jit(solution)/shard_map/image_inner/pallas_call | solution.py:448
  76.0 3.0 %collective-permute-done.25.refs_1_ = f32[2,8,16,256]{3,2,1,0:T(8,128)S(1)} collective-permute-done((f32[2,8,16,256]{3,2,1,0:T(8,128)S(1)}, f32[2,8,16,256]{3,2,1,0:T(8,128)S(1)}, u32[]{:S(2)}, u32[]{:S(2)}) %collective-permute-start.25) | collective-permute-done | bytes 262176 | tf_op jit(solution)/shard_map/ppermute | solution.py:525
  79.1 0.7 image_outer.1
  (19 shorter events, 0.0 us)
Async XLA Ops:
  0.6 10.4 %copy-start.1 = (f32[8,2,256]{2,1,0:T(2,128)S(1)}, f32[8,2,256]{2,1,0:T(2,128)}, u32[]{:S(2)}) copy-start(f32[8,2,256]{2,1,0:T(2,128)} %traces.1) | copy-start | bytes 49156
  1.9 11.4 %collective-permute-start = (f32[3,4,16,256]{3,2,1,0:T(8,128)S(1)}, f32[3,4,16,256]{3,2,1,0:T(8,128)S(1)}, u32[]{:S(2)}, u32[]{:S(2)}) collective-permute-start(f32[3,4,16,256]{3,2,1,0:T(8,128)S(1)} %get-tuple-element.64), channel_id=1, source_target_pairs={{0,1},{1,0},{2,3},{3,2},{4,5},{5,4},{6,7},{7,6},{8,9},{9,8},{10,11... | collective-permute-start | bytes 589832 | tf_op jit(solution)/shard_map/ppermute | solution.py:60
  5.0 8.3 %collective-permute-start.1 = (f32[3,4,16,256]{3,2,1,0:T(8,128)S(1)}, f32[3,4,16,256]{3,2,1,0:T(8,128)S(1)}, u32[]{:S(2)}, u32[]{:S(2)}) collective-permute-start(f32[3,4,16,256]{3,2,1,0:T(8,128)S(1)} %get-tuple-element.65), channel_id=1, source_target_pairs={{1,2},{2,1},{5,6},{6,5},{9,10},{10,9},{13,14},{14,13},{17,18},{18,... | collective-permute-start | bytes 589832 | tf_op jit(solution)/shard_map/ppermute | solution.py:61
  5.6 5.3 %copy-start.5 = (f32[8,2]{0,1:T(2,128)S(1)}, f32[8,2]{0,1:T(2,128)}, u32[]{:S(2)}) copy-start(f32[8,2]{0,1:T(2,128)} %param.16) | copy-start | bytes 196
  5.7 11.2 %collective-permute-start.8 = (f32[2,4,16,256]{3,2,1,0:T(8,128)S(1)}, f32[2,4,16,256]{3,2,1,0:T(8,128)S(1)}, u32[]{:S(2)}, u32[]{:S(2)}) collective-permute-start(f32[2,4,16,256]{3,2,1,0:T(8,128)S(1)} %get-tuple-element.87), channel_id=1, source_target_pairs={{0,1},{1,0},{2,3},{3,2},{4,5},{5,4},{6,7},{7,6},{8,9},{9,8},{10,11... | collective-permute-start | bytes 393224 | tf_op jit(solution)/shard_map/ppermute | solution.py:60
  10.1 0.9 %copy-start.3 = (s32[2,256]{1,0:T(2,128)S(1)}, s32[2,256]{1,0:T(2,128)}, u32[]{:S(2)}) copy-start(s32[2,256]{1,0:T(2,128)} %receiver_cell.1) | copy-start | bytes 6148
  10.1 0.9 %copy-start.4 = (s32[2]{0:T(128)S(1)}, s32[2]{0:T(128)}, u32[]{:S(2)}) copy-start(s32[2]{0:T(128)} %source_cell.1) | copy-start | bytes 28
  10.1 6.8 %collective-permute-start.9 = (f32[2,4,16,256]{3,2,1,0:T(8,128)S(1)}, f32[2,4,16,256]{3,2,1,0:T(8,128)S(1)}, u32[]{:S(2)}, u32[]{:S(2)}) collective-permute-start(f32[2,4,16,256]{3,2,1,0:T(8,128)S(1)} %get-tuple-element.88), channel_id=1, source_target_pairs={{1,2},{2,1},{5,6},{6,5},{9,10},{10,9},{13,14},{14,13},{17,18},{18,... | collective-permute-start | bytes 393224 | tf_op jit(solution)/shard_map/ppermute | solution.py:61
  11.0 2.2 %copy-start = (f32[16,16,256]{2,1,0:T(8,128)S(1)}, f32[16,16,256]{2,1,0:T(8,128)}, u32[]{:S(2)}) copy-start(f32[16,16,256]{2,1,0:T(8,128)} %courant.1) | copy-start | bytes 786436
  14.0 8.9 %collective-permute-start.2 = (f32[2,8,16,256]{3,2,1,0:T(8,128)S(1)}, f32[2,8,16,256]{3,2,1,0:T(8,128)S(1)}, u32[]{:S(2)}, u32[]{:S(2)}) collective-permute-start(f32[2,8,16,256]{3,2,1,0:T(8,128)S(1)} %get-tuple-element.71), channel_id=1, source_target_pairs={{0,1},{1,0},{2,3},{3,2},{4,5},{5,4},{6,7},{7,6},{8,9},{9,8},{10,11... | collective-permute-start | bytes 786440 | tf_op jit(solution)/shard_map/ppermute | solution.py:60
  16.2 6.8 %collective-permute-start.3 = (f32[2,8,16,256]{3,2,1,0:T(8,128)S(1)}, f32[2,8,16,256]{3,2,1,0:T(8,128)S(1)}, u32[]{:S(2)}, u32[]{:S(2)}) collective-permute-start(f32[2,8,16,256]{3,2,1,0:T(8,128)S(1)} %get-tuple-element.72), channel_id=1, source_target_pairs={{1,2},{2,1},{5,6},{6,5},{9,10},{10,9},{13,14},{14,13},{17,18},{18,... | collective-permute-start | bytes 786440 | tf_op jit(solution)/shard_map/ppermute | solution.py:61
  17.7 11.6 %collective-permute-start.10 = (f32[2,8,16,256]{3,2,1,0:T(8,128)S(1)}, f32[2,8,16,256]{3,2,1,0:T(8,128)S(1)}, u32[]{:S(2)}, u32[]{:S(2)}) collective-permute-start(f32[2,8,16,256]{3,2,1,0:T(8,128)S(1)} %get-tuple-element.92), channel_id=1, source_target_pairs={{0,1},{1,0},{2,3},{3,2},{4,5},{5,4},{6,7},{7,6},{8,9},{9,8},{10,11... | collective-permute-start | bytes 786440 | tf_op jit(solution)/shard_map/ppermute | solution.py:60
  21.4 7.9 %collective-permute-start.11 = (f32[2,8,16,256]{3,2,1,0:T(8,128)S(1)}, f32[2,8,16,256]{3,2,1,0:T(8,128)S(1)}, u32[]{:S(2)}, u32[]{:S(2)}) collective-permute-start(f32[2,8,16,256]{3,2,1,0:T(8,128)S(1)} %get-tuple-element.93), channel_id=1, source_target_pairs={{1,2},{2,1},{5,6},{6,5},{9,10},{10,9},{13,14},{14,13},{17,18},{18,... | collective-permute-start | bytes 786440 | tf_op jit(solution)/shard_map/ppermute | solution.py:61
  24.5 10.8 %collective-permute-start.4 = (f32[2,8,16,256]{3,2,1,0:T(8,128)S(1)}, f32[2,8,16,256]{3,2,1,0:T(8,128)S(1)}, u32[]{:S(2)}, u32[]{:S(2)}) collective-permute-start(f32[2,8,16,256]{3,2,1,0:T(8,128)S(1)} %get-tuple-element.76), channel_id=1, source_target_pairs={{0,1},{1,0},{2,3},{3,2},{4,5},{5,4},{6,7},{7,6},{8,9},{9,8},{10,11... | collective-permute-start | bytes 786440 | tf_op jit(solution)/shard_map/ppermute | solution.py:60
  28.6 6.7 %collective-permute-start.5 = (f32[2,8,16,256]{3,2,1,0:T(8,128)S(1)}, f32[2,8,16,256]{3,2,1,0:T(8,128)S(1)}, u32[]{:S(2)}, u32[]{:S(2)}) collective-permute-start(f32[2,8,16,256]{3,2,1,0:T(8,128)S(1)} %get-tuple-element.77), channel_id=1, source_target_pairs={{1,2},{2,1},{5,6},{6,5},{9,10},{10,9},{13,14},{14,13},{17,18},{18,... | collective-permute-start | bytes 786440 | tf_op jit(solution)/shard_map/ppermute | solution.py:61
  30.8 11.3 %collective-permute-start.12 = (f32[2,8,16,256]{3,2,1,0:T(8,128)S(1)}, f32[2,8,16,256]{3,2,1,0:T(8,128)S(1)}, u32[]{:S(2)}, u32[]{:S(2)}) collective-permute-start(f32[2,8,16,256]{3,2,1,0:T(8,128)S(1)} %get-tuple-element.96), channel_id=1, source_target_pairs={{0,1},{1,0},{2,3},{3,2},{4,5},{5,4},{6,7},{7,6},{8,9},{9,8},{10,11... | collective-permute-start | bytes 786440 | tf_op jit(solution)/shard_map/ppermute | solution.py:60
  34.6 7.5 %collective-permute-start.13 = (f32[2,8,16,256]{3,2,1,0:T(8,128)S(1)}, f32[2,8,16,256]{3,2,1,0:T(8,128)S(1)}, u32[]{:S(2)}, u32[]{:S(2)}) collective-permute-start(f32[2,8,16,256]{3,2,1,0:T(8,128)S(1)} %get-tuple-element.97), channel_id=1, source_target_pairs={{1,2},{2,1},{5,6},{6,5},{9,10},{10,9},{13,14},{14,13},{17,18},{18,... | collective-permute-start | bytes 786440 | tf_op jit(solution)/shard_map/ppermute | solution.py:61
  36.8 11.6 %collective-permute-start.6 = (f32[2,8,16,256]{3,2,1,0:T(8,128)S(1)}, f32[2,8,16,256]{3,2,1,0:T(8,128)S(1)}, u32[]{:S(2)}, u32[]{:S(2)}) collective-permute-start(f32[2,8,16,256]{3,2,1,0:T(8,128)S(1)} %get-tuple-element.80), channel_id=1, source_target_pairs={{0,1},{1,0},{2,3},{3,2},{4,5},{5,4},{6,7},{7,6},{8,9},{9,8},{10,11... | collective-permute-start | bytes 786440 | tf_op jit(solution)/shard_map/ppermute | solution.py:60
  41.4 7.0 %collective-permute-start.7 = (f32[2,8,16,256]{3,2,1,0:T(8,128)S(1)}, f32[2,8,16,256]{3,2,1,0:T(8,128)S(1)}, u32[]{:S(2)}, u32[]{:S(2)}) collective-permute-start(f32[2,8,16,256]{3,2,1,0:T(8,128)S(1)} %get-tuple-element.81), channel_id=1, source_target_pairs={{1,2},{2,1},{5,6},{6,5},{9,10},{10,9},{13,14},{14,13},{17,18},{18,... | collective-permute-start | bytes 786440 | tf_op jit(solution)/shard_map/ppermute | solution.py:61
  43.6 10.8 %collective-permute-start.14 = (f32[2,8,16,256]{3,2,1,0:T(8,128)S(1)}, f32[2,8,16,256]{3,2,1,0:T(8,128)S(1)}, u32[]{:S(2)}, u32[]{:S(2)}) collective-permute-start(f32[2,8,16,256]{3,2,1,0:T(8,128)S(1)} %get-tuple-element.100), channel_id=1, source_target_pairs={{0,1},{1,0},{2,3},{3,2},{4,5},{5,4},{6,7},{7,6},{8,9},{9,8},{10,11... | collective-permute-start | bytes 786440 | tf_op jit(solution)/shard_map/ppermute | solution.py:60
  47.3 7.2 %collective-permute-start.15 = (f32[2,8,16,256]{3,2,1,0:T(8,128)S(1)}, f32[2,8,16,256]{3,2,1,0:T(8,128)S(1)}, u32[]{:S(2)}, u32[]{:S(2)}) collective-permute-start(f32[2,8,16,256]{3,2,1,0:T(8,128)S(1)} %get-tuple-element.101), channel_id=1, source_target_pairs={{1,2},{2,1},{5,6},{6,5},{9,10},{10,9},{13,14},{14,13},{17,18},{18,... | collective-permute-start | bytes 786440 | tf_op jit(solution)/shard_map/ppermute | solution.py:61
  49.9 10.8 %collective-permute-start.18 = (f32[2,4,16,256]{3,2,1,0:T(8,128)S(1)}, f32[2,4,16,256]{3,2,1,0:T(8,128)S(1)}, u32[]{:S(2)}, u32[]{:S(2)}) collective-permute-start(f32[2,4,16,256]{3,2,1,0:T(8,128)S(1)} %get-tuple-element.107), channel_id=1, source_target_pairs={{0,1},{1,0},{2,3},{3,2},{4,5},{5,4},{6,7},{7,6},{8,9},{9,8},{10,11... | collective-permute-start | bytes 393224 | tf_op jit(solution)/shard_map/ppermute | solution.py:60
  53.6 7.6 %collective-permute-start.19 = (f32[2,4,16,256]{3,2,1,0:T(8,128)S(1)}, f32[2,4,16,256]{3,2,1,0:T(8,128)S(1)}, u32[]{:S(2)}, u32[]{:S(2)}) collective-permute-start(f32[2,4,16,256]{3,2,1,0:T(8,128)S(1)} %get-tuple-element.108), channel_id=1, source_target_pairs={{1,2},{2,1},{5,6},{6,5},{9,10},{10,9},{13,14},{14,13},{17,18},{18,... | collective-permute-start | bytes 393224 | tf_op jit(solution)/shard_map/ppermute | solution.py:61
  55.9 6.5 %collective-permute-start.20 = (f32[2,4,16,256]{3,2,1,0:T(8,128)S(1)}, f32[2,4,16,256]{3,2,1,0:T(8,128)S(1)}, u32[]{:S(2)}, u32[]{:S(2)}) collective-permute-start(f32[2,4,16,256]{3,2,1,0:T(8,128)S(1)} %get-tuple-element.112), channel_id=1, source_target_pairs={{0,1},{1,0},{2,3},{3,2},{4,5},{5,4},{6,7},{7,6},{8,9},{9,8},{10,11... | collective-permute-start | bytes 393224 | tf_op jit(solution)/shard_map/ppermute | solution.py:60
  57.8 4.7 %collective-permute-start.21 = (f32[2,4,16,256]{3,2,1,0:T(8,128)S(1)}, f32[2,4,16,256]{3,2,1,0:T(8,128)S(1)}, u32[]{:S(2)}, u32[]{:S(2)}) collective-permute-start(f32[2,4,16,256]{3,2,1,0:T(8,128)S(1)} %get-tuple-element.113), channel_id=1, source_target_pairs={{1,2},{2,1},{5,6},{6,5},{9,10},{10,9},{13,14},{14,13},{17,18},{18,... | collective-permute-start | bytes 393224 | tf_op jit(solution)/shard_map/ppermute | solution.py:61
  60.7 3.5 %collective-permute-start.17 = (f32[2,8,16,256]{3,2,1,0:T(8,128)S(1)}, f32[2,8,16,256]{3,2,1,0:T(8,128)S(1)}, u32[]{:S(2)}, u32[]{:S(2)}) collective-permute-start(f32[2,8,16,256]{3,2,1,0:T(8,128)S(1)} %get-tuple-element.106.refs_1_), channel_id=1, source_target_pairs={{0,4},{4,0},{8,12},{12,8},{1,5},{5,1},{9,13},{13,9},{2,6},{6,2},{1... | collective-permute-start | bytes 786440 | tf_op jit(solution)/shard_map/ppermute | solution.py:531
  60.8 3.5 %collective-permute-start.16 = (f32[2,8,16,256]{3,2,1,0:T(8,128)S(1)}, f32[2,8,16,256]{3,2,1,0:T(8,128)S(1)}, u32[]{:S(2)}, u32[]{:S(2)}) collective-permute-start(f32[2,8,16,256]{3,2,1,0:T(8,128)S(1)} %get-tuple-element.84.refs_0_), channel_id=1, source_target_pairs={{0,4},{4,0},{8,12},{12,8},{1,5},{5,1},{9,13},{13,9},{2,6},{6,2},{1... | collective-permute-start | bytes 786440 | tf_op jit(solution)/shard_map/ppermute | solution.py:531
  63.6 0.7 copy-start.2
  63.6 3.1 %collective-permute-start.23 = (f32[2,8,16,256]{3,2,1,0:T(8,128)S(1)}, f32[2,8,16,256]{3,2,1,0:T(8,128)S(1)}, u32[]{:S(2)}, u32[]{:S(2)}) collective-permute-start(f32[2,8,16,256]{3,2,1,0:T(8,128)S(1)} %get-tuple-element.116.refs_5_.refs_1_), channel_id=1, source_target_pairs={{0,4},{4,0},{8,12},{12,8},{1,5},{5,1},{9,13},{13,9},{2,6},{6,2},{1... | collective-permute-start | bytes 786440 | tf_op jit(solution)/shard_map/ppermute | solution.py:531
  63.8 3.0 %collective-permute-start.22 = (f32[2,8,16,256]{3,2,1,0:T(8,128)S(1)}, f32[2,8,16,256]{3,2,1,0:T(8,128)S(1)}, u32[]{:S(2)}, u32[]{:S(2)}) collective-permute-start(f32[2,8,16,256]{3,2,1,0:T(8,128)S(1)} %get-tuple-element.111.refs_4_.refs_0_), channel_id=1, source_target_pairs={{0,4},{4,0},{8,12},{12,8},{1,5},{5,1},{9,13},{13,9},{2,6},{6,2},{1... | collective-permute-start | bytes 786440 | tf_op jit(solution)/shard_map/ppermute | solution.py:531
  65.2 9.2 %collective-permute-start.24 = (f32[2,8,16,256]{3,2,1,0:T(8,128)S(1)}, f32[2,8,16,256]{3,2,1,0:T(8,128)S(1)}, u32[]{:S(2)}, u32[]{:S(2)}) collective-permute-start(f32[2,8,16,256]{3,2,1,0:T(8,128)S(1)} %shard_map.133), channel_id=1, source_target_pairs={{0,8},{4,12},{8,0},{12,4},{1,9},{5,13},{9,1},{13,5},{2,10},{6,14},... | collective-permute-start | bytes 786440 | tf_op jit(solution)/shard_map/ppermute | solution.py:525
  67.6 11.4 %collective-permute-start.25 = (f32[2,8,16,256]{3,2,1,0:T(8,128)S(1)}, f32[2,8,16,256]{3,2,1,0:T(8,128)S(1)}, u32[]{:S(2)}, u32[]{:S(2)}) collective-permute-start(f32[2,8,16,256]{3,2,1,0:T(8,128)S(1)} %shard_map.134), channel_id=1, source_target_pairs={{0,8},{4,12},{8,0},{12,4},{1,9},{5,13},{9,1},{13,5},{2,10},{6,14},... | collective-permute-start | bytes 786440 | tf_op jit(solution)/shard_map/ppermute | solution.py:525

commit v3 on v2

--- a/solution.py
+++ b/solution.py
@@ -76,20 +76,15 @@
     return (1 - odd) * (rows + width), odd * (rows + width)
 
 
-def pack_kernel(groups, rows, *refs):
-    source, receiver, courant = refs[:3]
-    outs = refs[3 : 3 + 2 * groups]
-    sem = refs[-1]
+def pack_kernel(source, receiver, courant, even_edge, odd_edge, sem):
+    groups, rows = source.shape[:2]
     copies = []
-    for side, start in enumerate(edge_starts(rows, REACH)):
+    for out, start in zip((even_edge, odd_edge), edge_starts(rows, REACH)):
         planes = pl.ds(start, REACH)
-        for group in range(groups):
-            out = outs[2 * group + side]
-            pieces = [source.at[group, planes], receiver.at[group, planes]]
-            if group == 0:
-                pieces.append(courant.at[planes])
-            for index, piece in enumerate(pieces):
-                copies.append(pltpu.make_async_copy(piece, out.at[index], sem.at[len(copies)]))
+        pieces = [array.at[group, planes] for group in range(groups) for array in (source, receiver)]
+        pieces.append(courant.at[planes])
+        for index, piece in enumerate(pieces):
+            copies.append(pltpu.make_async_copy(piece, out.at[index], sem.at[len(copies)]))
     for copy in copies:
         copy.start()
     for copy in copies:
@@ -101,16 +96,14 @@
 
 
 def pack(source_now, receiver_now, courant_sq):
-    groups, rows, size_y, size_z = source_now.shape
-    shapes = []
-    for group in range(groups):
-        shapes += [struct((3 if group == 0 else 2, REACH, size_y, size_z))] * 2
-    return pl.pallas_call(
-        functools.partial(pack_kernel, groups, rows),
-        out_shape=shapes,
+    groups, _, size_y, size_z = source_now.shape
+    count = 2 * groups + 1
+    return pl.pallas_call(
+        pack_kernel,
+        out_shape=[struct((count, REACH, size_y, size_z))] * 2,
         in_specs=[hbm()] * 3,
-        out_specs=[vmem()] * len(shapes),
-        scratch_shapes=[pltpu.SemaphoreType.DMA((2 * (2 * groups + 1),))],
+        out_specs=[vmem()] * 2,
+        scratch_shapes=[pltpu.SemaphoreType.DMA((2 * count,))],
         compiler_params=params(),
         name="pack",
     )(*stay(source_now, receiver_now, courant_sq))
@@ -220,20 +213,20 @@
     return [[(at, CHUNK)] for at in range(start, stop, CHUNK)]
 
 
-def first_kernel(rows, has_courant, width, now, before, courant, even, odd, inject, along_z, along_y, fresh, held, even_edge, odd_edge, *scaled):
+def first_kernel(group, rows, has_courant, width, now, before, courant, even, odd, inject, along_z, along_y, fresh, held, even_edge, odd_edge, *scaled):
     even_at, odd_at = halo_starts(rows, REACH)
     if has_courant:
         (courant_out,) = scaled
         courant_out[REACH : REACH + rows] = SCALE * courant[...]
-        courant_out[pl.ds(even_at, REACH)] = SCALE * even[2]
-        courant_out[pl.ds(odd_at, REACH)] = SCALE * odd[2]
+        courant_out[pl.ds(even_at, REACH)] = SCALE * even[even.shape[0] - 1]
+        courant_out[pl.ds(odd_at, REACH)] = SCALE * odd[odd.shape[0] - 1]
         courant = courant_out
     z_band, y_band = along_z[...], along_y[...]
     for kind in range(2):
         field = held.at[kind]
         field[REACH : REACH + rows] = now[kind]
-        field[pl.ds(even_at, REACH)] = even[kind]
-        field[pl.ds(odd_at, REACH)] = odd[kind]
+        field[pl.ds(even_at, REACH)] = even[2 * group + kind]
+        field[pl.ds(odd_at, REACH)] = odd[2 * group + kind]
 
         def write(i, plane, new, kind=kind):
             fresh[kind, plane] = new
@@ -257,7 +250,7 @@
     if has_courant:
         shapes.append(struct((rows + 2 * REACH, size_y, size_z)))
     return pl.pallas_call(
-        functools.partial(first_kernel, rows, has_courant, width),
+        functools.partial(first_kernel, group, rows, has_courant, width),
         out_shape=shapes,
         in_specs=[vmem()] * 8,
         out_specs=[vmem()] * len(shapes),
@@ -303,73 +296,66 @@
     )(now, before, *halos, courant, inject, along_z, along_y)
 
 
-def inner_kernel(group, rows, step, now, before, courant, inject, along_z, along_y, *refs):
-    final, source_out, receiver_out, sem = refs[-4:]
-    count = rows - 2 * REACH
+def inner_kernel(groups, rows, step, *refs):
+    now, before, inject = refs[:groups], refs[groups : 2 * groups], refs[2 * groups : 3 * groups]
+    courant, along_z, along_y, final = refs[3 * groups :]
     z_band, y_band = along_z[...], along_y[...]
-    copies = []
-    for kind, out in enumerate((source_out, receiver_out)):
-
-        def write(i, plane, new, kind=kind):
-            final[kind, plane - REACH] = new
-
-        for runs in chunks(REACH, rows - REACH):
-            advance(now.at[kind], 0, before.at[kind], REACH, courant, REACH, inject.at[kind], REACH, runs, step, z_band, y_band, write)
-        copies.append(pltpu.make_async_copy(final.at[kind], out.at[group, pl.ds(REACH, count)], sem.at[kind]))
-        copies[kind].start()
-    for copy in copies:
-        copy.wait()
-
-
-def inner_round(group, groups, step, now, before, courant, inject, along_z, along_y, outs):
-    rows, size_y, size_z = now.shape[1:]
-    whole = struct((groups, rows, size_y, size_z))
-    return pl.pallas_call(
-        functools.partial(inner_kernel, group, rows, step),
-        out_shape=[struct((2, rows - 2 * REACH, size_y, size_z)), whole, whole],
-        in_specs=[vmem()] * 6 + [hbm()] * len(outs),
-        out_specs=[vmem(), hbm(), hbm()],
-        scratch_shapes=[pltpu.SemaphoreType.DMA((2,))],
-        input_output_aliases={6: 1, 7: 2} if outs else {},
-        compiler_params=params(),
-    )(now, before, courant, inject, along_z, along_y, *outs)
-
-
-def outer_kernel(group, rows, step, now, before, even, odd, courant, inject, along_z, along_y, *refs):
-    final, source_out, receiver_out, wide, sem = refs[-5:]
+    for group in range(groups):
+        for kind in range(2):
+
+            def write(i, plane, new, place=2 * group + kind):
+                final[place, plane - REACH] = new
+
+            for runs in chunks(REACH, rows - REACH):
+                advance(now[group].at[kind], 0, before[group].at[kind], REACH, courant, REACH, inject[group].at[kind], REACH, runs, step, z_band, y_band, write)
+
+
+def inner_round(step, now, before, courant, inject, along_z, along_y):
+    groups = len(now)
+    rows, size_y, size_z = now[0].shape[1:]
+    return pl.pallas_call(
+        functools.partial(inner_kernel, groups, rows, step),
+        out_shape=struct((2 * groups, rows - 2 * REACH, size_y, size_z)),
+        in_specs=[vmem()] * (3 * groups + 3),
+        out_specs=vmem(),
+        compiler_params=params(),
+        name="inner",
+    )(*now, *before, *inject, courant, along_z, along_y)
+
+
+def outer_kernel(groups, rows, step, *refs):
+    now, before, inject = refs[:groups], refs[groups : 2 * groups], refs[2 * groups : 3 * groups]
+    even, odd = refs[3 * groups : 4 * groups], refs[4 * groups : 5 * groups]
+    courant, along_z, along_y, final, wide = refs[5 * groups :]
     even_at, odd_at = halo_starts(rows, REACH)
     z_band, y_band = along_z[...], along_y[...]
-    copies = []
-    for kind, out in enumerate((source_out, receiver_out)):
-        field = wide.at[kind]
-        field[REACH : REACH + rows] = now[kind]
-        field[pl.ds(even_at, REACH)] = even[kind]
-        field[pl.ds(odd_at, REACH)] = odd[kind]
-
-        def write(i, plane, new, kind=kind):
-            final[kind, i] = new
-
-        runs = [(0, REACH), (rows - REACH, REACH)]
-        advance(field, REACH, before.at[kind], REACH, courant, REACH, inject.at[kind], REACH, runs, step, z_band, y_band, write)
-        for side, (first, count) in enumerate(runs):
-            piece = final.at[kind, pl.ds(side * REACH, REACH)]
-            copies.append(pltpu.make_async_copy(piece, out.at[group, pl.ds(first, count)], sem.at[2 * kind + side]))
-            copies[-1].start()
-    for copy in copies:
-        copy.wait()
-
-
-def outer_round(group, step, now, before, halos, courant, inject, along_z, along_y, outs):
-    rows, size_y, size_z = now.shape[1:]
-    return pl.pallas_call(
-        functools.partial(outer_kernel, group, rows, step),
-        out_shape=[struct((2, 2 * REACH, size_y, size_z))] + [struct(out.shape) for out in outs],
-        in_specs=[vmem()] * 8 + [hbm()] * len(outs),
-        out_specs=[vmem(), hbm(), hbm()],
-        scratch_shapes=[pltpu.VMEM((2, rows + 2 * REACH, size_y, size_z), jnp.float32), pltpu.SemaphoreType.DMA((4,))],
-        input_output_aliases={8: 1, 9: 2},
-        compiler_params=params(),
-    )(now, before, *halos, courant, inject, along_z, along_y, *outs)
+    for group in range(groups):
+        for kind in range(2):
+            field = wide.at[2 * group + kind]
+            field[REACH : REACH + rows] = now[group][kind]
+            field[pl.ds(even_at, REACH)] = even[group][kind]
+            field[pl.ds(odd_at, REACH)] = odd[group][kind]
+
+            def write(i, plane, new, place=2 * group + kind):
+                final[place, i] = new
+
+            runs = [(0, REACH), (rows - REACH, REACH)]
+            advance(field, REACH, before[group].at[kind], REACH, courant, REACH, inject[group].at[kind], REACH, runs, step, z_band, y_band, write)
+
+
+def outer_round(step, now, before, halos, courant, inject, along_z, along_y):
+    groups = len(now)
+    rows, size_y, size_z = now[0].shape[1:]
+    even, odd = zip(*halos)
+    return pl.pallas_call(
+        functools.partial(outer_kernel, groups, rows, step),
+        out_shape=struct((2 * groups, 2 * REACH, size_y, size_z)),
+        in_specs=[vmem()] * (5 * groups + 3),
+        out_specs=vmem(),
+        scratch_shapes=[pltpu.VMEM((2 * groups, rows + 2 * REACH, size_y, size_z), jnp.float32)],
+        compiler_params=params(),
+        name="outer",
+    )(*now, *before, *inject, *even, *odd, courant, along_z, along_y)
 
 
 def shifted(plane, amount):
@@ -401,15 +387,16 @@
                 def one_plane(x, carry):
                     total = None
                     for field in fields:
-                        term = field[1, x] * shifted(field[0, x], 2 * lag)
-                        total = term if total is None else total + term
+                        for source in range(0, field.shape[0], 2):
+                            term = field[source + 1, x] * shifted(field[source, x], 2 * lag)
+                            total = term if total is None else total + term
                     total = shifted(total, -lag)
                     for other in others:
                         total = total + other[slot, x]
                     image[slot, x] = total
                     return carry
 
-                lax.fori_loop(0, rows, one_plane, 0, unroll=2)
+                lax.fori_loop(0, rows, one_plane, 0, unroll=4)
 
         return carry
 
@@ -431,29 +418,43 @@
     )(offset_perm, *fields)
 
 
-def inner_image_kernel(shots, offset_perm, *refs):
-    inner_fields, outer_fields = refs[:shots], refs[shots : 2 * shots]
-    others = refs[2 * shots : -4]
-    image, outer, inner, sem = refs[-4:]
-    partial_image(0, offset_perm, inner_fields, inner, others)
-    copy = pltpu.make_async_copy(inner, image.at[:, pl.ds(REACH, inner.shape[1])], sem)
-    copy.start()
-    partial_image(0, offset_perm, outer_fields, outer)
-    copy.wait()
-
-
-def inner_image(slots, rows, offset_perm, inner_fields, outer_fields, others):
-    _, inner_rows, size_y, size_z = inner_fields[0].shape
-    shots = len(inner_fields)
-    return pl.pallas_call(
-        functools.partial(inner_image_kernel, shots),
-        out_shape=[struct((slots, rows, size_y, size_z)), struct((slots, 2 * REACH, size_y, size_z))],
-        in_specs=[smem()] + [vmem()] * (2 * shots + len(others)),
-        out_specs=[hbm(), vmem()],
-        scratch_shapes=[pltpu.VMEM((slots, inner_rows, size_y, size_z), jnp.float32), pltpu.SemaphoreType.DMA(())],
+def inner_image_kernel(offset_perm, own_inner, other_inner, own_outer, other_outer, *refs):
+    others = refs[:-6]
+    image, source_out, receiver_out, outer, inner, sem = refs[-6:]
+    groups, rows = source_out.shape[:2]
+    copies = []
+    for group in range(groups):
+        for kind, out in enumerate((source_out, receiver_out)):
+            place = 2 * group + kind
+            pieces = (
+                (own_inner.at[place], REACH, rows - 2 * REACH),
+                (own_outer.at[place, pl.ds(0, REACH)], 0, REACH),
+                (own_outer.at[place, pl.ds(REACH, REACH)], rows - REACH, REACH),
+            )
+            for piece, first, count in pieces:
+                copies.append(pltpu.make_async_copy(piece, out.at[group, pl.ds(first, count)], sem.at[len(copies)]))
+                copies[-1].start()
+    partial_image(0, offset_perm, (own_inner, other_inner), inner, others)
+    copies.append(pltpu.make_async_copy(inner, image.at[:, pl.ds(REACH, rows - 2 * REACH)], sem.at[len(copies)]))
+    copies[-1].start()
+    partial_image(0, offset_perm, (own_outer, other_outer), outer)
+    for copy in copies:
+        copy.wait()
+
+
+def inner_image(slots, inner, outer, others, offset_perm):
+    places, inner_rows, size_y, size_z = inner[0].shape
+    rows = inner_rows + 2 * REACH
+    whole = struct((places // 2, rows, size_y, size_z))
+    return pl.pallas_call(
+        inner_image_kernel,
+        out_shape=[struct((slots, rows, size_y, size_z)), whole, whole, struct((slots, 2 * REACH, size_y, size_z))],
+        in_specs=[smem()] + [vmem()] * (4 + len(others)),
+        out_specs=[hbm()] * 3 + [vmem()],
+        scratch_shapes=[pltpu.VMEM((slots, inner_rows, size_y, size_z), jnp.float32), pltpu.SemaphoreType.DMA((3 * places + 1,))],
         compiler_params=params(),
         name="image_inner",
-    )(offset_perm, *inner_fields, *outer_fields, *others)
+    )(offset_perm, *inner, *outer, *others)
 
 
 def outer_image_kernel(rows, *refs):
@@ -486,61 +487,51 @@
 
 
 def program(source_now, source_prev, receiver_now, receiver_prev, courant_sq, source_cell, wavelet, receiver_cell, traces, offset_perm):
-    groups, rows, _, _ = source_now.shape
+    groups, _, _, _ = source_now.shape
     steps = wavelet.shape[0]
     shot_devices = lax.axis_size("shot")
     slots = offset_perm.shape[0] // shot_devices
     everyone = range(groups)
 
-    edges = pack(source_now, receiver_now, courant_sq)
-    halos = [trade(edges[2 * g], edges[2 * g + 1]) for g in everyone]
+    given = trade(*pack(source_now, receiver_now, courant_sq))
     fields = (source_now, receiver_now, source_prev, receiver_prev)
     along_z, along_y, *rest = prepare(source_cell, wavelet, receiver_cell, traces, fields)
     inject, now, before = rest[:groups], rest[groups : 2 * groups], rest[2 * groups :]
 
+    halos = [None] * groups
     courant = courant_sq
     for g in everyone:
-        result = first_round(g, 2 * REACH, now[g], before[g], courant, halos[g], inject[g], along_z, along_y)
+        result = first_round(g, 2 * REACH, now[g], before[g], courant, given, inject[g], along_z, along_y)
         now[g], before[g] = result[:2]
         if g == 0:
             courant = result[4]
         halos[g] = trade(*result[2:4])
-    outs = ()
-    inner, outer = [None] * groups, [None] * groups
     for step in range(1, steps - 1, 2):
-        width = 2 * REACH if step + 2 < steps - 1 else REACH
+        last = step + 2 >= steps - 1
         for g in everyone:
-            now[g], before[g], even, odd = pair_round(step, width, now[g], before[g], halos[g], courant, inject[g], along_z, along_y)
+            now[g], before[g], even, odd = pair_round(step, REACH if last else 2 * REACH, now[g], before[g], halos[g], courant, inject[g], along_z, along_y)
             halos[g] = trade(even, odd)
-            if width == REACH:
-                inner[g], *outs = inner_round(g, groups, steps - 1, now[g], before[g], courant, inject[g], along_z, along_y, outs)
 
     swap = [(i, i ^ 1) for i in range(shot_devices)]
     pairs = shot_devices // 2
 
-    def travel(parts):
+    def part_sums(fields):
+        parts = [image_part(ahead, slots, offset_perm, fields) for ahead in range(1, pairs)]
         sums = []
         for ahead, part in enumerate(parts, 1):
             route = [(2 * p + c, 2 * ((p + ahead) % pairs) + c) for p in range(pairs) for c in range(2)]
             sums.append(lax.ppermute(part, "shot", route))
         return sums
 
-    def traded(fields):
-        others = []
-        for g in everyone:
-            others.append(lax.ppermute(fields[g], "shot", swap))
-        return fields + others
-
-    inner = traded(inner)
-    parts = [image_part(ahead, slots, offset_perm, inner) for ahead in range(1, pairs)]
-    inner_sums = travel(parts)
-    for g in everyone:
-        outer[g], *outs = outer_round(g, steps - 1, now[g], before[g], halos[g], courant, inject[g], along_z, along_y, outs)
-    outer = traded(outer)
-    outer_sums = travel([image_part(ahead, slots, offset_perm, outer) for ahead in range(1, pairs)])
-    image, own = inner_image(slots, rows, offset_perm, inner, outer, inner_sums)
+    own = inner_round(steps - 1, now, before, courant, inject, along_z, along_y)
+    inner = (own, lax.ppermute(own, "shot", swap))
+    inner_sums = part_sums(inner)
+    own = outer_round(steps - 1, now, before, halos, courant, inject, along_z, along_y)
+    outer = (own, lax.ppermute(own, "shot", swap))
+    outer_sums = part_sums(outer)
+    image, source_final, receiver_final, own = inner_image(slots, inner, outer, inner_sums, offset_perm)
     image = outer_image(image, own, outer_sums)
-    return (image, *outs)
+    return image, source_final, receiver_final
 
 
 def solution(mesh):

time: 80.4 us -> 84.4 us (1.050)
  the two profiles are of different devices: /device:TPU:0 before, /device:TPU:12 now
where the time goes in v3:
time: 84.4 us; the launch traced here: 84 us
  starting transfers between devices  37.1 us (44%)
  waiting for transfers between devices  25.9 us (31%)
  Pallas kernels  19.7 us (23%)
  between operations  1.14 us (1%)
    ppermute x9, starting transfers between devices, trade(): odd = lax.ppermute(odd_edge, 'slab', odd_pairs(count))  32.6 us
    ppermute x9, waiting for transfers between devices, trade(): odd = lax.ppermute(odd_edge, 'slab', odd_pairs(count))  12.7 us
    pallas_call x6, Pallas kernels, pair_round(): pl.pallas_call(functools.partial(pair_kernel, rows, step, width), out_sha...  9.3 us
    ppermute x2, waiting for transfers between devices, part_sums(): sums.append(lax.ppermute(part, 'shot', route))  9.24 us
    ppermute x9, waiting for transfers between devices, trade(): even = lax.ppermute(even_edge, 'slab', even_pairs(count))  3.92 us
    ppermute x2, starting transfers between devices, part_sums(): sums.append(lax.ppermute(part, 'shot', route))  2.57 us
    pallas_call x1, Pallas kernels, prepare(): pl.pallas_call(functools.partial(prepare_kernel, groups, rows), out_shape...  2.19 us
    ppermute x9, starting transfers between devices, trade(): even = lax.ppermute(even_edge, 'slab', even_pairs(count))  1.75 us
  transfers between devices with their start and end apart: 22, of which 12 were waited for; matrix products, arithmetic and copies ran while one was open for 0% of the time, Pallas kernels for 20%

profile of v3, /device:TPU:12, one launch (start us, length us, event | category | flops | bytes accessed | tf_op | source)
XLA Modules:
  0.0 84.0 jit_solution(9791624268951183918)
XLA Ops:
  0.6 1.2 %pack.1 = (f32[5,4,16,256]{3,2,1,0:T(8,128)S(1)}, f32[5,4,16,256]{3,2,1,0:T(8,128)S(1)}) custom-call(f32[2,16,16,256]{3,2,1,0:T(8,128)} %source.3, f32[2,16,16,256]{3,2,1,0:T(8,128)} %receiver.3, f32[16,16,256]{2,1,0:T(8,128)} %courant.3), custom_call_target="tpu_custom_call" | custom-call | tf_op jit(solution)/shard_map/pack/pallas_call | solution.py:101
  1.9 0.0 copy-start.5
  1.9 0.5 collective-permute-start
  2.4 4.7 %collective-permute-start.1 = (f32[5,4,16,256]{3,2,1,0:T(8,128)S(1)}, f32[5,4,16,256]{3,2,1,0:T(8,128)S(1)}, u32[]{:S(2)}, u32[]{:S(2)}) collective-permute-start(f32[5,4,16,256]{3,2,1,0:T(8,128)S(1)} %get-tuple-element.53), channel_id=1, source_target_pairs={{1,2},{2,1},{5,6},{6,5},{9,10},{10,9},{13,14},{14,13},{17,18},{18,... | collective-permute-start | bytes 983048 | tf_op jit(solution)/shard_map/ppermute | solution.py:61
  7.1 0.0 copy-done.5
  7.1 0.1 copy.14.wavelet
  7.2 2.2 %prepare.1 = (bf16[256,256]{1,0:T(8,128)(2,1)S(1)}, bf16[128,256]{1,0:T(8,128)(2,1)S(1)}, f32[2,24,16,128]{3,2,1,0:T(8,128)S(1)}, f32[2,24,16,128]{3,2,1,0:T(8,1...) custom-call(s32[2]{0:T(128)S(1)} %copy-done.4, ...), custom_call_target="tpu_custom_call" | custom-call | tf_op jit(solution)/shard_map/prepare/pallas_call | solution.py:173
  9.4 1.9 %collective-permute-done.even = f32[5,4,16,256]{3,2,1,0:T(8,128)S(1)} collective-permute-done((f32[5,4,16,256]{3,2,1,0:T(8,128)S(1)}, f32[5,4,16,256]{3,2,1,0:T(8,128)S(1)}, u32[]{:S(2)}, u32[]{:S(2)}) %collective-permute-start) | collective-permute-done | bytes 327712 | tf_op jit(solution)/shard_map/ppermute | solution.py:60
  11.4 3.2 %collective-permute-done.1.odd = f32[5,4,16,256]{3,2,1,0:T(8,128)S(1)} collective-permute-done((f32[5,4,16,256]{3,2,1,0:T(8,128)S(1)}, f32[5,4,16,256]{3,2,1,0:T(8,128)S(1)}, u32[]{:S(2)}, u32[]{:S(2)}) %collective-permute-start.1) | collective-permute-done | bytes 327712 | tf_op jit(solution)/shard_map/ppermute | solution.py:61
  14.5 0.8 shard_map.121
  15.3 0.1 collective-permute-start.2
  15.4 3.6 %collective-permute-start.3 = (f32[2,8,16,256]{3,2,1,0:T(8,128)S(1)}, f32[2,8,16,256]{3,2,1,0:T(8,128)S(1)}, u32[]{:S(2)}, u32[]{:S(2)}) collective-permute-start(f32[2,8,16,256]{3,2,1,0:T(8,128)S(1)} %get-tuple-element.60), channel_id=1, source_target_pairs={{1,2},{2,1},{5,6},{6,5},{9,10},{10,9},{13,14},{14,13},{17,18},{18,... | collective-permute-start | bytes 786440 | tf_op jit(solution)/shard_map/ppermute | solution.py:61
  19.1 0.8 shard_map.125
  19.8 0.1 collective-permute-start.8
  19.9 2.7 %collective-permute-start.9 = (f32[2,8,16,256]{3,2,1,0:T(8,128)S(1)}, f32[2,8,16,256]{3,2,1,0:T(8,128)S(1)}, u32[]{:S(2)}, u32[]{:S(2)}) collective-permute-start(f32[2,8,16,256]{3,2,1,0:T(8,128)S(1)} %get-tuple-element.77), channel_id=1, source_target_pairs={{1,2},{2,1},{5,6},{6,5},{9,10},{10,9},{13,14},{14,13},{17,18},{18,... | collective-permute-start | bytes 786440 | tf_op jit(solution)/shard_map/ppermute | solution.py:61
  22.6 1.7 %collective-permute-done.2.even = f32[2,8,16,256]{3,2,1,0:T(8,128)S(1)} collective-permute-done((f32[2,8,16,256]{3,2,1,0:T(8,128)S(1)}, f32[2,8,16,256]{3,2,1,0:T(8,128)S(1)}, u32[]{:S(2)}, u32[]{:S(2)}) %collective-permute-start.2) | collective-permute-done | bytes 262176 | tf_op jit(solution)/shard_map/ppermute | solution.py:60
  24.3 1.9 %collective-permute-done.3.odd = f32[2,8,16,256]{3,2,1,0:T(8,128)S(1)} collective-permute-done((f32[2,8,16,256]{3,2,1,0:T(8,128)S(1)}, f32[2,8,16,256]{3,2,1,0:T(8,128)S(1)}, u32[]{:S(2)}, u32[]{:S(2)}) %collective-permute-start.3) | collective-permute-done | bytes 262176 | tf_op jit(solution)/shard_map/ppermute | solution.py:61
  26.2 1.6 %shard_map.122 = (f32[2,16,16,256]{3,2,1,0:T(8,128)S(1)}, f32[2,24,16,256]{3,2,1,0:T(8,128)S(1)}, f32[2,8,16,256]{3,2,1,0:T(8,128)S(1)}, f32[2,8,16,256]{3,2,1,0:T(8,128)S(1)}) custom-call(f32[2,16,16,256]{3,2,1,0:T(8,128)S(1)} %get-tuple-element.57.now, f32[2,24,16,256]{3,2,1,0:T(8,128)S(1)} %get-tuple-element.58.before, ...), custom_call_target="tpu_custom_call" | custom-call | tf_op jit(solution)/shard_map/pallas_call | solution.py:289
  27.7 0.1 collective-permute-start.4
  27.8 4.0 %collective-permute-start.5 = (f32[2,8,16,256]{3,2,1,0:T(8,128)S(1)}, f32[2,8,16,256]{3,2,1,0:T(8,128)S(1)}, u32[]{:S(2)}, u32[]{:S(2)}) collective-permute-start(f32[2,8,16,256]{3,2,1,0:T(8,128)S(1)} %get-tuple-element.65), channel_id=1, source_target_pairs={{1,2},{2,1},{5,6},{6,5},{9,10},{10,9},{13,14},{14,13},{17,18},{18,... | collective-permute-start | bytes 786440 | tf_op jit(solution)/shard_map/ppermute | solution.py:61
  31.8 0.0 collective-permute-done.8.even
  31.8 0.0 collective-permute-done.9.odd
  31.8 1.6 %shard_map.126 = (f32[2,16,16,256]{3,2,1,0:T(8,128)S(1)}, f32[2,24,16,256]{3,2,1,0:T(8,128)S(1)}, f32[2,8,16,256]{3,2,1,0:T(8,128)S(1)}, f32[2,8,16,256]{3,2,1,0:T(8,128)S(1)}) custom-call(f32[2,16,16,256]{3,2,1,0:T(8,128)S(1)} %get-tuple-element.74.now, f32[2,24,16,256]{3,2,1,0:T(8,128)S(1)} %get-tuple-element.75.before, ...), custom_call_target="tpu_custom_call" | custom-call | tf_op jit(solution)/shard_map/pallas_call | solution.py:289
  33.4 0.1 collective-permute-start.10
  33.5 3.3 %collective-permute-start.11 = (f32[2,8,16,256]{3,2,1,0:T(8,128)S(1)}, f32[2,8,16,256]{3,2,1,0:T(8,128)S(1)}, u32[]{:S(2)}, u32[]{:S(2)}) collective-permute-start(f32[2,8,16,256]{3,2,1,0:T(8,128)S(1)} %get-tuple-element.81), channel_id=1, source_target_pairs={{1,2},{2,1},{5,6},{6,5},{9,10},{10,9},{13,14},{14,13},{17,18},{18,... | collective-permute-start | bytes 786440 | tf_op jit(solution)/shard_map/ppermute | solution.py:61
  36.8 0.0 collective-permute-done.4.even
  36.8 1.5 %collective-permute-done.5.odd = f32[2,8,16,256]{3,2,1,0:T(8,128)S(1)} collective-permute-done((f32[2,8,16,256]{3,2,1,0:T(8,128)S(1)}, f32[2,8,16,256]{3,2,1,0:T(8,128)S(1)}, u32[]{:S(2)}, u32[]{:S(2)}) %collective-permute-start.5) | collective-permute-done | bytes 262176 | tf_op jit(solution)/shard_map/ppermute | solution.py:61
  38.2 1.6 %shard_map.123 = (f32[2,16,16,256]{3,2,1,0:T(8,128)S(1)}, f32[2,24,16,256]{3,2,1,0:T(8,128)S(1)}, f32[2,8,16,256]{3,2,1,0:T(8,128)S(1)}, f32[2,8,16,256]{3,2,1,0:T(8,128)S(1)}) custom-call(f32[2,16,16,256]{3,2,1,0:T(8,128)S(1)} %get-tuple-element.62.now, f32[2,24,16,256]{3,2,1,0:T(8,128)S(1)} %get-tuple-element.63.before, ...), custom_call_target="tpu_custom_call" | custom-call | tf_op jit(solution)/shard_map/pallas_call | solution.py:289
  39.8 0.1 collective-permute-start.6
  39.9 4.4 %collective-permute-start.7 = (f32[2,8,16,256]{3,2,1,0:T(8,128)S(1)}, f32[2,8,16,256]{3,2,1,0:T(8,128)S(1)}, u32[]{:S(2)}, u32[]{:S(2)}) collective-permute-start(f32[2,8,16,256]{3,2,1,0:T(8,128)S(1)} %get-tuple-element.69), channel_id=1, source_target_pairs={{1,2},{2,1},{5,6},{6,5},{9,10},{10,9},{13,14},{14,13},{17,18},{18,... | collective-permute-start | bytes 786440 | tf_op jit(solution)/shard_map/ppermute | solution.py:61
  44.3 0.0 collective-permute-done.10.even
  44.3 0.0 collective-permute-done.11.odd
  44.3 1.6 %shard_map.127 = (f32[2,16,16,256]{3,2,1,0:T(8,128)S(1)}, f32[2,24,16,256]{3,2,1,0:T(8,128)S(1)}, f32[2,8,16,256]{3,2,1,0:T(8,128)S(1)}, f32[2,8,16,256]{3,2,1,0:T(8,128)S(1)}) custom-call(f32[2,16,16,256]{3,2,1,0:T(8,128)S(1)} %get-tuple-element.78.now, f32[2,24,16,256]{3,2,1,0:T(8,128)S(1)} %get-tuple-element.79.before, ...), custom_call_target="tpu_custom_call" | custom-call | tf_op jit(solution)/shard_map/pallas_call | solution.py:289
  45.9 0.1 collective-permute-start.12
  46.0 4.1 %collective-permute-start.13 = (f32[2,8,16,256]{3,2,1,0:T(8,128)S(1)}, f32[2,8,16,256]{3,2,1,0:T(8,128)S(1)}, u32[]{:S(2)}, u32[]{:S(2)}) collective-permute-start(f32[2,8,16,256]{3,2,1,0:T(8,128)S(1)} %get-tuple-element.85), channel_id=1, source_target_pairs={{1,2},{2,1},{5,6},{6,5},{9,10},{10,9},{13,14},{14,13},{17,18},{18,... | collective-permute-start | bytes 786440 | tf_op jit(solution)/shard_map/ppermute | solution.py:61
  50.1 0.0 collective-permute-done.6.even
  50.1 1.2 %collective-permute-done.7.odd = f32[2,8,16,256]{3,2,1,0:T(8,128)S(1)} collective-permute-done((f32[2,8,16,256]{3,2,1,0:T(8,128)S(1)}, f32[2,8,16,256]{3,2,1,0:T(8,128)S(1)}, u32[]{:S(2)}, u32[]{:S(2)}) %collective-permute-start.7) | collective-permute-done | bytes 262176 | tf_op jit(solution)/shard_map/ppermute | solution.py:61
  51.3 1.5 %shard_map.124 = (f32[2,16,16,256]{3,2,1,0:T(8,128)S(1)}, f32[2,24,16,256]{3,2,1,0:T(8,128)S(1)}, f32[2,4,16,256]{3,2,1,0:T(8,128)S(1)}, f32[2,4,16,256]{3,2,1,0:T(8,128)S(1)}) custom-call(f32[2,16,16,256]{3,2,1,0:T(8,128)S(1)} %get-tuple-element.66.now, f32[2,24,16,256]{3,2,1,0:T(8,128)S(1)} %get-tuple-element.67.before, ...), custom_call_target="tpu_custom_call" | custom-call | tf_op jit(solution)/shard_map/pallas_call | solution.py:289
  52.8 0.1 collective-permute-start.15
  52.9 0.3 collective-permute-done.12.even
  53.2 1.1 %collective-permute-done.13.odd = f32[2,8,16,256]{3,2,1,0:T(8,128)S(1)} collective-permute-done((f32[2,8,16,256]{3,2,1,0:T(8,128)S(1)}, f32[2,8,16,256]{3,2,1,0:T(8,128)S(1)}, u32[]{:S(2)}, u32[]{:S(2)}) %collective-permute-start.13) | collective-permute-done | bytes 262176 | tf_op jit(solution)/shard_map/ppermute | solution.py:61
  54.2 1.5 %shard_map.128 = (f32[2,16,16,256]{3,2,1,0:T(8,128)S(1)}, f32[2,24,16,256]{3,2,1,0:T(8,128)S(1)}, f32[2,4,16,256]{3,2,1,0:T(8,128)S(1)}, f32[2,4,16,256]{3,2,1,0:T(8,128)S(1)}) custom-call(f32[2,16,16,256]{3,2,1,0:T(8,128)S(1)} %get-tuple-element.82.now, f32[2,24,16,256]{3,2,1,0:T(8,128)S(1)} %get-tuple-element.83.before, ...), custom_call_target="tpu_custom_call" | custom-call | tf_op jit(solution)/shard_map/pallas_call | solution.py:289
  55.8 0.7 collective-permute-start.16
  56.5 3.6 %collective-permute-start.17 = (f32[2,4,16,256]{3,2,1,0:T(8,128)S(1)}, f32[2,4,16,256]{3,2,1,0:T(8,128)S(1)}, u32[]{:S(2)}, u32[]{:S(2)}) collective-permute-start(f32[2,4,16,256]{3,2,1,0:T(8,128)S(1)} %get-tuple-element.91), channel_id=1, source_target_pairs={{1,2},{2,1},{5,6},{6,5},{9,10},{10,9},{13,14},{14,13},{17,18},{18,... | collective-permute-start | bytes 393224 | tf_op jit(solution)/shard_map/ppermute | solution.py:61
  60.1 2.2 %collective-permute-start.18 = (f32[2,4,16,256]{3,2,1,0:T(8,128)S(1)}, f32[2,4,16,256]{3,2,1,0:T(8,128)S(1)}, u32[]{:S(2)}, u32[]{:S(2)}) collective-permute-start(f32[2,4,16,256]{3,2,1,0:T(8,128)S(1)} %get-tuple-element.92), channel_id=1, source_target_pairs={{1,2},{2,1},{5,6},{6,5},{9,10},{10,9},{13,14},{14,13},{17,18},{18,... | collective-permute-start | bytes 393224 | tf_op jit(solution)/shard_map/ppermute | solution.py:61
  62.3 0.6 inner.1.refs_0_.own_inner
  63.0 0.0 copy-start.2
  63.0 0.1 collective-permute-start.14
  63.1 0.0 collective-permute-done.15.refs_6_
  63.1 0.0 collective-permute-done.16.refs_7_
  63.1 0.2 collective-permute-done.17.refs_8_
  63.3 3.6 %collective-permute-done.18.refs_9_ = f32[2,4,16,256]{3,2,1,0:T(8,128)S(1)} collective-permute-done((f32[2,4,16,256]{3,2,1,0:T(8,128)S(1)}, f32[2,4,16,256]{3,2,1,0:T(8,128)S(1)}, u32[]{:S(2)}, u32[]{:S(2)}) %collective-permute-start.18) | collective-permute-done | bytes 131104 | tf_op jit(solution)/shard_map/ppermute | solution.py:61
  67.0 0.7 outer.1.own_outer.refs_0_
  67.7 0.1 collective-permute-start.19
  67.8 0.0 collective-permute-done.14.refs_1_.other_inner
  67.8 0.8 %shard_map.129 = f32[2,8,16,256]{3,2,1,0:T(8,128)S(1)} custom-call(s32[8]{0:T(128)S(1)} %copy-done.2, f32[4,8,16,256]{3,2,1,0:T(8,128)S(1)} %inner.1.refs_0_.own_inner, f32[4,8,16,256]{3,2,1,0:T(8,128)S(1)} %collective-permute-done.14.refs_1_.other_inner), custom_call_target="tpu_custom_call" | custom-call | tf_op jit(solution)/shard_map/pallas_call | solution.py:412
  68.7 1.6 %collective-permute-start.20 = (f32[2,8,16,256]{3,2,1,0:T(8,128)S(1)}, f32[2,8,16,256]{3,2,1,0:T(8,128)S(1)}, u32[]{:S(2)}, u32[]{:S(2)}) collective-permute-start(f32[2,8,16,256]{3,2,1,0:T(8,128)S(1)} %shard_map.129), channel_id=1, source_target_pairs={{0,8},{4,12},{8,0},{12,4},{1,9},{5,13},{9,1},{13,5},{2,10},{6,14},... | collective-permute-start | bytes 786440 | tf_op jit(solution)/shard_map/ppermute | solution.py:523
  70.3 0.0 collective-permute-done.19.other_outer.refs_1_
  70.3 0.8 %shard_map.130 = f32[2,8,16,256]{3,2,1,0:T(8,128)S(1)} custom-call(s32[8]{0:T(128)S(1)} %copy-done.2, f32[4,8,16,256]{3,2,1,0:T(8,128)S(1)} %outer.1.own_outer.refs_0_, f32[4,8,16,256]{3,2,1,0:T(8,128)S(1)} %collective-permute-done.19.other_outer.refs_1_), custom_call_target="tpu_custom_call" | custom-call | tf_op jit(solution)/shard_map/pallas_call | solution.py:412
  71.1 1.0 %collective-permute-start.21 = (f32[2,8,16,256]{3,2,1,0:T(8,128)S(1)}, f32[2,8,16,256]{3,2,1,0:T(8,128)S(1)}, u32[]{:S(2)}, u32[]{:S(2)}) collective-permute-start(f32[2,8,16,256]{3,2,1,0:T(8,128)S(1)} %shard_map.130), channel_id=1, source_target_pairs={{0,8},{4,12},{8,0},{12,4},{1,9},{5,13},{9,1},{13,5},{2,10},{6,14},... | collective-permute-start | bytes 786440 | tf_op jit(solution)/shard_map/ppermute | solution.py:523
  72.1 5.8 %collective-permute-done.20.refs_0_ = f32[2,8,16,256]{3,2,1,0:T(8,128)S(1)} collective-permute-done((f32[2,8,16,256]{3,2,1,0:T(8,128)S(1)}, f32[2,8,16,256]{3,2,1,0:T(8,128)S(1)}, u32[]{:S(2)}, u32[]{:S(2)}) %collective-permute-start.20) | collective-permute-done | bytes 262176 | tf_op jit(solution)/shard_map/ppermute | solution.py:523
  77.9 1.7 %image_inner.1 = (f32[2,16,16,256]{3,2,1,0:T(8,128)}, f32[2,16,16,256]{3,2,1,0:T(8,128)}, f32[2,16,16,256]{3,2,1,0:T(8,128)}, f32[2,8,16,256]{3,2,1,0:T(8,128)S(1)}) custom-call(s32[8]{0:T(128)S(1)} %copy-done.2, f32[4,8,16,256]{3,2,1,0:T(8,128)S(1)} %inner.1.refs_0_.own_inner, f32[4,8,16,256]{3,2,1,0:T(8,128)S(1)} %collective-permute-done.14.refs_1_.other_inner, ...), custom_call_target="tpu_custom_call" | custom-call | tf_op jit(solution)/shard_map/image_inner/pallas_call | solution.py:449
  79.7 3.4 %collective-permute-done.21.refs_1_ = f32[2,8,16,256]{3,2,1,0:T(8,128)S(1)} collective-permute-done((f32[2,8,16,256]{3,2,1,0:T(8,128)S(1)}, f32[2,8,16,256]{3,2,1,0:T(8,128)S(1)}, u32[]{:S(2)}, u32[]{:S(2)}) %collective-permute-start.21) | collective-permute-done | bytes 262176 | tf_op jit(solution)/shard_map/ppermute | solution.py:523
  83.1 0.7 image_outer.1
  (9 shorter events, 0.0 us)
Async XLA Ops:
  0.6 6.6 %copy-start.1 = (f32[8,2,256]{2,1,0:T(2,128)S(1)}, f32[8,2,256]{2,1,0:T(2,128)}, u32[]{:S(2)}) copy-start(f32[8,2,256]{2,1,0:T(2,128)} %traces.1) | copy-start | bytes 49156
  1.9 5.3 %copy-start.5 = (f32[8,2]{0,1:T(2,128)S(1)}, f32[8,2]{0,1:T(2,128)}, u32[]{:S(2)}) copy-start(f32[8,2]{0,1:T(2,128)} %param.16) | copy-start | bytes 196
  1.9 9.5 %collective-permute-start = (f32[5,4,16,256]{3,2,1,0:T(8,128)S(1)}, f32[5,4,16,256]{3,2,1,0:T(8,128)S(1)}, u32[]{:S(2)}, u32[]{:S(2)}) collective-permute-start(f32[5,4,16,256]{3,2,1,0:T(8,128)S(1)} %get-tuple-element.52), channel_id=1, source_target_pairs={{0,1},{1,0},{2,3},{3,2},{4,5},{5,4},{6,7},{7,6},{8,9},{9,8},{10,11... | collective-permute-start | bytes 983048 | tf_op jit(solution)/shard_map/ppermute | solution.py:60
  2.4 4.8 %copy-start.3 = (s32[2,256]{1,0:T(2,128)S(1)}, s32[2,256]{1,0:T(2,128)}, u32[]{:S(2)}) copy-start(s32[2,256]{1,0:T(2,128)} %receiver_cell.1) | copy-start | bytes 6148
  2.4 4.8 %copy-start.4 = (s32[2]{0:T(128)S(1)}, s32[2]{0:T(128)}, u32[]{:S(2)}) copy-start(s32[2]{0:T(128)} %source_cell.1) | copy-start | bytes 28
  2.4 12.2 %collective-permute-start.1 = (f32[5,4,16,256]{3,2,1,0:T(8,128)S(1)}, f32[5,4,16,256]{3,2,1,0:T(8,128)S(1)}, u32[]{:S(2)}, u32[]{:S(2)}) collective-permute-start(f32[5,4,16,256]{3,2,1,0:T(8,128)S(1)} %get-tuple-element.53), channel_id=1, source_target_pairs={{1,2},{2,1},{5,6},{6,5},{9,10},{10,9},{13,14},{14,13},{17,18},{18,... | collective-permute-start | bytes 983048 | tf_op jit(solution)/shard_map/ppermute | solution.py:61
  7.2 7.3 %copy-start = (f32[16,16,256]{2,1,0:T(8,128)S(1)}, f32[16,16,256]{2,1,0:T(8,128)}, u32[]{:S(2)}) copy-start(f32[16,16,256]{2,1,0:T(8,128)} %courant.3) | copy-start | bytes 786436
  15.3 8.9 %collective-permute-start.2 = (f32[2,8,16,256]{3,2,1,0:T(8,128)S(1)}, f32[2,8,16,256]{3,2,1,0:T(8,128)S(1)}, u32[]{:S(2)}, u32[]{:S(2)}) collective-permute-start(f32[2,8,16,256]{3,2,1,0:T(8,128)S(1)} %get-tuple-element.59), channel_id=1, source_target_pairs={{0,1},{1,0},{2,3},{3,2},{4,5},{5,4},{6,7},{7,6},{8,9},{9,8},{10,11... | collective-permute-start | bytes 786440 | tf_op jit(solution)/shard_map/ppermute | solution.py:60
  15.4 10.8 %collective-permute-start.3 = (f32[2,8,16,256]{3,2,1,0:T(8,128)S(1)}, f32[2,8,16,256]{3,2,1,0:T(8,128)S(1)}, u32[]{:S(2)}, u32[]{:S(2)}) collective-permute-start(f32[2,8,16,256]{3,2,1,0:T(8,128)S(1)} %get-tuple-element.60), channel_id=1, source_target_pairs={{1,2},{2,1},{5,6},{6,5},{9,10},{10,9},{13,14},{14,13},{17,18},{18,... | collective-permute-start | bytes 786440 | tf_op jit(solution)/shard_map/ppermute | solution.py:61
  19.8 12.0 %collective-permute-start.8 = (f32[2,8,16,256]{3,2,1,0:T(8,128)S(1)}, f32[2,8,16,256]{3,2,1,0:T(8,128)S(1)}, u32[]{:S(2)}, u32[]{:S(2)}) collective-permute-start(f32[2,8,16,256]{3,2,1,0:T(8,128)S(1)} %get-tuple-element.76), channel_id=1, source_target_pairs={{0,1},{1,0},{2,3},{3,2},{4,5},{5,4},{6,7},{7,6},{8,9},{9,8},{10,11... | collective-permute-start | bytes 786440 | tf_op jit(solution)/shard_map/ppermute | solution.py:60
  19.9 11.9 %collective-permute-start.9 = (f32[2,8,16,256]{3,2,1,0:T(8,128)S(1)}, f32[2,8,16,256]{3,2,1,0:T(8,128)S(1)}, u32[]{:S(2)}, u32[]{:S(2)}) collective-permute-start(f32[2,8,16,256]{3,2,1,0:T(8,128)S(1)} %get-tuple-element.77), channel_id=1, source_target_pairs={{1,2},{2,1},{5,6},{6,5},{9,10},{10,9},{13,14},{14,13},{17,18},{18,... | collective-permute-start | bytes 786440 | tf_op jit(solution)/shard_map/ppermute | solution.py:61
  27.7 9.0 %collective-permute-start.4 = (f32[2,8,16,256]{3,2,1,0:T(8,128)S(1)}, f32[2,8,16,256]{3,2,1,0:T(8,128)S(1)}, u32[]{:S(2)}, u32[]{:S(2)}) collective-permute-start(f32[2,8,16,256]{3,2,1,0:T(8,128)S(1)} %get-tuple-element.64), channel_id=1, source_target_pairs={{0,1},{1,0},{2,3},{3,2},{4,5},{5,4},{6,7},{7,6},{8,9},{9,8},{10,11... | collective-permute-start | bytes 786440 | tf_op jit(solution)/shard_map/ppermute | solution.py:60
  27.8 10.4 %collective-permute-start.5 = (f32[2,8,16,256]{3,2,1,0:T(8,128)S(1)}, f32[2,8,16,256]{3,2,1,0:T(8,128)S(1)}, u32[]{:S(2)}, u32[]{:S(2)}) collective-permute-start(f32[2,8,16,256]{3,2,1,0:T(8,128)S(1)} %get-tuple-element.65), channel_id=1, source_target_pairs={{1,2},{2,1},{5,6},{6,5},{9,10},{10,9},{13,14},{14,13},{17,18},{18,... | collective-permute-start | bytes 786440 | tf_op jit(solution)/shard_map/ppermute | solution.py:61
  33.4 10.9 %collective-permute-start.10 = (f32[2,8,16,256]{3,2,1,0:T(8,128)S(1)}, f32[2,8,16,256]{3,2,1,0:T(8,128)S(1)}, u32[]{:S(2)}, u32[]{:S(2)}) collective-permute-start(f32[2,8,16,256]{3,2,1,0:T(8,128)S(1)} %get-tuple-element.80), channel_id=1, source_target_pairs={{0,1},{1,0},{2,3},{3,2},{4,5},{5,4},{6,7},{7,6},{8,9},{9,8},{10,11... | collective-permute-start | bytes 786440 | tf_op jit(solution)/shard_map/ppermute | solution.py:60
  33.5 10.9 %collective-permute-start.11 = (f32[2,8,16,256]{3,2,1,0:T(8,128)S(1)}, f32[2,8,16,256]{3,2,1,0:T(8,128)S(1)}, u32[]{:S(2)}, u32[]{:S(2)}) collective-permute-start(f32[2,8,16,256]{3,2,1,0:T(8,128)S(1)} %get-tuple-element.81), channel_id=1, source_target_pairs={{1,2},{2,1},{5,6},{6,5},{9,10},{10,9},{13,14},{14,13},{17,18},{18,... | collective-permute-start | bytes 786440 | tf_op jit(solution)/shard_map/ppermute | solution.py:61
  39.8 10.3 %collective-permute-start.6 = (f32[2,8,16,256]{3,2,1,0:T(8,128)S(1)}, f32[2,8,16,256]{3,2,1,0:T(8,128)S(1)}, u32[]{:S(2)}, u32[]{:S(2)}) collective-permute-start(f32[2,8,16,256]{3,2,1,0:T(8,128)S(1)} %get-tuple-element.68), channel_id=1, source_target_pairs={{0,1},{1,0},{2,3},{3,2},{4,5},{5,4},{6,7},{7,6},{8,9},{9,8},{10,11... | collective-permute-start | bytes 786440 | tf_op jit(solution)/shard_map/ppermute | solution.py:60
  39.9 11.4 %collective-permute-start.7 = (f32[2,8,16,256]{3,2,1,0:T(8,128)S(1)}, f32[2,8,16,256]{3,2,1,0:T(8,128)S(1)}, u32[]{:S(2)}, u32[]{:S(2)}) collective-permute-start(f32[2,8,16,256]{3,2,1,0:T(8,128)S(1)} %get-tuple-element.69), channel_id=1, source_target_pairs={{1,2},{2,1},{5,6},{6,5},{9,10},{10,9},{13,14},{14,13},{17,18},{18,... | collective-permute-start | bytes 786440 | tf_op jit(solution)/shard_map/ppermute | solution.py:61
  45.9 7.3 %collective-permute-start.12 = (f32[2,8,16,256]{3,2,1,0:T(8,128)S(1)}, f32[2,8,16,256]{3,2,1,0:T(8,128)S(1)}, u32[]{:S(2)}, u32[]{:S(2)}) collective-permute-start(f32[2,8,16,256]{3,2,1,0:T(8,128)S(1)} %get-tuple-element.84), channel_id=1, source_target_pairs={{0,1},{1,0},{2,3},{3,2},{4,5},{5,4},{6,7},{7,6},{8,9},{9,8},{10,11... | collective-permute-start | bytes 786440 | tf_op jit(solution)/shard_map/ppermute | solution.py:60
  46.0 8.3 %collective-permute-start.13 = (f32[2,8,16,256]{3,2,1,0:T(8,128)S(1)}, f32[2,8,16,256]{3,2,1,0:T(8,128)S(1)}, u32[]{:S(2)}, u32[]{:S(2)}) collective-permute-start(f32[2,8,16,256]{3,2,1,0:T(8,128)S(1)} %get-tuple-element.85), channel_id=1, source_target_pairs={{1,2},{2,1},{5,6},{6,5},{9,10},{10,9},{13,14},{14,13},{17,18},{18,... | collective-permute-start | bytes 786440 | tf_op jit(solution)/shard_map/ppermute | solution.py:61
  52.8 10.3 %collective-permute-start.15 = (f32[2,4,16,256]{3,2,1,0:T(8,128)S(1)}, f32[2,4,16,256]{3,2,1,0:T(8,128)S(1)}, u32[]{:S(2)}, u32[]{:S(2)}) collective-permute-start(f32[2,4,16,256]{3,2,1,0:T(8,128)S(1)} %get-tuple-element.89), channel_id=1, source_target_pairs={{0,1},{1,0},{2,3},{3,2},{4,5},{5,4},{6,7},{7,6},{8,9},{9,8},{10,11... | collective-permute-start | bytes 393224 | tf_op jit(solution)/shard_map/ppermute | solution.py:60
  55.8 7.3 %collective-permute-start.16 = (f32[2,4,16,256]{3,2,1,0:T(8,128)S(1)}, f32[2,4,16,256]{3,2,1,0:T(8,128)S(1)}, u32[]{:S(2)}, u32[]{:S(2)}) collective-permute-start(f32[2,4,16,256]{3,2,1,0:T(8,128)S(1)} %get-tuple-element.90), channel_id=1, source_target_pairs={{0,1},{1,0},{2,3},{3,2},{4,5},{5,4},{6,7},{7,6},{8,9},{9,8},{10,11... | collective-permute-start | bytes 393224 | tf_op jit(solution)/shard_map/ppermute | solution.py:60
  56.5 6.8 %collective-permute-start.17 = (f32[2,4,16,256]{3,2,1,0:T(8,128)S(1)}, f32[2,4,16,256]{3,2,1,0:T(8,128)S(1)}, u32[]{:S(2)}, u32[]{:S(2)}) collective-permute-start(f32[2,4,16,256]{3,2,1,0:T(8,128)S(1)} %get-tuple-element.91), channel_id=1, source_target_pairs={{1,2},{2,1},{5,6},{6,5},{9,10},{10,9},{13,14},{14,13},{17,18},{18,... | collective-permute-start | bytes 393224 | tf_op jit(solution)/shard_map/ppermute | solution.py:61
  60.1 6.9 %collective-permute-start.18 = (f32[2,4,16,256]{3,2,1,0:T(8,128)S(1)}, f32[2,4,16,256]{3,2,1,0:T(8,128)S(1)}, u32[]{:S(2)}, u32[]{:S(2)}) collective-permute-start(f32[2,4,16,256]{3,2,1,0:T(8,128)S(1)} %get-tuple-element.92), channel_id=1, source_target_pairs={{1,2},{2,1},{5,6},{6,5},{9,10},{10,9},{13,14},{14,13},{17,18},{18,... | collective-permute-start | bytes 393224 | tf_op jit(solution)/shard_map/ppermute | solution.py:61
  63.0 4.8 %copy-start.2 = (s32[8]{0:T(128)S(1)}, s32[8]{0:T(128)}, u32[]{:S(2)}) copy-start(s32[8]{0:T(128)} %offset_perm.5) | copy-start | bytes 100
  63.0 4.8 %collective-permute-start.14 = (f32[4,8,16,256]{3,2,1,0:T(8,128)S(1)}, f32[4,8,16,256]{3,2,1,0:T(8,128)S(1)}, u32[]{:S(2)}, u32[]{:S(2)}) collective-permute-start(f32[4,8,16,256]{3,2,1,0:T(8,128)S(1)} %inner.1.refs_0_.own_inner), channel_id=1, source_target_pairs={{0,4},{4,0},{8,12},{12,8},{1,5},{5,1},{9,13},{13,9},{2,6},{6,2},{1... | collective-permute-start | bytes 1572872 | tf_op jit(solution)/shard_map/ppermute | solution.py:527
  67.7 2.5 %collective-permute-start.19 = (f32[4,8,16,256]{3,2,1,0:T(8,128)S(1)}, f32[4,8,16,256]{3,2,1,0:T(8,128)S(1)}, u32[]{:S(2)}, u32[]{:S(2)}) collective-permute-start(f32[4,8,16,256]{3,2,1,0:T(8,128)S(1)} %outer.1.own_outer.refs_0_), channel_id=1, source_target_pairs={{0,4},{4,0},{8,12},{12,8},{1,5},{5,1},{9,13},{13,9},{2,6},{6,2},{1... | collective-permute-start | bytes 1572872 | tf_op jit(solution)/shard_map/ppermute | solution.py:530
  68.7 9.2 %collective-permute-start.20 = (f32[2,8,16,256]{3,2,1,0:T(8,128)S(1)}, f32[2,8,16,256]{3,2,1,0:T(8,128)S(1)}, u32[]{:S(2)}, u32[]{:S(2)}) collective-permute-start(f32[2,8,16,256]{3,2,1,0:T(8,128)S(1)} %shard_map.129), channel_id=1, source_target_pairs={{0,8},{4,12},{8,0},{12,4},{1,9},{5,13},{9,1},{13,5},{2,10},{6,14},... | collective-permute-start | bytes 786440 | tf_op jit(solution)/shard_map/ppermute | solution.py:523
  71.1 12.0 %collective-permute-start.21 = (f32[2,8,16,256]{3,2,1,0:T(8,128)S(1)}, f32[2,8,16,256]{3,2,1,0:T(8,128)S(1)}, u32[]{:S(2)}, u32[]{:S(2)}) collective-permute-start(f32[2,8,16,256]{3,2,1,0:T(8,128)S(1)} %shard_map.130), channel_id=1, source_target_pairs={{0,8},{4,12},{8,0},{12,4},{1,9},{5,13},{9,1},{13,5},{2,10},{6,14},... | collective-permute-start | bytes 786440 | tf_op jit(solution)/shard_map/ppermute | solution.py:523

commit v4 on v3

--- a/solution.py
+++ b/solution.py
@@ -76,15 +76,18 @@
     return (1 - odd) * (rows + width), odd * (rows + width)
 
 
-def pack_kernel(source, receiver, courant, even_edge, odd_edge, sem):
+def pack_kernel(source, receiver, courant, *refs):
     groups, rows = source.shape[:2]
+    outs, sem = refs[:-1], refs[-1]
     copies = []
-    for out, start in zip((even_edge, odd_edge), edge_starts(rows, REACH)):
-        planes = pl.ds(start, REACH)
-        pieces = [array.at[group, planes] for group in range(groups) for array in (source, receiver)]
-        pieces.append(courant.at[planes])
-        for index, piece in enumerate(pieces):
-            copies.append(pltpu.make_async_copy(piece, out.at[index], sem.at[len(copies)]))
+    for group in range(groups):
+        for side, start in enumerate(edge_starts(rows, REACH)):
+            planes = pl.ds(start, REACH)
+            pieces = [source.at[group, planes], receiver.at[group, planes]]
+            if group == 0:
+                pieces.append(courant.at[planes])
+            for index, piece in enumerate(pieces):
+                copies.append(pltpu.make_async_copy(piece, outs[2 * group + side].at[index], sem.at[len(copies)]))
     for copy in copies:
         copy.start()
     for copy in copies:
@@ -97,13 +100,13 @@
 
 def pack(source_now, receiver_now, courant_sq):
     groups, _, size_y, size_z = source_now.shape
-    count = 2 * groups + 1
+    shapes = [struct((3 if group == 0 else 2, REACH, size_y, size_z)) for group in range(groups) for _ in range(2)]
     return pl.pallas_call(
         pack_kernel,
-        out_shape=[struct((count, REACH, size_y, size_z))] * 2,
+        out_shape=shapes,
         in_specs=[hbm()] * 3,
-        out_specs=[vmem()] * 2,
-        scratch_shapes=[pltpu.SemaphoreType.DMA((2 * count,))],
+        out_specs=[vmem()] * len(shapes),
+        scratch_shapes=[pltpu.SemaphoreType.DMA((4 * groups + 2,))],
         compiler_params=params(),
         name="pack",
     )(*stay(source_now, receiver_now, courant_sq))
@@ -213,20 +216,20 @@
     return [[(at, CHUNK)] for at in range(start, stop, CHUNK)]
 
 
-def first_kernel(group, rows, has_courant, width, now, before, courant, even, odd, inject, along_z, along_y, fresh, held, even_edge, odd_edge, *scaled):
+def first_kernel(rows, has_courant, width, now, before, courant, even, odd, inject, along_z, along_y, fresh, held, even_edge, odd_edge, *scaled):
     even_at, odd_at = halo_starts(rows, REACH)
     if has_courant:
         (courant_out,) = scaled
         courant_out[REACH : REACH + rows] = SCALE * courant[...]
-        courant_out[pl.ds(even_at, REACH)] = SCALE * even[even.shape[0] - 1]
-        courant_out[pl.ds(odd_at, REACH)] = SCALE * odd[odd.shape[0] - 1]
+        courant_out[pl.ds(even_at, REACH)] = SCALE * even[2]
+        courant_out[pl.ds(odd_at, REACH)] = SCALE * odd[2]
         courant = courant_out
     z_band, y_band = along_z[...], along_y[...]
     for kind in range(2):
         field = held.at[kind]
         field[REACH : REACH + rows] = now[kind]
-        field[pl.ds(even_at, REACH)] = even[2 * group + kind]
-        field[pl.ds(odd_at, REACH)] = odd[2 * group + kind]
+        field[pl.ds(even_at, REACH)] = even[kind]
+        field[pl.ds(odd_at, REACH)] = odd[kind]
 
         def write(i, plane, new, kind=kind):
             fresh[kind, plane] = new
@@ -250,7 +253,7 @@
     if has_courant:
         shapes.append(struct((rows + 2 * REACH, size_y, size_z)))
     return pl.pallas_call(
-        functools.partial(first_kernel, group, rows, has_courant, width),
+        functools.partial(first_kernel, rows, has_courant, width),
         out_shape=shapes,
         in_specs=[vmem()] * 8,
         out_specs=[vmem()] * len(shapes),
@@ -493,7 +496,8 @@
     slots = offset_perm.shape[0] // shot_devices
     everyone = range(groups)
 
-    given = trade(*pack(source_now, receiver_now, courant_sq))
+    edges = pack(source_now, receiver_now, courant_sq)
+    given = [trade(edges[2 * g], edges[2 * g + 1]) for g in everyone]
     fields = (source_now, receiver_now, source_prev, receiver_prev)
     along_z, along_y, *rest = prepare(source_cell, wavelet, receiver_cell, traces, fields)
     inject, now, before = rest[:groups], rest[groups : 2 * groups], rest[2 * groups :]
@@ -501,7 +505,7 @@
     halos = [None] * groups
     courant = courant_sq
     for g in everyone:
-        result = first_round(g, 2 * REACH, now[g], before[g], courant, given, inject[g], along_z, along_y)
+        result = first_round(g, 2 * REACH, now[g], before[g], courant, given[g], inject[g], along_z, along_y)
         now[g], before[g] = result[:2]
         if g == 0:
             courant = result[4]

time: 84.4 us -> 79.3 us (0.940)
  the two profiles are of different devices: /device:TPU:12 before, /device:TPU:0 now
where the time goes in v4:
time: 79.3 us; the launch traced here: 78 us
  starting transfers between devices  44.7 us (56%)
  Pallas kernels  19.8 us (25%)
  waiting for transfers between devices  12.2 us (15%)
  between operations  1.14 us (1%)
    ppermute x10, starting transfers between devices, trade(): even = lax.ppermute(even_edge, 'slab', even_pairs(count))  35.1 us
    pallas_call x6, Pallas kernels, pair_round(): pl.pallas_call(functools.partial(pair_kernel, rows, step, width), out_sha...  9.31 us
    ppermute x2, waiting for transfers between devices, part_sums(): sums.append(lax.ppermute(part, 'shot', route))  9.16 us
    ppermute x10, starting transfers between devices, trade(): odd = lax.ppermute(odd_edge, 'slab', odd_pairs(count))  6.94 us
    ppermute x10, waiting for transfers between devices, trade(): even = lax.ppermute(even_edge, 'slab', even_pairs(count))  3.05 us
    ppermute x2, starting transfers between devices, part_sums(): sums.append(lax.ppermute(part, 'shot', route))  2.58 us
    pallas_call x1, Pallas kernels, prepare(): pl.pallas_call(functools.partial(prepare_kernel, groups, rows), out_shape...  2.19 us
    pallas_call x1, Pallas kernels, inner_image(): pl.pallas_call(inner_image_kernel, out_shape=[struct((slots, rows, size_y...  1.7 us
  transfers between devices with their start and end apart: 24, of which 5 were waited for; matrix products, arithmetic and copies ran while one was open for 0% of the time, Pallas kernels for 23%

profile of v4, /device:TPU:0, one launch (start us, length us, event | category | flops | bytes accessed | tf_op | source)
XLA Modules:
  0.0 78.0 jit_solution(2160472464274858641)
XLA Ops:
  0.6 1.2 %pack.1 = (f32[3,4,16,256]{3,2,1,0:T(8,128)S(1)}, f32[3,4,16,256]{3,2,1,0:T(8,128)S(1)}, f32[2,4,16,256]{3,2,1,0:T(8,128)S(1)}, f32[2,4,16,256]{3,2,1,0:T(8,128)S(1)}) custom-call(f32[2,16,16,256]{3,2,1,0:T(8,128)} %source.3, f32[2,16,16,256]{3,2,1,0:T(8,128)} %receiver.3, f32[16,16,256]{2,1,0:T(8,128)} %courant.3), custom_call_target="tpu_custom_call" | custom-call | tf_op jit(solution)/shard_map/pack/pallas_call | solution.py:104
  1.9 3.1 %collective-permute-start = (f32[3,4,16,256]{3,2,1,0:T(8,128)S(1)}, f32[3,4,16,256]{3,2,1,0:T(8,128)S(1)}, u32[]{:S(2)}, u32[]{:S(2)}) collective-permute-start(f32[3,4,16,256]{3,2,1,0:T(8,128)S(1)} %get-tuple-element.54), channel_id=1, source_target_pairs={{0,1},{1,0},{2,3},{3,2},{4,5},{5,4},{6,7},{7,6},{8,9},{9,8},{10,11... | collective-permute-start | bytes 589832 | tf_op jit(solution)/shard_map/ppermute | solution.py:60
  5.0 0.7 collective-permute-start.1
  5.6 0.0 copy-start.5
  5.7 4.5 %collective-permute-start.8 = (f32[2,4,16,256]{3,2,1,0:T(8,128)S(1)}, f32[2,4,16,256]{3,2,1,0:T(8,128)S(1)}, u32[]{:S(2)}, u32[]{:S(2)}) collective-permute-start(f32[2,4,16,256]{3,2,1,0:T(8,128)S(1)} %get-tuple-element.75), channel_id=1, source_target_pairs={{0,1},{1,0},{2,3},{3,2},{4,5},{5,4},{6,7},{7,6},{8,9},{9,8},{10,11... | collective-permute-start | bytes 393224 | tf_op jit(solution)/shard_map/ppermute | solution.py:60
  10.1 0.8 %collective-permute-start.9 = (f32[2,4,16,256]{3,2,1,0:T(8,128)S(1)}, f32[2,4,16,256]{3,2,1,0:T(8,128)S(1)}, u32[]{:S(2)}, u32[]{:S(2)}) collective-permute-start(f32[2,4,16,256]{3,2,1,0:T(8,128)S(1)} %get-tuple-element.76), channel_id=1, source_target_pairs={{1,2},{2,1},{5,6},{6,5},{9,10},{10,9},{13,14},{14,13},{17,18},{18,... | collective-permute-start | bytes 393224 | tf_op jit(solution)/shard_map/ppermute | solution.py:61
  10.9 0.1 copy.14.wavelet
  11.0 2.2 %prepare.1 = (bf16[256,256]{1,0:T(8,128)(2,1)S(1)}, bf16[128,256]{1,0:T(8,128)(2,1)S(1)}, f32[2,24,16,128]{3,2,1,0:T(8,128)S(1)}, f32[2,24,16,128]{3,2,1,0:T(8,1...) custom-call(s32[2]{0:T(128)S(1)} %copy-done.4, ...), custom_call_target="tpu_custom_call" | custom-call | tf_op jit(solution)/shard_map/prepare/pallas_call | solution.py:176
  13.2 0.0 collective-permute-done.even
  13.2 0.0 collective-permute-done.1.odd
  13.3 0.8 shard_map.121
  14.0 2.2 %collective-permute-start.2 = (f32[2,8,16,256]{3,2,1,0:T(8,128)S(1)}, f32[2,8,16,256]{3,2,1,0:T(8,128)S(1)}, u32[]{:S(2)}, u32[]{:S(2)}) collective-permute-start(f32[2,8,16,256]{3,2,1,0:T(8,128)S(1)} %get-tuple-element.61), channel_id=1, source_target_pairs={{0,1},{1,0},{2,3},{3,2},{4,5},{5,4},{6,7},{7,6},{8,9},{9,8},{10,11... | collective-permute-start | bytes 786440 | tf_op jit(solution)/shard_map/ppermute | solution.py:60
  16.2 0.7 collective-permute-start.3
  16.9 0.0 collective-permute-done.8.even
  16.9 0.0 collective-permute-done.9.odd
  16.9 0.8 shard_map.125
  17.7 3.7 %collective-permute-start.10 = (f32[2,8,16,256]{3,2,1,0:T(8,128)S(1)}, f32[2,8,16,256]{3,2,1,0:T(8,128)S(1)}, u32[]{:S(2)}, u32[]{:S(2)}) collective-permute-start(f32[2,8,16,256]{3,2,1,0:T(8,128)S(1)} %get-tuple-element.80), channel_id=1, source_target_pairs={{0,1},{1,0},{2,3},{3,2},{4,5},{5,4},{6,7},{7,6},{8,9},{9,8},{10,11... | collective-permute-start | bytes 786440 | tf_op jit(solution)/shard_map/ppermute | solution.py:60
  21.4 0.7 collective-permute-start.11
  22.1 0.9 %collective-permute-done.2.even = f32[2,8,16,256]{3,2,1,0:T(8,128)S(1)} collective-permute-done((f32[2,8,16,256]{3,2,1,0:T(8,128)S(1)}, f32[2,8,16,256]{3,2,1,0:T(8,128)S(1)}, u32[]{:S(2)}, u32[]{:S(2)}) %collective-permute-start.2) | collective-permute-done | bytes 262176 | tf_op jit(solution)/shard_map/ppermute | solution.py:60
  23.0 0.0 collective-permute-done.3.odd
  23.0 1.6 %shard_map.122 = (f32[2,16,16,256]{3,2,1,0:T(8,128)S(1)}, f32[2,24,16,256]{3,2,1,0:T(8,128)S(1)}, f32[2,8,16,256]{3,2,1,0:T(8,128)S(1)}, f32[2,8,16,256]{3,2,1,0:T(8,128)S(1)}) custom-call(f32[2,16,16,256]{3,2,1,0:T(8,128)S(1)} %get-tuple-element.59.now, f32[2,24,16,256]{3,2,1,0:T(8,128)S(1)} %get-tuple-element.60.before, ...), custom_call_target="tpu_custom_call" | custom-call | tf_op jit(solution)/shard_map/pallas_call | solution.py:292
  24.5 4.1 %collective-permute-start.4 = (f32[2,8,16,256]{3,2,1,0:T(8,128)S(1)}, f32[2,8,16,256]{3,2,1,0:T(8,128)S(1)}, u32[]{:S(2)}, u32[]{:S(2)}) collective-permute-start(f32[2,8,16,256]{3,2,1,0:T(8,128)S(1)} %get-tuple-element.66), channel_id=1, source_target_pairs={{0,1},{1,0},{2,3},{3,2},{4,5},{5,4},{6,7},{7,6},{8,9},{9,8},{10,11... | collective-permute-start | bytes 786440 | tf_op jit(solution)/shard_map/ppermute | solution.py:60
  28.6 0.7 collective-permute-start.5
  29.3 0.0 collective-permute-done.10.even
  29.3 0.0 collective-permute-done.11.odd
  29.3 1.6 %shard_map.126 = (f32[2,16,16,256]{3,2,1,0:T(8,128)S(1)}, f32[2,24,16,256]{3,2,1,0:T(8,128)S(1)}, f32[2,8,16,256]{3,2,1,0:T(8,128)S(1)}, f32[2,8,16,256]{3,2,1,0:T(8,128)S(1)}) custom-call(f32[2,16,16,256]{3,2,1,0:T(8,128)S(1)} %get-tuple-element.78.now, f32[2,24,16,256]{3,2,1,0:T(8,128)S(1)} %get-tuple-element.79.before, ...), custom_call_target="tpu_custom_call" | custom-call | tf_op jit(solution)/shard_map/pallas_call | solution.py:292
  30.9 3.8 %collective-permute-start.12 = (f32[2,8,16,256]{3,2,1,0:T(8,128)S(1)}, f32[2,8,16,256]{3,2,1,0:T(8,128)S(1)}, u32[]{:S(2)}, u32[]{:S(2)}) collective-permute-start(f32[2,8,16,256]{3,2,1,0:T(8,128)S(1)} %get-tuple-element.84), channel_id=1, source_target_pairs={{0,1},{1,0},{2,3},{3,2},{4,5},{5,4},{6,7},{7,6},{8,9},{9,8},{10,11... | collective-permute-start | bytes 786440 | tf_op jit(solution)/shard_map/ppermute | solution.py:60
  34.7 0.7 collective-permute-start.13
  35.4 0.0 collective-permute-done.4.even
  35.4 0.0 collective-permute-done.5.odd
  35.4 1.6 %shard_map.123 = (f32[2,16,16,256]{3,2,1,0:T(8,128)S(1)}, f32[2,24,16,256]{3,2,1,0:T(8,128)S(1)}, f32[2,8,16,256]{3,2,1,0:T(8,128)S(1)}, f32[2,8,16,256]{3,2,1,0:T(8,128)S(1)}) custom-call(f32[2,16,16,256]{3,2,1,0:T(8,128)S(1)} %get-tuple-element.64.now, f32[2,24,16,256]{3,2,1,0:T(8,128)S(1)} %get-tuple-element.65.before, ...), custom_call_target="tpu_custom_call" | custom-call | tf_op jit(solution)/shard_map/pallas_call | solution.py:292
  37.0 4.5 %collective-permute-start.6 = (f32[2,8,16,256]{3,2,1,0:T(8,128)S(1)}, f32[2,8,16,256]{3,2,1,0:T(8,128)S(1)}, u32[]{:S(2)}, u32[]{:S(2)}) collective-permute-start(f32[2,8,16,256]{3,2,1,0:T(8,128)S(1)} %get-tuple-element.70), channel_id=1, source_target_pairs={{0,1},{1,0},{2,3},{3,2},{4,5},{5,4},{6,7},{7,6},{8,9},{9,8},{10,11... | collective-permute-start | bytes 786440 | tf_op jit(solution)/shard_map/ppermute | solution.py:60
  41.5 0.7 collective-permute-start.7
  42.2 0.0 collective-permute-done.12.even
  42.2 0.0 collective-permute-done.13.odd
  42.2 1.6 %shard_map.127 = (f32[2,16,16,256]{3,2,1,0:T(8,128)S(1)}, f32[2,24,16,256]{3,2,1,0:T(8,128)S(1)}, f32[2,8,16,256]{3,2,1,0:T(8,128)S(1)}, f32[2,8,16,256]{3,2,1,0:T(8,128)S(1)}) custom-call(f32[2,16,16,256]{3,2,1,0:T(8,128)S(1)} %get-tuple-element.82.now, f32[2,24,16,256]{3,2,1,0:T(8,128)S(1)} %get-tuple-element.83.before, ...), custom_call_target="tpu_custom_call" | custom-call | tf_op jit(solution)/shard_map/pallas_call | solution.py:292
  43.7 3.6 %collective-permute-start.14 = (f32[2,8,16,256]{3,2,1,0:T(8,128)S(1)}, f32[2,8,16,256]{3,2,1,0:T(8,128)S(1)}, u32[]{:S(2)}, u32[]{:S(2)}) collective-permute-start(f32[2,8,16,256]{3,2,1,0:T(8,128)S(1)} %get-tuple-element.88), channel_id=1, source_target_pairs={{0,1},{1,0},{2,3},{3,2},{4,5},{5,4},{6,7},{7,6},{8,9},{9,8},{10,11... | collective-permute-start | bytes 786440 | tf_op jit(solution)/shard_map/ppermute | solution.py:60
  47.4 0.7 collective-permute-start.15
  48.1 0.3 collective-permute-done.6.even
  48.4 1.5 %shard_map.124 = (f32[2,16,16,256]{3,2,1,0:T(8,128)S(1)}, f32[2,24,16,256]{3,2,1,0:T(8,128)S(1)}, f32[2,4,16,256]{3,2,1,0:T(8,128)S(1)}, f32[2,4,16,256]{3,2,1,0:T(8,128)S(1)}) custom-call(f32[2,16,16,256]{3,2,1,0:T(8,128)S(1)} %get-tuple-element.68.now, f32[2,24,16,256]{3,2,1,0:T(8,128)S(1)} %get-tuple-element.69.before, ...), custom_call_target="tpu_custom_call" | custom-call | tf_op jit(solution)/shard_map/pallas_call | solution.py:292
  49.9 3.7 %collective-permute-start.17 = (f32[2,4,16,256]{3,2,1,0:T(8,128)S(1)}, f32[2,4,16,256]{3,2,1,0:T(8,128)S(1)}, u32[]{:S(2)}, u32[]{:S(2)}) collective-permute-start(f32[2,4,16,256]{3,2,1,0:T(8,128)S(1)} %get-tuple-element.93), channel_id=1, source_target_pairs={{0,1},{1,0},{2,3},{3,2},{4,5},{5,4},{6,7},{7,6},{8,9},{9,8},{10,11... | collective-permute-start | bytes 393224 | tf_op jit(solution)/shard_map/ppermute | solution.py:60
  53.7 0.8 %collective-permute-start.19 = (f32[2,4,16,256]{3,2,1,0:T(8,128)S(1)}, f32[2,4,16,256]{3,2,1,0:T(8,128)S(1)}, u32[]{:S(2)}, u32[]{:S(2)}) collective-permute-start(f32[2,4,16,256]{3,2,1,0:T(8,128)S(1)} %get-tuple-element.95), channel_id=1, source_target_pairs={{1,2},{2,1},{5,6},{6,5},{9,10},{10,9},{13,14},{14,13},{17,18},{18,... | collective-permute-start | bytes 393224 | tf_op jit(solution)/shard_map/ppermute | solution.py:61
  54.5 0.0 collective-permute-done.15.odd
  54.5 1.5 %shard_map.128 = (f32[2,16,16,256]{3,2,1,0:T(8,128)S(1)}, f32[2,24,16,256]{3,2,1,0:T(8,128)S(1)}, f32[2,4,16,256]{3,2,1,0:T(8,128)S(1)}, f32[2,4,16,256]{3,2,1,0:T(8,128)S(1)}) custom-call(f32[2,16,16,256]{3,2,1,0:T(8,128)S(1)} %get-tuple-element.86.now, f32[2,24,16,256]{3,2,1,0:T(8,128)S(1)} %get-tuple-element.87.before, ...), custom_call_target="tpu_custom_call" | custom-call | tf_op jit(solution)/shard_map/pallas_call | solution.py:292
  56.0 1.8 %collective-permute-start.18 = (f32[2,4,16,256]{3,2,1,0:T(8,128)S(1)}, f32[2,4,16,256]{3,2,1,0:T(8,128)S(1)}, u32[]{:S(2)}, u32[]{:S(2)}) collective-permute-start(f32[2,4,16,256]{3,2,1,0:T(8,128)S(1)} %get-tuple-element.94), channel_id=1, source_target_pairs={{0,1},{1,0},{2,3},{3,2},{4,5},{5,4},{6,7},{7,6},{8,9},{9,8},{10,11... | collective-permute-start | bytes 393224 | tf_op jit(solution)/shard_map/ppermute | solution.py:60
  57.9 0.7 collective-permute-start.20
  58.5 0.6 inner.1.refs_0_.own_inner
  59.2 0.0 copy-start.2
  59.2 0.1 collective-permute-start.16
  59.3 0.0 collective-permute-done.19.refs_8_
  59.3 1.8 %collective-permute-done.18.refs_7_ = f32[2,4,16,256]{3,2,1,0:T(8,128)S(1)} collective-permute-done((f32[2,4,16,256]{3,2,1,0:T(8,128)S(1)}, f32[2,4,16,256]{3,2,1,0:T(8,128)S(1)}, u32[]{:S(2)}, u32[]{:S(2)}) %collective-permute-start.18) | collective-permute-done | bytes 131104 | tf_op jit(solution)/shard_map/ppermute | solution.py:60
  61.1 0.0 collective-permute-done.20.refs_9_
  61.1 0.8 outer.1.own_outer.refs_0_
  61.8 0.1 collective-permute-start.21
  61.9 0.0 collective-permute-done.16.refs_1_.other_inner
  61.9 0.8 %shard_map.129 = f32[2,8,16,256]{3,2,1,0:T(8,128)S(1)} custom-call(s32[8]{0:T(128)S(1)} %copy-done.2, f32[4,8,16,256]{3,2,1,0:T(8,128)S(1)} %inner.1.refs_0_.own_inner, f32[4,8,16,256]{3,2,1,0:T(8,128)S(1)} %collective-permute-done.16.refs_1_.other_inner), custom_call_target="tpu_custom_call" | custom-call | tf_op jit(solution)/shard_map/pallas_call | solution.py:415
  62.8 1.6 %collective-permute-start.22 = (f32[2,8,16,256]{3,2,1,0:T(8,128)S(1)}, f32[2,8,16,256]{3,2,1,0:T(8,128)S(1)}, u32[]{:S(2)}, u32[]{:S(2)}) collective-permute-start(f32[2,8,16,256]{3,2,1,0:T(8,128)S(1)} %shard_map.129), channel_id=1, source_target_pairs={{0,8},{4,12},{8,0},{12,4},{1,9},{5,13},{9,1},{13,5},{2,10},{6,14},... | collective-permute-start | bytes 786440 | tf_op jit(solution)/shard_map/ppermute | solution.py:527
  64.3 0.0 collective-permute-done.21.other_outer.refs_1_
  64.3 0.8 %shard_map.130 = f32[2,8,16,256]{3,2,1,0:T(8,128)S(1)} custom-call(s32[8]{0:T(128)S(1)} %copy-done.2, f32[4,8,16,256]{3,2,1,0:T(8,128)S(1)} %outer.1.own_outer.refs_0_, f32[4,8,16,256]{3,2,1,0:T(8,128)S(1)} %collective-permute-done.21.other_outer.refs_1_), custom_call_target="tpu_custom_call" | custom-call | tf_op jit(solution)/shard_map/pallas_call | solution.py:415
  65.2 1.0 %collective-permute-start.23 = (f32[2,8,16,256]{3,2,1,0:T(8,128)S(1)}, f32[2,8,16,256]{3,2,1,0:T(8,128)S(1)}, u32[]{:S(2)}, u32[]{:S(2)}) collective-permute-start(f32[2,8,16,256]{3,2,1,0:T(8,128)S(1)} %shard_map.130), channel_id=1, source_target_pairs={{0,8},{4,12},{8,0},{12,4},{1,9},{5,13},{9,1},{13,5},{2,10},{6,14},... | collective-permute-start | bytes 786440 | tf_op jit(solution)/shard_map/ppermute | solution.py:527
  66.2 5.8 %collective-permute-done.22.refs_0_ = f32[2,8,16,256]{3,2,1,0:T(8,128)S(1)} collective-permute-done((f32[2,8,16,256]{3,2,1,0:T(8,128)S(1)}, f32[2,8,16,256]{3,2,1,0:T(8,128)S(1)}, u32[]{:S(2)}, u32[]{:S(2)}) %collective-permute-start.22) | collective-permute-done | bytes 262176 | tf_op jit(solution)/shard_map/ppermute | solution.py:527
  72.0 1.7 %image_inner.1 = (f32[2,16,16,256]{3,2,1,0:T(8,128)}, f32[2,16,16,256]{3,2,1,0:T(8,128)}, f32[2,16,16,256]{3,2,1,0:T(8,128)}, f32[2,8,16,256]{3,2,1,0:T(8,128)S(1)}) custom-call(s32[8]{0:T(128)S(1)} %copy-done.2, f32[4,8,16,256]{3,2,1,0:T(8,128)S(1)} %inner.1.refs_0_.own_inner, f32[4,8,16,256]{3,2,1,0:T(8,128)S(1)} %collective-permute-done.16.refs_1_.other_inner, ...), custom_call_target="tpu_custom_call" | custom-call | tf_op jit(solution)/shard_map/image_inner/pallas_call | solution.py:452
  73.7 3.3 %collective-permute-done.23.refs_1_ = f32[2,8,16,256]{3,2,1,0:T(8,128)S(1)} collective-permute-done((f32[2,8,16,256]{3,2,1,0:T(8,128)S(1)}, f32[2,8,16,256]{3,2,1,0:T(8,128)S(1)}, u32[]{:S(2)}, u32[]{:S(2)}) %collective-permute-start.23) | collective-permute-done | bytes 262176 | tf_op jit(solution)/shard_map/ppermute | solution.py:527
  77.1 0.7 image_outer.1
  (13 shorter events, 0.0 us)
Async XLA Ops:
  0.6 10.4 %copy-start.1 = (f32[8,2,256]{2,1,0:T(2,128)S(1)}, f32[8,2,256]{2,1,0:T(2,128)}, u32[]{:S(2)}) copy-start(f32[8,2,256]{2,1,0:T(2,128)} %traces.1) | copy-start | bytes 49156
  1.9 11.4 %collective-permute-start = (f32[3,4,16,256]{3,2,1,0:T(8,128)S(1)}, f32[3,4,16,256]{3,2,1,0:T(8,128)S(1)}, u32[]{:S(2)}, u32[]{:S(2)}) collective-permute-start(f32[3,4,16,256]{3,2,1,0:T(8,128)S(1)} %get-tuple-element.54), channel_id=1, source_target_pairs={{0,1},{1,0},{2,3},{3,2},{4,5},{5,4},{6,7},{7,6},{8,9},{9,8},{10,11... | collective-permute-start | bytes 589832 | tf_op jit(solution)/shard_map/ppermute | solution.py:60
  5.0 8.3 %collective-permute-start.1 = (f32[3,4,16,256]{3,2,1,0:T(8,128)S(1)}, f32[3,4,16,256]{3,2,1,0:T(8,128)S(1)}, u32[]{:S(2)}, u32[]{:S(2)}) collective-permute-start(f32[3,4,16,256]{3,2,1,0:T(8,128)S(1)} %get-tuple-element.55), channel_id=1, source_target_pairs={{1,2},{2,1},{5,6},{6,5},{9,10},{10,9},{13,14},{14,13},{17,18},{18,... | collective-permute-start | bytes 589832 | tf_op jit(solution)/shard_map/ppermute | solution.py:61
  5.6 5.3 %copy-start.5 = (f32[8,2]{0,1:T(2,128)S(1)}, f32[8,2]{0,1:T(2,128)}, u32[]{:S(2)}) copy-start(f32[8,2]{0,1:T(2,128)} %param.16) | copy-start | bytes 196
  5.7 11.2 %collective-permute-start.8 = (f32[2,4,16,256]{3,2,1,0:T(8,128)S(1)}, f32[2,4,16,256]{3,2,1,0:T(8,128)S(1)}, u32[]{:S(2)}, u32[]{:S(2)}) collective-permute-start(f32[2,4,16,256]{3,2,1,0:T(8,128)S(1)} %get-tuple-element.75), channel_id=1, source_target_pairs={{0,1},{1,0},{2,3},{3,2},{4,5},{5,4},{6,7},{7,6},{8,9},{9,8},{10,11... | collective-permute-start | bytes 393224 | tf_op jit(solution)/shard_map/ppermute | solution.py:60
  10.1 0.9 %copy-start.3 = (s32[2,256]{1,0:T(2,128)S(1)}, s32[2,256]{1,0:T(2,128)}, u32[]{:S(2)}) copy-start(s32[2,256]{1,0:T(2,128)} %receiver_cell.1) | copy-start | bytes 6148
  10.1 0.9 %copy-start.4 = (s32[2]{0:T(128)S(1)}, s32[2]{0:T(128)}, u32[]{:S(2)}) copy-start(s32[2]{0:T(128)} %source_cell.1) | copy-start | bytes 28
  10.1 6.8 %collective-permute-start.9 = (f32[2,4,16,256]{3,2,1,0:T(8,128)S(1)}, f32[2,4,16,256]{3,2,1,0:T(8,128)S(1)}, u32[]{:S(2)}, u32[]{:S(2)}) collective-permute-start(f32[2,4,16,256]{3,2,1,0:T(8,128)S(1)} %get-tuple-element.76), channel_id=1, source_target_pairs={{1,2},{2,1},{5,6},{6,5},{9,10},{10,9},{13,14},{14,13},{17,18},{18,... | collective-permute-start | bytes 393224 | tf_op jit(solution)/shard_map/ppermute | solution.py:61
  11.0 2.2 %copy-start = (f32[16,16,256]{2,1,0:T(8,128)S(1)}, f32[16,16,256]{2,1,0:T(8,128)}, u32[]{:S(2)}) copy-start(f32[16,16,256]{2,1,0:T(8,128)} %courant.3) | copy-start | bytes 786436
  14.0 8.9 %collective-permute-start.2 = (f32[2,8,16,256]{3,2,1,0:T(8,128)S(1)}, f32[2,8,16,256]{3,2,1,0:T(8,128)S(1)}, u32[]{:S(2)}, u32[]{:S(2)}) collective-permute-start(f32[2,8,16,256]{3,2,1,0:T(8,128)S(1)} %get-tuple-element.61), channel_id=1, source_target_pairs={{0,1},{1,0},{2,3},{3,2},{4,5},{5,4},{6,7},{7,6},{8,9},{9,8},{10,11... | collective-permute-start | bytes 786440 | tf_op jit(solution)/shard_map/ppermute | solution.py:60
  16.2 6.8 %collective-permute-start.3 = (f32[2,8,16,256]{3,2,1,0:T(8,128)S(1)}, f32[2,8,16,256]{3,2,1,0:T(8,128)S(1)}, u32[]{:S(2)}, u32[]{:S(2)}) collective-permute-start(f32[2,8,16,256]{3,2,1,0:T(8,128)S(1)} %get-tuple-element.62), channel_id=1, source_target_pairs={{1,2},{2,1},{5,6},{6,5},{9,10},{10,9},{13,14},{14,13},{17,18},{18,... | collective-permute-start | bytes 786440 | tf_op jit(solution)/shard_map/ppermute | solution.py:61
  17.7 11.6 %collective-permute-start.10 = (f32[2,8,16,256]{3,2,1,0:T(8,128)S(1)}, f32[2,8,16,256]{3,2,1,0:T(8,128)S(1)}, u32[]{:S(2)}, u32[]{:S(2)}) collective-permute-start(f32[2,8,16,256]{3,2,1,0:T(8,128)S(1)} %get-tuple-element.80), channel_id=1, source_target_pairs={{0,1},{1,0},{2,3},{3,2},{4,5},{5,4},{6,7},{7,6},{8,9},{9,8},{10,11... | collective-permute-start | bytes 786440 | tf_op jit(solution)/shard_map/ppermute | solution.py:60
  21.4 7.9 %collective-permute-start.11 = (f32[2,8,16,256]{3,2,1,0:T(8,128)S(1)}, f32[2,8,16,256]{3,2,1,0:T(8,128)S(1)}, u32[]{:S(2)}, u32[]{:S(2)}) collective-permute-start(f32[2,8,16,256]{3,2,1,0:T(8,128)S(1)} %get-tuple-element.81), channel_id=1, source_target_pairs={{1,2},{2,1},{5,6},{6,5},{9,10},{10,9},{13,14},{14,13},{17,18},{18,... | collective-permute-start | bytes 786440 | tf_op jit(solution)/shard_map/ppermute | solution.py:61
  24.5 10.8 %collective-permute-start.4 = (f32[2,8,16,256]{3,2,1,0:T(8,128)S(1)}, f32[2,8,16,256]{3,2,1,0:T(8,128)S(1)}, u32[]{:S(2)}, u32[]{:S(2)}) collective-permute-start(f32[2,8,16,256]{3,2,1,0:T(8,128)S(1)} %get-tuple-element.66), channel_id=1, source_target_pairs={{0,1},{1,0},{2,3},{3,2},{4,5},{5,4},{6,7},{7,6},{8,9},{9,8},{10,11... | collective-permute-start | bytes 786440 | tf_op jit(solution)/shard_map/ppermute | solution.py:60
  28.6 6.8 %collective-permute-start.5 = (f32[2,8,16,256]{3,2,1,0:T(8,128)S(1)}, f32[2,8,16,256]{3,2,1,0:T(8,128)S(1)}, u32[]{:S(2)}, u32[]{:S(2)}) collective-permute-start(f32[2,8,16,256]{3,2,1,0:T(8,128)S(1)} %get-tuple-element.67), channel_id=1, source_target_pairs={{1,2},{2,1},{5,6},{6,5},{9,10},{10,9},{13,14},{14,13},{17,18},{18,... | collective-permute-start | bytes 786440 | tf_op jit(solution)/shard_map/ppermute | solution.py:61
  30.9 11.3 %collective-permute-start.12 = (f32[2,8,16,256]{3,2,1,0:T(8,128)S(1)}, f32[2,8,16,256]{3,2,1,0:T(8,128)S(1)}, u32[]{:S(2)}, u32[]{:S(2)}) collective-permute-start(f32[2,8,16,256]{3,2,1,0:T(8,128)S(1)} %get-tuple-element.84), channel_id=1, source_target_pairs={{0,1},{1,0},{2,3},{3,2},{4,5},{5,4},{6,7},{7,6},{8,9},{9,8},{10,11... | collective-permute-start | bytes 786440 | tf_op jit(solution)/shard_map/ppermute | solution.py:60
  34.7 7.5 %collective-permute-start.13 = (f32[2,8,16,256]{3,2,1,0:T(8,128)S(1)}, f32[2,8,16,256]{3,2,1,0:T(8,128)S(1)}, u32[]{:S(2)}, u32[]{:S(2)}) collective-permute-start(f32[2,8,16,256]{3,2,1,0:T(8,128)S(1)} %get-tuple-element.85), channel_id=1, source_target_pairs={{1,2},{2,1},{5,6},{6,5},{9,10},{10,9},{13,14},{14,13},{17,18},{18,... | collective-permute-start | bytes 786440 | tf_op jit(solution)/shard_map/ppermute | solution.py:61
  37.0 11.5 %collective-permute-start.6 = (f32[2,8,16,256]{3,2,1,0:T(8,128)S(1)}, f32[2,8,16,256]{3,2,1,0:T(8,128)S(1)}, u32[]{:S(2)}, u32[]{:S(2)}) collective-permute-start(f32[2,8,16,256]{3,2,1,0:T(8,128)S(1)} %get-tuple-element.70), channel_id=1, source_target_pairs={{0,1},{1,0},{2,3},{3,2},{4,5},{5,4},{6,7},{7,6},{8,9},{9,8},{10,11... | collective-permute-start | bytes 786440 | tf_op jit(solution)/shard_map/ppermute | solution.py:60
  41.5 6.9 %collective-permute-start.7 = (f32[2,8,16,256]{3,2,1,0:T(8,128)S(1)}, f32[2,8,16,256]{3,2,1,0:T(8,128)S(1)}, u32[]{:S(2)}, u32[]{:S(2)}) collective-permute-start(f32[2,8,16,256]{3,2,1,0:T(8,128)S(1)} %get-tuple-element.71), channel_id=1, source_target_pairs={{1,2},{2,1},{5,6},{6,5},{9,10},{10,9},{13,14},{14,13},{17,18},{18,... | collective-permute-start | bytes 786440 | tf_op jit(solution)/shard_map/ppermute | solution.py:61
  43.7 10.8 %collective-permute-start.14 = (f32[2,8,16,256]{3,2,1,0:T(8,128)S(1)}, f32[2,8,16,256]{3,2,1,0:T(8,128)S(1)}, u32[]{:S(2)}, u32[]{:S(2)}) collective-permute-start(f32[2,8,16,256]{3,2,1,0:T(8,128)S(1)} %get-tuple-element.88), channel_id=1, source_target_pairs={{0,1},{1,0},{2,3},{3,2},{4,5},{5,4},{6,7},{7,6},{8,9},{9,8},{10,11... | collective-permute-start | bytes 786440 | tf_op jit(solution)/shard_map/ppermute | solution.py:60
  47.4 7.1 %collective-permute-start.15 = (f32[2,8,16,256]{3,2,1,0:T(8,128)S(1)}, f32[2,8,16,256]{3,2,1,0:T(8,128)S(1)}, u32[]{:S(2)}, u32[]{:S(2)}) collective-permute-start(f32[2,8,16,256]{3,2,1,0:T(8,128)S(1)} %get-tuple-element.89), channel_id=1, source_target_pairs={{1,2},{2,1},{5,6},{6,5},{9,10},{10,9},{13,14},{14,13},{17,18},{18,... | collective-permute-start | bytes 786440 | tf_op jit(solution)/shard_map/ppermute | solution.py:61
  49.9 9.3 %collective-permute-start.17 = (f32[2,4,16,256]{3,2,1,0:T(8,128)S(1)}, f32[2,4,16,256]{3,2,1,0:T(8,128)S(1)}, u32[]{:S(2)}, u32[]{:S(2)}) collective-permute-start(f32[2,4,16,256]{3,2,1,0:T(8,128)S(1)} %get-tuple-element.93), channel_id=1, source_target_pairs={{0,1},{1,0},{2,3},{3,2},{4,5},{5,4},{6,7},{7,6},{8,9},{9,8},{10,11... | collective-permute-start | bytes 393224 | tf_op jit(solution)/shard_map/ppermute | solution.py:60
  53.7 5.6 %collective-permute-start.19 = (f32[2,4,16,256]{3,2,1,0:T(8,128)S(1)}, f32[2,4,16,256]{3,2,1,0:T(8,128)S(1)}, u32[]{:S(2)}, u32[]{:S(2)}) collective-permute-start(f32[2,4,16,256]{3,2,1,0:T(8,128)S(1)} %get-tuple-element.95), channel_id=1, source_target_pairs={{1,2},{2,1},{5,6},{6,5},{9,10},{10,9},{13,14},{14,13},{17,18},{18,... | collective-permute-start | bytes 393224 | tf_op jit(solution)/shard_map/ppermute | solution.py:61
  56.0 5.0 %collective-permute-start.18 = (f32[2,4,16,256]{3,2,1,0:T(8,128)S(1)}, f32[2,4,16,256]{3,2,1,0:T(8,128)S(1)}, u32[]{:S(2)}, u32[]{:S(2)}) collective-permute-start(f32[2,4,16,256]{3,2,1,0:T(8,128)S(1)} %get-tuple-element.94), channel_id=1, source_target_pairs={{0,1},{1,0},{2,3},{3,2},{4,5},{5,4},{6,7},{7,6},{8,9},{9,8},{10,11... | collective-permute-start | bytes 393224 | tf_op jit(solution)/shard_map/ppermute | solution.py:60
  57.9 3.2 %collective-permute-start.20 = (f32[2,4,16,256]{3,2,1,0:T(8,128)S(1)}, f32[2,4,16,256]{3,2,1,0:T(8,128)S(1)}, u32[]{:S(2)}, u32[]{:S(2)}) collective-permute-start(f32[2,4,16,256]{3,2,1,0:T(8,128)S(1)} %get-tuple-element.96), channel_id=1, source_target_pairs={{1,2},{2,1},{5,6},{6,5},{9,10},{10,9},{13,14},{14,13},{17,18},{18,... | collective-permute-start | bytes 393224 | tf_op jit(solution)/shard_map/ppermute | solution.py:61
  59.2 2.8 %copy-start.2 = (s32[8]{0:T(128)S(1)}, s32[8]{0:T(128)}, u32[]{:S(2)}) copy-start(s32[8]{0:T(128)} %offset_perm.5) | copy-start | bytes 100
  59.2 2.7 %collective-permute-start.16 = (f32[4,8,16,256]{3,2,1,0:T(8,128)S(1)}, f32[4,8,16,256]{3,2,1,0:T(8,128)S(1)}, u32[]{:S(2)}, u32[]{:S(2)}) collective-permute-start(f32[4,8,16,256]{3,2,1,0:T(8,128)S(1)} %inner.1.refs_0_.own_inner), channel_id=1, source_target_pairs={{0,4},{4,0},{8,12},{12,8},{1,5},{5,1},{9,13},{13,9},{2,6},{6,2},{1... | collective-permute-start | bytes 1572872 | tf_op jit(solution)/shard_map/ppermute | solution.py:531
  61.8 2.5 %collective-permute-start.21 = (f32[4,8,16,256]{3,2,1,0:T(8,128)S(1)}, f32[4,8,16,256]{3,2,1,0:T(8,128)S(1)}, u32[]{:S(2)}, u32[]{:S(2)}) collective-permute-start(f32[4,8,16,256]{3,2,1,0:T(8,128)S(1)} %outer.1.own_outer.refs_0_), channel_id=1, source_target_pairs={{0,4},{4,0},{8,12},{12,8},{1,5},{5,1},{9,13},{13,9},{2,6},{6,2},{1... | collective-permute-start | bytes 1572872 | tf_op jit(solution)/shard_map/ppermute | solution.py:534
  62.8 9.2 %collective-permute-start.22 = (f32[2,8,16,256]{3,2,1,0:T(8,128)S(1)}, f32[2,8,16,256]{3,2,1,0:T(8,128)S(1)}, u32[]{:S(2)}, u32[]{:S(2)}) collective-permute-start(f32[2,8,16,256]{3,2,1,0:T(8,128)S(1)} %shard_map.129), channel_id=1, source_target_pairs={{0,8},{4,12},{8,0},{12,4},{1,9},{5,13},{9,1},{13,5},{2,10},{6,14},... | collective-permute-start | bytes 786440 | tf_op jit(solution)/shard_map/ppermute | solution.py:527
  65.2 11.9 %collective-permute-start.23 = (f32[2,8,16,256]{3,2,1,0:T(8,128)S(1)}, f32[2,8,16,256]{3,2,1,0:T(8,128)S(1)}, u32[]{:S(2)}, u32[]{:S(2)}) collective-permute-start(f32[2,8,16,256]{3,2,1,0:T(8,128)S(1)} %shard_map.130), channel_id=1, source_target_pairs={{0,8},{4,12},{8,0},{12,4},{1,9},{5,13},{9,1},{13,5},{2,10},{6,14},... | collective-permute-start | bytes 786440 | tf_op jit(solution)/shard_map/ppermute | solution.py:527

commit v5 on v4

--- a/solution.py
+++ b/solution.py
@@ -119,19 +119,26 @@
     return value
 
 
-def prepare_kernel(groups, rows, source_cell, wavelet, receiver_cell, traces, source, receiver, source_before, receiver_before, along_z, along_y, *refs):
-    planes, now, before, sem = refs[:groups], refs[groups : 2 * groups], refs[2 * groups : 3 * groups], refs[-1]
-    copies = []
-    for group in range(groups):
-        pieces = ((source, now, 0), (receiver, now, 1), (source_before, before, 0), (receiver_before, before, 1))
-        for array, place, kind in pieces:
-            copies.append(pltpu.make_async_copy(array.at[group], place[group].at[kind], sem.at[len(copies)]))
+def fetch(pieces, sem):
+    copies = [pltpu.make_async_copy(array, place, sem.at[index]) for index, (array, place) in enumerate(pieces)]
     for copy in copies:
         copy.start()
+    return copies
+
+
+def prepare_kernel(groups, rows, source_cell, wavelet, offset_perm, receiver_cell, traces, source, receiver, source_before, receiver_before, along_z, along_y, lags, *refs):
+    planes, now, before, sem = refs[:groups], refs[groups : 2 * groups], refs[2 * groups : 3 * groups], refs[-1]
+    pieces = []
+    for group in range(groups):
+        pieces += [(source.at[group], now[group].at[0]), (receiver.at[group], now[group].at[1])]
+        pieces += [(source_before.at[group], before[group].at[0]), (receiver_before.at[group], before[group].at[1])]
+    copies = fetch(pieces, sem)
     _, plane_count, size_y, _ = planes[0].shape
     steps = traces.shape[0]
     size_z = along_z.shape[0]
     block = along_y.shape[0]
+    for slot in range(offset_perm.shape[0]):
+        lags[slot : slot + 1, :] = jnp.full((1, LANES), offset_perm[slot], jnp.int32)
     row = lax.broadcasted_iota(jnp.int32, (size_z, size_z), 0)
     col = lax.broadcasted_iota(jnp.int32, (size_z, size_z), 1)
     along_z[...] = band(jnp.abs(row - col)).astype(jnp.bfloat16)
@@ -155,38 +162,44 @@
         count = receiver_cell.shape[1]
         wide = first + lax.broadcasted_iota(jnp.int32, (cells, count), 0)
         here = jnp.broadcast_to(receiver_cell[group : group + 1, :], (cells, count))
-        hot = (wide == here).astype(jnp.float32)
-        data = traces[:, group, :]
-        data = jnp.concatenate([data, jnp.zeros((LANES - steps, count), jnp.float32)], axis=0)
+        hot = (wide == here).astype(jnp.float32).astype(jnp.bfloat16)
+        left, terms = traces[:, group, :], []
+        for _ in range(3):
+            term = left.astype(jnp.bfloat16).astype(jnp.float32)
+            terms.append(term)
+            left = left - term
+        terms.append(jnp.zeros((LANES - 3 * steps, count), jnp.float32))
         summed = lax.dot_general(
             hot,
-            data,
+            jnp.concatenate(terms, axis=0).astype(jnp.bfloat16),
             (((1,), (1,)), ((), ())),
-            precision=lax.Precision.HIGHEST,
             preferred_element_type=jnp.float32,
         )
+        summed = summed + pltpu.roll(summed, LANES - steps, 1) + pltpu.roll(summed, LANES - 2 * steps, 1)
         planes[group][1] = summed.reshape(plane_count, size_y, LANES)
     for copy in copies:
         copy.wait()
 
 
-def prepare(source_cell, wavelet, receiver_cell, traces, fields):
+def prepare(source_cell, wavelet, offset_perm, receiver_cell, traces, fields):
     groups, rows, size_y, size_z = fields[0].shape
     block = CHUNK * size_y
+    field = struct((2, rows, size_y, size_z))
+    shapes = [
+        struct((size_z, size_z), jnp.bfloat16),
+        struct((block, 2 * block), jnp.bfloat16),
+        struct((offset_perm.shape[0], LANES), jnp.int32),
+    ]
+    shapes += [struct((2, rows + 2 * REACH, size_y, LANES))] * groups + [field] * (2 * groups)
     return pl.pallas_call(
         functools.partial(prepare_kernel, groups, rows),
-        out_shape=[
-            struct((size_z, size_z), jnp.bfloat16),
-            struct((block, 2 * block), jnp.bfloat16),
-        ]
-        + [struct((2, rows + 2 * REACH, size_y, LANES))] * groups
-        + [struct((2, rows, size_y, size_z))] * (2 * groups),
-        in_specs=[smem(), smem(), vmem(), vmem()] + [hbm()] * 4,
-        out_specs=[vmem()] * (2 + 3 * groups),
+        out_shape=shapes,
+        in_specs=[smem()] * 3 + [vmem()] * 2 + [hbm()] * 4,
+        out_specs=[vmem()] * len(shapes),
         scratch_shapes=[pltpu.SemaphoreType.DMA((4 * groups,))],
         compiler_params=params(),
         name="prepare",
-    )(source_cell, wavelet, receiver_cell, traces, *stay(*fields))
+    )(source_cell, wavelet, offset_perm, receiver_cell, traces, *stay(*fields))
 
 
 def advance(now, at, before, before_at, courant, courant_at, inject, inject_at, runs, step, along_z, along_y, write):
@@ -216,9 +229,9 @@
     return [[(at, CHUNK)] for at in range(start, stop, CHUNK)]
 
 
-def first_kernel(rows, has_courant, width, now, before, courant, even, odd, inject, along_z, along_y, fresh, held, even_edge, odd_edge, *scaled):
+def first_kernel(rows, width, now, before, courant, even, odd, inject, along_z, along_y, fresh, held, even_edge, odd_edge, *scaled):
     even_at, odd_at = halo_starts(rows, REACH)
-    if has_courant:
+    if scaled:
         (courant_out,) = scaled
         courant_out[REACH : REACH + rows] = SCALE * courant[...]
         courant_out[pl.ds(even_at, REACH)] = SCALE * even[2]
@@ -247,13 +260,12 @@
 
 def first_round(group, width, now, before, courant, halos, inject, along_z, along_y):
     rows, size_y, size_z = now.shape[1:]
-    has_courant = group == 0
     edge = struct((2, width, size_y, size_z))
     shapes = [struct(now.shape), struct((2, rows + 2 * REACH, size_y, size_z)), edge, edge]
-    if has_courant:
+    if group == 0:
         shapes.append(struct((rows + 2 * REACH, size_y, size_z)))
     return pl.pallas_call(
-        functools.partial(first_kernel, rows, has_courant, width),
+        functools.partial(first_kernel, rows, width),
         out_shape=shapes,
         in_specs=[vmem()] * 8,
         out_specs=[vmem()] * len(shapes),
@@ -299,66 +311,56 @@
     )(now, before, *halos, courant, inject, along_z, along_y)
 
 
-def inner_kernel(groups, rows, step, *refs):
-    now, before, inject = refs[:groups], refs[groups : 2 * groups], refs[2 * groups : 3 * groups]
-    courant, along_z, along_y, final = refs[3 * groups :]
+def inner_kernel(group, rows, step, now, before, courant, inject, along_z, along_y, *refs):
+    final = refs[-1]
     z_band, y_band = along_z[...], along_y[...]
-    for group in range(groups):
-        for kind in range(2):
-
-            def write(i, plane, new, place=2 * group + kind):
-                final[place, plane - REACH] = new
-
-            for runs in chunks(REACH, rows - REACH):
-                advance(now[group].at[kind], 0, before[group].at[kind], REACH, courant, REACH, inject[group].at[kind], REACH, runs, step, z_band, y_band, write)
-
-
-def inner_round(step, now, before, courant, inject, along_z, along_y):
-    groups = len(now)
-    rows, size_y, size_z = now[0].shape[1:]
-    return pl.pallas_call(
-        functools.partial(inner_kernel, groups, rows, step),
+    for kind in range(2):
+
+        def write(i, plane, new, place=2 * group + kind):
+            final[place, plane - REACH] = new
+
+        for runs in chunks(REACH, rows - REACH):
+            advance(now.at[kind], 0, before.at[kind], REACH, courant, REACH, inject.at[kind], REACH, runs, step, z_band, y_band, write)
+
+
+def inner_round(group, groups, step, now, before, courant, inject, along_z, along_y, final):
+    rows, size_y, size_z = now.shape[1:]
+    return pl.pallas_call(
+        functools.partial(inner_kernel, group, rows, step),
         out_shape=struct((2 * groups, rows - 2 * REACH, size_y, size_z)),
-        in_specs=[vmem()] * (3 * groups + 3),
+        in_specs=[vmem()] * (6 + len(final)),
         out_specs=vmem(),
-        compiler_params=params(),
-        name="inner",
-    )(*now, *before, *inject, courant, along_z, along_y)
-
-
-def outer_kernel(groups, rows, step, *refs):
-    now, before, inject = refs[:groups], refs[groups : 2 * groups], refs[2 * groups : 3 * groups]
-    even, odd = refs[3 * groups : 4 * groups], refs[4 * groups : 5 * groups]
-    courant, along_z, along_y, final, wide = refs[5 * groups :]
+        input_output_aliases={6: 0} if final else {},
+        compiler_params=params(),
+    )(now, before, courant, inject, along_z, along_y, *final)
+
+
+def outer_kernel(rows, step, now, before, even, odd, courant, inject, along_z, along_y, final, wide):
     even_at, odd_at = halo_starts(rows, REACH)
     z_band, y_band = along_z[...], along_y[...]
-    for group in range(groups):
-        for kind in range(2):
-            field = wide.at[2 * group + kind]
-            field[REACH : REACH + rows] = now[group][kind]
-            field[pl.ds(even_at, REACH)] = even[group][kind]
-            field[pl.ds(odd_at, REACH)] = odd[group][kind]
-
-            def write(i, plane, new, place=2 * group + kind):
-                final[place, i] = new
-
-            runs = [(0, REACH), (rows - REACH, REACH)]
-            advance(field, REACH, before[group].at[kind], REACH, courant, REACH, inject[group].at[kind], REACH, runs, step, z_band, y_band, write)
+    for kind in range(2):
+        field = wide.at[kind]
+        field[REACH : REACH + rows] = now[kind]
+        field[pl.ds(even_at, REACH)] = even[kind]
+        field[pl.ds(odd_at, REACH)] = odd[kind]
+
+        def write(i, plane, new, kind=kind):
+            final[kind, i] = new
+
+        runs = [(0, REACH), (rows - REACH, REACH)]
+        advance(field, REACH, before.at[kind], REACH, courant, REACH, inject.at[kind], REACH, runs, step, z_band, y_band, write)
 
 
 def outer_round(step, now, before, halos, courant, inject, along_z, along_y):
-    groups = len(now)
-    rows, size_y, size_z = now[0].shape[1:]
-    even, odd = zip(*halos)
-    return pl.pallas_call(
-        functools.partial(outer_kernel, groups, rows, step),
-        out_shape=struct((2 * groups, 2 * REACH, size_y, size_z)),
-        in_specs=[vmem()] * (5 * groups + 3),
+    rows, size_y, size_z = now.shape[1:]
+    return pl.pallas_call(
+        functools.partial(outer_kernel, rows, step),
+        out_shape=struct((2, 2 * REACH, size_y, size_z)),
+        in_specs=[vmem()] * 8,
         out_specs=vmem(),
-        scratch_shapes=[pltpu.VMEM((2 * groups, rows + 2 * REACH, size_y, size_z), jnp.float32)],
-        compiler_params=params(),
-        name="outer",
-    )(*now, *before, *inject, *even, *odd, courant, along_z, along_y)
+        scratch_shapes=[pltpu.VMEM((2, rows + 2 * REACH, size_y, size_z), jnp.float32)],
+        compiler_params=params(),
+    )(now, before, *halos, courant, inject, along_z, along_y)
 
 
 def shifted(plane, amount):
@@ -372,8 +374,8 @@
     return jnp.where(inside, pltpu.roll(plane, amount % size_y, 0), 0.0)
 
 
-def partial_image(ahead, offset_perm, fields, image, others=()):
-    count = offset_perm.shape[0]
+def partial_image(ahead, lags, fields, image, others=()):
+    count = lags.shape[0]
     half_span = count // 2
     slots, rows = image.shape[:2]
     here = lax.axis_index("shot")
@@ -381,7 +383,7 @@
     owner = 2 * lax.rem(lax.div(here, 2) + ahead, pairs) + lax.rem(here, 2)
 
     def one_slot(slot, carry):
-        index = offset_perm[owner * slots + slot]
+        index = jnp.max(lags[pl.ds(owner * slots + slot, 1), :])
         for lag_index in range(count):
             lag = lag_index - half_span
 
@@ -406,58 +408,56 @@
     lax.fori_loop(0, slots, one_slot, 0)
 
 
-def image_kernel(ahead, offset_perm, *refs):
-    partial_image(ahead, offset_perm, refs[:-1], refs[-1])
-
-
-def image_part(ahead, slots, offset_perm, fields):
+def image_kernel(ahead, lags, *refs):
+    partial_image(ahead, lags, refs[:-1], refs[-1])
+
+
+def image_part(ahead, slots, lags, fields):
     _, rows, size_y, size_z = fields[0].shape
     return pl.pallas_call(
         functools.partial(image_kernel, ahead),
         out_shape=struct((slots, rows, size_y, size_z)),
-        in_specs=[smem()] + [vmem()] * len(fields),
+        in_specs=[vmem()] * (1 + len(fields)),
         out_specs=vmem(),
         compiler_params=params(),
-    )(offset_perm, *fields)
-
-
-def inner_image_kernel(offset_perm, own_inner, other_inner, own_outer, other_outer, *refs):
-    others = refs[:-6]
+    )(lags, *fields)
+
+
+def inner_image_kernel(groups, rows, lags, *refs):
+    inner_fields, outer_fields, others = refs[:2], refs[2 : 2 + 2 * groups], refs[2 + 2 * groups : -6]
     image, source_out, receiver_out, outer, inner, sem = refs[-6:]
-    groups, rows = source_out.shape[:2]
     copies = []
     for group in range(groups):
         for kind, out in enumerate((source_out, receiver_out)):
-            place = 2 * group + kind
             pieces = (
-                (own_inner.at[place], REACH, rows - 2 * REACH),
-                (own_outer.at[place, pl.ds(0, REACH)], 0, REACH),
-                (own_outer.at[place, pl.ds(REACH, REACH)], rows - REACH, REACH),
+                (inner_fields[0].at[2 * group + kind], REACH, rows - 2 * REACH),
+                (outer_fields[group].at[kind, pl.ds(0, REACH)], 0, REACH),
+                (outer_fields[group].at[kind, pl.ds(REACH, REACH)], rows - REACH, REACH),
             )
             for piece, first, count in pieces:
                 copies.append(pltpu.make_async_copy(piece, out.at[group, pl.ds(first, count)], sem.at[len(copies)]))
                 copies[-1].start()
-    partial_image(0, offset_perm, (own_inner, other_inner), inner, others)
+    partial_image(0, lags, inner_fields, inner, others)
     copies.append(pltpu.make_async_copy(inner, image.at[:, pl.ds(REACH, rows - 2 * REACH)], sem.at[len(copies)]))
     copies[-1].start()
-    partial_image(0, offset_perm, (own_outer, other_outer), outer)
+    partial_image(0, lags, outer_fields, outer)
     for copy in copies:
         copy.wait()
 
 
-def inner_image(slots, inner, outer, others, offset_perm):
+def inner_image(slots, inner, outer, others, lags):
     places, inner_rows, size_y, size_z = inner[0].shape
-    rows = inner_rows + 2 * REACH
-    whole = struct((places // 2, rows, size_y, size_z))
-    return pl.pallas_call(
-        inner_image_kernel,
+    groups, rows = places // 2, inner_rows + 2 * REACH
+    whole = struct((groups, rows, size_y, size_z))
+    return pl.pallas_call(
+        functools.partial(inner_image_kernel, groups, rows),
         out_shape=[struct((slots, rows, size_y, size_z)), whole, whole, struct((slots, 2 * REACH, size_y, size_z))],
-        in_specs=[smem()] + [vmem()] * (4 + len(others)),
+        in_specs=[vmem()] * (1 + len(inner) + len(outer) + len(others)),
         out_specs=[hbm()] * 3 + [vmem()],
         scratch_shapes=[pltpu.VMEM((slots, inner_rows, size_y, size_z), jnp.float32), pltpu.SemaphoreType.DMA((3 * places + 1,))],
         compiler_params=params(),
         name="image_inner",
-    )(offset_perm, *inner, *outer, *others)
+    )(lags, *inner, *outer, *others)
 
 
 def outer_image_kernel(rows, *refs):
@@ -499,7 +499,7 @@
     edges = pack(source_now, receiver_now, courant_sq)
     given = [trade(edges[2 * g], edges[2 * g + 1]) for g in everyone]
     fields = (source_now, receiver_now, source_prev, receiver_prev)
-    along_z, along_y, *rest = prepare(source_cell, wavelet, receiver_cell, traces, fields)
+    along_z, along_y, lags, *rest = prepare(source_cell, wavelet, offset_perm, receiver_cell, traces, fields)
     inject, now, before = rest[:groups], rest[groups : 2 * groups], rest[2 * groups :]
 
     halos = [None] * groups
@@ -510,31 +510,39 @@
         if g == 0:
             courant = result[4]
         halos[g] = trade(*result[2:4])
+    final = ()
     for step in range(1, steps - 1, 2):
         last = step + 2 >= steps - 1
         for g in everyone:
             now[g], before[g], even, odd = pair_round(step, REACH if last else 2 * REACH, now[g], before[g], halos[g], courant, inject[g], along_z, along_y)
             halos[g] = trade(even, odd)
+            if last:
+                final = (inner_round(g, groups, steps - 1, now[g], before[g], courant, inject[g], along_z, along_y, final),)
 
     swap = [(i, i ^ 1) for i in range(shot_devices)]
     pairs = shot_devices // 2
 
+    def traded(own):
+        return lax.ppermute(own, "shot", swap)
+
     def part_sums(fields):
-        parts = [image_part(ahead, slots, offset_perm, fields) for ahead in range(1, pairs)]
+        parts = [image_part(ahead, slots, lags, fields) for ahead in range(1, pairs)]
         sums = []
         for ahead, part in enumerate(parts, 1):
             route = [(2 * p + c, 2 * ((p + ahead) % pairs) + c) for p in range(pairs) for c in range(2)]
             sums.append(lax.ppermute(part, "shot", route))
         return sums
 
-    own = inner_round(steps - 1, now, before, courant, inject, along_z, along_y)
-    inner = (own, lax.ppermute(own, "shot", swap))
+    inner = (*final, traded(*final))
     inner_sums = part_sums(inner)
-    own = outer_round(steps - 1, now, before, halos, courant, inject, along_z, along_y)
-    outer = (own, lax.ppermute(own, "shot", swap))
+    own, other = [], []
+    for g in everyone:
+        own.append(outer_round(steps - 1, now[g], before[g], halos[g], courant, inject[g], along_z, along_y))
+        other.append(traded(own[g]))
+    outer = (*own, *other)
     outer_sums = part_sums(outer)
-    image, source_final, receiver_final, own = inner_image(slots, inner, outer, inner_sums, offset_perm)
-    image = outer_image(image, own, outer_sums)
+    image, source_final, receiver_final, part = inner_image(slots, inner, outer, inner_sums, lags)
+    image = outer_image(image, part, outer_sums)
     return image, source_final, receiver_final
 
 

time: 79.3 us -> 82.5 us (1.040)
  waiting for transfers between devices: 12.2 us -> 15 us
  starting transfers between devices: 44.7 us -> 45.8 us
    ppermute x10, waiting for transfers between devices: 3.05 us -> 5.27 us  [trade(): even = lax.ppermute(even_edge, 'slab', even_pairs(count))]
    ppermute x10, starting transfers between devices: 35.1 us -> 36.4 us  [trade(): even = lax.ppermute(even_edge, 'slab', even_pairs(count))]
    pallas_call x5 -> x7, Pallas kernels: 4.62 us -> 4.7 us  [the longest x2 1.54 us: first_round(): pl.pallas_call(functools.partial(first_kernel, rows, width), out_shape=sh...]
  transfers between devices with their start and end apart: 24 -> 25, of which waited for: 5 -> 6; matrix products, arithmetic and copies ran while one was open for 0% -> 0% of each run, Pallas kernels for 23% -> 19%
where the time goes in v5:
time: 82.5 us; the launch traced here: 81.4 us
  starting transfers between devices  45.8 us (56%)
  Pallas kernels  19.3 us (23%)
  waiting for transfers between devices  15 us (18%)
  between operations  1.14 us (1%)
    ppermute x10, starting transfers between devices, trade(): even = lax.ppermute(even_edge, 'slab', even_pairs(count))  36.4 us
    ppermute x2, waiting for transfers between devices, part_sums(): sums.append(lax.ppermute(part, 'shot', route))  9.71 us
    pallas_call x6, Pallas kernels, pair_round(): pl.pallas_call(functools.partial(pair_kernel, rows, step, width), out_sha...  8.84 us
    ppermute x10, starting transfers between devices, trade(): odd = lax.ppermute(odd_edge, 'slab', odd_pairs(count))  6.94 us
    ppermute x10, waiting for transfers between devices, trade(): even = lax.ppermute(even_edge, 'slab', even_pairs(count))  5.27 us
    pallas_call x1, Pallas kernels, prepare(): pl.pallas_call(functools.partial(prepare_kernel, groups, rows), out_shape...  2.43 us
    ppermute x2, starting transfers between devices, part_sums(): sums.append(lax.ppermute(part, 'shot', route))  2.34 us
  transfers between devices with their start and end apart: 25, of which 6 were waited for; matrix products, arithmetic and copies ran while one was open for 0% of the time, Pallas kernels for 19%

profile of v5, /device:TPU:0, one launch (start us, length us, event | category | flops | bytes accessed | tf_op | source)
XLA Modules:
  0.0 81.4 jit_solution(4481624353889495788)
XLA Ops:
  0.6 1.2 %pack.1 = (f32[3,4,16,256]{3,2,1,0:T(8,128)S(1)}, f32[3,4,16,256]{3,2,1,0:T(8,128)S(1)}, f32[2,4,16,256]{3,2,1,0:T(8,128)S(1)}, f32[2,4,16,256]{3,2,1,0:T(8,128)S(1)}) custom-call(f32[2,16,16,256]{3,2,1,0:T(8,128)} %source.3, f32[2,16,16,256]{3,2,1,0:T(8,128)} %receiver.3, f32[16,16,256]{2,1,0:T(8,128)} %courant.3), custom_call_target="tpu_custom_call" | custom-call | tf_op jit(solution)/shard_map/pack/pallas_call | solution.py:104
  1.9 3.1 %collective-permute-start = (f32[3,4,16,256]{3,2,1,0:T(8,128)S(1)}, f32[3,4,16,256]{3,2,1,0:T(8,128)S(1)}, u32[]{:S(2)}, u32[]{:S(2)}) collective-permute-start(f32[3,4,16,256]{3,2,1,0:T(8,128)S(1)} %get-tuple-element.58), channel_id=1, source_target_pairs={{0,1},{1,0},{2,3},{3,2},{4,5},{5,4},{6,7},{7,6},{8,9},{9,8},{10,11... | collective-permute-start | bytes 589832 | tf_op jit(solution)/shard_map/ppermute | solution.py:60
  5.0 0.7 collective-permute-start.1
  5.6 0.0 copy-start.5
  5.7 4.5 %collective-permute-start.2 = (f32[2,4,16,256]{3,2,1,0:T(8,128)S(1)}, f32[2,4,16,256]{3,2,1,0:T(8,128)S(1)}, u32[]{:S(2)}, u32[]{:S(2)}) collective-permute-start(f32[2,4,16,256]{3,2,1,0:T(8,128)S(1)} %get-tuple-element.64), channel_id=1, source_target_pairs={{0,1},{1,0},{2,3},{3,2},{4,5},{5,4},{6,7},{7,6},{8,9},{9,8},{10,11... | collective-permute-start | bytes 393224 | tf_op jit(solution)/shard_map/ppermute | solution.py:60
  10.1 0.8 collective-permute-start.3
  10.9 0.1 copy.15.wavelet
  11.0 0.0 copy-start
  11.0 2.4 %prepare.1 = (bf16[256,256]{1,0:T(8,128)(2,1)S(1)}, bf16[128,256]{1,0:T(8,128)(2,1)S(1)}, s32[8,128]{1,0:T(8,128)S(1)}, f32[2,24,16,128]{3,2,1,0:T(8,128)S(1)}, ...) custom-call(s32[2]{0:T(128)S(1)} %copy-done.3, ...), custom_call_target="tpu_custom_call" | custom-call | tf_op jit(solution)/shard_map/prepare/pallas_call | solution.py:194
  13.5 0.0 collective-permute-done.even
  13.5 0.0 collective-permute-done.1.odd
  13.5 0.8 shard_map.121
  14.3 1.9 %collective-permute-start.10 = (f32[2,8,16,256]{3,2,1,0:T(8,128)S(1)}, f32[2,8,16,256]{3,2,1,0:T(8,128)S(1)}, u32[]{:S(2)}, u32[]{:S(2)}) collective-permute-start(f32[2,8,16,256]{3,2,1,0:T(8,128)S(1)} %get-tuple-element.83), channel_id=1, source_target_pairs={{0,1},{1,0},{2,3},{3,2},{4,5},{5,4},{6,7},{7,6},{8,9},{9,8},{10,11... | collective-permute-start | bytes 786440 | tf_op jit(solution)/shard_map/ppermute | solution.py:60
  16.1 0.7 collective-permute-start.11
  16.8 0.0 collective-permute-done.2.even
  16.8 0.0 collective-permute-done.3.odd
  16.8 0.8 shard_map.122
  17.6 3.8 %collective-permute-start.4 = (f32[2,8,16,256]{3,2,1,0:T(8,128)S(1)}, f32[2,8,16,256]{3,2,1,0:T(8,128)S(1)}, u32[]{:S(2)}, u32[]{:S(2)}) collective-permute-start(f32[2,8,16,256]{3,2,1,0:T(8,128)S(1)} %get-tuple-element.69), channel_id=1, source_target_pairs={{0,1},{1,0},{2,3},{3,2},{4,5},{5,4},{6,7},{7,6},{8,9},{9,8},{10,11... | collective-permute-start | bytes 786440 | tf_op jit(solution)/shard_map/ppermute | solution.py:60
  21.4 0.7 collective-permute-start.5
  22.1 1.0 %collective-permute-done.10.even = f32[2,8,16,256]{3,2,1,0:T(8,128)S(1)} collective-permute-done((f32[2,8,16,256]{3,2,1,0:T(8,128)S(1)}, f32[2,8,16,256]{3,2,1,0:T(8,128)S(1)}, u32[]{:S(2)}, u32[]{:S(2)}) %collective-permute-start.10) | collective-permute-done | bytes 262176 | tf_op jit(solution)/shard_map/ppermute | solution.py:60
  23.1 0.0 collective-permute-done.11.odd
  23.1 1.5 %shard_map.126 = (f32[2,16,16,256]{3,2,1,0:T(8,128)S(1)}, f32[2,24,16,256]{3,2,1,0:T(8,128)S(1)}, f32[2,8,16,256]{3,2,1,0:T(8,128)S(1)}, f32[2,8,16,256]{3,2,1,0:T(8,128)S(1)}) custom-call(f32[2,16,16,256]{3,2,1,0:T(8,128)S(1)} %get-tuple-element.81.now, f32[2,24,16,256]{3,2,1,0:T(8,128)S(1)} %get-tuple-element.82.before, ...), custom_call_target="tpu_custom_call" | custom-call | tf_op jit(solution)/shard_map/pallas_call | solution.py:304
  24.6 4.2 %collective-permute-start.12 = (f32[2,8,16,256]{3,2,1,0:T(8,128)S(1)}, f32[2,8,16,256]{3,2,1,0:T(8,128)S(1)}, u32[]{:S(2)}, u32[]{:S(2)}) collective-permute-start(f32[2,8,16,256]{3,2,1,0:T(8,128)S(1)} %get-tuple-element.87), channel_id=1, source_target_pairs={{0,1},{1,0},{2,3},{3,2},{4,5},{5,4},{6,7},{7,6},{8,9},{9,8},{10,11... | collective-permute-start | bytes 786440 | tf_op jit(solution)/shard_map/ppermute | solution.py:60
  28.8 0.7 collective-permute-start.13
  29.5 0.0 collective-permute-done.5.odd
  29.5 1.5 %shard_map.123 = (f32[2,16,16,256]{3,2,1,0:T(8,128)S(1)}, f32[2,24,16,256]{3,2,1,0:T(8,128)S(1)}, f32[2,8,16,256]{3,2,1,0:T(8,128)S(1)}, f32[2,8,16,256]{3,2,1,0:T(8,128)S(1)}) custom-call(f32[2,16,16,256]{3,2,1,0:T(8,128)S(1)} %get-tuple-element.67.now, f32[2,24,16,256]{3,2,1,0:T(8,128)S(1)} %get-tuple-element.68.before, ...), custom_call_target="tpu_custom_call" | custom-call | tf_op jit(solution)/shard_map/pallas_call | solution.py:304
  31.0 3.8 %collective-permute-start.6 = (f32[2,8,16,256]{3,2,1,0:T(8,128)S(1)}, f32[2,8,16,256]{3,2,1,0:T(8,128)S(1)}, u32[]{:S(2)}, u32[]{:S(2)}) collective-permute-start(f32[2,8,16,256]{3,2,1,0:T(8,128)S(1)} %get-tuple-element.73), channel_id=1, source_target_pairs={{0,1},{1,0},{2,3},{3,2},{4,5},{5,4},{6,7},{7,6},{8,9},{9,8},{10,11... | collective-permute-start | bytes 786440 | tf_op jit(solution)/shard_map/ppermute | solution.py:60
  34.8 0.7 collective-permute-start.7
  35.4 0.0 collective-permute-done.12.even
  35.5 0.0 collective-permute-done.13.odd
  35.5 1.5 %shard_map.127 = (f32[2,16,16,256]{3,2,1,0:T(8,128)S(1)}, f32[2,24,16,256]{3,2,1,0:T(8,128)S(1)}, f32[2,8,16,256]{3,2,1,0:T(8,128)S(1)}, f32[2,8,16,256]{3,2,1,0:T(8,128)S(1)}) custom-call(f32[2,16,16,256]{3,2,1,0:T(8,128)S(1)} %get-tuple-element.85.now, f32[2,24,16,256]{3,2,1,0:T(8,128)S(1)} %get-tuple-element.86.before, ...), custom_call_target="tpu_custom_call" | custom-call | tf_op jit(solution)/shard_map/pallas_call | solution.py:304
  37.0 4.3 %collective-permute-start.14 = (f32[2,8,16,256]{3,2,1,0:T(8,128)S(1)}, f32[2,8,16,256]{3,2,1,0:T(8,128)S(1)}, u32[]{:S(2)}, u32[]{:S(2)}) collective-permute-start(f32[2,8,16,256]{3,2,1,0:T(8,128)S(1)} %get-tuple-element.91), channel_id=1, source_target_pairs={{0,1},{1,0},{2,3},{3,2},{4,5},{5,4},{6,7},{7,6},{8,9},{9,8},{10,11... | collective-permute-start | bytes 786440 | tf_op jit(solution)/shard_map/ppermute | solution.py:60
  41.3 0.7 collective-permute-start.15
  42.0 0.0 collective-permute-done.6.even
  42.0 1.5 %shard_map.124 = (f32[2,16,16,256]{3,2,1,0:T(8,128)S(1)}, f32[2,24,16,256]{3,2,1,0:T(8,128)S(1)}, f32[2,8,16,256]{3,2,1,0:T(8,128)S(1)}, f32[2,8,16,256]{3,2,1,0:T(8,128)S(1)}) custom-call(f32[2,16,16,256]{3,2,1,0:T(8,128)S(1)} %get-tuple-element.71.now, f32[2,24,16,256]{3,2,1,0:T(8,128)S(1)} %get-tuple-element.72.before, ...), custom_call_target="tpu_custom_call" | custom-call | tf_op jit(solution)/shard_map/pallas_call | solution.py:304
  43.5 3.9 %collective-permute-start.8 = (f32[2,8,16,256]{3,2,1,0:T(8,128)S(1)}, f32[2,8,16,256]{3,2,1,0:T(8,128)S(1)}, u32[]{:S(2)}, u32[]{:S(2)}) collective-permute-start(f32[2,8,16,256]{3,2,1,0:T(8,128)S(1)} %get-tuple-element.77), channel_id=1, source_target_pairs={{0,1},{1,0},{2,3},{3,2},{4,5},{5,4},{6,7},{7,6},{8,9},{9,8},{10,11... | collective-permute-start | bytes 786440 | tf_op jit(solution)/shard_map/ppermute | solution.py:60
  47.4 0.8 %collective-permute-start.9 = (f32[2,8,16,256]{3,2,1,0:T(8,128)S(1)}, f32[2,8,16,256]{3,2,1,0:T(8,128)S(1)}, u32[]{:S(2)}, u32[]{:S(2)}) collective-permute-start(f32[2,8,16,256]{3,2,1,0:T(8,128)S(1)} %get-tuple-element.78), channel_id=1, source_target_pairs={{1,2},{2,1},{5,6},{6,5},{9,10},{10,9},{13,14},{14,13},{17,18},{18,... | collective-permute-start | bytes 786440 | tf_op jit(solution)/shard_map/ppermute | solution.py:61
  48.3 0.1 collective-permute-done.14.even
  48.4 0.0 collective-permute-done.15.odd
  48.4 1.4 %shard_map.128 = (f32[2,16,16,256]{3,2,1,0:T(8,128)S(1)}, f32[2,24,16,256]{3,2,1,0:T(8,128)S(1)}, f32[2,4,16,256]{3,2,1,0:T(8,128)S(1)}, f32[2,4,16,256]{3,2,1,0:T(8,128)S(1)}) custom-call(f32[2,16,16,256]{3,2,1,0:T(8,128)S(1)} %get-tuple-element.89.now, f32[2,24,16,256]{3,2,1,0:T(8,128)S(1)} %get-tuple-element.90.before, ...), custom_call_target="tpu_custom_call" | custom-call | tf_op jit(solution)/shard_map/pallas_call | solution.py:304
  49.8 0.4 shard_map.129.refs_0_
  50.2 1.6 %collective-permute-done.8.even = f32[2,8,16,256]{3,2,1,0:T(8,128)S(1)} collective-permute-done((f32[2,8,16,256]{3,2,1,0:T(8,128)S(1)}, f32[2,8,16,256]{3,2,1,0:T(8,128)S(1)}, u32[]{:S(2)}, u32[]{:S(2)}) %collective-permute-start.8) | collective-permute-done | bytes 262176 | tf_op jit(solution)/shard_map/ppermute | solution.py:60
  51.8 1.4 %shard_map.125 = (f32[2,16,16,256]{3,2,1,0:T(8,128)S(1)}, f32[2,24,16,256]{3,2,1,0:T(8,128)S(1)}, f32[2,4,16,256]{3,2,1,0:T(8,128)S(1)}, f32[2,4,16,256]{3,2,1,0:T(8,128)S(1)}) custom-call(f32[2,16,16,256]{3,2,1,0:T(8,128)S(1)} %get-tuple-element.75.now, f32[2,24,16,256]{3,2,1,0:T(8,128)S(1)} %get-tuple-element.76.before, ...), custom_call_target="tpu_custom_call" | custom-call | tf_op jit(solution)/shard_map/pallas_call | solution.py:304
  53.2 0.4 shard_map.130.refs_0_
  53.6 0.1 collective-permute-start.16
  53.7 4.0 %collective-permute-start.17 = (f32[2,4,16,256]{3,2,1,0:T(8,128)S(1)}, f32[2,4,16,256]{3,2,1,0:T(8,128)S(1)}, u32[]{:S(2)}, u32[]{:S(2)}) collective-permute-start(f32[2,4,16,256]{3,2,1,0:T(8,128)S(1)} %get-tuple-element.95), channel_id=1, source_target_pairs={{0,1},{1,0},{2,3},{3,2},{4,5},{5,4},{6,7},{7,6},{8,9},{9,8},{10,11... | collective-permute-start | bytes 393224 | tf_op jit(solution)/shard_map/ppermute | solution.py:60
  57.7 0.7 collective-permute-start.18
  58.3 2.9 %collective-permute-start.19 = (f32[2,4,16,256]{3,2,1,0:T(8,128)S(1)}, f32[2,4,16,256]{3,2,1,0:T(8,128)S(1)}, u32[]{:S(2)}, u32[]{:S(2)}) collective-permute-start(f32[2,4,16,256]{3,2,1,0:T(8,128)S(1)} %get-tuple-element.97), channel_id=1, source_target_pairs={{0,1},{1,0},{2,3},{3,2},{4,5},{5,4},{6,7},{7,6},{8,9},{9,8},{10,11... | collective-permute-start | bytes 393224 | tf_op jit(solution)/shard_map/ppermute | solution.py:60
  61.2 0.7 collective-permute-start.20
  61.9 0.0 collective-permute-done.18.odd
  61.9 0.4 shard_map.131.refs_2_.refs_0_
  62.3 0.1 collective-permute-start.21
  62.4 2.6 %collective-permute-done.19.even = f32[2,4,16,256]{3,2,1,0:T(8,128)S(1)} collective-permute-done((f32[2,4,16,256]{3,2,1,0:T(8,128)S(1)}, f32[2,4,16,256]{3,2,1,0:T(8,128)S(1)}, u32[]{:S(2)}, u32[]{:S(2)}) %collective-permute-start.19) | collective-permute-done | bytes 131104 | tf_op jit(solution)/shard_map/ppermute | solution.py:60
  65.0 0.4 shard_map.132.refs_3_.refs_1_
  65.4 0.1 collective-permute-start.22
  65.5 0.0 collective-permute-done.16.refs_1_
  65.5 0.7 shard_map.133
  66.2 1.5 %collective-permute-start.23 = (f32[2,8,16,256]{3,2,1,0:T(8,128)S(1)}, f32[2,8,16,256]{3,2,1,0:T(8,128)S(1)}, u32[]{:S(2)}, u32[]{:S(2)}) collective-permute-start(f32[2,8,16,256]{3,2,1,0:T(8,128)S(1)} %shard_map.133), channel_id=1, source_target_pairs={{0,8},{4,12},{8,0},{12,4},{1,9},{5,13},{9,1},{13,5},{2,10},{6,14},... | collective-permute-start | bytes 786440 | tf_op jit(solution)/shard_map/ppermute | solution.py:533
  67.8 0.7 shard_map.134
  68.5 0.8 collective-permute-start.24
  69.3 6.2 %collective-permute-done.23.refs_6_ = f32[2,8,16,256]{3,2,1,0:T(8,128)S(1)} collective-permute-done((f32[2,8,16,256]{3,2,1,0:T(8,128)S(1)}, f32[2,8,16,256]{3,2,1,0:T(8,128)S(1)}, u32[]{:S(2)}, u32[]{:S(2)}) %collective-permute-start.23) | collective-permute-done | bytes 262176 | tf_op jit(solution)/shard_map/ppermute | solution.py:533
  75.5 1.5 %image_inner.1 = (f32[2,16,16,256]{3,2,1,0:T(8,128)}, f32[2,16,16,256]{3,2,1,0:T(8,128)}, f32[2,16,16,256]{3,2,1,0:T(8,128)}, f32[2,8,16,256]{3,2,1,0:T(8,128)S(1)}) custom-call(s32[8,128]{1,0:T(8,128)S(1)} %get-tuple-element.53.lags, f32[4,8,16,256]{3,2,1,0:T(8,128)S(1)} %shard_map.130.refs_0_, f32[4,8,16,256]{3,2,1,0:T(8,128)S(1)} %collective-permute-done.16.refs_1_, ...), custom_call_target="tpu_custom_call" | custom-call | tf_op jit(solution)/shard_map/image_inner/pallas_call | solution.py:452
  77.0 3.5 %collective-permute-done.24.refs_1_ = f32[2,8,16,256]{3,2,1,0:T(8,128)S(1)} collective-permute-done((f32[2,8,16,256]{3,2,1,0:T(8,128)S(1)}, f32[2,8,16,256]{3,2,1,0:T(8,128)S(1)}, u32[]{:S(2)}, u32[]{:S(2)}) %collective-permute-start.24) | collective-permute-done | bytes 262176 | tf_op jit(solution)/shard_map/ppermute | solution.py:533
  80.5 0.7 image_outer.1
  (17 shorter events, 0.0 us)
Async XLA Ops:
  0.6 10.4 %copy-start.1 = (f32[8,2,256]{2,1,0:T(2,128)S(1)}, f32[8,2,256]{2,1,0:T(2,128)}, u32[]{:S(2)}) copy-start(f32[8,2,256]{2,1,0:T(2,128)} %traces.1) | copy-start | bytes 49156
  1.9 11.6 %collective-permute-start = (f32[3,4,16,256]{3,2,1,0:T(8,128)S(1)}, f32[3,4,16,256]{3,2,1,0:T(8,128)S(1)}, u32[]{:S(2)}, u32[]{:S(2)}) collective-permute-start(f32[3,4,16,256]{3,2,1,0:T(8,128)S(1)} %get-tuple-element.58), channel_id=1, source_target_pairs={{0,1},{1,0},{2,3},{3,2},{4,5},{5,4},{6,7},{7,6},{8,9},{9,8},{10,11... | collective-permute-start | bytes 589832 | tf_op jit(solution)/shard_map/ppermute | solution.py:60
  5.0 8.5 %collective-permute-start.1 = (f32[3,4,16,256]{3,2,1,0:T(8,128)S(1)}, f32[3,4,16,256]{3,2,1,0:T(8,128)S(1)}, u32[]{:S(2)}, u32[]{:S(2)}) collective-permute-start(f32[3,4,16,256]{3,2,1,0:T(8,128)S(1)} %get-tuple-element.59), channel_id=1, source_target_pairs={{1,2},{2,1},{5,6},{6,5},{9,10},{10,9},{13,14},{14,13},{17,18},{18,... | collective-permute-start | bytes 589832 | tf_op jit(solution)/shard_map/ppermute | solution.py:61
  5.6 5.3 %copy-start.5 = (f32[8,2]{0,1:T(2,128)S(1)}, f32[8,2]{0,1:T(2,128)}, u32[]{:S(2)}) copy-start(f32[8,2]{0,1:T(2,128)} %param.16) | copy-start | bytes 196
  5.7 11.2 %collective-permute-start.2 = (f32[2,4,16,256]{3,2,1,0:T(8,128)S(1)}, f32[2,4,16,256]{3,2,1,0:T(8,128)S(1)}, u32[]{:S(2)}, u32[]{:S(2)}) collective-permute-start(f32[2,4,16,256]{3,2,1,0:T(8,128)S(1)} %get-tuple-element.64), channel_id=1, source_target_pairs={{0,1},{1,0},{2,3},{3,2},{4,5},{5,4},{6,7},{7,6},{8,9},{9,8},{10,11... | collective-permute-start | bytes 393224 | tf_op jit(solution)/shard_map/ppermute | solution.py:60
  10.1 0.9 %copy-start.2 = (s32[2,256]{1,0:T(2,128)S(1)}, s32[2,256]{1,0:T(2,128)}, u32[]{:S(2)}) copy-start(s32[2,256]{1,0:T(2,128)} %receiver_cell.1) | copy-start | bytes 6148
  10.1 0.9 %copy-start.3 = (s32[2]{0:T(128)S(1)}, s32[2]{0:T(128)}, u32[]{:S(2)}) copy-start(s32[2]{0:T(128)} %source_cell.1) | copy-start | bytes 28
  10.1 0.9 %copy-start.4 = (s32[8]{0:T(128)S(1)}, s32[8]{0:T(128)}, u32[]{:S(2)}) copy-start(s32[8]{0:T(128)} %offset_perm.1) | copy-start | bytes 100
  10.1 6.7 %collective-permute-start.3 = (f32[2,4,16,256]{3,2,1,0:T(8,128)S(1)}, f32[2,4,16,256]{3,2,1,0:T(8,128)S(1)}, u32[]{:S(2)}, u32[]{:S(2)}) collective-permute-start(f32[2,4,16,256]{3,2,1,0:T(8,128)S(1)} %get-tuple-element.65), channel_id=1, source_target_pairs={{1,2},{2,1},{5,6},{6,5},{9,10},{10,9},{13,14},{14,13},{17,18},{18,... | collective-permute-start | bytes 393224 | tf_op jit(solution)/shard_map/ppermute | solution.py:61
  11.0 2.5 %copy-start = (f32[16,16,256]{2,1,0:T(8,128)S(1)}, f32[16,16,256]{2,1,0:T(8,128)}, u32[]{:S(2)}) copy-start(f32[16,16,256]{2,1,0:T(8,128)} %courant.3) | copy-start | bytes 786436
  14.3 8.8 %collective-permute-start.10 = (f32[2,8,16,256]{3,2,1,0:T(8,128)S(1)}, f32[2,8,16,256]{3,2,1,0:T(8,128)S(1)}, u32[]{:S(2)}, u32[]{:S(2)}) collective-permute-start(f32[2,8,16,256]{3,2,1,0:T(8,128)S(1)} %get-tuple-element.83), channel_id=1, source_target_pairs={{0,1},{1,0},{2,3},{3,2},{4,5},{5,4},{6,7},{7,6},{8,9},{9,8},{10,11... | collective-permute-start | bytes 786440 | tf_op jit(solution)/shard_map/ppermute | solution.py:60
  16.1 6.9 %collective-permute-start.11 = (f32[2,8,16,256]{3,2,1,0:T(8,128)S(1)}, f32[2,8,16,256]{3,2,1,0:T(8,128)S(1)}, u32[]{:S(2)}, u32[]{:S(2)}) collective-permute-start(f32[2,8,16,256]{3,2,1,0:T(8,128)S(1)} %get-tuple-element.84), channel_id=1, source_target_pairs={{1,2},{2,1},{5,6},{6,5},{9,10},{10,9},{13,14},{14,13},{17,18},{18,... | collective-permute-start | bytes 786440 | tf_op jit(solution)/shard_map/ppermute | solution.py:61
  17.6 11.8 %collective-permute-start.4 = (f32[2,8,16,256]{3,2,1,0:T(8,128)S(1)}, f32[2,8,16,256]{3,2,1,0:T(8,128)S(1)}, u32[]{:S(2)}, u32[]{:S(2)}) collective-permute-start(f32[2,8,16,256]{3,2,1,0:T(8,128)S(1)} %get-tuple-element.69), channel_id=1, source_target_pairs={{0,1},{1,0},{2,3},{3,2},{4,5},{5,4},{6,7},{7,6},{8,9},{9,8},{10,11... | collective-permute-start | bytes 786440 | tf_op jit(solution)/shard_map/ppermute | solution.py:60
  21.4 8.0 %collective-permute-start.5 = (f32[2,8,16,256]{3,2,1,0:T(8,128)S(1)}, f32[2,8,16,256]{3,2,1,0:T(8,128)S(1)}, u32[]{:S(2)}, u32[]{:S(2)}) collective-permute-start(f32[2,8,16,256]{3,2,1,0:T(8,128)S(1)} %get-tuple-element.70), channel_id=1, source_target_pairs={{1,2},{2,1},{5,6},{6,5},{9,10},{10,9},{13,14},{14,13},{17,18},{18,... | collective-permute-start | bytes 786440 | tf_op jit(solution)/shard_map/ppermute | solution.py:61
  24.6 10.9 %collective-permute-start.12 = (f32[2,8,16,256]{3,2,1,0:T(8,128)S(1)}, f32[2,8,16,256]{3,2,1,0:T(8,128)S(1)}, u32[]{:S(2)}, u32[]{:S(2)}) collective-permute-start(f32[2,8,16,256]{3,2,1,0:T(8,128)S(1)} %get-tuple-element.87), channel_id=1, source_target_pairs={{0,1},{1,0},{2,3},{3,2},{4,5},{5,4},{6,7},{7,6},{8,9},{9,8},{10,11... | collective-permute-start | bytes 786440 | tf_op jit(solution)/shard_map/ppermute | solution.py:60
  28.8 6.7 %collective-permute-start.13 = (f32[2,8,16,256]{3,2,1,0:T(8,128)S(1)}, f32[2,8,16,256]{3,2,1,0:T(8,128)S(1)}, u32[]{:S(2)}, u32[]{:S(2)}) collective-permute-start(f32[2,8,16,256]{3,2,1,0:T(8,128)S(1)} %get-tuple-element.88), channel_id=1, source_target_pairs={{1,2},{2,1},{5,6},{6,5},{9,10},{10,9},{13,14},{14,13},{17,18},{18,... | collective-permute-start | bytes 786440 | tf_op jit(solution)/shard_map/ppermute | solution.py:61
  31.0 11.0 %collective-permute-start.6 = (f32[2,8,16,256]{3,2,1,0:T(8,128)S(1)}, f32[2,8,16,256]{3,2,1,0:T(8,128)S(1)}, u32[]{:S(2)}, u32[]{:S(2)}) collective-permute-start(f32[2,8,16,256]{3,2,1,0:T(8,128)S(1)} %get-tuple-element.73), channel_id=1, source_target_pairs={{0,1},{1,0},{2,3},{3,2},{4,5},{5,4},{6,7},{7,6},{8,9},{9,8},{10,11... | collective-permute-start | bytes 786440 | tf_op jit(solution)/shard_map/ppermute | solution.py:60
  34.8 7.2 %collective-permute-start.7 = (f32[2,8,16,256]{3,2,1,0:T(8,128)S(1)}, f32[2,8,16,256]{3,2,1,0:T(8,128)S(1)}, u32[]{:S(2)}, u32[]{:S(2)}) collective-permute-start(f32[2,8,16,256]{3,2,1,0:T(8,128)S(1)} %get-tuple-element.74), channel_id=1, source_target_pairs={{1,2},{2,1},{5,6},{6,5},{9,10},{10,9},{13,14},{14,13},{17,18},{18,... | collective-permute-start | bytes 786440 | tf_op jit(solution)/shard_map/ppermute | solution.py:61
  37.0 11.4 %collective-permute-start.14 = (f32[2,8,16,256]{3,2,1,0:T(8,128)S(1)}, f32[2,8,16,256]{3,2,1,0:T(8,128)S(1)}, u32[]{:S(2)}, u32[]{:S(2)}) collective-permute-start(f32[2,8,16,256]{3,2,1,0:T(8,128)S(1)} %get-tuple-element.91), channel_id=1, source_target_pairs={{0,1},{1,0},{2,3},{3,2},{4,5},{5,4},{6,7},{7,6},{8,9},{9,8},{10,11... | collective-permute-start | bytes 786440 | tf_op jit(solution)/shard_map/ppermute | solution.py:60
  41.3 7.1 %collective-permute-start.15 = (f32[2,8,16,256]{3,2,1,0:T(8,128)S(1)}, f32[2,8,16,256]{3,2,1,0:T(8,128)S(1)}, u32[]{:S(2)}, u32[]{:S(2)}) collective-permute-start(f32[2,8,16,256]{3,2,1,0:T(8,128)S(1)} %get-tuple-element.92), channel_id=1, source_target_pairs={{1,2},{2,1},{5,6},{6,5},{9,10},{10,9},{13,14},{14,13},{17,18},{18,... | collective-permute-start | bytes 786440 | tf_op jit(solution)/shard_map/ppermute | solution.py:61
  43.5 8.3 %collective-permute-start.8 = (f32[2,8,16,256]{3,2,1,0:T(8,128)S(1)}, f32[2,8,16,256]{3,2,1,0:T(8,128)S(1)}, u32[]{:S(2)}, u32[]{:S(2)}) collective-permute-start(f32[2,8,16,256]{3,2,1,0:T(8,128)S(1)} %get-tuple-element.77), channel_id=1, source_target_pairs={{0,1},{1,0},{2,3},{3,2},{4,5},{5,4},{6,7},{7,6},{8,9},{9,8},{10,11... | collective-permute-start | bytes 786440 | tf_op jit(solution)/shard_map/ppermute | solution.py:60
  47.4 4.4 %collective-permute-start.9 = (f32[2,8,16,256]{3,2,1,0:T(8,128)S(1)}, f32[2,8,16,256]{3,2,1,0:T(8,128)S(1)}, u32[]{:S(2)}, u32[]{:S(2)}) collective-permute-start(f32[2,8,16,256]{3,2,1,0:T(8,128)S(1)} %get-tuple-element.78), channel_id=1, source_target_pairs={{1,2},{2,1},{5,6},{6,5},{9,10},{10,9},{13,14},{14,13},{17,18},{18,... | collective-permute-start | bytes 786440 | tf_op jit(solution)/shard_map/ppermute | solution.py:61
  53.6 11.9 %collective-permute-start.16 = (f32[4,8,16,256]{3,2,1,0:T(8,128)S(1)}, f32[4,8,16,256]{3,2,1,0:T(8,128)S(1)}, u32[]{:S(2)}, u32[]{:S(2)}) collective-permute-start(f32[4,8,16,256]{3,2,1,0:T(8,128)S(1)} %shard_map.130.refs_0_), channel_id=1, source_target_pairs={{0,4},{4,0},{8,12},{12,8},{1,5},{5,1},{9,13},{13,9},{2,6},{6,2},{1... | collective-permute-start | bytes 1572872 | tf_op jit(solution)/shard_map/ppermute | solution.py:526
  53.7 8.2 %collective-permute-start.17 = (f32[2,4,16,256]{3,2,1,0:T(8,128)S(1)}, f32[2,4,16,256]{3,2,1,0:T(8,128)S(1)}, u32[]{:S(2)}, u32[]{:S(2)}) collective-permute-start(f32[2,4,16,256]{3,2,1,0:T(8,128)S(1)} %get-tuple-element.95), channel_id=1, source_target_pairs={{0,1},{1,0},{2,3},{3,2},{4,5},{5,4},{6,7},{7,6},{8,9},{9,8},{10,11... | collective-permute-start | bytes 393224 | tf_op jit(solution)/shard_map/ppermute | solution.py:60
  57.7 4.2 %collective-permute-start.18 = (f32[2,4,16,256]{3,2,1,0:T(8,128)S(1)}, f32[2,4,16,256]{3,2,1,0:T(8,128)S(1)}, u32[]{:S(2)}, u32[]{:S(2)}) collective-permute-start(f32[2,4,16,256]{3,2,1,0:T(8,128)S(1)} %get-tuple-element.96), channel_id=1, source_target_pairs={{1,2},{2,1},{5,6},{6,5},{9,10},{10,9},{13,14},{14,13},{17,18},{18,... | collective-permute-start | bytes 393224 | tf_op jit(solution)/shard_map/ppermute | solution.py:61
  58.3 6.7 %collective-permute-start.19 = (f32[2,4,16,256]{3,2,1,0:T(8,128)S(1)}, f32[2,4,16,256]{3,2,1,0:T(8,128)S(1)}, u32[]{:S(2)}, u32[]{:S(2)}) collective-permute-start(f32[2,4,16,256]{3,2,1,0:T(8,128)S(1)} %get-tuple-element.97), channel_id=1, source_target_pairs={{0,1},{1,0},{2,3},{3,2},{4,5},{5,4},{6,7},{7,6},{8,9},{9,8},{10,11... | collective-permute-start | bytes 393224 | tf_op jit(solution)/shard_map/ppermute | solution.py:60
  61.2 3.8 %collective-permute-start.20 = (f32[2,4,16,256]{3,2,1,0:T(8,128)S(1)}, f32[2,4,16,256]{3,2,1,0:T(8,128)S(1)}, u32[]{:S(2)}, u32[]{:S(2)}) collective-permute-start(f32[2,4,16,256]{3,2,1,0:T(8,128)S(1)} %get-tuple-element.98), channel_id=1, source_target_pairs={{1,2},{2,1},{5,6},{6,5},{9,10},{10,9},{13,14},{14,13},{17,18},{18,... | collective-permute-start | bytes 393224 | tf_op jit(solution)/shard_map/ppermute | solution.py:61
  62.3 5.4 %collective-permute-start.21 = (f32[2,8,16,256]{3,2,1,0:T(8,128)S(1)}, f32[2,8,16,256]{3,2,1,0:T(8,128)S(1)}, u32[]{:S(2)}, u32[]{:S(2)}) collective-permute-start(f32[2,8,16,256]{3,2,1,0:T(8,128)S(1)} %shard_map.131.refs_2_.refs_0_), channel_id=1, source_target_pairs={{0,4},{4,0},{8,12},{12,8},{1,5},{5,1},{9,13},{13,9},{2,6},{6,2},{1... | collective-permute-start | bytes 786440 | tf_op jit(solution)/shard_map/ppermute | solution.py:526
  65.4 2.3 %collective-permute-start.22 = (f32[2,8,16,256]{3,2,1,0:T(8,128)S(1)}, f32[2,8,16,256]{3,2,1,0:T(8,128)S(1)}, u32[]{:S(2)}, u32[]{:S(2)}) collective-permute-start(f32[2,8,16,256]{3,2,1,0:T(8,128)S(1)} %shard_map.132.refs_3_.refs_1_), channel_id=1, source_target_pairs={{0,4},{4,0},{8,12},{12,8},{1,5},{5,1},{9,13},{13,9},{2,6},{6,2},{1... | collective-permute-start | bytes 786440 | tf_op jit(solution)/shard_map/ppermute | solution.py:526
  66.2 9.2 %collective-permute-start.23 = (f32[2,8,16,256]{3,2,1,0:T(8,128)S(1)}, f32[2,8,16,256]{3,2,1,0:T(8,128)S(1)}, u32[]{:S(2)}, u32[]{:S(2)}) collective-permute-start(f32[2,8,16,256]{3,2,1,0:T(8,128)S(1)} %shard_map.133), channel_id=1, source_target_pairs={{0,8},{4,12},{8,0},{12,4},{1,9},{5,13},{9,1},{13,5},{2,10},{6,14},... | collective-permute-start | bytes 786440 | tf_op jit(solution)/shard_map/ppermute | solution.py:533
  68.5 12.0 %collective-permute-start.24 = (f32[2,8,16,256]{3,2,1,0:T(8,128)S(1)}, f32[2,8,16,256]{3,2,1,0:T(8,128)S(1)}, u32[]{:S(2)}, u32[]{:S(2)}) collective-permute-start(f32[2,8,16,256]{3,2,1,0:T(8,128)S(1)} %shard_map.134), channel_id=1, source_target_pairs={{0,8},{4,12},{8,0},{12,4},{1,9},{5,13},{9,1},{13,5},{2,10},{6,14},... | collective-permute-start | bytes 786440 | tf_op jit(solution)/shard_map/ppermute | solution.py:533

commit v6 on v5

--- a/solution.py
+++ b/solution.py
@@ -84,7 +84,7 @@
         for side, start in enumerate(edge_starts(rows, REACH)):
             planes = pl.ds(start, REACH)
             pieces = [source.at[group, planes], receiver.at[group, planes]]
-            if group == 0:
+            if group == groups - 1:
                 pieces.append(courant.at[planes])
             for index, piece in enumerate(pieces):
                 copies.append(pltpu.make_async_copy(piece, outs[2 * group + side].at[index], sem.at[len(copies)]))
@@ -100,7 +100,7 @@
 
 def pack(source_now, receiver_now, courant_sq):
     groups, _, size_y, size_z = source_now.shape
-    shapes = [struct((3 if group == 0 else 2, REACH, size_y, size_z)) for group in range(groups) for _ in range(2)]
+    shapes = [struct((3 if group == groups - 1 else 2, REACH, size_y, size_z)) for group in range(groups) for _ in range(2)]
     return pl.pallas_call(
         pack_kernel,
         out_shape=shapes,
@@ -126,15 +126,19 @@
     return copies
 
 
-def prepare_kernel(groups, rows, source_cell, wavelet, offset_perm, receiver_cell, traces, source, receiver, source_before, receiver_before, along_z, along_y, lags, *refs):
-    planes, now, before, sem = refs[:groups], refs[groups : 2 * groups], refs[2 * groups : 3 * groups], refs[-1]
-    pieces = []
-    for group in range(groups):
-        pieces += [(source.at[group], now[group].at[0]), (receiver.at[group], now[group].at[1])]
-        pieces += [(source_before.at[group], before[group].at[0]), (receiver_before.at[group], before[group].at[1])]
+def prepare_kernel(group, rows, source_cell, wavelet, offset_perm, receiver_cell, traces, source, receiver, source_before, receiver_before, planes, now, before, *refs):
+    tables, sem = refs[:-1], refs[-1]
+    pieces = [(source.at[group], now.at[0]), (receiver.at[group], now.at[1])]
+    pieces += [(source_before.at[group], before.at[0]), (receiver_before.at[group], before.at[1])]
     copies = fetch(pieces, sem)
-    _, plane_count, size_y, _ = planes[0].shape
-    steps = traces.shape[0]
+    if tables:
+        make_tables(planes.shape[2], offset_perm, *tables)
+    spread_data(group, rows, source_cell, wavelet, receiver_cell, traces, planes)
+    for copy in copies:
+        copy.wait()
+
+
+def make_tables(size_y, offset_perm, along_z, along_y, lags):
     size_z = along_z.shape[0]
     block = along_y.shape[0]
     for slot in range(offset_perm.shape[0]):
@@ -148,57 +152,59 @@
     half = jnp.where(same, band(jnp.abs(row - col)), 0.0).astype(jnp.bfloat16)
     along_y[:, :block] = half
     along_y[:, block:] = half
+
+
+def spread_data(group, rows, source_cell, wavelet, receiver_cell, traces, planes):
+    _, plane_count, size_y, _ = planes.shape
+    steps = traces.shape[0]
     first = (lax.axis_index("slab") * rows - REACH) * size_y
     cells = plane_count * size_y
     lane = lax.broadcasted_iota(jnp.int32, (1, LANES), 1)
-    for group in range(groups):
-        ids = first + lax.broadcasted_iota(jnp.int32, (cells, 1), 0)
-        amplitude = jnp.zeros((1, LANES), jnp.float32)
-        for step in range(steps):
-            amplitude = jnp.where(lane == step, wavelet[step, group], amplitude)
-        hit = jnp.broadcast_to(ids, (cells, LANES)) == source_cell[group]
-        spread = jnp.where(hit, jnp.broadcast_to(amplitude, (cells, LANES)), 0.0)
-        planes[group][0] = spread.reshape(plane_count, size_y, LANES)
-        count = receiver_cell.shape[1]
-        wide = first + lax.broadcasted_iota(jnp.int32, (cells, count), 0)
-        here = jnp.broadcast_to(receiver_cell[group : group + 1, :], (cells, count))
-        hot = (wide == here).astype(jnp.float32).astype(jnp.bfloat16)
-        left, terms = traces[:, group, :], []
-        for _ in range(3):
-            term = left.astype(jnp.bfloat16).astype(jnp.float32)
-            terms.append(term)
-            left = left - term
-        terms.append(jnp.zeros((LANES - 3 * steps, count), jnp.float32))
-        summed = lax.dot_general(
-            hot,
-            jnp.concatenate(terms, axis=0).astype(jnp.bfloat16),
-            (((1,), (1,)), ((), ())),
-            preferred_element_type=jnp.float32,
-        )
-        summed = summed + pltpu.roll(summed, LANES - steps, 1) + pltpu.roll(summed, LANES - 2 * steps, 1)
-        planes[group][1] = summed.reshape(plane_count, size_y, LANES)
-    for copy in copies:
-        copy.wait()
-
-
-def prepare(source_cell, wavelet, offset_perm, receiver_cell, traces, fields):
-    groups, rows, size_y, size_z = fields[0].shape
+    ids = first + lax.broadcasted_iota(jnp.int32, (cells, 1), 0)
+    amplitude = jnp.zeros((1, LANES), jnp.float32)
+    for step in range(steps):
+        amplitude = jnp.where(lane == step, wavelet[step, group], amplitude)
+    hit = jnp.broadcast_to(ids, (cells, LANES)) == source_cell[group]
+    spread = jnp.where(hit, jnp.broadcast_to(amplitude, (cells, LANES)), 0.0)
+    planes[0] = spread.reshape(plane_count, size_y, LANES)
+    count = receiver_cell.shape[1]
+    wide = first + lax.broadcasted_iota(jnp.int32, (cells, count), 0)
+    here = jnp.broadcast_to(receiver_cell[group : group + 1, :], (cells, count))
+    hot = (wide == here).astype(jnp.float32).astype(jnp.bfloat16)
+    left, terms = traces[:, group, :], []
+    for _ in range(3):
+        term = left.astype(jnp.bfloat16).astype(jnp.float32)
+        terms.append(term)
+        left = left - term
+    terms.append(jnp.zeros((LANES - 3 * steps, count), jnp.float32))
+    summed = lax.dot_general(
+        hot,
+        jnp.concatenate(terms, axis=0).astype(jnp.bfloat16),
+        (((1,), (1,)), ((), ())),
+        preferred_element_type=jnp.float32,
+    )
+    summed = summed + pltpu.roll(summed, LANES - steps, 1) + pltpu.roll(summed, LANES - 2 * steps, 1)
+    planes[1] = summed.reshape(plane_count, size_y, LANES)
+
+
+def prepare(group, source_cell, wavelet, offset_perm, receiver_cell, traces, fields):
+    _, rows, size_y, size_z = fields[0].shape
     block = CHUNK * size_y
     field = struct((2, rows, size_y, size_z))
-    shapes = [
-        struct((size_z, size_z), jnp.bfloat16),
-        struct((block, 2 * block), jnp.bfloat16),
-        struct((offset_perm.shape[0], LANES), jnp.int32),
-    ]
-    shapes += [struct((2, rows + 2 * REACH, size_y, LANES))] * groups + [field] * (2 * groups)
-    return pl.pallas_call(
-        functools.partial(prepare_kernel, groups, rows),
+    shapes = [struct((2, rows + 2 * REACH, size_y, LANES)), field, field]
+    if group == 0:
+        shapes += [
+            struct((size_z, size_z), jnp.bfloat16),
+            struct((block, 2 * block), jnp.bfloat16),
+            struct((offset_perm.shape[0], LANES), jnp.int32),
+        ]
+    return pl.pallas_call(
+        functools.partial(prepare_kernel, group, rows),
         out_shape=shapes,
         in_specs=[smem()] * 3 + [vmem()] * 2 + [hbm()] * 4,
         out_specs=[vmem()] * len(shapes),
-        scratch_shapes=[pltpu.SemaphoreType.DMA((4 * groups,))],
-        compiler_params=params(),
-        name="prepare",
+        scratch_shapes=[pltpu.SemaphoreType.DMA((4,))],
+        compiler_params=params(),
     )(source_cell, wavelet, offset_perm, receiver_cell, traces, *stay(*fields))
 
 
@@ -229,14 +235,13 @@
     return [[(at, CHUNK)] for at in range(start, stop, CHUNK)]
 
 
-def first_kernel(rows, width, now, before, courant, even, odd, inject, along_z, along_y, fresh, held, even_edge, odd_edge, *scaled):
+def first_kernel(rows, last, width, now, before, courant, even, odd, inject, along_z, along_y, fresh, held, even_edge, odd_edge, scaled):
     even_at, odd_at = halo_starts(rows, REACH)
-    if scaled:
-        (courant_out,) = scaled
-        courant_out[REACH : REACH + rows] = SCALE * courant[...]
-        courant_out[pl.ds(even_at, REACH)] = SCALE * even[2]
-        courant_out[pl.ds(odd_at, REACH)] = SCALE * odd[2]
-        courant = courant_out
+    inside = REACH if last else 0
+    scaled[inside : inside + rows] = SCALE * courant[...]
+    if last:
+        scaled[pl.ds(even_at, REACH)] = SCALE * even[2]
+        scaled[pl.ds(odd_at, REACH)] = SCALE * odd[2]
     z_band, y_band = along_z[...], along_y[...]
     for kind in range(2):
         field = held.at[kind]
@@ -248,7 +253,7 @@
             fresh[kind, plane] = new
 
         for runs in chunks(0, rows):
-            advance(field, REACH, before.at[kind], 0, courant, REACH, inject.at[kind], REACH, runs, 0, z_band, y_band, write)
+            advance(field, REACH, before.at[kind], 0, scaled, inside, inject.at[kind], REACH, runs, 0, z_band, y_band, write)
     send(rows, width, fresh, even_edge, odd_edge)
 
 
@@ -258,17 +263,22 @@
     odd_edge[...] = fresh[:, pl.ds(odd_from, width)]
 
 
-def first_round(group, width, now, before, courant, halos, inject, along_z, along_y):
+def first_round(group, groups, width, now, before, courant, halos, inject, along_z, along_y):
     rows, size_y, size_z = now.shape[1:]
+    last = group == groups - 1
     edge = struct((2, width, size_y, size_z))
     shapes = [struct(now.shape), struct((2, rows + 2 * REACH, size_y, size_z)), edge, edge]
-    if group == 0:
+    scratch = []
+    if last:
         shapes.append(struct((rows + 2 * REACH, size_y, size_z)))
-    return pl.pallas_call(
-        functools.partial(first_kernel, rows, width),
+    else:
+        scratch.append(pltpu.VMEM((rows, size_y, size_z), jnp.float32))
+    return pl.pallas_call(
+        functools.partial(first_kernel, rows, last, width),
         out_shape=shapes,
         in_specs=[vmem()] * 8,
         out_specs=[vmem()] * len(shapes),
+        scratch_shapes=scratch,
         compiler_params=params(),
     )(now, before, courant, *halos, inject, along_z, along_y)
 
@@ -499,17 +509,18 @@
     edges = pack(source_now, receiver_now, courant_sq)
     given = [trade(edges[2 * g], edges[2 * g + 1]) for g in everyone]
     fields = (source_now, receiver_now, source_prev, receiver_prev)
-    along_z, along_y, lags, *rest = prepare(source_cell, wavelet, offset_perm, receiver_cell, traces, fields)
-    inject, now, before = rest[:groups], rest[groups : 2 * groups], rest[2 * groups :]
+    inject, now, before = [None] * groups, [None] * groups, [None] * groups
+    for g in everyone:
+        inject[g], now[g], before[g], *tables = prepare(g, source_cell, wavelet, offset_perm, receiver_cell, traces, fields)
+        if g == 0:
+            along_z, along_y, lags = tables
 
     halos = [None] * groups
-    courant = courant_sq
     for g in everyone:
-        result = first_round(g, 2 * REACH, now[g], before[g], courant, given[g], inject[g], along_z, along_y)
+        result = first_round(g, groups, 2 * REACH, now[g], before[g], courant_sq, given[g], inject[g], along_z, along_y)
         now[g], before[g] = result[:2]
-        if g == 0:
-            courant = result[4]
         halos[g] = trade(*result[2:4])
+    courant = result[4]
     final = ()
     for step in range(1, steps - 1, 2):
         last = step + 2 >= steps - 1

time: 82.5 us -> 84.3 us (1.022)
  Pallas kernels: 19.3 us -> 20.8 us
  waiting for transfers between devices: 15 us -> 15.9 us
    pallas_call x3 -> x4, Pallas kernels: 3.96 us -> 5.49 us  [the longest x2 3.99 us: prepare(): pl.pallas_call(functools.partial(prepare_kernel, group, rows), out_shape=...]
    ppermute x10, waiting for transfers between devices: 5.27 us -> 6.23 us  [trade(): even = lax.ppermute(even_edge, 'slab', even_pairs(count))]
  transfers between devices with their start and end apart: 25 -> 25, of which waited for: 6 -> 5; matrix products, arithmetic and copies ran while one was open for 0% -> 0% of each run, Pallas kernels for 19% -> 21%
where the time goes in v6:
time: 84.3 us; the launch traced here: 83.1 us
  starting transfers between devices  45.1 us (53%)
  Pallas kernels  20.8 us (25%)
  waiting for transfers between devices  15.9 us (19%)
  between operations  1.15 us (1%)
    ppermute x10, starting transfers between devices, trade(): even = lax.ppermute(even_edge, 'slab', even_pairs(count))  35.6 us
    ppermute x2, waiting for transfers between devices, part_sums(): sums.append(lax.ppermute(part, 'shot', route))  9.69 us
    pallas_call x6, Pallas kernels, pair_round(): pl.pallas_call(functools.partial(pair_kernel, rows, step, width), out_sha...  8.85 us
    ppermute x10, starting transfers between devices, trade(): odd = lax.ppermute(odd_edge, 'slab', odd_pairs(count))  6.94 us
    ppermute x10, waiting for transfers between devices, trade(): even = lax.ppermute(even_edge, 'slab', even_pairs(count))  6.23 us
    pallas_call x2, Pallas kernels, prepare(): pl.pallas_call(functools.partial(prepare_kernel, group, rows), out_shape=...  3.99 us
    ppermute x2, starting transfers between devices, part_sums(): sums.append(lax.ppermute(part, 'shot', route))  2.36 us
  transfers between devices with their start and end apart: 25, of which 5 were waited for; matrix products, arithmetic and copies ran while one was open for 0% of the time, Pallas kernels for 21%

profile of v6, /device:TPU:0, one launch (start us, length us, event | category | flops | bytes accessed | tf_op | source)
XLA Modules:
  0.0 83.1 jit_solution(15213007647146313534)
XLA Ops:
  0.6 1.2 %pack.1 = (f32[2,4,16,256]{3,2,1,0:T(8,128)S(1)}, f32[2,4,16,256]{3,2,1,0:T(8,128)S(1)}, f32[3,4,16,256]{3,2,1,0:T(8,128)S(1)}, f32[3,4,16,256]{3,2,1,0:T(8,128)S(1)}) custom-call(f32[2,16,16,256]{3,2,1,0:T(8,128)} %source.5, f32[2,16,16,256]{3,2,1,0:T(8,128)} %receiver.5, f32[16,16,256]{2,1,0:T(8,128)} %courant.5), custom_call_target="tpu_custom_call" | custom-call | tf_op jit(solution)/shard_map/pack/pallas_call | solution.py:104
  1.9 3.1 %collective-permute-start = (f32[3,4,16,256]{3,2,1,0:T(8,128)S(1)}, f32[3,4,16,256]{3,2,1,0:T(8,128)S(1)}, u32[]{:S(2)}, u32[]{:S(2)}) collective-permute-start(f32[3,4,16,256]{3,2,1,0:T(8,128)S(1)} %get-tuple-element.56), channel_id=1, source_target_pairs={{0,1},{1,0},{2,3},{3,2},{4,5},{5,4},{6,7},{7,6},{8,9},{9,8},{10,11... | collective-permute-start | bytes 589832 | tf_op jit(solution)/shard_map/ppermute | solution.py:60
  5.0 0.7 collective-permute-start.1
  5.6 0.0 copy-start.5
  5.7 4.5 %collective-permute-start.8 = (f32[2,4,16,256]{3,2,1,0:T(8,128)S(1)}, f32[2,4,16,256]{3,2,1,0:T(8,128)S(1)}, u32[]{:S(2)}, u32[]{:S(2)}) collective-permute-start(f32[2,4,16,256]{3,2,1,0:T(8,128)S(1)} %get-tuple-element.78), channel_id=1, source_target_pairs={{0,1},{1,0},{2,3},{3,2},{4,5},{5,4},{6,7},{7,6},{8,9},{9,8},{10,11... | collective-permute-start | bytes 393224 | tf_op jit(solution)/shard_map/ppermute | solution.py:60
  10.1 0.8 collective-permute-start.9
  10.9 0.1 copy.15.wavelet
  11.0 2.0 %shard_map.121 = (f32[2,24,16,128]{3,2,1,0:T(8,128)S(1)}, f32[2,16,16,256]{3,2,1,0:T(8,128)S(1)}, f32[2,16,16,256]{3,2,1,0:T(8,128)S(1)}, bf16[256,256]{1,0:T(8,...) custom-call(s32[2]{0:T(128)S(1)} %copy-done.3, f32[8,2]{1,0:T(8,128)S(1)} %copy.15.wavelet, ...), custom_call_target="tpu_custom_call" | custom-call | tf_op jit(solution)/shard_map/pallas_call | solution.py:201
  13.0 0.0 copy-start
  13.0 2.0 %shard_map.122 = (f32[2,24,16,128]{3,2,1,0:T(8,128)S(1)}, f32[2,16,16,256]{3,2,1,0:T(8,128)S(1)}, f32[2,16,16,256]{3,2,1,0:T(8,128)S(1)}) custom-call(s32[2]{0:T(128)S(1)} %copy-done.3, f32[8,2]{1,0:T(8,128)S(1)} %copy.15.wavelet, s32[8]{0:T(128)S(1)} %copy-done.4, s32[2,256]{1,0:T(2,128)S(1)} %copy-done.2, f32[8,2,256]{2,1,0:T(2,128)S(1)} %copy-done.1, ...), custom_call_target="tpu_custom_call" | custom-call | tf_op jit(solution)/shard_map/pallas_call | solution.py:201
  15.0 0.0 collective-permute-done.8.even
  15.1 0.0 collective-permute-done.9.odd
  15.1 0.7 shard_map.127
  15.8 2.4 %collective-permute-start.10 = (f32[2,8,16,256]{3,2,1,0:T(8,128)S(1)}, f32[2,8,16,256]{3,2,1,0:T(8,128)S(1)}, u32[]{:S(2)}, u32[]{:S(2)}) collective-permute-start(f32[2,8,16,256]{3,2,1,0:T(8,128)S(1)} %get-tuple-element.83), channel_id=1, source_target_pairs={{0,1},{1,0},{2,3},{3,2},{4,5},{5,4},{6,7},{7,6},{8,9},{9,8},{10,11... | collective-permute-start | bytes 786440 | tf_op jit(solution)/shard_map/ppermute | solution.py:60
  18.3 0.7 collective-permute-start.11
  19.0 0.8 shard_map.123
  19.7 3.1 %collective-permute-start.2 = (f32[2,8,16,256]{3,2,1,0:T(8,128)S(1)}, f32[2,8,16,256]{3,2,1,0:T(8,128)S(1)}, u32[]{:S(2)}, u32[]{:S(2)}) collective-permute-start(f32[2,8,16,256]{3,2,1,0:T(8,128)S(1)} %get-tuple-element.63), channel_id=1, source_target_pairs={{0,1},{1,0},{2,3},{3,2},{4,5},{5,4},{6,7},{7,6},{8,9},{9,8},{10,11... | collective-permute-start | bytes 786440 | tf_op jit(solution)/shard_map/ppermute | solution.py:60
  22.8 0.7 collective-permute-start.3
  23.4 2.0 %collective-permute-done.10.even = f32[2,8,16,256]{3,2,1,0:T(8,128)S(1)} collective-permute-done((f32[2,8,16,256]{3,2,1,0:T(8,128)S(1)}, f32[2,8,16,256]{3,2,1,0:T(8,128)S(1)}, u32[]{:S(2)}, u32[]{:S(2)}) %collective-permute-start.10) | collective-permute-done | bytes 262176 | tf_op jit(solution)/shard_map/ppermute | solution.py:60
  25.4 0.0 collective-permute-done.11.odd
  25.4 1.5 %shard_map.128 = (f32[2,16,16,256]{3,2,1,0:T(8,128)S(1)}, f32[2,24,16,256]{3,2,1,0:T(8,128)S(1)}, f32[2,8,16,256]{3,2,1,0:T(8,128)S(1)}, f32[2,8,16,256]{3,2,1,0:T(8,128)S(1)}) custom-call(f32[2,16,16,256]{3,2,1,0:T(8,128)S(1)} %get-tuple-element.81.now, f32[2,24,16,256]{3,2,1,0:T(8,128)S(1)} %get-tuple-element.82.before, ...), custom_call_target="tpu_custom_call" | custom-call | tf_op jit(solution)/shard_map/pallas_call | solution.py:314
  26.9 3.7 %collective-permute-start.12 = (f32[2,8,16,256]{3,2,1,0:T(8,128)S(1)}, f32[2,8,16,256]{3,2,1,0:T(8,128)S(1)}, u32[]{:S(2)}, u32[]{:S(2)}) collective-permute-start(f32[2,8,16,256]{3,2,1,0:T(8,128)S(1)} %get-tuple-element.87), channel_id=1, source_target_pairs={{0,1},{1,0},{2,3},{3,2},{4,5},{5,4},{6,7},{7,6},{8,9},{9,8},{10,11... | collective-permute-start | bytes 786440 | tf_op jit(solution)/shard_map/ppermute | solution.py:60
  30.6 0.7 collective-permute-start.13
  31.3 0.0 collective-permute-done.3.odd
  31.3 1.5 %shard_map.124 = (f32[2,16,16,256]{3,2,1,0:T(8,128)S(1)}, f32[2,24,16,256]{3,2,1,0:T(8,128)S(1)}, f32[2,8,16,256]{3,2,1,0:T(8,128)S(1)}, f32[2,8,16,256]{3,2,1,0:T(8,128)S(1)}) custom-call(f32[2,16,16,256]{3,2,1,0:T(8,128)S(1)} %get-tuple-element.61.now, f32[2,24,16,256]{3,2,1,0:T(8,128)S(1)} %get-tuple-element.62.before, ...), custom_call_target="tpu_custom_call" | custom-call | tf_op jit(solution)/shard_map/pallas_call | solution.py:314
  32.8 3.3 %collective-permute-start.4 = (f32[2,8,16,256]{3,2,1,0:T(8,128)S(1)}, f32[2,8,16,256]{3,2,1,0:T(8,128)S(1)}, u32[]{:S(2)}, u32[]{:S(2)}) collective-permute-start(f32[2,8,16,256]{3,2,1,0:T(8,128)S(1)} %get-tuple-element.68), channel_id=1, source_target_pairs={{0,1},{1,0},{2,3},{3,2},{4,5},{5,4},{6,7},{7,6},{8,9},{9,8},{10,11... | collective-permute-start | bytes 786440 | tf_op jit(solution)/shard_map/ppermute | solution.py:60
  36.2 0.7 collective-permute-start.5
  36.8 0.0 collective-permute-done.12.even
  36.9 1.5 %shard_map.129 = (f32[2,16,16,256]{3,2,1,0:T(8,128)S(1)}, f32[2,24,16,256]{3,2,1,0:T(8,128)S(1)}, f32[2,8,16,256]{3,2,1,0:T(8,128)S(1)}, f32[2,8,16,256]{3,2,1,0:T(8,128)S(1)}) custom-call(f32[2,16,16,256]{3,2,1,0:T(8,128)S(1)} %get-tuple-element.85.now, f32[2,24,16,256]{3,2,1,0:T(8,128)S(1)} %get-tuple-element.86.before, ...), custom_call_target="tpu_custom_call" | custom-call | tf_op jit(solution)/shard_map/pallas_call | solution.py:314
  38.4 4.2 %collective-permute-start.14 = (f32[2,8,16,256]{3,2,1,0:T(8,128)S(1)}, f32[2,8,16,256]{3,2,1,0:T(8,128)S(1)}, u32[]{:S(2)}, u32[]{:S(2)}) collective-permute-start(f32[2,8,16,256]{3,2,1,0:T(8,128)S(1)} %get-tuple-element.91), channel_id=1, source_target_pairs={{0,1},{1,0},{2,3},{3,2},{4,5},{5,4},{6,7},{7,6},{8,9},{9,8},{10,11... | collective-permute-start | bytes 786440 | tf_op jit(solution)/shard_map/ppermute | solution.py:60
  42.6 0.7 collective-permute-start.15
  43.3 0.0 collective-permute-done.4.even
  43.3 1.5 %shard_map.125 = (f32[2,16,16,256]{3,2,1,0:T(8,128)S(1)}, f32[2,24,16,256]{3,2,1,0:T(8,128)S(1)}, f32[2,8,16,256]{3,2,1,0:T(8,128)S(1)}, f32[2,8,16,256]{3,2,1,0:T(8,128)S(1)}) custom-call(f32[2,16,16,256]{3,2,1,0:T(8,128)S(1)} %get-tuple-element.66.now, f32[2,24,16,256]{3,2,1,0:T(8,128)S(1)} %get-tuple-element.67.before, ...), custom_call_target="tpu_custom_call" | custom-call | tf_op jit(solution)/shard_map/pallas_call | solution.py:314
  44.8 3.9 %collective-permute-start.6 = (f32[2,8,16,256]{3,2,1,0:T(8,128)S(1)}, f32[2,8,16,256]{3,2,1,0:T(8,128)S(1)}, u32[]{:S(2)}, u32[]{:S(2)}) collective-permute-start(f32[2,8,16,256]{3,2,1,0:T(8,128)S(1)} %get-tuple-element.72), channel_id=1, source_target_pairs={{0,1},{1,0},{2,3},{3,2},{4,5},{5,4},{6,7},{7,6},{8,9},{9,8},{10,11... | collective-permute-start | bytes 786440 | tf_op jit(solution)/shard_map/ppermute | solution.py:60
  48.6 0.8 %collective-permute-start.7 = (f32[2,8,16,256]{3,2,1,0:T(8,128)S(1)}, f32[2,8,16,256]{3,2,1,0:T(8,128)S(1)}, u32[]{:S(2)}, u32[]{:S(2)}) collective-permute-start(f32[2,8,16,256]{3,2,1,0:T(8,128)S(1)} %get-tuple-element.73), channel_id=1, source_target_pairs={{1,2},{2,1},{5,6},{6,5},{9,10},{10,9},{13,14},{14,13},{17,18},{18,... | collective-permute-start | bytes 786440 | tf_op jit(solution)/shard_map/ppermute | solution.py:61
  49.5 0.0 collective-permute-done.14.even
  49.5 0.0 collective-permute-done.15.odd
  49.5 1.4 %shard_map.130 = (f32[2,16,16,256]{3,2,1,0:T(8,128)S(1)}, f32[2,24,16,256]{3,2,1,0:T(8,128)S(1)}, f32[2,4,16,256]{3,2,1,0:T(8,128)S(1)}, f32[2,4,16,256]{3,2,1,0:T(8,128)S(1)}) custom-call(f32[2,16,16,256]{3,2,1,0:T(8,128)S(1)} %get-tuple-element.89.now, f32[2,24,16,256]{3,2,1,0:T(8,128)S(1)} %get-tuple-element.90.before, ...), custom_call_target="tpu_custom_call" | custom-call | tf_op jit(solution)/shard_map/pallas_call | solution.py:314
  51.0 0.4 shard_map.131.refs_0_
  51.4 1.6 %collective-permute-done.6.even = f32[2,8,16,256]{3,2,1,0:T(8,128)S(1)} collective-permute-done((f32[2,8,16,256]{3,2,1,0:T(8,128)S(1)}, f32[2,8,16,256]{3,2,1,0:T(8,128)S(1)}, u32[]{:S(2)}, u32[]{:S(2)}) %collective-permute-start.6) | collective-permute-done | bytes 262176 | tf_op jit(solution)/shard_map/ppermute | solution.py:60
  53.0 0.0 collective-permute-done.7.odd
  53.0 1.4 %shard_map.126 = (f32[2,16,16,256]{3,2,1,0:T(8,128)S(1)}, f32[2,24,16,256]{3,2,1,0:T(8,128)S(1)}, f32[2,4,16,256]{3,2,1,0:T(8,128)S(1)}, f32[2,4,16,256]{3,2,1,0:T(8,128)S(1)}) custom-call(f32[2,16,16,256]{3,2,1,0:T(8,128)S(1)} %get-tuple-element.70.now, f32[2,24,16,256]{3,2,1,0:T(8,128)S(1)} %get-tuple-element.71.before, ...), custom_call_target="tpu_custom_call" | custom-call | tf_op jit(solution)/shard_map/pallas_call | solution.py:314
  54.4 0.4 shard_map.132.refs_0_
  54.8 0.1 collective-permute-start.16
  54.9 4.0 %collective-permute-start.17 = (f32[2,4,16,256]{3,2,1,0:T(8,128)S(1)}, f32[2,4,16,256]{3,2,1,0:T(8,128)S(1)}, u32[]{:S(2)}, u32[]{:S(2)}) collective-permute-start(f32[2,4,16,256]{3,2,1,0:T(8,128)S(1)} %get-tuple-element.95), channel_id=1, source_target_pairs={{0,1},{1,0},{2,3},{3,2},{4,5},{5,4},{6,7},{7,6},{8,9},{9,8},{10,11... | collective-permute-start | bytes 393224 | tf_op jit(solution)/shard_map/ppermute | solution.py:60
  58.9 0.7 collective-permute-start.18
  59.6 3.3 %collective-permute-start.19 = (f32[2,4,16,256]{3,2,1,0:T(8,128)S(1)}, f32[2,4,16,256]{3,2,1,0:T(8,128)S(1)}, u32[]{:S(2)}, u32[]{:S(2)}) collective-permute-start(f32[2,4,16,256]{3,2,1,0:T(8,128)S(1)} %get-tuple-element.97), channel_id=1, source_target_pairs={{0,1},{1,0},{2,3},{3,2},{4,5},{5,4},{6,7},{7,6},{8,9},{9,8},{10,11... | collective-permute-start | bytes 393224 | tf_op jit(solution)/shard_map/ppermute | solution.py:60
  62.9 0.7 collective-permute-start.20
  63.6 0.0 collective-permute-done.18.odd
  63.6 0.4 shard_map.133.refs_2_.refs_0_
  64.1 0.1 collective-permute-start.21
  64.1 2.6 %collective-permute-done.19.even = f32[2,4,16,256]{3,2,1,0:T(8,128)S(1)} collective-permute-done((f32[2,4,16,256]{3,2,1,0:T(8,128)S(1)}, f32[2,4,16,256]{3,2,1,0:T(8,128)S(1)}, u32[]{:S(2)}, u32[]{:S(2)}) %collective-permute-start.19) | collective-permute-done | bytes 131104 | tf_op jit(solution)/shard_map/ppermute | solution.py:60
  66.7 0.4 shard_map.134.refs_3_.refs_1_
  67.2 0.1 collective-permute-start.22
  67.2 0.0 collective-permute-done.16.refs_1_
  67.3 0.7 shard_map.135
  68.0 1.6 %collective-permute-start.23 = (f32[2,8,16,256]{3,2,1,0:T(8,128)S(1)}, f32[2,8,16,256]{3,2,1,0:T(8,128)S(1)}, u32[]{:S(2)}, u32[]{:S(2)}) collective-permute-start(f32[2,8,16,256]{3,2,1,0:T(8,128)S(1)} %shard_map.135), channel_id=1, source_target_pairs={{0,8},{4,12},{8,0},{12,4},{1,9},{5,13},{9,1},{13,5},{2,10},{6,14},... | collective-permute-start | bytes 786440 | tf_op jit(solution)/shard_map/ppermute | solution.py:544
  69.5 0.0 collective-permute-done.21.refs_4_.refs_2_
  69.5 0.7 shard_map.136
  70.2 0.8 collective-permute-start.24
  71.0 6.2 %collective-permute-done.23.refs_6_ = f32[2,8,16,256]{3,2,1,0:T(8,128)S(1)} collective-permute-done((f32[2,8,16,256]{3,2,1,0:T(8,128)S(1)}, f32[2,8,16,256]{3,2,1,0:T(8,128)S(1)}, u32[]{:S(2)}, u32[]{:S(2)}) %collective-permute-start.23) | collective-permute-done | bytes 262176 | tf_op jit(solution)/shard_map/ppermute | solution.py:544
  77.2 1.5 %image_inner.1 = (f32[2,16,16,256]{3,2,1,0:T(8,128)}, f32[2,16,16,256]{3,2,1,0:T(8,128)}, f32[2,16,16,256]{3,2,1,0:T(8,128)}, f32[2,8,16,256]{3,2,1,0:T(8,128)S(1)}) custom-call(s32[8,128]{1,0:T(8,128)S(1)} %get-tuple-element.53.lags, f32[4,8,16,256]{3,2,1,0:T(8,128)S(1)} %shard_map.132.refs_0_, f32[4,8,16,256]{3,2,1,0:T(8,128)S(1)} %collective-permute-done.16.refs_1_, ...), custom_call_target="tpu_custom_call" | custom-call | tf_op jit(solution)/shard_map/image_inner/pallas_call | solution.py:462
  78.7 3.5 %collective-permute-done.24.refs_1_ = f32[2,8,16,256]{3,2,1,0:T(8,128)S(1)} collective-permute-done((f32[2,8,16,256]{3,2,1,0:T(8,128)S(1)}, f32[2,8,16,256]{3,2,1,0:T(8,128)S(1)}, u32[]{:S(2)}, u32[]{:S(2)}) %collective-permute-start.24) | collective-permute-done | bytes 262176 | tf_op jit(solution)/shard_map/ppermute | solution.py:544
  82.2 0.7 image_outer.1
  (18 shorter events, 0.0 us)
Async XLA Ops:
  0.6 10.4 %copy-start.1 = (f32[8,2,256]{2,1,0:T(2,128)S(1)}, f32[8,2,256]{2,1,0:T(2,128)}, u32[]{:S(2)}) copy-start(f32[8,2,256]{2,1,0:T(2,128)} %traces.3) | copy-start | bytes 49156
  1.9 17.1 %collective-permute-start = (f32[3,4,16,256]{3,2,1,0:T(8,128)S(1)}, f32[3,4,16,256]{3,2,1,0:T(8,128)S(1)}, u32[]{:S(2)}, u32[]{:S(2)}) collective-permute-start(f32[3,4,16,256]{3,2,1,0:T(8,128)S(1)} %get-tuple-element.56), channel_id=1, source_target_pairs={{0,1},{1,0},{2,3},{3,2},{4,5},{5,4},{6,7},{7,6},{8,9},{9,8},{10,11... | collective-permute-start | bytes 589832 | tf_op jit(solution)/shard_map/ppermute | solution.py:60
  5.0 14.0 %collective-permute-start.1 = (f32[3,4,16,256]{3,2,1,0:T(8,128)S(1)}, f32[3,4,16,256]{3,2,1,0:T(8,128)S(1)}, u32[]{:S(2)}, u32[]{:S(2)}) collective-permute-start(f32[3,4,16,256]{3,2,1,0:T(8,128)S(1)} %get-tuple-element.57), channel_id=1, source_target_pairs={{1,2},{2,1},{5,6},{6,5},{9,10},{10,9},{13,14},{14,13},{17,18},{18,... | collective-permute-start | bytes 589832 | tf_op jit(solution)/shard_map/ppermute | solution.py:61
  5.6 5.3 %copy-start.5 = (f32[8,2]{0,1:T(2,128)S(1)}, f32[8,2]{0,1:T(2,128)}, u32[]{:S(2)}) copy-start(f32[8,2]{0,1:T(2,128)} %param.16) | copy-start | bytes 196
  5.7 9.4 %collective-permute-start.8 = (f32[2,4,16,256]{3,2,1,0:T(8,128)S(1)}, f32[2,4,16,256]{3,2,1,0:T(8,128)S(1)}, u32[]{:S(2)}, u32[]{:S(2)}) collective-permute-start(f32[2,4,16,256]{3,2,1,0:T(8,128)S(1)} %get-tuple-element.78), channel_id=1, source_target_pairs={{0,1},{1,0},{2,3},{3,2},{4,5},{5,4},{6,7},{7,6},{8,9},{9,8},{10,11... | collective-permute-start | bytes 393224 | tf_op jit(solution)/shard_map/ppermute | solution.py:60
  10.1 0.9 %copy-start.2 = (s32[2,256]{1,0:T(2,128)S(1)}, s32[2,256]{1,0:T(2,128)}, u32[]{:S(2)}) copy-start(s32[2,256]{1,0:T(2,128)} %receiver_cell.3) | copy-start | bytes 6148
  10.1 0.9 %copy-start.3 = (s32[2]{0:T(128)S(1)}, s32[2]{0:T(128)}, u32[]{:S(2)}) copy-start(s32[2]{0:T(128)} %source_cell.3) | copy-start | bytes 28
  10.1 0.9 %copy-start.4 = (s32[8]{0:T(128)S(1)}, s32[8]{0:T(128)}, u32[]{:S(2)}) copy-start(s32[8]{0:T(128)} %offset_perm.3) | copy-start | bytes 100
  10.1 4.9 %collective-permute-start.9 = (f32[2,4,16,256]{3,2,1,0:T(8,128)S(1)}, f32[2,4,16,256]{3,2,1,0:T(8,128)S(1)}, u32[]{:S(2)}, u32[]{:S(2)}) collective-permute-start(f32[2,4,16,256]{3,2,1,0:T(8,128)S(1)} %get-tuple-element.79), channel_id=1, source_target_pairs={{1,2},{2,1},{5,6},{6,5},{9,10},{10,9},{13,14},{14,13},{17,18},{18,... | collective-permute-start | bytes 393224 | tf_op jit(solution)/shard_map/ppermute | solution.py:61
  13.0 2.0 %copy-start = (f32[16,16,256]{2,1,0:T(8,128)S(1)}, f32[16,16,256]{2,1,0:T(8,128)}, u32[]{:S(2)}) copy-start(f32[16,16,256]{2,1,0:T(8,128)} %courant.5) | copy-start | bytes 786436
  15.8 9.6 %collective-permute-start.10 = (f32[2,8,16,256]{3,2,1,0:T(8,128)S(1)}, f32[2,8,16,256]{3,2,1,0:T(8,128)S(1)}, u32[]{:S(2)}, u32[]{:S(2)}) collective-permute-start(f32[2,8,16,256]{3,2,1,0:T(8,128)S(1)} %get-tuple-element.83), channel_id=1, source_target_pairs={{0,1},{1,0},{2,3},{3,2},{4,5},{5,4},{6,7},{7,6},{8,9},{9,8},{10,11... | collective-permute-start | bytes 786440 | tf_op jit(solution)/shard_map/ppermute | solution.py:60
  18.3 7.2 %collective-permute-start.11 = (f32[2,8,16,256]{3,2,1,0:T(8,128)S(1)}, f32[2,8,16,256]{3,2,1,0:T(8,128)S(1)}, u32[]{:S(2)}, u32[]{:S(2)}) collective-permute-start(f32[2,8,16,256]{3,2,1,0:T(8,128)S(1)} %get-tuple-element.84), channel_id=1, source_target_pairs={{1,2},{2,1},{5,6},{6,5},{9,10},{10,9},{13,14},{14,13},{17,18},{18,... | collective-permute-start | bytes 786440 | tf_op jit(solution)/shard_map/ppermute | solution.py:61
  19.7 11.6 %collective-permute-start.2 = (f32[2,8,16,256]{3,2,1,0:T(8,128)S(1)}, f32[2,8,16,256]{3,2,1,0:T(8,128)S(1)}, u32[]{:S(2)}, u32[]{:S(2)}) collective-permute-start(f32[2,8,16,256]{3,2,1,0:T(8,128)S(1)} %get-tuple-element.63), channel_id=1, source_target_pairs={{0,1},{1,0},{2,3},{3,2},{4,5},{5,4},{6,7},{7,6},{8,9},{9,8},{10,11... | collective-permute-start | bytes 786440 | tf_op jit(solution)/shard_map/ppermute | solution.py:60
  22.8 8.5 %collective-permute-start.3 = (f32[2,8,16,256]{3,2,1,0:T(8,128)S(1)}, f32[2,8,16,256]{3,2,1,0:T(8,128)S(1)}, u32[]{:S(2)}, u32[]{:S(2)}) collective-permute-start(f32[2,8,16,256]{3,2,1,0:T(8,128)S(1)} %get-tuple-element.64), channel_id=1, source_target_pairs={{1,2},{2,1},{5,6},{6,5},{9,10},{10,9},{13,14},{14,13},{17,18},{18,... | collective-permute-start | bytes 786440 | tf_op jit(solution)/shard_map/ppermute | solution.py:61
  26.9 9.9 %collective-permute-start.12 = (f32[2,8,16,256]{3,2,1,0:T(8,128)S(1)}, f32[2,8,16,256]{3,2,1,0:T(8,128)S(1)}, u32[]{:S(2)}, u32[]{:S(2)}) collective-permute-start(f32[2,8,16,256]{3,2,1,0:T(8,128)S(1)} %get-tuple-element.87), channel_id=1, source_target_pairs={{0,1},{1,0},{2,3},{3,2},{4,5},{5,4},{6,7},{7,6},{8,9},{9,8},{10,11... | collective-permute-start | bytes 786440 | tf_op jit(solution)/shard_map/ppermute | solution.py:60
  30.6 6.2 %collective-permute-start.13 = (f32[2,8,16,256]{3,2,1,0:T(8,128)S(1)}, f32[2,8,16,256]{3,2,1,0:T(8,128)S(1)}, u32[]{:S(2)}, u32[]{:S(2)}) collective-permute-start(f32[2,8,16,256]{3,2,1,0:T(8,128)S(1)} %get-tuple-element.88), channel_id=1, source_target_pairs={{1,2},{2,1},{5,6},{6,5},{9,10},{10,9},{13,14},{14,13},{17,18},{18,... | collective-permute-start | bytes 786440 | tf_op jit(solution)/shard_map/ppermute | solution.py:61
  32.8 10.4 %collective-permute-start.4 = (f32[2,8,16,256]{3,2,1,0:T(8,128)S(1)}, f32[2,8,16,256]{3,2,1,0:T(8,128)S(1)}, u32[]{:S(2)}, u32[]{:S(2)}) collective-permute-start(f32[2,8,16,256]{3,2,1,0:T(8,128)S(1)} %get-tuple-element.68), channel_id=1, source_target_pairs={{0,1},{1,0},{2,3},{3,2},{4,5},{5,4},{6,7},{7,6},{8,9},{9,8},{10,11... | collective-permute-start | bytes 786440 | tf_op jit(solution)/shard_map/ppermute | solution.py:60
  36.2 7.1 %collective-permute-start.5 = (f32[2,8,16,256]{3,2,1,0:T(8,128)S(1)}, f32[2,8,16,256]{3,2,1,0:T(8,128)S(1)}, u32[]{:S(2)}, u32[]{:S(2)}) collective-permute-start(f32[2,8,16,256]{3,2,1,0:T(8,128)S(1)} %get-tuple-element.69), channel_id=1, source_target_pairs={{1,2},{2,1},{5,6},{6,5},{9,10},{10,9},{13,14},{14,13},{17,18},{18,... | collective-permute-start | bytes 786440 | tf_op jit(solution)/shard_map/ppermute | solution.py:61
  38.4 11.2 %collective-permute-start.14 = (f32[2,8,16,256]{3,2,1,0:T(8,128)S(1)}, f32[2,8,16,256]{3,2,1,0:T(8,128)S(1)}, u32[]{:S(2)}, u32[]{:S(2)}) collective-permute-start(f32[2,8,16,256]{3,2,1,0:T(8,128)S(1)} %get-tuple-element.91), channel_id=1, source_target_pairs={{0,1},{1,0},{2,3},{3,2},{4,5},{5,4},{6,7},{7,6},{8,9},{9,8},{10,11... | collective-permute-start | bytes 786440 | tf_op jit(solution)/shard_map/ppermute | solution.py:60
  42.6 7.0 %collective-permute-start.15 = (f32[2,8,16,256]{3,2,1,0:T(8,128)S(1)}, f32[2,8,16,256]{3,2,1,0:T(8,128)S(1)}, u32[]{:S(2)}, u32[]{:S(2)}) collective-permute-start(f32[2,8,16,256]{3,2,1,0:T(8,128)S(1)} %get-tuple-element.92), channel_id=1, source_target_pairs={{1,2},{2,1},{5,6},{6,5},{9,10},{10,9},{13,14},{14,13},{17,18},{18,... | collective-permute-start | bytes 786440 | tf_op jit(solution)/shard_map/ppermute | solution.py:61
  44.8 8.2 %collective-permute-start.6 = (f32[2,8,16,256]{3,2,1,0:T(8,128)S(1)}, f32[2,8,16,256]{3,2,1,0:T(8,128)S(1)}, u32[]{:S(2)}, u32[]{:S(2)}) collective-permute-start(f32[2,8,16,256]{3,2,1,0:T(8,128)S(1)} %get-tuple-element.72), channel_id=1, source_target_pairs={{0,1},{1,0},{2,3},{3,2},{4,5},{5,4},{6,7},{7,6},{8,9},{9,8},{10,11... | collective-permute-start | bytes 786440 | tf_op jit(solution)/shard_map/ppermute | solution.py:60
  48.6 4.4 %collective-permute-start.7 = (f32[2,8,16,256]{3,2,1,0:T(8,128)S(1)}, f32[2,8,16,256]{3,2,1,0:T(8,128)S(1)}, u32[]{:S(2)}, u32[]{:S(2)}) collective-permute-start(f32[2,8,16,256]{3,2,1,0:T(8,128)S(1)} %get-tuple-element.73), channel_id=1, source_target_pairs={{1,2},{2,1},{5,6},{6,5},{9,10},{10,9},{13,14},{14,13},{17,18},{18,... | collective-permute-start | bytes 786440 | tf_op jit(solution)/shard_map/ppermute | solution.py:61
  54.8 12.4 %collective-permute-start.16 = (f32[4,8,16,256]{3,2,1,0:T(8,128)S(1)}, f32[4,8,16,256]{3,2,1,0:T(8,128)S(1)}, u32[]{:S(2)}, u32[]{:S(2)}) collective-permute-start(f32[4,8,16,256]{3,2,1,0:T(8,128)S(1)} %shard_map.132.refs_0_), channel_id=1, source_target_pairs={{0,4},{4,0},{8,12},{12,8},{1,5},{5,1},{9,13},{13,9},{2,6},{6,2},{1... | collective-permute-start | bytes 1572872 | tf_op jit(solution)/shard_map/ppermute | solution.py:537
  54.9 8.7 %collective-permute-start.17 = (f32[2,4,16,256]{3,2,1,0:T(8,128)S(1)}, f32[2,4,16,256]{3,2,1,0:T(8,128)S(1)}, u32[]{:S(2)}, u32[]{:S(2)}) collective-permute-start(f32[2,4,16,256]{3,2,1,0:T(8,128)S(1)} %get-tuple-element.95), channel_id=1, source_target_pairs={{0,1},{1,0},{2,3},{3,2},{4,5},{5,4},{6,7},{7,6},{8,9},{9,8},{10,11... | collective-permute-start | bytes 393224 | tf_op jit(solution)/shard_map/ppermute | solution.py:60
  58.9 4.7 %collective-permute-start.18 = (f32[2,4,16,256]{3,2,1,0:T(8,128)S(1)}, f32[2,4,16,256]{3,2,1,0:T(8,128)S(1)}, u32[]{:S(2)}, u32[]{:S(2)}) collective-permute-start(f32[2,4,16,256]{3,2,1,0:T(8,128)S(1)} %get-tuple-element.96), channel_id=1, source_target_pairs={{1,2},{2,1},{5,6},{6,5},{9,10},{10,9},{13,14},{14,13},{17,18},{18,... | collective-permute-start | bytes 393224 | tf_op jit(solution)/shard_map/ppermute | solution.py:61
  59.6 7.1 %collective-permute-start.19 = (f32[2,4,16,256]{3,2,1,0:T(8,128)S(1)}, f32[2,4,16,256]{3,2,1,0:T(8,128)S(1)}, u32[]{:S(2)}, u32[]{:S(2)}) collective-permute-start(f32[2,4,16,256]{3,2,1,0:T(8,128)S(1)} %get-tuple-element.97), channel_id=1, source_target_pairs={{0,1},{1,0},{2,3},{3,2},{4,5},{5,4},{6,7},{7,6},{8,9},{9,8},{10,11... | collective-permute-start | bytes 393224 | tf_op jit(solution)/shard_map/ppermute | solution.py:60
  62.9 3.8 %collective-permute-start.20 = (f32[2,4,16,256]{3,2,1,0:T(8,128)S(1)}, f32[2,4,16,256]{3,2,1,0:T(8,128)S(1)}, u32[]{:S(2)}, u32[]{:S(2)}) collective-permute-start(f32[2,4,16,256]{3,2,1,0:T(8,128)S(1)} %get-tuple-element.98), channel_id=1, source_target_pairs={{1,2},{2,1},{5,6},{6,5},{9,10},{10,9},{13,14},{14,13},{17,18},{18,... | collective-permute-start | bytes 393224 | tf_op jit(solution)/shard_map/ppermute | solution.py:61
  64.1 5.4 %collective-permute-start.21 = (f32[2,8,16,256]{3,2,1,0:T(8,128)S(1)}, f32[2,8,16,256]{3,2,1,0:T(8,128)S(1)}, u32[]{:S(2)}, u32[]{:S(2)}) collective-permute-start(f32[2,8,16,256]{3,2,1,0:T(8,128)S(1)} %shard_map.133.refs_2_.refs_0_), channel_id=1, source_target_pairs={{0,4},{4,0},{8,12},{12,8},{1,5},{5,1},{9,13},{13,9},{2,6},{6,2},{1... | collective-permute-start | bytes 786440 | tf_op jit(solution)/shard_map/ppermute | solution.py:537
  67.2 2.3 %collective-permute-start.22 = (f32[2,8,16,256]{3,2,1,0:T(8,128)S(1)}, f32[2,8,16,256]{3,2,1,0:T(8,128)S(1)}, u32[]{:S(2)}, u32[]{:S(2)}) collective-permute-start(f32[2,8,16,256]{3,2,1,0:T(8,128)S(1)} %shard_map.134.refs_3_.refs_1_), channel_id=1, source_target_pairs={{0,4},{4,0},{8,12},{12,8},{1,5},{5,1},{9,13},{13,9},{2,6},{6,2},{1... | collective-permute-start | bytes 786440 | tf_op jit(solution)/shard_map/ppermute | solution.py:537
  68.0 9.2 %collective-permute-start.23 = (f32[2,8,16,256]{3,2,1,0:T(8,128)S(1)}, f32[2,8,16,256]{3,2,1,0:T(8,128)S(1)}, u32[]{:S(2)}, u32[]{:S(2)}) collective-permute-start(f32[2,8,16,256]{3,2,1,0:T(8,128)S(1)} %shard_map.135), channel_id=1, source_target_pairs={{0,8},{4,12},{8,0},{12,4},{1,9},{5,13},{9,1},{13,5},{2,10},{6,14},... | collective-permute-start | bytes 786440 | tf_op jit(solution)/shard_map/ppermute | solution.py:544
  70.2 12.0 %collective-permute-start.24 = (f32[2,8,16,256]{3,2,1,0:T(8,128)S(1)}, f32[2,8,16,256]{3,2,1,0:T(8,128)S(1)}, u32[]{:S(2)}, u32[]{:S(2)}) collective-permute-start(f32[2,8,16,256]{3,2,1,0:T(8,128)S(1)} %shard_map.136), channel_id=1, source_target_pairs={{0,8},{4,12},{8,0},{12,4},{1,9},{5,13},{9,1},{13,5},{2,10},{6,14},... | collective-permute-start | bytes 786440 | tf_op jit(solution)/shard_map/ppermute | solution.py:544

commit v7 on v6

--- a/solution.py
+++ b/solution.py
@@ -126,23 +126,29 @@
     return copies
 
 
-def prepare_kernel(group, rows, source_cell, wavelet, offset_perm, receiver_cell, traces, source, receiver, source_before, receiver_before, planes, now, before, *refs):
+def prepare_kernel(group, rows, count, source_cell, wavelet, *refs):
+    prepare_shot(group, rows, refs[:count], source_cell, wavelet, *refs[count:])
+
+
+def prepare_shot(group, rows, offsets, source_cell, wavelet, receiver_cell, traces, source, receiver, source_before, receiver_before, planes, now, before, *refs):
     tables, sem = refs[:-1], refs[-1]
     pieces = [(source.at[group], now.at[0]), (receiver.at[group], now.at[1])]
     pieces += [(source_before.at[group], before.at[0]), (receiver_before.at[group], before.at[1])]
     copies = fetch(pieces, sem)
-    if tables:
-        make_tables(planes.shape[2], offset_perm, *tables)
+    if offsets:
+        (offset_perm,), lags = offsets, tables[-1]
+        for slot in range(offset_perm.shape[0]):
+            lags[slot : slot + 1, :] = jnp.full((1, LANES), offset_perm[slot], jnp.int32)
+    if group == 0:
+        make_bands(planes.shape[2], *tables[:2])
     spread_data(group, rows, source_cell, wavelet, receiver_cell, traces, planes)
     for copy in copies:
         copy.wait()
 
 
-def make_tables(size_y, offset_perm, along_z, along_y, lags):
+def make_bands(size_y, along_z, along_y):
     size_z = along_z.shape[0]
     block = along_y.shape[0]
-    for slot in range(offset_perm.shape[0]):
-        lags[slot : slot + 1, :] = jnp.full((1, LANES), offset_perm[slot], jnp.int32)
     row = lax.broadcasted_iota(jnp.int32, (size_z, size_z), 0)
     col = lax.broadcasted_iota(jnp.int32, (size_z, size_z), 1)
     along_z[...] = band(jnp.abs(row - col)).astype(jnp.bfloat16)
@@ -196,16 +202,18 @@
         shapes += [
             struct((size_z, size_z), jnp.bfloat16),
             struct((block, 2 * block), jnp.bfloat16),
-            struct((offset_perm.shape[0], LANES), jnp.int32),
         ]
-    return pl.pallas_call(
-        functools.partial(prepare_kernel, group, rows),
+    offsets = (offset_perm,) if group == source_cell.shape[0] - 1 else ()
+    if offsets:
+        shapes.append(struct((offset_perm.shape[0], LANES), jnp.int32))
+    return pl.pallas_call(
+        functools.partial(prepare_kernel, group, rows, len(offsets)),
         out_shape=shapes,
-        in_specs=[smem()] * 3 + [vmem()] * 2 + [hbm()] * 4,
+        in_specs=[smem()] * (2 + len(offsets)) + [vmem()] * 2 + [hbm()] * 4,
         out_specs=[vmem()] * len(shapes),
         scratch_shapes=[pltpu.SemaphoreType.DMA((4,))],
         compiler_params=params(),
-    )(source_cell, wavelet, offset_perm, receiver_cell, traces, *stay(*fields))
+    )(source_cell, wavelet, *offsets, receiver_cell, traces, *stay(*fields))
 
 
 def advance(now, at, before, before_at, courant, courant_at, inject, inject_at, runs, step, along_z, along_y, write):
@@ -513,7 +521,8 @@
     for g in everyone:
         inject[g], now[g], before[g], *tables = prepare(g, source_cell, wavelet, offset_perm, receiver_cell, traces, fields)
         if g == 0:
-            along_z, along_y, lags = tables
+            along_z, along_y = tables[:2]
+    lags = tables[-1]
 
     halos = [None] * groups
     for g in everyone:

time: 84.3 us -> 84.3 us (level)
  no operation moved by 1% of the time
where the time goes in v7:
time: 84.3 us; the launch traced here: 83.1 us
  starting transfers between devices  45.1 us (53%)
  Pallas kernels  20.8 us (25%)
  waiting for transfers between devices  16 us (19%)
  between operations  1.16 us (1%)
    ppermute x10, starting transfers between devices, trade(): even = lax.ppermute(even_edge, 'slab', even_pairs(count))  35.6 us
    ppermute x2, waiting for transfers between devices, part_sums(): sums.append(lax.ppermute(part, 'shot', route))  9.69 us
    pallas_call x6, Pallas kernels, pair_round(): pl.pallas_call(functools.partial(pair_kernel, rows, step, width), out_sha...  8.84 us
    ppermute x10, starting transfers between devices, trade(): odd = lax.ppermute(odd_edge, 'slab', odd_pairs(count))  6.94 us
    ppermute x10, waiting for transfers between devices, trade(): even = lax.ppermute(even_edge, 'slab', even_pairs(count))  6.25 us
    pallas_call x2, Pallas kernels, prepare(): pl.pallas_call(functools.partial(prepare_kernel, group, rows, len(offsets...  3.98 us
    ppermute x2, starting transfers between devices, part_sums(): sums.append(lax.ppermute(part, 'shot', route))  2.35 us
  transfers between devices with their start and end apart: 25, of which 5 were waited for; matrix products, arithmetic and copies ran while one was open for 0% of the time, Pallas kernels for 21%

profile of v7, /device:TPU:0, one launch (start us, length us, event | category | flops | bytes accessed | tf_op | source)
XLA Modules:
  0.0 83.1 jit_solution(11340376788465214434)
XLA Ops:
  0.6 1.2 %pack.1 = (f32[2,4,16,256]{3,2,1,0:T(8,128)S(1)}, f32[2,4,16,256]{3,2,1,0:T(8,128)S(1)}, f32[3,4,16,256]{3,2,1,0:T(8,128)S(1)}, f32[3,4,16,256]{3,2,1,0:T(8,128)S(1)}) custom-call(f32[2,16,16,256]{3,2,1,0:T(8,128)} %refs_2_.3, f32[2,16,16,256]{3,2,1,0:T(8,128)} %refs_3_.3, f32[16,16,256]{2,1,0:T(8,128)} %courant.5), custom_call_target="tpu_custom_call" | custom-call | tf_op jit(solution)/shard_map/pack/pallas_call | solution.py:104
  1.9 3.1 %collective-permute-start = (f32[3,4,16,256]{3,2,1,0:T(8,128)S(1)}, f32[3,4,16,256]{3,2,1,0:T(8,128)S(1)}, u32[]{:S(2)}, u32[]{:S(2)}) collective-permute-start(f32[3,4,16,256]{3,2,1,0:T(8,128)S(1)} %get-tuple-element.56), channel_id=1, source_target_pairs={{0,1},{1,0},{2,3},{3,2},{4,5},{5,4},{6,7},{7,6},{8,9},{9,8},{10,11... | collective-permute-start | bytes 589832 | tf_op jit(solution)/shard_map/ppermute | solution.py:60
  5.0 0.7 collective-permute-start.1
  5.6 0.0 copy-start.5
  5.7 4.5 %collective-permute-start.8 = (f32[2,4,16,256]{3,2,1,0:T(8,128)S(1)}, f32[2,4,16,256]{3,2,1,0:T(8,128)S(1)}, u32[]{:S(2)}, u32[]{:S(2)}) collective-permute-start(f32[2,4,16,256]{3,2,1,0:T(8,128)S(1)} %get-tuple-element.78), channel_id=1, source_target_pairs={{0,1},{1,0},{2,3},{3,2},{4,5},{5,4},{6,7},{7,6},{8,9},{9,8},{10,11... | collective-permute-start | bytes 393224 | tf_op jit(solution)/shard_map/ppermute | solution.py:60
  10.1 0.8 collective-permute-start.9
  10.9 0.1 copy.15.wavelet
  11.0 2.0 %shard_map.122 = (f32[2,24,16,128]{3,2,1,0:T(8,128)S(1)}, f32[2,16,16,256]{3,2,1,0:T(8,128)S(1)}, f32[2,16,16,256]{3,2,1,0:T(8,128)S(1)}, bf16[256,256]{1,0:T(8,128)(2,1)S(1)}, bf16[128,256]{1,0:T(8,128)(2,1)S(1)}) custom-call(s32[2]{0:T(128)S(1)} %copy-done.3, f32[8,2]{1,0:T(8,128)S(1)} %copy.15.wavelet, s32[2,256]{1,0:T(2,128)S(1)} %copy-done.2, ...), custom_call_target="tpu_custom_call" | custom-call | tf_op jit(solution)/shard_map/pallas_call | solution.py:209
  13.0 0.0 copy-start
  13.0 2.0 %shard_map.121 = (f32[2,24,16,128]{3,2,1,0:T(8,128)S(1)}, f32[2,16,16,256]{3,2,1,0:T(8,128)S(1)}, f32[2,16,16,256]{3,2,1,0:T(8,128)S(1)}, s32[8,128]{1,0:T(8,128)S(1)}) custom-call(s32[2]{0:T(128)S(1)} %copy-done.3, f32[8,2]{1,0:T(8,128)S(1)} %copy.15.wavelet, s32[8]{0:T(128)S(1)} %copy-done.4, s32[2,256]{1,0:T(2,128)S(1)} %copy-done.2, ...), custom_call_target="tpu_custom_call" | custom-call | tf_op jit(solution)/shard_map/pallas_call | solution.py:209
  15.0 0.0 collective-permute-done.8.even
  15.1 0.0 collective-permute-done.9.odd
  15.1 0.7 shard_map.127
  15.8 2.4 %collective-permute-start.10 = (f32[2,8,16,256]{3,2,1,0:T(8,128)S(1)}, f32[2,8,16,256]{3,2,1,0:T(8,128)S(1)}, u32[]{:S(2)}, u32[]{:S(2)}) collective-permute-start(f32[2,8,16,256]{3,2,1,0:T(8,128)S(1)} %get-tuple-element.83), channel_id=1, source_target_pairs={{0,1},{1,0},{2,3},{3,2},{4,5},{5,4},{6,7},{7,6},{8,9},{9,8},{10,11... | collective-permute-start | bytes 786440 | tf_op jit(solution)/shard_map/ppermute | solution.py:60
  18.3 0.7 collective-permute-start.11
  18.9 0.0 collective-permute-done.even
  18.9 0.0 collective-permute-done.1.odd
  19.0 0.8 shard_map.123
  19.7 3.1 %collective-permute-start.2 = (f32[2,8,16,256]{3,2,1,0:T(8,128)S(1)}, f32[2,8,16,256]{3,2,1,0:T(8,128)S(1)}, u32[]{:S(2)}, u32[]{:S(2)}) collective-permute-start(f32[2,8,16,256]{3,2,1,0:T(8,128)S(1)} %get-tuple-element.63), channel_id=1, source_target_pairs={{0,1},{1,0},{2,3},{3,2},{4,5},{5,4},{6,7},{7,6},{8,9},{9,8},{10,11... | collective-permute-start | bytes 786440 | tf_op jit(solution)/shard_map/ppermute | solution.py:60
  22.8 0.7 collective-permute-start.3
  23.4 2.0 %collective-permute-done.10.even = f32[2,8,16,256]{3,2,1,0:T(8,128)S(1)} collective-permute-done((f32[2,8,16,256]{3,2,1,0:T(8,128)S(1)}, f32[2,8,16,256]{3,2,1,0:T(8,128)S(1)}, u32[]{:S(2)}, u32[]{:S(2)}) %collective-permute-start.10) | collective-permute-done | bytes 262176 | tf_op jit(solution)/shard_map/ppermute | solution.py:60
  25.4 0.0 collective-permute-done.11.odd
  25.4 1.5 %shard_map.128 = (f32[2,16,16,256]{3,2,1,0:T(8,128)S(1)}, f32[2,24,16,256]{3,2,1,0:T(8,128)S(1)}, f32[2,8,16,256]{3,2,1,0:T(8,128)S(1)}, f32[2,8,16,256]{3,2,1,0:T(8,128)S(1)}) custom-call(f32[2,16,16,256]{3,2,1,0:T(8,128)S(1)} %get-tuple-element.81.now, f32[2,24,16,256]{3,2,1,0:T(8,128)S(1)} %get-tuple-element.82.before, ...), custom_call_target="tpu_custom_call" | custom-call | tf_op jit(solution)/shard_map/pallas_call | solution.py:322
  26.9 4.0 %collective-permute-start.12 = (f32[2,8,16,256]{3,2,1,0:T(8,128)S(1)}, f32[2,8,16,256]{3,2,1,0:T(8,128)S(1)}, u32[]{:S(2)}, u32[]{:S(2)}) collective-permute-start(f32[2,8,16,256]{3,2,1,0:T(8,128)S(1)} %get-tuple-element.87), channel_id=1, source_target_pairs={{0,1},{1,0},{2,3},{3,2},{4,5},{5,4},{6,7},{7,6},{8,9},{9,8},{10,11... | collective-permute-start | bytes 786440 | tf_op jit(solution)/shard_map/ppermute | solution.py:60
  30.9 0.7 collective-permute-start.13
  31.6 0.0 collective-permute-done.3.odd
  31.6 1.5 %shard_map.124 = (f32[2,16,16,256]{3,2,1,0:T(8,128)S(1)}, f32[2,24,16,256]{3,2,1,0:T(8,128)S(1)}, f32[2,8,16,256]{3,2,1,0:T(8,128)S(1)}, f32[2,8,16,256]{3,2,1,0:T(8,128)S(1)}) custom-call(f32[2,16,16,256]{3,2,1,0:T(8,128)S(1)} %get-tuple-element.61.now, f32[2,24,16,256]{3,2,1,0:T(8,128)S(1)} %get-tuple-element.62.before, ...), custom_call_target="tpu_custom_call" | custom-call | tf_op jit(solution)/shard_map/pallas_call | solution.py:322
  33.1 3.1 %collective-permute-start.4 = (f32[2,8,16,256]{3,2,1,0:T(8,128)S(1)}, f32[2,8,16,256]{3,2,1,0:T(8,128)S(1)}, u32[]{:S(2)}, u32[]{:S(2)}) collective-permute-start(f32[2,8,16,256]{3,2,1,0:T(8,128)S(1)} %get-tuple-element.68), channel_id=1, source_target_pairs={{0,1},{1,0},{2,3},{3,2},{4,5},{5,4},{6,7},{7,6},{8,9},{9,8},{10,11... | collective-permute-start | bytes 786440 | tf_op jit(solution)/shard_map/ppermute | solution.py:60
  36.2 0.7 collective-permute-start.5
  36.8 0.0 collective-permute-done.12.even
  36.9 1.5 %shard_map.129 = (f32[2,16,16,256]{3,2,1,0:T(8,128)S(1)}, f32[2,24,16,256]{3,2,1,0:T(8,128)S(1)}, f32[2,8,16,256]{3,2,1,0:T(8,128)S(1)}, f32[2,8,16,256]{3,2,1,0:T(8,128)S(1)}) custom-call(f32[2,16,16,256]{3,2,1,0:T(8,128)S(1)} %get-tuple-element.85.now, f32[2,24,16,256]{3,2,1,0:T(8,128)S(1)} %get-tuple-element.86.before, ...), custom_call_target="tpu_custom_call" | custom-call | tf_op jit(solution)/shard_map/pallas_call | solution.py:322
  38.4 4.2 %collective-permute-start.14 = (f32[2,8,16,256]{3,2,1,0:T(8,128)S(1)}, f32[2,8,16,256]{3,2,1,0:T(8,128)S(1)}, u32[]{:S(2)}, u32[]{:S(2)}) collective-permute-start(f32[2,8,16,256]{3,2,1,0:T(8,128)S(1)} %get-tuple-element.91), channel_id=1, source_target_pairs={{0,1},{1,0},{2,3},{3,2},{4,5},{5,4},{6,7},{7,6},{8,9},{9,8},{10,11... | collective-permute-start | bytes 786440 | tf_op jit(solution)/shard_map/ppermute | solution.py:60
  42.6 0.7 collective-permute-start.15
  43.3 0.0 collective-permute-done.4.even
  43.3 1.5 %shard_map.125 = (f32[2,16,16,256]{3,2,1,0:T(8,128)S(1)}, f32[2,24,16,256]{3,2,1,0:T(8,128)S(1)}, f32[2,8,16,256]{3,2,1,0:T(8,128)S(1)}, f32[2,8,16,256]{3,2,1,0:T(8,128)S(1)}) custom-call(f32[2,16,16,256]{3,2,1,0:T(8,128)S(1)} %get-tuple-element.66.now, f32[2,24,16,256]{3,2,1,0:T(8,128)S(1)} %get-tuple-element.67.before, ...), custom_call_target="tpu_custom_call" | custom-call | tf_op jit(solution)/shard_map/pallas_call | solution.py:322
  44.8 4.0 %collective-permute-start.6 = (f32[2,8,16,256]{3,2,1,0:T(8,128)S(1)}, f32[2,8,16,256]{3,2,1,0:T(8,128)S(1)}, u32[]{:S(2)}, u32[]{:S(2)}) collective-permute-start(f32[2,8,16,256]{3,2,1,0:T(8,128)S(1)} %get-tuple-element.72), channel_id=1, source_target_pairs={{0,1},{1,0},{2,3},{3,2},{4,5},{5,4},{6,7},{7,6},{8,9},{9,8},{10,11... | collective-permute-start | bytes 786440 | tf_op jit(solution)/shard_map/ppermute | solution.py:60
  48.8 0.8 %collective-permute-start.7 = (f32[2,8,16,256]{3,2,1,0:T(8,128)S(1)}, f32[2,8,16,256]{3,2,1,0:T(8,128)S(1)}, u32[]{:S(2)}, u32[]{:S(2)}) collective-permute-start(f32[2,8,16,256]{3,2,1,0:T(8,128)S(1)} %get-tuple-element.73), channel_id=1, source_target_pairs={{1,2},{2,1},{5,6},{6,5},{9,10},{10,9},{13,14},{14,13},{17,18},{18,... | collective-permute-start | bytes 786440 | tf_op jit(solution)/shard_map/ppermute | solution.py:61
  49.7 0.0 collective-permute-done.14.even
  49.7 1.4 %shard_map.130 = (f32[2,16,16,256]{3,2,1,0:T(8,128)S(1)}, f32[2,24,16,256]{3,2,1,0:T(8,128)S(1)}, f32[2,4,16,256]{3,2,1,0:T(8,128)S(1)}, f32[2,4,16,256]{3,2,1,0:T(8,128)S(1)}) custom-call(f32[2,16,16,256]{3,2,1,0:T(8,128)S(1)} %get-tuple-element.89.now, f32[2,24,16,256]{3,2,1,0:T(8,128)S(1)} %get-tuple-element.90.before, ...), custom_call_target="tpu_custom_call" | custom-call | tf_op jit(solution)/shard_map/pallas_call | solution.py:322
  51.1 0.4 shard_map.131.refs_0_
  51.5 1.6 %collective-permute-done.6.even = f32[2,8,16,256]{3,2,1,0:T(8,128)S(1)} collective-permute-done((f32[2,8,16,256]{3,2,1,0:T(8,128)S(1)}, f32[2,8,16,256]{3,2,1,0:T(8,128)S(1)}, u32[]{:S(2)}, u32[]{:S(2)}) %collective-permute-start.6) | collective-permute-done | bytes 262176 | tf_op jit(solution)/shard_map/ppermute | solution.py:60
  53.2 0.0 collective-permute-done.7.odd
  53.2 1.4 %shard_map.126 = (f32[2,16,16,256]{3,2,1,0:T(8,128)S(1)}, f32[2,24,16,256]{3,2,1,0:T(8,128)S(1)}, f32[2,4,16,256]{3,2,1,0:T(8,128)S(1)}, f32[2,4,16,256]{3,2,1,0:T(8,128)S(1)}) custom-call(f32[2,16,16,256]{3,2,1,0:T(8,128)S(1)} %get-tuple-element.70.now, f32[2,24,16,256]{3,2,1,0:T(8,128)S(1)} %get-tuple-element.71.before, ...), custom_call_target="tpu_custom_call" | custom-call | tf_op jit(solution)/shard_map/pallas_call | solution.py:322
  54.6 0.4 shard_map.132.refs_0_
  55.0 0.1 collective-permute-start.16
  55.1 4.0 %collective-permute-start.17 = (f32[2,4,16,256]{3,2,1,0:T(8,128)S(1)}, f32[2,4,16,256]{3,2,1,0:T(8,128)S(1)}, u32[]{:S(2)}, u32[]{:S(2)}) collective-permute-start(f32[2,4,16,256]{3,2,1,0:T(8,128)S(1)} %get-tuple-element.95), channel_id=1, source_target_pairs={{0,1},{1,0},{2,3},{3,2},{4,5},{5,4},{6,7},{7,6},{8,9},{9,8},{10,11... | collective-permute-start | bytes 393224 | tf_op jit(solution)/shard_map/ppermute | solution.py:60
  59.1 0.7 collective-permute-start.18
  59.7 3.2 %collective-permute-start.19 = (f32[2,4,16,256]{3,2,1,0:T(8,128)S(1)}, f32[2,4,16,256]{3,2,1,0:T(8,128)S(1)}, u32[]{:S(2)}, u32[]{:S(2)}) collective-permute-start(f32[2,4,16,256]{3,2,1,0:T(8,128)S(1)} %get-tuple-element.97), channel_id=1, source_target_pairs={{0,1},{1,0},{2,3},{3,2},{4,5},{5,4},{6,7},{7,6},{8,9},{9,8},{10,11... | collective-permute-start | bytes 393224 | tf_op jit(solution)/shard_map/ppermute | solution.py:60
  62.9 0.7 collective-permute-start.20
  63.6 0.0 collective-permute-done.17.even
  63.6 0.4 shard_map.133.refs_2_.refs_0_
  64.1 0.1 collective-permute-start.21
  64.1 2.6 %collective-permute-done.19.even = f32[2,4,16,256]{3,2,1,0:T(8,128)S(1)} collective-permute-done((f32[2,4,16,256]{3,2,1,0:T(8,128)S(1)}, f32[2,4,16,256]{3,2,1,0:T(8,128)S(1)}, u32[]{:S(2)}, u32[]{:S(2)}) %collective-permute-start.19) | collective-permute-done | bytes 131104 | tf_op jit(solution)/shard_map/ppermute | solution.py:60
  66.7 0.4 shard_map.134.refs_3_.refs_1_
  67.2 0.1 collective-permute-start.22
  67.2 0.0 collective-permute-done.16.refs_1_
  67.3 0.7 shard_map.135
  68.0 1.5 %collective-permute-start.23 = (f32[2,8,16,256]{3,2,1,0:T(8,128)S(1)}, f32[2,8,16,256]{3,2,1,0:T(8,128)S(1)}, u32[]{:S(2)}, u32[]{:S(2)}) collective-permute-start(f32[2,8,16,256]{3,2,1,0:T(8,128)S(1)} %shard_map.135), channel_id=1, source_target_pairs={{0,8},{4,12},{8,0},{12,4},{1,9},{5,13},{9,1},{13,5},{2,10},{6,14},... | collective-permute-start | bytes 786440 | tf_op jit(solution)/shard_map/ppermute | solution.py:553
  69.5 0.7 shard_map.136
  70.2 0.8 collective-permute-start.24
  71.0 6.2 %collective-permute-done.23.refs_6_ = f32[2,8,16,256]{3,2,1,0:T(8,128)S(1)} collective-permute-done((f32[2,8,16,256]{3,2,1,0:T(8,128)S(1)}, f32[2,8,16,256]{3,2,1,0:T(8,128)S(1)}, u32[]{:S(2)}, u32[]{:S(2)}) %collective-permute-start.23) | collective-permute-done | bytes 262176 | tf_op jit(solution)/shard_map/ppermute | solution.py:553
  77.2 1.5 %image_inner.1 = (f32[2,16,16,256]{3,2,1,0:T(8,128)}, f32[2,16,16,256]{3,2,1,0:T(8,128)}, f32[2,16,16,256]{3,2,1,0:T(8,128)}, f32[2,8,16,256]{3,2,1,0:T(8,128)S(1)}) custom-call(s32[8,128]{1,0:T(8,128)S(1)} %get-tuple-element.53.lags, f32[4,8,16,256]{3,2,1,0:T(8,128)S(1)} %shard_map.132.refs_0_, f32[4,8,16,256]{3,2,1,0:T(8,128)S(1)} %collective-permute-done.16.refs_1_, ...), custom_call_target="tpu_custom_call" | custom-call | tf_op jit(solution)/shard_map/image_inner/pallas_call | solution.py:470
  78.7 3.5 %collective-permute-done.24.refs_1_ = f32[2,8,16,256]{3,2,1,0:T(8,128)S(1)} collective-permute-done((f32[2,8,16,256]{3,2,1,0:T(8,128)S(1)}, f32[2,8,16,256]{3,2,1,0:T(8,128)S(1)}, u32[]{:S(2)}, u32[]{:S(2)}) %collective-permute-start.24) | collective-permute-done | bytes 262176 | tf_op jit(solution)/shard_map/ppermute | solution.py:553
  82.2 0.7 image_outer.1
  (18 shorter events, 0.0 us)
Async XLA Ops:
  0.6 10.4 %copy-start.1 = (f32[8,2,256]{2,1,0:T(2,128)S(1)}, f32[8,2,256]{2,1,0:T(2,128)}, u32[]{:S(2)}) copy-start(f32[8,2,256]{2,1,0:T(2,128)} %refs_1_.3) | copy-start | bytes 49156
  1.9 17.1 %collective-permute-start = (f32[3,4,16,256]{3,2,1,0:T(8,128)S(1)}, f32[3,4,16,256]{3,2,1,0:T(8,128)S(1)}, u32[]{:S(2)}, u32[]{:S(2)}) collective-permute-start(f32[3,4,16,256]{3,2,1,0:T(8,128)S(1)} %get-tuple-element.56), channel_id=1, source_target_pairs={{0,1},{1,0},{2,3},{3,2},{4,5},{5,4},{6,7},{7,6},{8,9},{9,8},{10,11... | collective-permute-start | bytes 589832 | tf_op jit(solution)/shard_map/ppermute | solution.py:60
  5.0 14.0 %collective-permute-start.1 = (f32[3,4,16,256]{3,2,1,0:T(8,128)S(1)}, f32[3,4,16,256]{3,2,1,0:T(8,128)S(1)}, u32[]{:S(2)}, u32[]{:S(2)}) collective-permute-start(f32[3,4,16,256]{3,2,1,0:T(8,128)S(1)} %get-tuple-element.57), channel_id=1, source_target_pairs={{1,2},{2,1},{5,6},{6,5},{9,10},{10,9},{13,14},{14,13},{17,18},{18,... | collective-permute-start | bytes 589832 | tf_op jit(solution)/shard_map/ppermute | solution.py:61
  5.6 5.3 %copy-start.5 = (f32[8,2]{0,1:T(2,128)S(1)}, f32[8,2]{0,1:T(2,128)}, u32[]{:S(2)}) copy-start(f32[8,2]{0,1:T(2,128)} %param.16) | copy-start | bytes 196
  5.7 9.4 %collective-permute-start.8 = (f32[2,4,16,256]{3,2,1,0:T(8,128)S(1)}, f32[2,4,16,256]{3,2,1,0:T(8,128)S(1)}, u32[]{:S(2)}, u32[]{:S(2)}) collective-permute-start(f32[2,4,16,256]{3,2,1,0:T(8,128)S(1)} %get-tuple-element.78), channel_id=1, source_target_pairs={{0,1},{1,0},{2,3},{3,2},{4,5},{5,4},{6,7},{7,6},{8,9},{9,8},{10,11... | collective-permute-start | bytes 393224 | tf_op jit(solution)/shard_map/ppermute | solution.py:60
  10.1 0.9 %copy-start.2 = (s32[2,256]{1,0:T(2,128)S(1)}, s32[2,256]{1,0:T(2,128)}, u32[]{:S(2)}) copy-start(s32[2,256]{1,0:T(2,128)} %refs_0_.3) | copy-start | bytes 6148
  10.1 0.9 %copy-start.3 = (s32[2]{0:T(128)S(1)}, s32[2]{0:T(128)}, u32[]{:S(2)}) copy-start(s32[2]{0:T(128)} %source_cell.3) | copy-start | bytes 28
  10.1 4.9 %collective-permute-start.9 = (f32[2,4,16,256]{3,2,1,0:T(8,128)S(1)}, f32[2,4,16,256]{3,2,1,0:T(8,128)S(1)}, u32[]{:S(2)}, u32[]{:S(2)}) collective-permute-start(f32[2,4,16,256]{3,2,1,0:T(8,128)S(1)} %get-tuple-element.79), channel_id=1, source_target_pairs={{1,2},{2,1},{5,6},{6,5},{9,10},{10,9},{13,14},{14,13},{17,18},{18,... | collective-permute-start | bytes 393224 | tf_op jit(solution)/shard_map/ppermute | solution.py:61
  11.0 2.0 %copy-start.4 = (s32[8]{0:T(128)S(1)}, s32[8]{0:T(128)}, u32[]{:S(2)}) copy-start(s32[8]{0:T(128)} %refs_0_.2) | copy-start | bytes 100
  13.0 2.0 %copy-start = (f32[16,16,256]{2,1,0:T(8,128)S(1)}, f32[16,16,256]{2,1,0:T(8,128)}, u32[]{:S(2)}) copy-start(f32[16,16,256]{2,1,0:T(8,128)} %courant.5) | copy-start | bytes 786436
  15.8 9.6 %collective-permute-start.10 = (f32[2,8,16,256]{3,2,1,0:T(8,128)S(1)}, f32[2,8,16,256]{3,2,1,0:T(8,128)S(1)}, u32[]{:S(2)}, u32[]{:S(2)}) collective-permute-start(f32[2,8,16,256]{3,2,1,0:T(8,128)S(1)} %get-tuple-element.83), channel_id=1, source_target_pairs={{0,1},{1,0},{2,3},{3,2},{4,5},{5,4},{6,7},{7,6},{8,9},{9,8},{10,11... | collective-permute-start | bytes 786440 | tf_op jit(solution)/shard_map/ppermute | solution.py:60
  18.3 7.2 %collective-permute-start.11 = (f32[2,8,16,256]{3,2,1,0:T(8,128)S(1)}, f32[2,8,16,256]{3,2,1,0:T(8,128)S(1)}, u32[]{:S(2)}, u32[]{:S(2)}) collective-permute-start(f32[2,8,16,256]{3,2,1,0:T(8,128)S(1)} %get-tuple-element.84), channel_id=1, source_target_pairs={{1,2},{2,1},{5,6},{6,5},{9,10},{10,9},{13,14},{14,13},{17,18},{18,... | collective-permute-start | bytes 786440 | tf_op jit(solution)/shard_map/ppermute | solution.py:61
  19.7 11.9 %collective-permute-start.2 = (f32[2,8,16,256]{3,2,1,0:T(8,128)S(1)}, f32[2,8,16,256]{3,2,1,0:T(8,128)S(1)}, u32[]{:S(2)}, u32[]{:S(2)}) collective-permute-start(f32[2,8,16,256]{3,2,1,0:T(8,128)S(1)} %get-tuple-element.63), channel_id=1, source_target_pairs={{0,1},{1,0},{2,3},{3,2},{4,5},{5,4},{6,7},{7,6},{8,9},{9,8},{10,11... | collective-permute-start | bytes 786440 | tf_op jit(solution)/shard_map/ppermute | solution.py:60
  22.8 8.8 %collective-permute-start.3 = (f32[2,8,16,256]{3,2,1,0:T(8,128)S(1)}, f32[2,8,16,256]{3,2,1,0:T(8,128)S(1)}, u32[]{:S(2)}, u32[]{:S(2)}) collective-permute-start(f32[2,8,16,256]{3,2,1,0:T(8,128)S(1)} %get-tuple-element.64), channel_id=1, source_target_pairs={{1,2},{2,1},{5,6},{6,5},{9,10},{10,9},{13,14},{14,13},{17,18},{18,... | collective-permute-start | bytes 786440 | tf_op jit(solution)/shard_map/ppermute | solution.py:61
  26.9 9.9 %collective-permute-start.12 = (f32[2,8,16,256]{3,2,1,0:T(8,128)S(1)}, f32[2,8,16,256]{3,2,1,0:T(8,128)S(1)}, u32[]{:S(2)}, u32[]{:S(2)}) collective-permute-start(f32[2,8,16,256]{3,2,1,0:T(8,128)S(1)} %get-tuple-element.87), channel_id=1, source_target_pairs={{0,1},{1,0},{2,3},{3,2},{4,5},{5,4},{6,7},{7,6},{8,9},{9,8},{10,11... | collective-permute-start | bytes 786440 | tf_op jit(solution)/shard_map/ppermute | solution.py:60
  30.9 5.9 %collective-permute-start.13 = (f32[2,8,16,256]{3,2,1,0:T(8,128)S(1)}, f32[2,8,16,256]{3,2,1,0:T(8,128)S(1)}, u32[]{:S(2)}, u32[]{:S(2)}) collective-permute-start(f32[2,8,16,256]{3,2,1,0:T(8,128)S(1)} %get-tuple-element.88), channel_id=1, source_target_pairs={{1,2},{2,1},{5,6},{6,5},{9,10},{10,9},{13,14},{14,13},{17,18},{18,... | collective-permute-start | bytes 786440 | tf_op jit(solution)/shard_map/ppermute | solution.py:61
  33.1 10.2 %collective-permute-start.4 = (f32[2,8,16,256]{3,2,1,0:T(8,128)S(1)}, f32[2,8,16,256]{3,2,1,0:T(8,128)S(1)}, u32[]{:S(2)}, u32[]{:S(2)}) collective-permute-start(f32[2,8,16,256]{3,2,1,0:T(8,128)S(1)} %get-tuple-element.68), channel_id=1, source_target_pairs={{0,1},{1,0},{2,3},{3,2},{4,5},{5,4},{6,7},{7,6},{8,9},{9,8},{10,11... | collective-permute-start | bytes 786440 | tf_op jit(solution)/shard_map/ppermute | solution.py:60
  36.2 7.1 %collective-permute-start.5 = (f32[2,8,16,256]{3,2,1,0:T(8,128)S(1)}, f32[2,8,16,256]{3,2,1,0:T(8,128)S(1)}, u32[]{:S(2)}, u32[]{:S(2)}) collective-permute-start(f32[2,8,16,256]{3,2,1,0:T(8,128)S(1)} %get-tuple-element.69), channel_id=1, source_target_pairs={{1,2},{2,1},{5,6},{6,5},{9,10},{10,9},{13,14},{14,13},{17,18},{18,... | collective-permute-start | bytes 786440 | tf_op jit(solution)/shard_map/ppermute | solution.py:61
  38.4 11.3 %collective-permute-start.14 = (f32[2,8,16,256]{3,2,1,0:T(8,128)S(1)}, f32[2,8,16,256]{3,2,1,0:T(8,128)S(1)}, u32[]{:S(2)}, u32[]{:S(2)}) collective-permute-start(f32[2,8,16,256]{3,2,1,0:T(8,128)S(1)} %get-tuple-element.91), channel_id=1, source_target_pairs={{0,1},{1,0},{2,3},{3,2},{4,5},{5,4},{6,7},{7,6},{8,9},{9,8},{10,11... | collective-permute-start | bytes 786440 | tf_op jit(solution)/shard_map/ppermute | solution.py:60
  42.6 7.1 %collective-permute-start.15 = (f32[2,8,16,256]{3,2,1,0:T(8,128)S(1)}, f32[2,8,16,256]{3,2,1,0:T(8,128)S(1)}, u32[]{:S(2)}, u32[]{:S(2)}) collective-permute-start(f32[2,8,16,256]{3,2,1,0:T(8,128)S(1)} %get-tuple-element.92), channel_id=1, source_target_pairs={{1,2},{2,1},{5,6},{6,5},{9,10},{10,9},{13,14},{14,13},{17,18},{18,... | collective-permute-start | bytes 786440 | tf_op jit(solution)/shard_map/ppermute | solution.py:61
  44.8 8.4 %collective-permute-start.6 = (f32[2,8,16,256]{3,2,1,0:T(8,128)S(1)}, f32[2,8,16,256]{3,2,1,0:T(8,128)S(1)}, u32[]{:S(2)}, u32[]{:S(2)}) collective-permute-start(f32[2,8,16,256]{3,2,1,0:T(8,128)S(1)} %get-tuple-element.72), channel_id=1, source_target_pairs={{0,1},{1,0},{2,3},{3,2},{4,5},{5,4},{6,7},{7,6},{8,9},{9,8},{10,11... | collective-permute-start | bytes 786440 | tf_op jit(solution)/shard_map/ppermute | solution.py:60
  48.8 4.4 %collective-permute-start.7 = (f32[2,8,16,256]{3,2,1,0:T(8,128)S(1)}, f32[2,8,16,256]{3,2,1,0:T(8,128)S(1)}, u32[]{:S(2)}, u32[]{:S(2)}) collective-permute-start(f32[2,8,16,256]{3,2,1,0:T(8,128)S(1)} %get-tuple-element.73), channel_id=1, source_target_pairs={{1,2},{2,1},{5,6},{6,5},{9,10},{10,9},{13,14},{14,13},{17,18},{18,... | collective-permute-start | bytes 786440 | tf_op jit(solution)/shard_map/ppermute | solution.py:61
  55.0 12.2 %collective-permute-start.16 = (f32[4,8,16,256]{3,2,1,0:T(8,128)S(1)}, f32[4,8,16,256]{3,2,1,0:T(8,128)S(1)}, u32[]{:S(2)}, u32[]{:S(2)}) collective-permute-start(f32[4,8,16,256]{3,2,1,0:T(8,128)S(1)} %shard_map.132.refs_0_), channel_id=1, source_target_pairs={{0,4},{4,0},{8,12},{12,8},{1,5},{5,1},{9,13},{13,9},{2,6},{6,2},{1... | collective-permute-start | bytes 1572872 | tf_op jit(solution)/shard_map/ppermute | solution.py:546
  55.1 8.5 %collective-permute-start.17 = (f32[2,4,16,256]{3,2,1,0:T(8,128)S(1)}, f32[2,4,16,256]{3,2,1,0:T(8,128)S(1)}, u32[]{:S(2)}, u32[]{:S(2)}) collective-permute-start(f32[2,4,16,256]{3,2,1,0:T(8,128)S(1)} %get-tuple-element.95), channel_id=1, source_target_pairs={{0,1},{1,0},{2,3},{3,2},{4,5},{5,4},{6,7},{7,6},{8,9},{9,8},{10,11... | collective-permute-start | bytes 393224 | tf_op jit(solution)/shard_map/ppermute | solution.py:60
  59.1 4.5 %collective-permute-start.18 = (f32[2,4,16,256]{3,2,1,0:T(8,128)S(1)}, f32[2,4,16,256]{3,2,1,0:T(8,128)S(1)}, u32[]{:S(2)}, u32[]{:S(2)}) collective-permute-start(f32[2,4,16,256]{3,2,1,0:T(8,128)S(1)} %get-tuple-element.96), channel_id=1, source_target_pairs={{1,2},{2,1},{5,6},{6,5},{9,10},{10,9},{13,14},{14,13},{17,18},{18,... | collective-permute-start | bytes 393224 | tf_op jit(solution)/shard_map/ppermute | solution.py:61
  59.7 7.0 %collective-permute-start.19 = (f32[2,4,16,256]{3,2,1,0:T(8,128)S(1)}, f32[2,4,16,256]{3,2,1,0:T(8,128)S(1)}, u32[]{:S(2)}, u32[]{:S(2)}) collective-permute-start(f32[2,4,16,256]{3,2,1,0:T(8,128)S(1)} %get-tuple-element.97), channel_id=1, source_target_pairs={{0,1},{1,0},{2,3},{3,2},{4,5},{5,4},{6,7},{7,6},{8,9},{9,8},{10,11... | collective-permute-start | bytes 393224 | tf_op jit(solution)/shard_map/ppermute | solution.py:60
  62.9 3.8 %collective-permute-start.20 = (f32[2,4,16,256]{3,2,1,0:T(8,128)S(1)}, f32[2,4,16,256]{3,2,1,0:T(8,128)S(1)}, u32[]{:S(2)}, u32[]{:S(2)}) collective-permute-start(f32[2,4,16,256]{3,2,1,0:T(8,128)S(1)} %get-tuple-element.98), channel_id=1, source_target_pairs={{1,2},{2,1},{5,6},{6,5},{9,10},{10,9},{13,14},{14,13},{17,18},{18,... | collective-permute-start | bytes 393224 | tf_op jit(solution)/shard_map/ppermute | solution.py:61
  64.1 5.4 %collective-permute-start.21 = (f32[2,8,16,256]{3,2,1,0:T(8,128)S(1)}, f32[2,8,16,256]{3,2,1,0:T(8,128)S(1)}, u32[]{:S(2)}, u32[]{:S(2)}) collective-permute-start(f32[2,8,16,256]{3,2,1,0:T(8,128)S(1)} %shard_map.133.refs_2_.refs_0_), channel_id=1, source_target_pairs={{0,4},{4,0},{8,12},{12,8},{1,5},{5,1},{9,13},{13,9},{2,6},{6,2},{1... | collective-permute-start | bytes 786440 | tf_op jit(solution)/shard_map/ppermute | solution.py:546
  67.2 2.3 %collective-permute-start.22 = (f32[2,8,16,256]{3,2,1,0:T(8,128)S(1)}, f32[2,8,16,256]{3,2,1,0:T(8,128)S(1)}, u32[]{:S(2)}, u32[]{:S(2)}) collective-permute-start(f32[2,8,16,256]{3,2,1,0:T(8,128)S(1)} %shard_map.134.refs_3_.refs_1_), channel_id=1, source_target_pairs={{0,4},{4,0},{8,12},{12,8},{1,5},{5,1},{9,13},{13,9},{2,6},{6,2},{1... | collective-permute-start | bytes 786440 | tf_op jit(solution)/shard_map/ppermute | solution.py:546
  68.0 9.2 %collective-permute-start.23 = (f32[2,8,16,256]{3,2,1,0:T(8,128)S(1)}, f32[2,8,16,256]{3,2,1,0:T(8,128)S(1)}, u32[]{:S(2)}, u32[]{:S(2)}) collective-permute-start(f32[2,8,16,256]{3,2,1,0:T(8,128)S(1)} %shard_map.135), channel_id=1, source_target_pairs={{0,8},{4,12},{8,0},{12,4},{1,9},{5,13},{9,1},{13,5},{2,10},{6,14},... | collective-permute-start | bytes 786440 | tf_op jit(solution)/shard_map/ppermute | solution.py:553
  70.2 12.0 %collective-permute-start.24 = (f32[2,8,16,256]{3,2,1,0:T(8,128)S(1)}, f32[2,8,16,256]{3,2,1,0:T(8,128)S(1)}, u32[]{:S(2)}, u32[]{:S(2)}) collective-permute-start(f32[2,8,16,256]{3,2,1,0:T(8,128)S(1)} %shard_map.136), channel_id=1, source_target_pairs={{0,8},{4,12},{8,0},{12,4},{1,9},{5,13},{9,1},{13,5},{2,10},{6,14},... | collective-permute-start | bytes 786440 | tf_op jit(solution)/shard_map/ppermute | solution.py:553
